TPU v7x, 32 devices: a whole 2x2x4 slice. The times are simulated.
32 devices in a mesh: rep: 2 (over x), fsdp: 16 (over z, y, core).
Axes of the slice: x: 2, y: 2, z: 4, core: 2. Of those that a mesh axis runs over, the one named last changes fastest.
Arguments:
- tokens: bfloat16 [4096, 1536], P(('rep', 'fsdp')), may hold values from -6 to 6
- cotangent: bfloat16 [4096, 1536], P(('rep', 'fsdp')), may hold values from -6 to 6
- positions: int32 [4096], P(('rep', 'fsdp')), may hold values from 0 to 2047
- segments: int32 [2, 2048], P('rep'), may hold values from 0 to 7, never falling along the last dimension, each value on 1 to 1536 neighbouring positions
- routes: int32 [2, 4096, 8], P(None, ('rep', 'fsdp')), may hold values from 0 to 15, all different within a row; in each aligned block of 128 rows (0 to 127, 128 to 255, ..., all dimensions but the last counted through in order) at most 96 rows name the same one
- attn_gain: bfloat16 [2, 1536], P(None, 'fsdp'), may hold values from 0.5 to 1.5
- w_query: bfloat16 [2, 1536, 1536], P(None, 'fsdp'), may hold values from -0.15625 to 0.15625
- w_key: bfloat16 [2, 1536, 512], P(None, 'fsdp'), may hold values from -0.15625 to 0.15625
- w_value: bfloat16 [2, 1536, 512], P(None, 'fsdp'), may hold values from -0.15625 to 0.15625
- w_out: bfloat16 [2, 1536, 1536], P(None, 'fsdp'), may hold values from -0.875 to 0.875
- ffn_gain: bfloat16 [2, 1536], P(None, 'fsdp'), may hold values from 0.5 to 1.5
- router: bfloat16 [2, 1536, 16], P(None, 'fsdp'), may hold values from -0.078125 to 0.078125
- w_gate: bfloat16 [2, 16, 1536, 512], P(None, 'fsdp'), may hold values from -0.15625 to 0.15625
- w_up: bfloat16 [2, 16, 1536, 512], P(None, 'fsdp'), may hold values from -0.15625 to 0.15625
- w_down: bfloat16 [2, 16, 512, 1536], P(None, 'fsdp'), may hold values from -1 to 1
Outputs:
- activations: bfloat16 [4096, 1536], P(('rep', 'fsdp'))
- grad_tokens: float32 [4096, 1536], P(('rep', 'fsdp'))
- grad_attn_gain: float32 [2, 1536], P(None, 'fsdp')
- grad_w_query: float32 [2, 1536, 1536], P(None, 'fsdp')
- grad_w_key: float32 [2, 1536, 512], P(None, 'fsdp')
- grad_w_value: float32 [2, 1536, 512], P(None, 'fsdp')
- grad_w_out: float32 [2, 1536, 1536], P(None, 'fsdp')
- grad_ffn_gain: float32 [2, 1536], P(None, 'fsdp')
- grad_router: float32 [2, 1536, 16], P(None, 'fsdp')
- grad_w_gate: float32 [2, 16, 1536, 512], P(None, 'fsdp')
- grad_w_up: float32 [2, 16, 1536, 512], P(None, 'fsdp')
- grad_w_down: float32 [2, 16, 512, 1536], P(None, 'fsdp')
Inputs may be any that keep to these rules, and one draw needn't show every extreme that they name: `routes`: in each block of 128 rows of one layer (the rows of one device) no expert is named by more than 96 rows, and this most is reached. `segments`: within a sequence segment ids never fall; a document has at most 1536 tokens, and some document of every sequence has exactly that many.
All inputs are finite; a program needn't handle non-finite values.
Results may differ from a plain program's by a relative error of at most 0.03.
Values may be sent and summed in bfloat16 or wider, within the bound.
A program may use at most 256 MiB of HBM per device.

v0:
```python
from functools import partial
import math

import jax
import jax.numpy as jnp
from jax import lax
from jax.sharding import PartitionSpec as P

HEADS = 24
KV_HEADS = 8
HD = 64
LAYERS = 2


epsilon = 1e-06
masked_value = -1e30
highest = lax.Precision.HIGHEST


def rope_tables(positions, half_width):
    frequency = jnp.exp(-jnp.log(10000.0) * jnp.arange(half_width, dtype=jnp.float32) / half_width)
    angles = positions.astype(jnp.float32)[:, None] * frequency[None, :]
    return (jnp.cos(angles), jnp.sin(angles))


def rotate(field, cosine, sine_table, direction):
    half_width = field.shape[-1] // 2
    first_half = field[..., :half_width]
    second_half = field[..., half_width:]
    cos_rows = cosine[:, None, :]
    sin_rows = direction * sine_table[:, None, :]
    return jnp.concatenate(
        [
            first_half * cos_rows - second_half * sin_rows,
            second_half * cos_rows + first_half * sin_rows,
        ],
        -1,
    )


def keep_same(current):
    return current


def allowed_pairs(mask_args, offset, key_width):
    query_index, query_segment, segment_flat, seq_width = mask_args
    key_index = offset + jnp.arange(key_width, dtype=jnp.int32)
    key_segment = lax.dynamic_slice_in_dim(segment_flat, offset, key_width)
    same_doc = query_segment[:, None] == key_segment[None, :]
    same_seq = query_index[:, None] // seq_width == key_index[None, :] // seq_width
    return same_doc & same_seq & (key_index[None, :] <= query_index[:, None])


def head_rows(table, offset, key_width):
    return lax.dynamic_slice_in_dim(table, offset, key_width, 0).reshape(key_width, KV_HEADS, HD)


def block_scores(query_heads, key_rows):
    return jnp.einsum(
        "grtd,kgd->grtk", query_heads, key_rows, preferred_element_type=jnp.float32
    ) / math.sqrt(HD)


def attention_forward(query_heads, keys_all, values_all, mask_args):
    group_rows = keys_all.shape[0]
    key_width = math.gcd(group_rows, 512)
    head_shape = query_heads.shape[:3]
    numbers = jnp.arange(group_rows // key_width, dtype=jnp.int32)

    def max_step(running, block_number):
        offset = block_number * key_width
        allowed = allowed_pairs(mask_args, offset, key_width)

        def max_active(current):
            run_max, run_total = current
            scores = block_scores(query_heads, head_rows(keys_all, offset, key_width))
            new_max = jnp.maximum(run_max, jnp.max(jnp.where(allowed, scores, masked_value), -1))
            weights = jnp.where(allowed, jnp.exp(scores - new_max[..., None]), 0.0)
            return (new_max, run_total * jnp.exp(run_max - new_max) + jnp.sum(weights, -1))

        return (lax.cond(jnp.any(allowed), max_active, keep_same, running), None)

    start_max = jnp.full(head_shape, masked_value, jnp.float32)
    (run_max, run_total), _ = lax.scan(
        max_step, (start_max, jnp.zeros(head_shape, jnp.float32)), numbers
    )
    log_total = run_max + jnp.log(run_total)

    def value_step(running, block_number):
        offset = block_number * key_width
        allowed = allowed_pairs(mask_args, offset, key_width)

        def value_active(current):
            scores = block_scores(query_heads, head_rows(keys_all, offset, key_width))
            probabilities = jnp.where(allowed, jnp.exp(scores - log_total[..., None]), 0.0).astype(
                jnp.bfloat16
            )
            return current + jnp.einsum(
                "grtk,kgd->grtd",
                probabilities,
                head_rows(values_all, offset, key_width),
                preferred_element_type=jnp.float32,
            )

        return (lax.cond(jnp.any(allowed), value_active, keep_same, running), None)

    attended, _ = lax.scan(value_step, jnp.zeros(query_heads.shape, jnp.float32), numbers)
    return (log_total, attended)


def attention_backward(query_heads, keys_all, values_all, log_total, grad_heads, mask_args):
    group_rows = keys_all.shape[0]
    key_width = math.gcd(group_rows, 512)
    head_shape = query_heads.shape[:3]
    numbers = jnp.arange(group_rows // key_width, dtype=jnp.int32)
    scale = 1.0 / math.sqrt(HD)

    def block_terms(offset, allowed):
        key_rows = head_rows(keys_all, offset, key_width)
        value_rows = head_rows(values_all, offset, key_width)
        probabilities = jnp.where(
            allowed, jnp.exp(block_scores(query_heads, key_rows) - log_total[..., None]), 0.0
        )
        grad_probs = jnp.einsum(
            "grtd,kgd->grtk", grad_heads, value_rows, preferred_element_type=jnp.float32
        )
        return (key_rows, probabilities, grad_probs)

    def delta_step(running, block_number):
        offset = block_number * key_width
        allowed = allowed_pairs(mask_args, offset, key_width)

        def delta_active(current):
            key_rows, probabilities, grad_probs = block_terms(offset, allowed)
            return current + jnp.sum(probabilities * grad_probs, -1)

        return (lax.cond(jnp.any(allowed), delta_active, keep_same, running), None)

    row_delta, _ = lax.scan(delta_step, jnp.zeros(head_shape, jnp.float32), numbers)

    def grad_step(running, block_number):
        offset = block_number * key_width
        allowed = allowed_pairs(mask_args, offset, key_width)

        def grad_active(current):
            grad_query, grad_keys, grad_values = current
            key_rows, probabilities, grad_probs = block_terms(offset, allowed)
            grad_scores = (probabilities * (grad_probs - row_delta[..., None])).astype(jnp.bfloat16)
            grad_query = (
                grad_query
                + jnp.einsum(
                    "grtk,kgd->grtd", grad_scores, key_rows, preferred_element_type=jnp.float32
                )
                * scale
            )
            key_part = (
                jnp.einsum(
                    "grtk,grtd->kgd", grad_scores, query_heads, preferred_element_type=jnp.float32
                )
                * scale
            )
            value_part = jnp.einsum(
                "grtk,grtd->kgd",
                probabilities.astype(jnp.bfloat16),
                grad_heads,
                preferred_element_type=jnp.float32,
            )
            grad_keys = lax.dynamic_update_slice_in_dim(
                grad_keys, key_part.reshape(key_width, KV_HEADS * HD), offset, 0
            )
            grad_values = lax.dynamic_update_slice_in_dim(
                grad_values, value_part.reshape(key_width, KV_HEADS * HD), offset, 0
            )
            return (grad_query, grad_keys, grad_values)

        return (lax.cond(jnp.any(allowed), grad_active, keep_same, running), None)

    empty_rows = jnp.zeros((group_rows, KV_HEADS * HD), jnp.float32)
    results, _ = lax.scan(
        grad_step, (jnp.zeros(query_heads.shape, jnp.float32), empty_rows, empty_rows), numbers
    )
    return results


def route_slots(route_rows, experts, capacity):
    token_count, top = route_rows.shape
    onehot = route_rows[:, :, None] == jnp.arange(experts, dtype=jnp.int32)[None, None, :]
    per_token = jnp.sum(onehot.astype(jnp.int32), 1)
    earlier = jnp.cumsum(per_token, 0) - per_token
    slot_index = route_rows * capacity + jnp.sum(jnp.where(onehot, earlier[:, None, :], 0), -1)
    flat_slot = slot_index.reshape(-1)
    entries = jnp.arange(token_count * top, dtype=jnp.int32)
    token_table = (
        jnp.full((experts * capacity,), token_count, jnp.int32).at[flat_slot].set(entries // top)
    )
    entry_table = (
        jnp.full((experts * capacity,), token_count * top, jnp.int32).at[flat_slot].set(entries)
    )
    return (onehot, flat_slot, token_table, entry_table)


def expert_apply(gate_w, up_w, down_w, received):
    local_count = gate_w.shape[0]
    grouped = received.reshape(-1, local_count, received.shape[1], received.shape[2])
    act_gate = jnp.einsum("sjcd,jdf->sjcf", grouped, gate_w, preferred_element_type=jnp.float32)
    act_up = jnp.einsum("sjcd,jdf->sjcf", grouped, up_w, preferred_element_type=jnp.float32)
    hidden = (jax.nn.silu(act_gate) * act_up).astype(jnp.bfloat16)
    output = jnp.einsum(
        "sjcf,jfd->sjcd", hidden, down_w, preferred_element_type=jnp.float32
    ).astype(jnp.bfloat16)
    returned = lax.all_to_all(
        output.reshape(received.shape), "fsdp", split_axis=0, concat_axis=0, tiled=True
    )
    return (returned, received)


def expert_backward(gate_w, up_w, down_w, received, arrived):
    local_count = gate_w.shape[0]
    grouped_shape = (-1, local_count, received.shape[1], received.shape[2])
    grouped = received.reshape(grouped_shape)
    incoming = arrived.reshape(grouped_shape)
    act_gate = jnp.einsum("sjcd,jdf->sjcf", grouped, gate_w, preferred_element_type=jnp.float32)
    act_up = jnp.einsum("sjcd,jdf->sjcf", grouped, up_w, preferred_element_type=jnp.float32)
    sigmoid_gate = jax.nn.sigmoid(act_gate)
    swish = act_gate * sigmoid_gate
    hidden = (swish * act_up).astype(jnp.bfloat16)
    grad_hidden = jnp.einsum("sjcd,jfd->sjcf", incoming, down_w, preferred_element_type=jnp.float32)
    grad_gate_act = (
        grad_hidden * act_up * sigmoid_gate * (1.0 + act_gate * (1.0 - sigmoid_gate))
    ).astype(jnp.bfloat16)
    grad_up_act = (grad_hidden * swish).astype(jnp.bfloat16)
    grad_inputs = jnp.einsum(
        "sjcf,jdf->sjcd", grad_gate_act, gate_w, preferred_element_type=jnp.float32
    ) + jnp.einsum("sjcf,jdf->sjcd", grad_up_act, up_w, preferred_element_type=jnp.float32)
    grad_gate_w = jnp.einsum(
        "sjcd,sjcf->jdf", grouped, grad_gate_act, preferred_element_type=jnp.float32
    )
    grad_up_w = jnp.einsum(
        "sjcd,sjcf->jdf", grouped, grad_up_act, preferred_element_type=jnp.float32
    )
    grad_down_w = jnp.einsum("sjcf,sjcd->jfd", hidden, incoming, preferred_element_type=jnp.float32)
    return (grad_inputs.reshape(received.shape), grad_gate_w, grad_up_w, grad_down_w)


def on_device(
    tokens,
    cotangent,
    positions,
    segments,
    routes,
    attn_gain,
    w_query,
    w_key,
    w_value,
    w_out,
    ffn_gain,
    router,
    w_gate,
    w_up,
    w_down,
):
    row_count, model_width = tokens.shape
    fsdp_size = lax.axis_size("fsdp")
    my_index = lax.axis_index("fsdp")
    experts = w_gate.shape[1] * fsdp_size
    top = routes.shape[2]
    capacity = min(row_count, 3 * row_count * top // (2 * experts))
    seq_width = segments.shape[1]
    segment_flat = segments.reshape(-1)
    query_index = my_index * row_count + jnp.arange(row_count, dtype=jnp.int32)
    query_segment = lax.dynamic_slice_in_dim(segment_flat, my_index * row_count, row_count)
    mask_args = (query_index, query_segment, segment_flat, seq_width)
    cosine, sine_table = rope_tables(positions, HD // 2)
    group_heads = HEADS // KV_HEADS
    kv_width = KV_HEADS * HD
    residual = tokens.astype(jnp.float32)
    saved = []
    for layer_index in range(LAYERS):
        fetched = (
            lax.all_gather(attn_gain[layer_index], "fsdp", axis=0, tiled=True),
            lax.all_gather(w_query[layer_index], "fsdp", axis=0, tiled=True),
            lax.all_gather(w_key[layer_index], "fsdp", axis=0, tiled=True),
            lax.all_gather(w_value[layer_index], "fsdp", axis=0, tiled=True),
            lax.all_gather(w_out[layer_index], "fsdp", axis=0, tiled=True),
            lax.all_gather(ffn_gain[layer_index], "fsdp", axis=0, tiled=True),
            lax.all_gather(router[layer_index], "fsdp", axis=0, tiled=True),
        )
        gain_one, query_w, key_w, value_w, out_w, gain_two, router_w = fetched
        inverse_one = lax.rsqrt(jnp.mean(residual * residual, -1, keepdims=True) + epsilon)
        normed_one = residual * inverse_one
        x_attn = (normed_one * gain_one.astype(jnp.float32)).astype(jnp.bfloat16)
        query_pre = jnp.dot(x_attn, query_w, preferred_element_type=jnp.float32).reshape(
            row_count, HEADS, HD
        )
        query_rot = rotate(query_pre, cosine, sine_table, 1.0).astype(jnp.bfloat16)
        query_heads = query_rot.reshape(row_count, KV_HEADS, group_heads, HD).transpose(1, 2, 0, 3)
        key_pre = jnp.dot(x_attn, key_w, preferred_element_type=jnp.float32).reshape(
            row_count, KV_HEADS, HD
        )
        key_rot = (
            rotate(key_pre, cosine, sine_table, 1.0)
            .astype(jnp.bfloat16)
            .reshape(row_count, kv_width)
        )
        value_rows = jnp.dot(x_attn, value_w, preferred_element_type=jnp.float32).astype(
            jnp.bfloat16
        )
        keys_all, values_all = (
            lax.all_gather(key_rot, "fsdp", axis=0, tiled=True),
            lax.all_gather(value_rows, "fsdp", axis=0, tiled=True),
        )
        log_total, attended = attention_forward(query_heads, keys_all, values_all, mask_args)
        attended_rows = (
            attended.transpose(2, 0, 1, 3).reshape(row_count, model_width).astype(jnp.bfloat16)
        )
        middle = residual + jnp.dot(attended_rows, out_w, preferred_element_type=jnp.float32)
        inverse_two = lax.rsqrt(jnp.mean(middle * middle, -1, keepdims=True) + epsilon)
        normed_two = middle * inverse_two
        x_moe = (normed_two * gain_two.astype(jnp.float32)).astype(jnp.bfloat16)
        onehot, flat_slot, token_table, entry_table = route_slots(
            routes[layer_index], experts, capacity
        )
        logits = jnp.dot(x_moe, router_w, preferred_element_type=jnp.float32)
        chosen = jnp.sum(jnp.where(onehot, logits[:, None, :], 0.0), -1)
        gate_values = jax.nn.softmax(chosen, axis=-1)
        padded_rows = jnp.concatenate([x_moe, jnp.zeros((1, model_width), jnp.bfloat16)], 0)
        send_rows = padded_rows[token_table].reshape(experts, capacity, model_width)
        apply_layer = partial(
            expert_apply, w_gate[layer_index], w_up[layer_index], w_down[layer_index]
        )
        returned, received = apply_layer(
            lax.all_to_all(send_rows, "fsdp", split_axis=0, concat_axis=0, tiled=True)
        )
        slot_values = (
            returned.reshape(experts * capacity, model_width)[flat_slot]
            .reshape(row_count, top, model_width)
            .astype(jnp.float32)
        )
        mixed = jnp.sum(gate_values[:, :, None] * slot_values, 1)
        saved.append(
            (
                fetched,
                inverse_one,
                normed_one,
                x_attn,
                query_heads,
                keys_all,
                values_all,
                log_total,
                attended_rows,
                inverse_two,
                normed_two,
                x_moe,
                onehot,
                flat_slot,
                entry_table,
                gate_values,
                slot_values,
                received,
            )
        )
        residual = middle + mixed
    activations = residual.astype(jnp.bfloat16)
    grad_residual = cotangent.astype(jnp.float32)
    layer_grads = [None] * LAYERS
    for layer_index in reversed(range(LAYERS)):
        (
            fetched,
            inverse_one,
            normed_one,
            x_attn,
            query_heads,
            keys_all,
            values_all,
            log_total,
            attended_rows,
            inverse_two,
            normed_two,
            x_moe,
            onehot,
            flat_slot,
            entry_table,
            gate_values,
            slot_values,
            received,
        ) = saved[layer_index]
        gain_one, query_w, key_w, value_w, out_w, gain_two, router_w = (
            lax.all_gather(attn_gain[layer_index], "fsdp", axis=0, tiled=True),
            lax.all_gather(w_query[layer_index], "fsdp", axis=0, tiled=True),
            lax.all_gather(w_key[layer_index], "fsdp", axis=0, tiled=True),
            lax.all_gather(w_value[layer_index], "fsdp", axis=0, tiled=True),
            lax.all_gather(w_out[layer_index], "fsdp", axis=0, tiled=True),
            lax.all_gather(ffn_gain[layer_index], "fsdp", axis=0, tiled=True),
            lax.all_gather(router[layer_index], "fsdp", axis=0, tiled=True),
        )
        grad_mix = lax.optimization_barrier(grad_residual.astype(jnp.bfloat16)).astype(jnp.float32)
        grad_gate = jnp.sum(slot_values * grad_mix[:, None, :], -1)
        slot_grads = (
            (gate_values[:, :, None] * grad_mix[:, None, :])
            .astype(jnp.bfloat16)
            .reshape(row_count * top, model_width)
        )
        padded_grads = jnp.concatenate([slot_grads, jnp.zeros((1, model_width), jnp.bfloat16)], 0)
        send_grads = padded_grads[entry_table].reshape(experts, capacity, model_width)
        arrived = lax.all_to_all(send_grads, "fsdp", split_axis=0, concat_axis=0, tiled=True)
        grad_inputs, grad_gate_w, grad_up_w, grad_down_w = expert_backward(
            w_gate[layer_index], w_up[layer_index], w_down[layer_index], received, arrived
        )
        grad_back = lax.all_to_all(
            grad_inputs.astype(jnp.bfloat16), "fsdp", split_axis=0, concat_axis=0, tiled=True
        ).astype(grad_inputs.dtype)
        grad_moe = jnp.sum(
            grad_back.reshape(experts * capacity, model_width)[flat_slot].reshape(
                row_count, top, model_width
            ),
            1,
        )
        grad_chosen = gate_values * (
            grad_gate - jnp.sum(gate_values * grad_gate, -1, keepdims=True)
        )
        grad_logits = jnp.sum(jnp.where(onehot, grad_chosen[:, :, None], 0.0), 1)
        grad_x_moe = grad_moe + jnp.dot(
            grad_logits, router_w.astype(jnp.float32).T, precision=highest
        )
        grad_norm_two = grad_x_moe * gain_two.astype(jnp.float32)
        grad_middle = grad_residual + inverse_two * (
            grad_norm_two - normed_two * jnp.mean(grad_norm_two * normed_two, -1, keepdims=True)
        )
        grad_branch = lax.optimization_barrier(grad_middle.astype(jnp.bfloat16))
        grad_attended = jnp.dot(grad_branch, out_w.T, preferred_element_type=jnp.float32).astype(
            jnp.bfloat16
        )
        grad_heads = grad_attended.reshape(row_count, KV_HEADS, group_heads, HD).transpose(
            1, 2, 0, 3
        )
        grad_query, grad_keys, grad_values = attention_backward(
            query_heads, keys_all, values_all, log_total, grad_heads, mask_args
        )
        own_keys, own_values = (
            lax.psum_scatter(
                grad_keys.astype(jnp.bfloat16), "fsdp", scatter_dimension=0, tiled=True
            ).astype(jnp.float32),
            lax.psum_scatter(
                grad_values.astype(jnp.bfloat16), "fsdp", scatter_dimension=0, tiled=True
            ).astype(jnp.float32),
        )
        query_rows = grad_query.transpose(2, 0, 1, 3).reshape(row_count, HEADS, HD)
        grad_q_rows = (
            rotate(query_rows, cosine, sine_table, -1.0)
            .astype(jnp.bfloat16)
            .reshape(row_count, model_width)
        )
        grad_k_rows = (
            rotate(own_keys.reshape(row_count, KV_HEADS, HD), cosine, sine_table, -1.0)
            .astype(jnp.bfloat16)
            .reshape(row_count, kv_width)
        )
        grad_v_rows = own_values.astype(jnp.bfloat16)
        grad_x_attn = (
            jnp.dot(grad_q_rows, query_w.T, preferred_element_type=jnp.float32)
            + jnp.dot(grad_k_rows, key_w.T, preferred_element_type=jnp.float32)
            + jnp.dot(grad_v_rows, value_w.T, preferred_element_type=jnp.float32)
        )
        grad_norm_one = grad_x_attn * gain_one.astype(jnp.float32)
        grad_previous = grad_middle + inverse_one * (
            grad_norm_one - normed_one * jnp.mean(grad_norm_one * normed_one, -1, keepdims=True)
        )
        projection_grads = jnp.concatenate([grad_q_rows, grad_k_rows, grad_v_rows], 1)
        gain_one_terms = grad_x_attn * normed_one
        gain_two_terms = grad_x_moe * normed_two
        moe_cols = x_moe.astype(jnp.float32)
        projections = jnp.einsum(
            "tc,tw->cw", x_attn, projection_grads, preferred_element_type=jnp.float32
        )
        outputs = jnp.einsum(
            "tc,tw->cw", attended_rows, grad_branch, preferred_element_type=jnp.float32
        )
        routing = jnp.einsum("tc,te->ce", moe_cols, grad_logits, precision=highest)
        grad_block = lax.psum_scatter(
            jnp.concatenate(
                [
                    projections,
                    outputs,
                    routing,
                    jnp.sum(gain_one_terms, 0)[:, None],
                    jnp.sum(gain_two_terms, 0)[:, None],
                ],
                1,
            ).astype(jnp.bfloat16),
            "fsdp",
            scatter_dimension=0,
            tiled=True,
        ).astype(jnp.float32)
        edge_key = model_width + kv_width
        edge_value = edge_key + kv_width
        edge_out = edge_value + model_width
        edge_router = edge_out + experts
        grad_one = grad_block[:, edge_router]
        grad_query_w = grad_block[:, :model_width]
        grad_key_w = grad_block[:, model_width:edge_key]
        grad_value_w = grad_block[:, edge_key:edge_value]
        grad_out_w = grad_block[:, edge_value:edge_out]
        grad_two = grad_block[:, edge_router + 1]
        grad_router_w = grad_block[:, edge_out:edge_router]
        layer_grads[layer_index] = (
            grad_one,
            grad_query_w,
            grad_key_w,
            grad_value_w,
            grad_out_w,
            grad_two,
            grad_router_w,
            grad_gate_w,
            grad_up_w,
            grad_down_w,
        )
        grad_residual = grad_previous
    (
        stacked_one,
        stacked_query,
        stacked_key,
        stacked_value,
        stacked_out,
        stacked_two,
        stacked_router,
        stacked_gate,
        stacked_up,
        stacked_down,
    ) = [jnp.stack([entry[position] for entry in layer_grads]) for position in range(10)]
    (
        stacked_one,
        stacked_query,
        stacked_key,
        stacked_value,
        stacked_out,
        stacked_two,
        stacked_router,
        stacked_gate,
        stacked_up,
        stacked_down,
    ) = (
        lax.psum(stacked_one.astype(jnp.bfloat16), "rep").astype(jnp.float32),
        lax.psum(stacked_query.astype(jnp.bfloat16), "rep").astype(jnp.float32),
        lax.psum(stacked_key.astype(jnp.bfloat16), "rep").astype(jnp.float32),
        lax.psum(stacked_value.astype(jnp.bfloat16), "rep").astype(jnp.float32),
        lax.psum(stacked_out.astype(jnp.bfloat16), "rep").astype(jnp.float32),
        lax.psum(stacked_two.astype(jnp.bfloat16), "rep").astype(jnp.float32),
        lax.psum(stacked_router.astype(jnp.bfloat16), "rep").astype(jnp.float32),
        lax.psum(stacked_gate.astype(jnp.bfloat16), "rep").astype(jnp.float32),
        lax.psum(stacked_up.astype(jnp.bfloat16), "rep").astype(jnp.float32),
        lax.psum(stacked_down.astype(jnp.bfloat16), "rep").astype(jnp.float32),
    )
    return (
        activations,
        grad_residual,
        stacked_one,
        stacked_query,
        stacked_key,
        stacked_value,
        stacked_out,
        stacked_two,
        stacked_router,
        stacked_gate,
        stacked_up,
        stacked_down,
    )


def solution(mesh):
    placed = (
        P(("rep", "fsdp"), None),
        P(("rep", "fsdp"), None),
        P(("rep", "fsdp")),
        P("rep", None),
        P(None, ("rep", "fsdp"), None),
        P(None, "fsdp"),
        P(None, "fsdp", None),
        P(None, "fsdp", None),
        P(None, "fsdp", None),
        P(None, "fsdp", None),
        P(None, "fsdp"),
        P(None, "fsdp", None),
        P(None, "fsdp", None, None),
        P(None, "fsdp", None, None),
        P(None, "fsdp", None, None),
    )
    return jax.shard_map(
        on_device,
        mesh=mesh,
        in_specs=placed,
        out_specs=(
            P(("rep", "fsdp"), None),
            P(("rep", "fsdp"), None),
            P(None, "fsdp"),
            P(None, "fsdp", None),
            P(None, "fsdp", None),
            P(None, "fsdp", None),
            P(None, "fsdp", None),
            P(None, "fsdp"),
            P(None, "fsdp", None),
            P(None, "fsdp", None, None),
            P(None, "fsdp", None, None),
            P(None, "fsdp", None, None),
        ),
        check_vma=False,
    )
```

profile of v0, /device:TPU:0, one launch (start us, length us, event | category | flops | bytes accessed | tf_op | source)
XLA Modules:
  0.0 2665.1 jit_solution(5443889740318834024)
XLA Ops:
  15.0 63.4 %all-reduce.8 = (bf16[1536]{0:T(1024)(128)(2,1)S(1)}, bf16[1536]{0:T(1024)(128)(2,1)S(1)}, bf16[1536]{0:T(1024)(128)(2,1)S(1)}, bf16[1536]{0:T(1024)(128)(2,1)S(1)}) all-reduce(bf16[1536]{0:T(1024)(128)(2,1)S(1)} %dynamic-update-slice, bf16[1536]{0:T(1024)(128)(2,1)S(1)} %dynamic-update-slice.1, ...), channel_id=2, replica_groups=mesh['rep'=2,'fsdp'=16] {'fsdp'}, use_global_device_ids=true, to_apply=%add.4 | all-reduce | flops 6144 | bytes 24576
  84.1 10.8 all-gather.35.cloned.1.call-done
  104.7 33.3 %all-gather.29.cloned.1.call-done = bf16[2048,512]{1,0:T(8,128)(2,1)} async-done(((bf16[128,512]{1,0:T(8,128)(2,1)}), bf16[2048,512]{1,0:T(8,128)(2,1)}) %all-gather.29.cloned.1.call-update) | async-done | bytes 2097168 | tf_op jit(solution)/shard_map/all_gather | solution.py:310
  141.9 50.9 %all-gather.37.cloned.1.call-done = bf16[1,1536,1536]{2,1,0:T(8,128)(2,1)} async-done(((bf16[1,96,1536]{2,1,0:T(8,128)(2,1)}), bf16[1,1536,1536]{2,1,0:T(8,128)(2,1)}) %all-gather.37.cloned.1.call-update) | async-done | bytes 4718608 | tf_op jit(solution)/shard_map/all_gather | solution.py:281
  197.4 37.9 %all-gather.27.cloned.1.call-done = bf16[2048,512]{0,1:T(8,128)(2,1)} async-done(((bf16[128,512]{0,1:T(8,128)(2,1)}), bf16[2048,512]{0,1:T(8,128)(2,1)}) %all-gather.27.cloned.1.call-update) | async-done | bytes 2097168 | tf_op jit(solution)/shard_map/all_gather | solution.py:309
  235.2 15.5 while.144
  251.5 16.0 while.145
  267.6 22.7 all-gather.41.cloned.1.call-done
  307.5 94.8 %all-to-all-done = bf16[16,96,1536]{2,1,0:T(8,128)(2,1)} async-done(((bf16[16,96,1536]{2,1,0:T(8,128)(2,1)}), bf16[16,96,1536]{2,1,0:T(8,128)(2,1)}, u32[]{:S(2)}, u32[]{:S(2)}) %all-to-all-start) | async-done | bytes 4718624 | tf_op jit(solution)/shard_map/all_to_all | solution.py:332
  420.8 25.1 all-to-all-start.1
  446.8 122.7 %all-gather.6 = bf16[1,1536,16]{2,0,1:T(2,128)(2,1)S(1)} all-gather(bf16[1,96,16]{2,0,1:T(2,128)(2,1)S(1)} %copy.375), channel_id=8, replica_groups=mesh['rep'=2,'fsdp'=16] {'fsdp'}, dimensions={1}, use_global_device_ids=true | all-gather | bytes 52224 | tf_op jit(solution)/shard_map/all_gather | solution.py:286
  571.4 9.6 gather_fusion.1
  600.7 49.2 %all-gather.33.cloned.1.call-done = bf16[2048,512]{1,0:T(8,128)(2,1)} async-done(((bf16[128,512]{1,0:T(8,128)(2,1)}), bf16[2048,512]{1,0:T(8,128)(2,1)}) %all-gather.33.cloned.1.call-update) | async-done | bytes 2097168 | tf_op jit(solution)/shard_map/all_gather | solution.py:310
  653.8 38.8 %all-gather.31.cloned.1.call-done = bf16[2048,512]{0,1:T(8,128)(2,1)} async-done(((bf16[128,512]{0,1:T(8,128)(2,1)}), bf16[2048,512]{0,1:T(8,128)(2,1)}) %all-gather.31.cloned.1.call-update) | async-done | bytes 2097168 | tf_op jit(solution)/shard_map/all_gather | solution.py:309
  692.6 15.5 while.146
  708.8 16.0 while.147
  725.0 22.7 all-gather.49.cloned.1.call-done
  763.6 99.2 %all-gather.13 = bf16[1,1536,16]{2,0,1:T(2,128)(2,1)S(1)} all-gather(bf16[1,96,16]{2,0,1:T(2,128)(2,1)S(1)} %copy.376), channel_id=15, replica_groups=mesh['rep'=2,'fsdp'=16] {'fsdp'}, dimensions={1}, use_global_device_ids=true | all-gather | bytes 52224 | tf_op jit(solution)/shard_map/all_gather | solution.py:286
  875.2 21.8 all-to-all-start.4
  897.0 6.8 fusion.211
  910.5 73.3 %all-to-all-done.4 = bf16[16,96,1536]{2,1,0:T(8,128)(2,1)} async-done(((bf16[16,96,1536]{2,1,0:T(8,128)(2,1)}), bf16[16,96,1536]{2,1,0:T(8,128)(2,1)}, u32[]{:S(2)}, u32[]{:S(2)}) %all-to-all-start.4) | async-done | bytes 4718624 | tf_op jit(solution)/shard_map/all_to_all | solution.py:405
  983.8 8.4 fusion.195
  997.5 22.5 all-to-all-start.3
  1028.6 78.3 %all-to-all-done.3 = bf16[16,96,1536]{2,1,0:T(8,128)(2,1)} async-done(((bf16[16,96,1536]{2,1,0:T(8,128)(2,1)}), bf16[16,96,1536]{2,1,0:T(8,128)(2,1)}, u32[]{:S(2)}, u32[]{:S(2)}) %all-to-all-start.3) | async-done | bytes 4718624 | tf_op jit(solution)/shard_map/all_to_all | solution.py:211
  1106.8 21.8 all-to-all-start.5
  1129.1 9.6 gather_fusion.3
  1143.2 72.2 %all-to-all-done.5 = bf16[16,96,1536]{2,1,0:T(8,128)(2,1)} async-done(((bf16[16,96,1536]{2,1,0:T(8,128)(2,1)}), bf16[16,96,1536]{2,1,0:T(8,128)(2,1)}, u32[]{:S(2)}, u32[]{:S(2)}) %all-to-all-start.5) | async-done | bytes 4718624 | tf_op jit(solution)/shard_map/all_to_all | solution.py:409
  1215.4 7.4 bitcast_convert_fusion.1
  1222.8 11.4 gather_fusion.5
  1246.3 17.2 while.148
  1266.7 40.7 %while.149 = (s32[]{:T(128)}, f32[8,3,128,64]{2,3,1,0:T(8,128)S(1)}, bf16[2048,512]{0,1:T(8,128)(2,1)}, bf16[2048,512]{0,1:T(8,128)(2,1)}, s32[128]{0:T(128)S(1)...) while((s32[]{:T(128)}, f32[8,3,128,64]{2,3,1,0:T(8,128)S(1)}, ...), condition=%wide.region_60.61_spmd.clone.clone, body=%wide.region_56.60_spmd.clone.clone.sunk | while | flops 1023682688 | bytes 75797680 | solution.py:179
  1270.5 26.3 conditional.37
  1326.5 150.2 %reduce-scatter.19.cloned.1.call-done = bf16[128,512]{1,0:T(8,128)(2,1)} async-done(((bf16[2048,512]{1,0:T(8,128)(2,1)}), bf16[128,512]{1,0:T(8,128)(2,1)}) %reduce-scatter.19.cloned.1.call-update) | async-done | bytes 131088
  1481.8 60.2 %reduce-scatter.21.cloned.1.call-done = bf16[128,512]{1,0:T(8,128)(2,1)} async-done(((bf16[2048,512]{1,0:T(8,128)(2,1)}), bf16[128,512]{1,0:T(8,128)(2,1)}) %reduce-scatter.21.cloned.1.call-update) | async-done | bytes 131088
  1555.6 108.0 %all_to_all.40 = bf16[16,96,1536]{2,1,0:T(8,128)(2,1)S(1)} all-to-all(bf16[16,96,1536]{2,1,0:T(8,128)(2,1)} %bitcast.801), channel_id=1, replica_groups=mesh['rep'=2,'fsdp'=16] {'fsdp'}, dimensions={0} | all-to-all | bytes 9437184 | tf_op jit(solution)/shard_map/all_to_all | solution.py:405
  1682.3 84.7 %all-to-all-done.7 = bf16[16,96,1536]{2,1,0:T(8,128)(2,1)} async-done(((bf16[16,96,1536]{2,1,0:T(8,128)(2,1)}), bf16[16,96,1536]{2,1,0:T(8,128)(2,1)}, u32[]{:S(2)}, u32[]{:S(2)}) %all-to-all-start.7) | async-done | bytes 4718624 | tf_op jit(solution)/shard_map/all_to_all | solution.py:409
  1767.0 7.4 bitcast_convert_fusion
  1774.4 11.8 gather_fusion.7
  1797.9 17.2 while.150
  1818.9 43.3 %while.151 = (s32[]{:T(128)}, f32[8,3,128,64]{2,3,1,0:T(8,128)S(1)}, bf16[2048,512]{0,1:T(8,128)(2,1)}, bf16[2048,512]{0,1:T(8,128)(2,1)}, s32[128]{0:T(128)S(1)...) while((s32[]{:T(128)}, f32[8,3,128,64]{2,3,1,0:T(8,128)S(1)}, ...), condition=%wide.region_80.81_spmd.clone.clone, body=%wide.region_76.80_spmd.clone.clone.sunk | while | flops 1023682688 | bytes 75797680 | solution.py:179
  1823.2 26.3 conditional.39
  1880.6 19.4 concatenate.114
  1911.3 120.4 %reduce-scatter.23.cloned.1.call-done = bf16[128,512]{1,0:T(8,128)(2,1)} async-done(((bf16[2048,512]{1,0:T(8,128)(2,1)}), bf16[128,512]{1,0:T(8,128)(2,1)}) %reduce-scatter.23.cloned.1.call-update) | async-done | bytes 131088
  2035.4 61.6 %reduce-scatter.25.cloned.1.call-done = bf16[128,512]{1,0:T(8,128)(2,1)} async-done(((bf16[2048,512]{1,0:T(8,128)(2,1)}), bf16[128,512]{1,0:T(8,128)(2,1)}) %reduce-scatter.25.cloned.1.call-update) | async-done | bytes 131088
  2106.2 20.4 concatenate.112
  2162.3 75.5 %reduce-scatter.17.cloned.1.call-done = bf16[96,4114]{1,0:T(8,128)(2,1)} async-done(((bf16[1536,4114]{1,0:T(8,128)(2,1)}), bf16[96,4114]{1,0:T(8,128)(2,1)}) %reduce-scatter.17.cloned.1.call-update) | async-done | bytes 789904 | tf_op jit(solution)/shard_map/reduce_scatter | solution.py:479
  2239.8 139.3 %reduce-scatter.15.cloned.1.call-done = bf16[96,4114]{1,0:T(8,128)(2,1)} async-done(((bf16[1536,4114]{1,0:T(8,128)(2,1)}), bf16[96,4114]{1,0:T(8,128)(2,1)}) %reduce-scatter.15.cloned.1.call-update) | async-done | bytes 789904 | tf_op jit(solution)/shard_map/reduce_scatter | solution.py:479
  2396.3 245.0 %all-reduce.13.cloned.1.call-done = (bf16[2,96,1536]{2,1,0:T(8,128)(2,1)}, bf16[2,96,512]{2,1,0:T(8,128)(2,1)}, bf16[2,96,512]{2,1,0:T(8,128)(2,1)}, bf16[2,96,1...) async-done(((bf16[2,96,1536]{2,1,0:T(8,128)(2,1)}, bf16[2,96,512]{2,1,0:T(8,128)(2,1)}, ...) | async-done | bytes 11010064 | tf_op jit(solution)/shard_map/psum | solution.py:543
  (845 shorter events, 512.8 us)
Async XLA Ops:
  7.2 72.4 %all-gather.39.cloned.1.call-start = ((), (), s32[]{:S(2)}) async-start(), calls=%async_computation.22 | async-start | bytes 1671168 | tf_op jit(solution)/shard_map/all_gather | solution.py:283
  9.0 85.9 %all-gather.35.cloned.1.call-start = ((), (), s32[]{:S(2)}) async-start(), calls=%async_computation.20 | async-start | bytes 1671168 | tf_op jit(solution)/shard_map/all_gather | solution.py:282
  10.7 127.3 %all-gather.29.cloned.1.call-start = ((), (), s32[]{:S(2)}) async-start(), calls=%async_computation.15 | async-start | bytes 2228224 | tf_op jit(solution)/shard_map/all_gather | solution.py:310
  78.4 114.4 %copy-start.89 = (f32[1536]{0:T(1024)}, f32[1536]{0:T(1024)S(1)}, u32[]{:S(2)}) copy-start(f32[1536]{0:T(1024)S(1)} %convert_element_type.437) | copy-start | bytes 18436
  79.6 113.3 %copy-start.118 = (f32[128]{0:T(128)}, f32[128]{0:T(128)S(1)}, u32[]{:S(2)}) copy-start(f32[128]{0:T(128)S(1)} %add_rsqrt_fusion.3) | copy-start | bytes 1540
  82.3 110.5 %all-gather.37.cloned.1.call-start = ((), (), s32[]{:S(2)}) async-start(), calls=%async_computation.21 | async-start | bytes 5013504 | tf_op jit(solution)/shard_map/all_gather | solution.py:281
  83.3 152.0 %all-gather.27.cloned.1.call-start = ((), (), s32[]{:S(2)}) async-start(), calls=%async_computation.14 | async-start | bytes 2228224 | tf_op jit(solution)/shard_map/all_gather | solution.py:309
  84.1 516.4 %copy-start.66 = (f32[128,32]{0,1:T(8,128)}, f32[128,32]{0,1:T(8,128)S(1)}, u32[]{:S(2)}) copy-start(f32[128,32]{0,1:T(8,128)S(1)} %get-tuple-element.3138) | copy-start | bytes 49156
  97.8 192.5 %all-gather.41.cloned.1.call-start = ((), (), s32[]{:S(2)}) async-start(), calls=%async_computation.23 | async-start | bytes 5013504 | tf_op jit(solution)/shard_map/all_gather | solution.py:284
  98.8 194.8 %copy-start.103 = (f32[1536]{0:T(1024)}, f32[1536]{0:T(1024)S(1)}, u32[]{:S(2)}) copy-start(f32[1536]{0:T(1024)S(1)} %convert_element_type.438) | copy-start | bytes 18436
  98.8 98.4 %copy-start.109 = (s32[128,8]{0,1:T(8,128)}, s32[128,8]{0,1:T(8,128)S(1)}, u32[]{:S(2)}) copy-start(s32[128,8]{0,1:T(8,128)S(1)} %get-tuple-element.3132) | copy-start | bytes 12292
  98.8 471.3 %copy-start.107 = (s32[128,8]{0,1:T(8,128)}, s32[128,8]{0,1:T(8,128)S(1)}, u32[]{:S(2)}) copy-start(s32[128,8]{0,1:T(8,128)S(1)} %get-tuple-element.3135) | copy-start | bytes 12292
  100.0 469.8 %copy-start.121 = (s32[1024,1]{0,1:T(1,128)}, s32[1024,1]{0,1:T(1,128)S(1)}, u32[]{:S(2)}) copy-start(s32[1024,1]{0,1:T(1,128)S(1)} %compare_select_fusion.25) | copy-start | bytes 12292
  294.6 275.3 %copy-start.32 = (bf16[128,1536]{1,0:T(8,128)(2,1)}, bf16[128,1536]{1,0:T(8,128)(2,1)S(1)}, u32[]{:S(2)}) copy-start(bf16[128,1536]{1,0:T(8,128)(2,1)S(1)} %multiply_convert_fusion.2) | copy-start | bytes 1179652
  300.8 101.4 %all-to-all-start = ((bf16[16,96,1536]{2,1,0:T(8,128)(2,1)}), bf16[16,96,1536]{2,1,0:T(8,128)(2,1)}, u32[]{:S(2)}, u32[]{:S(2)}) async-start(bf16[16,96,1536]{2,1,0:T(8,128)(2,1)} %bitcast.799), calls=%async_computation | async-start | bytes 9437184 | tf_op jit(solution)/shard_map/all_to_all | solution.py:332
  305.9 279.1 %all-gather.47.cloned.1.call-start = ((), (), s32[]{:S(2)}) async-start(), calls=%async_computation.26 | async-start | bytes 1671168 | tf_op jit(solution)/shard_map/all_gather | solution.py:283
  306.7 281.0 %all-gather.43.cloned.1.call-start = ((), (), s32[]{:S(2)}) async-start(), calls=%async_computation.24 | async-start | bytes 1671168 | tf_op jit(solution)/shard_map/all_gather | solution.py:282
  420.8 150.6 %all-to-all-start.1 = ((bf16[16,96,1536]{2,1,0:T(8,128)(2,1)}), bf16[16,96,1536]{2,1,0:T(8,128)(2,1)}, u32[]{:S(2)}, u32[]{:S(2)}) async-start(bf16[16,96,1536]{2,1,0:T(8,128)(2,1)} %convolution_convert_fusion.5), calls=%async_computation.1 | async-start | bytes 9437184 | tf_op jit(solution)/shard_map/all_to_all | solution.py:211
  445.9 150.3 %all-gather.45.cloned.1.call-start = ((), (), s32[]{:S(2)}) async-start(), calls=%async_computation.25 | async-start | bytes 5013504 | tf_op jit(solution)/shard_map/all_gather | solution.py:281
  446.6 203.2 %all-gather.33.cloned.1.call-start = ((), (), s32[]{:S(2)}) async-start(), calls=%async_computation.17 | async-start | bytes 2228224 | tf_op jit(solution)/shard_map/all_gather | solution.py:310
  587.7 104.9 %all-gather.31.cloned.1.call-start = ((), (), s32[]{:S(2)}) async-start(), calls=%async_computation.16 | async-start | bytes 2228224 | tf_op jit(solution)/shard_map/all_gather | solution.py:309
  590.6 157.1 %all-gather.49.cloned.1.call-start = ((), (), s32[]{:S(2)}) async-start(), calls=%async_computation.27 | async-start | bytes 5013504 | tf_op jit(solution)/shard_map/all_gather | solution.py:284
  591.2 648.9 %copy-start.97 = (f32[1536]{0:T(1024)}, f32[1536]{0:T(1024)S(1)}, u32[]{:S(2)}) copy-start(f32[1536]{0:T(1024)S(1)} %convert_element_type.440) | copy-start | bytes 18436
  751.0 489.1 %copy-start.129 = (f32[128]{0:T(128)}, f32[128]{0:T(128)S(1)}, u32[]{:S(2)}) copy-start(f32[128]{0:T(128)S(1)} %add_rsqrt_fusion) | copy-start | bytes 1540
  752.0 115.8 %copy-start.34 = (bf16[128,1536]{1,0:T(8,128)(2,1)}, bf16[128,1536]{1,0:T(8,128)(2,1)S(1)}, u32[]{:S(2)}) copy-start(bf16[128,1536]{1,0:T(8,128)(2,1)S(1)} %multiply_convert_fusion) | copy-start | bytes 1179652
  758.2 104.9 %copy-start.47 = (bf16[128,1536]{1,0:T(8,128)(2,1)S(1)}, bf16[128,1536]{1,0:T(8,128)(2,1)}, u32[]{:S(2)}) copy-start(bf16[128,1536]{1,0:T(8,128)(2,1)} %param.48) | copy-start | bytes 1179652
  758.2 117.0 %all-to-all-start.2 = ((bf16[16,96,1536]{2,1,0:T(8,128)(2,1)}), bf16[16,96,1536]{2,1,0:T(8,128)(2,1)}, u32[]{:S(2)}, u32[]{:S(2)}) async-start(bf16[16,96,1536]{2,1,0:T(8,128)(2,1)} %bitcast.798), calls=%async_computation.2 | async-start | bytes 9437184 | tf_op jit(solution)/shard_map/all_to_all | solution.py:332
  763.4 104.6 %copy-start.110 = (s32[128,8]{0,1:T(8,128)S(1)}, s32[128,8]{0,1:T(8,128)}, u32[]{:S(2)}) copy-start(s32[128,8]{0,1:T(8,128)} %copy-done.109) | copy-start | bytes 12292
  875.2 108.6 %all-to-all-start.4 = ((bf16[16,96,1536]{2,1,0:T(8,128)(2,1)}), bf16[16,96,1536]{2,1,0:T(8,128)(2,1)}, u32[]{:S(2)}, u32[]{:S(2)}) async-start(bf16[16,96,1536]{2,1,0:T(8,128)(2,1)} %bitcast.800), calls=%async_computation.4 | async-start | bytes 9437184 | tf_op jit(solution)/shard_map/all_to_all | solution.py:405
  997.5 109.3 %all-to-all-start.3 = ((bf16[16,96,1536]{2,1,0:T(8,128)(2,1)}), bf16[16,96,1536]{2,1,0:T(8,128)(2,1)}, u32[]{:S(2)}, u32[]{:S(2)}) async-start(bf16[16,96,1536]{2,1,0:T(8,128)(2,1)} %convolution_convert_fusion.4), calls=%async_computation.3 | async-start | bytes 9437184 | tf_op jit(solution)/shard_map/all_to_all | solution.py:211
  1106.8 108.6 %all-to-all-start.5 = ((bf16[16,96,1536]{2,1,0:T(8,128)(2,1)}), bf16[16,96,1536]{2,1,0:T(8,128)(2,1)}, u32[]{:S(2)}, u32[]{:S(2)}) async-start(bf16[16,96,1536]{2,1,0:T(8,128)(2,1)} %add_convert_fusion.1), calls=%async_computation.5 | async-start | bytes 9437184 | tf_op jit(solution)/shard_map/all_to_all | solution.py:409
  1128.6 348.1 %reduce-scatter.19.cloned.1.call-start = ((), (), s32[]{:S(2)}) async-start(), calls=%async_computation.28 | async-start | bytes 2228224
  1311.4 230.5 %reduce-scatter.21.cloned.1.call-start = ((), (), s32[]{:S(2)}) async-start(), calls=%async_computation.29 | async-start | bytes 2228224
  1326.5 215.4 %copy-start.21 = (f32[128,1536]{1,0:T(8,128)S(1)}, f32[128,1536]{1,0:T(8,128)}, u32[]{:S(2)}) copy-start(f32[128,1536]{1,0:T(8,128)} %copy-done.19) | copy-start | bytes 2359300
  1555.6 108.0 %copy-start.51 = (f32[16,96,512]{2,1,0:T(8,128)S(1)}, f32[16,96,512]{2,1,0:T(8,128)}, u32[]{:S(2)}) copy-start(f32[16,96,512]{2,1,0:T(8,128)} %copy-done.50) | copy-start | bytes 9437188
  1555.6 108.0 %copy-start.53 = (f32[16,96,512]{2,1,0:T(8,128)S(1)}, f32[16,96,512]{2,1,0:T(8,128)}, u32[]{:S(2)}) copy-start(f32[16,96,512]{2,1,0:T(8,128)} %copy-done.52) | copy-start | bytes 9437188
  1555.6 108.0 %copy-start.136 = (bf16[2,1,512,1536]{3,2,1,0:T(8,128)(2,1)S(1)}, bf16[2,1,512,1536]{3,2,1,0:T(8,128)(2,1)}, u32[]{:S(2)}) copy-start(bf16[2,1,512,1536]{3,2,1,0:T(8,128)(2,1)} %param.61) | copy-start | bytes 9437188
  1674.9 92.1 %all-to-all-start.7 = ((bf16[16,96,1536]{2,1,0:T(8,128)(2,1)}), bf16[16,96,1536]{2,1,0:T(8,128)(2,1)}, u32[]{:S(2)}, u32[]{:S(2)}) async-start(bf16[16,96,1536]{2,1,0:T(8,128)(2,1)} %add_convert_fusion), calls=%async_computation.7 | async-start | bytes 9437184 | tf_op jit(solution)/shard_map/all_to_all | solution.py:409
  1680.3 351.5 %reduce-scatter.23.cloned.1.call-start = ((), (), s32[]{:S(2)}) async-start(), calls=%async_computation.30 | async-start | bytes 2228224
  1682.3 108.5 %copy-start.113 = (f32[128,16]{0,1:T(8,128)}, f32[128,16]{0,1:T(8,128)S(1)}, u32[]{:S(2)}) copy-start(f32[128,16]{0,1:T(8,128)S(1)} %select_reduce_fusion) | copy-start | bytes 24580
  1866.2 230.8 %reduce-scatter.25.cloned.1.call-start = ((), (), s32[]{:S(2)}) async-start(), calls=%async_computation.31 | async-start | bytes 2228224
  1870.3 367.4 %reduce-scatter.17.cloned.1.call-start = ((), (), s32[]{:S(2)}) async-start(), calls=%async_computation.19 | async-start | bytes 13787136 | tf_op jit(solution)/shard_map/reduce_scatter | solution.py:479
  1900.1 479.0 %reduce-scatter.15.cloned.1.call-start = ((), (), s32[]{:S(2)}) async-start(), calls=%async_computation.18 | async-start | bytes 13787136 | tf_op jit(solution)/shard_map/reduce_scatter | solution.py:479
  1906.3 127.2 %copy-start.31 = (bf16[1,1536,512]{2,1,0:T(8,128)(2,1)S(1)}, bf16[1,1536,512]{2,1,0:T(8,128)(2,1)}, u32[]{:S(2)}) copy-start(bf16[1,1536,512]{2,1,0:T(8,128)(2,1)} %all-gather.35.cloned.1.call-done) | copy-start | bytes 4718596
  1911.3 185.7 %copy-start.15 = (bf16[128,1536]{1,0:T(8,128)(2,1)S(1)}, bf16[128,1536]{1,0:T(8,128)(2,1)}, u32[]{:S(2)}) copy-start(bf16[128,1536]{1,0:T(8,128)(2,1)} %param.47) | copy-start | bytes 1179652
  1911.3 185.7 %copy-start.90 = (f32[1536]{0:T(1024)S(1)}, f32[1536]{0:T(1024)}, u32[]{:S(2)}) copy-start(f32[1536]{0:T(1024)} %copy-done.89) | copy-start | bytes 18436
  1911.3 185.7 %copy-start.119 = (f32[128]{0:T(128)S(1)}, f32[128]{0:T(128)}, u32[]{:S(2)}) copy-start(f32[128]{0:T(128)} %copy-done.118) | copy-start | bytes 1540
  2126.6 514.8 %all-reduce.13.cloned.1.call-start = ((), (), s32[]{:S(2)}) async-start(), calls=%async_computation.32 | async-start | bytes 22020096 | tf_op jit(solution)/shard_map/psum | solution.py:543
  (133 other events, 1459.6 us)
Sparse Core Ops, SparseCore 0:
  10.9 42.5 all-gather.38
  56.3 38.5 all-gather.34
  97.7 40.2 all-gather.28
  140.7 52.1 all-gather.36
  195.4 39.7 all-gather.26
  237.9 52.3 all-gather.40
  309.6 85.3 all-gather.46
  397.9 44.8 all-gather.42
  449.6 104.3 all-gather.44
  587.8 62.0 all-gather.32
  652.6 39.9 all-gather.30
  695.3 52.3 all-gather.48
  1311.5 165.0 reduce-scatter.18
  1481.3 60.5 reduce-scatter.20
  1866.3 165.4 reduce-scatter.22
  2036.4 60.5 reduce-scatter.24
  2100.9 136.7 reduce-scatter.16
  2242.2 136.8 reduce-scatter.14
  2384.4 256.9 all-reduce.12
where the time goes:
time: 2680 us; the launch traced here: 2670 us
  waiting for transfers between devices  1520 us (57%)
  blocking collectives  399 us (15%)
  local copies, waits for them, and re-layouts  256 us (10%)
  matrix products  204 us (8%)
  other arithmetic  112 us (4%)
  starting transfers between devices  109 us (4%)
  loops' own time  43.9 us (2%)
    unnamed x23, waiting for transfers between devices  395 us
    psum x1, waiting for transfers between devices, on_device(): lax.psum(stacked_query.astype(jnp.bfloat16), 'rep').astype(jnp.float32)  245 us
    all_gather x2, blocking collectives, on_device(): lax.all_gather(router[layer_index], 'fsdp', axis=0, tiled=True)  222 us
    reduce_scatter x2, waiting for transfers between devices, on_device(): lax.psum_scatter(jnp.concatenate([projections, outputs, routing, jnp.sum(...  215 us
    all_to_all x2, waiting for transfers between devices, on_device(): lax.all_to_all(grad_inputs.astype(jnp.bfloat16), 'fsdp', split_axis=0, co...  157 us
    all_to_all x1, blocking collectives, on_device(): lax.all_to_all(send_grads, 'fsdp', split_axis=0, concat_axis=0, tiled=True)  108 us
    all_to_all x2, waiting for transfers between devices, on_device(): lax.all_to_all(send_rows, 'fsdp', split_axis=0, concat_axis=0, tiled=True)  94.8 us
    all_gather x2, waiting for transfers between devices, on_device(): lax.all_gather(value_rows, 'fsdp', axis=0, tiled=True)  82.5 us
  transfers between devices with their start and end apart: 26, of which 20 were waited for; matrix products, arithmetic and copies ran while one was open for 12% of the time, Pallas kernels for 0%

commit v1 on v0

v1 whole, which is shorter than its diff:
```python
import functools

import jax
import jax.numpy as jnp
from jax import lax
from jax.experimental import pallas as pl
from jax.experimental.pallas import tpu as pltpu
from jax.sharding import PartitionSpec as P

HEADS = 24
KV_HEADS = 8
HD = 64
LAYERS = 2
GROUP = HEADS // KV_HEADS
LANES = 128
CHUNK = 256
EPS = 1e-06
MASKED = -1e30
MESH = pl.DeviceIdType.MESH
F32 = jnp.float32
BF16 = jnp.bfloat16


def ring_place(chip, count):
    return lax.select(lax.rem(chip, 2) == 0, chip // 2, count - 1 - chip // 2)


def ring_chip(place, count):
    return lax.select(place < count // 2, 2 * place, 2 * (count - 1 - place) + 1)


def ring_setup(count):
    me = lax.axis_index("fsdp")
    chip, core = me // 2, lax.rem(me, 2)
    place = ring_place(chip, count)

    def at(offset):
        return ring_chip(lax.rem(place + offset + 2 * count, count), count)

    return chip, at, (at(1) * 2 + core, at(-1) * 2 + core)


def meet(neighbours):
    barrier = pltpu.get_barrier_semaphore()
    for other in neighbours:
        pl.semaphore_signal(barrier, inc=1, device_id={"fsdp": other}, device_id_type=MESH)
    pl.semaphore_wait(barrier, len(neighbours))


def ring_hops(count):
    half = count // 2
    return {(0, 0): half, (1, 1): half, (0, 1): half - 1, (1, 0): half - 1}


def gather_kernel(count, x_ref, side_ref, o_ref, all_ref, own_sem, send_sem, recv_sem, side_send, side_recv):
    chip, at, (right, left) = ring_setup(count)
    half_rows = x_ref.shape[0] // 2
    hops = ring_hops(count)
    steps = count // 2
    meet((right, left))
    own = pltpu.make_async_copy(x_ref, o_ref.at[chip], own_sem.at[0])
    own.start()
    own_side = pltpu.make_async_copy(side_ref, all_ref.at[chip], own_sem.at[1])
    own_side.start()

    def piece(direction, part, step):
        block = at(-step if direction == 0 else step)
        rows = pl.ds(part * half_rows, half_rows)
        target = o_ref.at[block, rows]
        return pltpu.make_async_remote_copy(
            src_ref=x_ref.at[rows] if step == 0 else target,
            dst_ref=target,
            send_sem=send_sem.at[direction, part, step],
            recv_sem=recv_sem.at[direction, part, step],
            device_id={"fsdp": right if direction == 0 else left},
            device_id_type=MESH,
        )

    def arrival(direction, part, step):
        block = at(-step - 1 if direction == 0 else step + 1)
        target = o_ref.at[block, pl.ds(part * half_rows, half_rows)]
        return pltpu.make_async_remote_copy(
            src_ref=target,
            dst_ref=target,
            send_sem=send_sem.at[direction, part, step],
            recv_sem=recv_sem.at[direction, part, step],
            device_id={"fsdp": right if direction == 0 else left},
            device_id_type=MESH,
        )

    def side_piece(direction, step, arrived):
        moved = step + 1 if arrived else step
        block = at(-moved if direction == 0 else moved)
        target = all_ref.at[block]
        return pltpu.make_async_remote_copy(
            src_ref=side_ref if step == 0 and not arrived else target,
            dst_ref=target,
            send_sem=side_send.at[direction, step],
            recv_sem=side_recv.at[direction, step],
            device_id={"fsdp": right if direction == 0 else left},
            device_id_type=MESH,
        )

    side_hops = (steps, steps - 1)
    for step in range(steps + 1):
        for direction in range(2):
            if 0 < step <= side_hops[direction]:
                side_piece(direction, step - 1, True).wait_recv()
            if step < side_hops[direction]:
                side_piece(direction, step, False).start()
        for key in hops:
            if 0 < step <= hops[key]:
                arrival(*key, step - 1).wait_recv()
            if step < hops[key]:
                piece(*key, step).start()
    for step in range(steps):
        for direction in range(2):
            if step < side_hops[direction]:
                side_piece(direction, step, False).wait_send()
        for key in hops:
            if step < hops[key]:
                piece(*key, step).wait_send()
    own.wait()
    own_side.wait()


def ring_gather(x, side, count):
    steps = count // 2
    return pl.pallas_call(
        functools.partial(gather_kernel, count),
        out_shape=(
            jax.ShapeDtypeStruct((count,) + x.shape, x.dtype),
            jax.ShapeDtypeStruct((count,) + side.shape, side.dtype),
        ),
        in_specs=[pl.BlockSpec(memory_space=pl.ANY)] * 2,
        out_specs=[pl.BlockSpec(memory_space=pl.ANY)] * 2,
        scratch_shapes=[
            pltpu.SemaphoreType.DMA((2,)),
            pltpu.SemaphoreType.DMA((2, 2, steps)),
            pltpu.SemaphoreType.DMA((2, 2, steps)),
            pltpu.SemaphoreType.DMA((2, steps)),
            pltpu.SemaphoreType.DMA((2, steps)),
        ],
        compiler_params=pltpu.CompilerParams(collective_id=0, has_side_effects=True),
        name="ring_gather",
    )(x, side)


def scatter_kernel(count, p_ref, o_ref, land, send_sem, recv_sem):
    chip, at, (right, left) = ring_setup(count)
    half_rows = o_ref.shape[0] // 2
    hops = ring_hops(count)
    steps = count // 2
    meet((right, left))

    def ahead(key, step):
        places = hops[key] - step
        return at(places if key[0] == 0 else -places)

    def piece(key, step):
        direction, part = key
        rows = pl.ds(part * half_rows, half_rows)
        first = p_ref.at[ahead(key, step), rows]
        return pltpu.make_async_remote_copy(
            src_ref=first if step == 0 else land.at[direction, part, step - 1],
            dst_ref=land.at[direction, part, step],
            send_sem=send_sem.at[direction, part, step],
            recv_sem=recv_sem.at[direction, part, step],
            device_id={"fsdp": right if direction == 0 else left},
            device_id_type=MESH,
        )

    for step in range(steps + 1):
        for key in hops:
            direction, part = key
            rows = pl.ds(part * half_rows, half_rows)
            if 0 < step <= hops[key]:
                piece(key, step - 1).wait_recv()
                if step < hops[key]:
                    slot = land.at[direction, part, step - 1]
                    total = slot[...].astype(F32) + p_ref[ahead(key, step), rows].astype(F32)
                    slot[...] = total.astype(BF16)
            if step < hops[key]:
                piece(key, step).start()
    for part in range(2):
        rows = pl.ds(part * half_rows, half_rows)
        total = p_ref[chip, rows].astype(F32)
        for direction in range(2):
            total = total + land[direction, part, hops[direction, part] - 1].astype(F32)
        o_ref[rows, :] = total
    for step in range(steps):
        for key in hops:
            if step < hops[key]:
                piece(key, step).wait_send()


def ring_scatter(partial, count):
    _, rows, width = partial.shape
    steps = count // 2
    return pl.pallas_call(
        functools.partial(scatter_kernel, count),
        out_shape=jax.ShapeDtypeStruct((rows, width), F32),
        in_specs=[pl.BlockSpec(memory_space=pltpu.VMEM)],
        out_specs=pl.BlockSpec(memory_space=pltpu.VMEM),
        scratch_shapes=[
            pltpu.VMEM((2, 2, steps, rows // 2, width), partial.dtype),
            pltpu.SemaphoreType.DMA((2, 2, steps)),
            pltpu.SemaphoreType.DMA((2, 2, steps)),
        ],
        compiler_params=pltpu.CompilerParams(
            collective_id=1, has_side_effects=True, vmem_limit_bytes=40 << 20
        ),
        name="ring_scatter",
    )(partial)


def dot(left, right, contract=((1,), (0,))):
    return lax.dot_general(left, right, (contract, ((), ())), preferred_element_type=F32)


NT = ((1,), (1,))
TN = ((0,), (0,))


def spin(field, cosine, sine):
    lane = lax.broadcasted_iota(jnp.int32, field.shape, 1)
    swapped = jnp.where(
        lane < HD // 2,
        -pltpu.roll(field, LANES - HD // 2, 1),
        pltpu.roll(field, HD // 2, 1),
    )
    return field * cosine + swapped * sine


def project_kernel(x_ref, w_ref, cos_ref, sin_ref, q_ref, kv_ref):
    rows = dot(x_ref[...], w_ref[...])
    cosine, sine = cos_ref[...], sin_ref[...]
    for head in range(GROUP):
        turned = spin(rows[:, head * LANES : (head + 1) * LANES], cosine, sine).astype(BF16)
        turned = (turned.astype(F32) * (HD**-0.5)).astype(BF16)
        for block in range(2):
            q_ref[block, head] = turned[block * LANES : (block + 1) * LANES]
    pair = rows[:, GROUP * LANES :]
    kv_ref[...] = spin(pair, cosine, sine).astype(BF16)


def project(x, w, cosine, sine):
    tokens, width = x.shape
    tile = 2 * LANES
    return pl.pallas_call(
        project_kernel,
        grid=(tokens // tile,),
        out_shape=(
            jax.ShapeDtypeStruct((tokens // LANES, GROUP, LANES, LANES), BF16),
            jax.ShapeDtypeStruct((tokens, LANES), BF16),
        ),
        in_specs=[
            pl.BlockSpec((tile, width), lambda i: (i, 0)),
            pl.BlockSpec(w.shape, lambda i: (0, 0)),
            pl.BlockSpec((tile, LANES), lambda i: (i, 0)),
            pl.BlockSpec((tile, LANES), lambda i: (i, 0)),
        ],
        out_specs=[
            pl.BlockSpec((2, GROUP, LANES, LANES), lambda i: (i, 0, 0, 0)),
            pl.BlockSpec((tile, LANES), lambda i: (i, 0)),
        ],
        name="project",
    )(x, w, cosine, sine)


def allowed_keys(begin, block, chunk):
    shape = (GROUP * LANES, CHUNK)
    key = chunk * CHUNK + lax.broadcasted_iota(jnp.int32, shape, 1)
    query = block * LANES + lax.rem(lax.broadcasted_iota(jnp.int32, shape, 0), LANES)
    return (key >= begin) & (key <= query)


def attend_kernel(info_ref, q_ref, kv_ref, begin_ref, w_ref, att_ref, lse_ref, out_ref):
    step = pl.program_id(0)
    block = 2 * step + info_ref[0]
    first = info_ref[1 + step] // CHUNK
    last = block * LANES // CHUNK
    q = q_ref[0].reshape(GROUP * LANES, LANES)
    begin = jnp.concatenate([begin_ref[0]] * GROUP, 0)

    def one(chunk, state):
        top, total, acc = state
        keys = kv_ref[pl.ds(pl.multiple_of(chunk * CHUNK, CHUNK), CHUNK), :]
        allowed = allowed_keys(begin, block, chunk)
        scores = jnp.where(allowed, dot(q, keys, NT), MASKED)
        new_top = jnp.maximum(top, jnp.max(scores, -1, keepdims=True))
        weights = jnp.where(allowed, jnp.exp(scores - new_top), 0.0)
        shrink = jnp.exp(top - new_top)
        total = total * shrink + jnp.sum(weights, -1, keepdims=True)
        return new_top, total, acc * shrink + dot(weights.astype(BF16), keys)

    rows = GROUP * LANES
    top, total, acc = lax.fori_loop(
        first,
        last + 1,
        one,
        (jnp.full((rows, 1), MASKED, F32), jnp.zeros((rows, 1), F32), jnp.zeros((rows, LANES), F32)),
    )
    lse_ref[0] = top + jnp.log(total)
    att = (acc / total).astype(BF16)
    wide = jnp.concatenate([att[h * LANES : (h + 1) * LANES] for h in range(GROUP)], 1)
    att_ref[0] = wide
    out_ref[0] = dot(wide, w_ref[...]).astype(BF16)


def attend(info, q, kv, begin, w):
    blocks = q.shape[0]
    wide = GROUP * LANES
    width = w.shape[1]
    return pl.pallas_call(
        attend_kernel,
        grid_spec=pltpu.PrefetchScalarGridSpec(
            num_scalar_prefetch=1,
            grid=(blocks,),
            in_specs=[
                pl.BlockSpec((1, GROUP, LANES, LANES), lambda i, s: (i, 0, 0, 0)),
                pl.BlockSpec(kv.shape, lambda i, s: (0, 0)),
                pl.BlockSpec((1, LANES, 1), lambda i, s: (i, 0, 0)),
                pl.BlockSpec(w.shape, lambda i, s: (0, 0)),
            ],
            out_specs=[
                pl.BlockSpec((1, LANES, wide), lambda i, s: (i, 0, 0)),
                pl.BlockSpec((1, wide, 1), lambda i, s: (i, 0, 0)),
                pl.BlockSpec((1, LANES, width), lambda i, s: (i, 0, 0)),
            ],
        ),
        out_shape=(
            jax.ShapeDtypeStruct((blocks, LANES, wide), BF16),
            jax.ShapeDtypeStruct((blocks, wide, 1), F32),
            jax.ShapeDtypeStruct((blocks, LANES, width), BF16),
        ),
        name="attend",
    )(info, q, kv, begin, w)


def attend_back_kernel(info_ref, q_ref, kv_ref, begin_ref, w_ref, att_ref, lse_ref, db_ref, cos_ref, sin_ref, dq_ref, dkv_ref):
    step = pl.program_id(0)
    block = 2 * step + info_ref[0]
    first = info_ref[1 + step] // CHUNK
    last = block * LANES // CHUNK

    @pl.when(step == 0)
    def _():
        dkv_ref[...] = jnp.zeros_like(dkv_ref)

    q = q_ref[0].reshape(GROUP * LANES, LANES)
    begin = jnp.concatenate([begin_ref[0]] * GROUP, 0)
    wide = dot(db_ref[0], w_ref[...], NT).astype(BF16)
    datt = jnp.concatenate([wide[:, h * LANES : (h + 1) * LANES] for h in range(GROUP)], 0)
    att = jnp.concatenate([att_ref[0, :, h * LANES : (h + 1) * LANES] for h in range(GROUP)], 0)
    delta = jnp.sum(datt.astype(F32) * att.astype(F32), -1, keepdims=True)
    lse = lse_ref[0]
    both = jnp.concatenate([q, datt], 0)

    def one(chunk, acc):
        place = pl.ds(pl.multiple_of(chunk * CHUNK, CHUNK), CHUNK)
        keys = kv_ref[place, :]
        allowed = allowed_keys(begin, block, chunk)
        weights = jnp.where(allowed, jnp.exp(dot(q, keys, NT) - lse), 0.0)
        slope = (weights * (dot(datt, keys, NT) - delta)).astype(BF16)
        dkv_ref[place, :] += dot(jnp.concatenate([slope, weights.astype(BF16)], 0), both, TN)
        return acc + dot(slope, keys)

    acc = lax.fori_loop(first, last + 1, one, jnp.zeros((GROUP * LANES, LANES), F32))
    cosine, sine = cos_ref[0], sin_ref[0]
    for head in range(GROUP):
        part = acc[head * LANES : (head + 1) * LANES] * (HD**-0.5)
        dq_ref[0, :, head * LANES : (head + 1) * LANES] = spin(part, cosine, -sine).astype(BF16)


def attend_back(info, q, kv, begin, w, att, lse, db, cosine, sine):
    blocks = q.shape[0]
    wide = GROUP * LANES
    width = w.shape[1]
    return pl.pallas_call(
        attend_back_kernel,
        grid_spec=pltpu.PrefetchScalarGridSpec(
            num_scalar_prefetch=1,
            grid=(blocks,),
            in_specs=[
                pl.BlockSpec((1, GROUP, LANES, LANES), lambda i, s: (i, 0, 0, 0)),
                pl.BlockSpec(kv.shape, lambda i, s: (0, 0)),
                pl.BlockSpec((1, LANES, 1), lambda i, s: (i, 0, 0)),
                pl.BlockSpec(w.shape, lambda i, s: (0, 0)),
                pl.BlockSpec((1, LANES, wide), lambda i, s: (i, 0, 0)),
                pl.BlockSpec((1, wide, 1), lambda i, s: (i, 0, 0)),
                pl.BlockSpec((1, LANES, width), lambda i, s: (i, 0, 0)),
                pl.BlockSpec((1, LANES, LANES), lambda i, s: (i, 0, 0)),
                pl.BlockSpec((1, LANES, LANES), lambda i, s: (i, 0, 0)),
            ],
            out_specs=[
                pl.BlockSpec((1, LANES, wide), lambda i, s: (i, 0, 0)),
                pl.BlockSpec(kv.shape, lambda i, s: (0, 0)),
            ],
        ),
        out_shape=(
            jax.ShapeDtypeStruct((blocks, LANES, wide), BF16),
            jax.ShapeDtypeStruct(kv.shape, F32),
        ),
        name="attend_back",
    )(info, q, kv, begin, w, att, lse, db, cosine, sine)


def on_device(
    tokens,
    cotangent,
    positions,
    segments,
    routes,
    attn_gain,
    w_query,
    w_key,
    w_value,
    w_out,
    ffn_gain,
    router,
    w_gate,
    w_up,
    w_down,
):
    rows, width = tokens.shape
    devices = lax.axis_size("fsdp")
    replicas = lax.axis_size("rep")
    count = devices // 2
    me = lax.axis_index("fsdp")
    chip, core = me // 2, lax.rem(me, 2)
    shard = w_query.shape[1]
    experts = w_gate.shape[1] * devices
    ff = w_gate.shape[3]
    pairs = [(index, index ^ 1) for index in range(devices)]

    def swap(array):
        return lax.ppermute(array, "fsdp", pairs)

    def by_core(own, other, axis):
        return jnp.where(
            core == 0, jnp.stack([own, other], axis), jnp.stack([other, own], axis)
        )

    def own_and_other(array):
        return (
            lax.dynamic_index_in_dim(array, core, 0, False),
            lax.dynamic_index_in_dim(array, 1 - core, 0, False),
        )

    def over_replicas(arrays):
        if replicas == 2:
            other = [lax.ppermute(a, "rep", [(0, 1), (1, 0)]) for a in arrays]
            return [a.astype(F32) + b.astype(F32) for a, b in zip(arrays, other)]
        return [lax.psum(a, "rep").astype(F32) for a in arrays]

    small = jnp.concatenate(
        [
            attn_gain.reshape(LAYERS, shard, 1),
            ffn_gain.reshape(LAYERS, shard, 1),
            router,
        ],
        -1,
    )
    small = lax.all_gather(small, "fsdp", axis=1, tiled=True)
    gains_one = small[:, :, 0].astype(F32)
    gains_two = small[:, :, 1].astype(F32)
    routers = small[:, :, 2:]
    by_chip = jnp.concatenate(
        [
            w_query.reshape(LAYERS, shard, count, GROUP * HD),
            w_key.reshape(LAYERS, shard, count, HD),
            w_value.reshape(LAYERS, shard, count, HD),
        ],
        -1,
    ).transpose(2, 0, 1, 3)
    head_width = by_chip.shape[-1]
    by_device = jnp.repeat(by_chip, 2, axis=0)
    mine = lax.all_to_all(by_device, "fsdp", split_axis=0, concat_axis=0, tiled=True)
    mine = mine.transpose(1, 0, 2, 3).reshape(LAYERS, width, head_width)
    hole = jnp.zeros((LAYERS, width, HD), BF16)
    w_heads = jnp.concatenate(
        [piece for h in range(GROUP) for piece in (mine[:, :, h * HD : (h + 1) * HD], hole)]
        + [mine[:, :, GROUP * HD :]],
        -1,
    )
    out_rows = by_core(w_out, swap(w_out), 1).reshape(LAYERS, GROUP, HD, width)
    w_outs = jnp.concatenate([jnp.zeros_like(out_rows), out_rows], 2).reshape(
        LAYERS, GROUP * LANES, width
    )
    gate_pair = by_core(w_gate[:, 0], swap(w_gate[:, 0]), 2).reshape(LAYERS, width, 2 * ff)
    up_pair = by_core(w_up[:, 0], swap(w_up[:, 0]), 2).reshape(LAYERS, width, 2 * ff)
    down_pair = by_core(w_down[:, 0], swap(w_down[:, 0]), 1).reshape(LAYERS, 2 * ff, width)

    flat = segments.reshape(-1)
    starts = jnp.sum(
        (flat[None, :] < jnp.arange(8, dtype=jnp.int32)[:, None]).astype(jnp.int32), 1
    )
    begin = jnp.sum(
        jnp.where(flat[:, None] == jnp.arange(8, dtype=jnp.int32)[None, :], starts[None, :], 0), 1
    )
    begin = begin.reshape(count, 2, rows)
    begin = lax.dynamic_index_in_dim(begin, core, 1, False)
    info = jnp.concatenate([core[None], begin[:, 0]]).astype(jnp.int32)
    begin = begin[:, :, None]

    side = jnp.concatenate(
        [positions.astype(F32)[None, :], jnp.zeros((experts - 1, rows), F32)], 0
    )
    cosine = sine = None
    hidden = tokens.astype(F32)
    saved = []

    def normal(values):
        inverse = lax.rsqrt(jnp.mean(values * values, -1, keepdims=True) + EPS)
        return inverse, values * inverse

    for layer in range(LAYERS):
        inverse_one, normed_one = normal(hidden)
        x_attn = (normed_one * gains_one[layer][None, :]).astype(BF16)
        x_all, side_all = ring_gather(x_attn, side, count)
        if layer == 0:
            place = side_all[:, 0, :].reshape(-1)
            lane = jnp.arange(LANES, dtype=jnp.int32)
            rate = jnp.exp(-jnp.log(10000.0) * (lane % (HD // 2)).astype(F32) / (HD // 2))
            angle = place[:, None] * jnp.where(lane < HD, rate, 0.0)[None, :]
            cosine, sine = jnp.cos(angle), jnp.sin(angle)
        x_all = x_all.reshape(count * rows, width)
        query, kv_own = project(x_all, w_heads[layer], cosine, sine)
        kv_own = kv_own.reshape(count, rows, LANES)
        kv = by_core(kv_own, swap(kv_own), 1).reshape(count * 2 * rows, LANES)
        att, lse, partial = attend(info, query, kv, begin, w_outs[layer])
        middle = hidden + ring_scatter(partial, count)
        inverse_two, normed_two = normal(middle)
        x_moe = (normed_two * gains_two[layer][None, :]).astype(BF16)
        logits = dot(x_moe, routers[layer])
        named = jnp.any(
            routes[layer][:, :, None] == jnp.arange(experts, dtype=jnp.int32)[None, None, :], 1
        )
        share = jax.nn.softmax(jnp.where(named, logits, -jnp.inf), axis=-1)
        m_all, share_all = ring_gather(x_moe, share.T, count)
        m_all = m_all.reshape(count * rows, width)
        share_mine = lax.dynamic_slice_in_dim(share_all, 2 * chip, 2, 1)
        share_mine = share_mine.transpose(0, 2, 1).reshape(count * rows, 2)
        share_wide = jnp.repeat(share_mine, ff, axis=1)
        act_gate = dot(m_all, gate_pair[layer])
        act_up = dot(m_all, up_pair[layer])
        weighted = (jax.nn.silu(act_gate) * act_up * share_wide).astype(BF16)
        partial = dot(weighted, down_pair[layer]).astype(BF16)
        mixed = ring_scatter(partial.reshape(count, rows, width), count)
        saved.append(
            (inverse_one, normed_one, x_all, query, kv, att, lse, inverse_two, normed_two)
            + (m_all, share_mine, share_wide, act_gate, act_up, weighted, mixed)
        )
        hidden = middle + mixed
    activations = hidden.astype(BF16)
    grad = cotangent.astype(F32)
    grads = [None] * LAYERS
    for layer in reversed(range(LAYERS)):
        (inverse_one, normed_one, x_all, query, kv, att, lse, inverse_two, normed_two) = saved[layer][:9]
        (m_all, share_mine, share_wide, act_gate, act_up, weighted, mixed) = saved[layer][9:]
        d_mix = grad.astype(BF16)
        balance = jnp.sum(mixed * d_mix.astype(F32), -1)
        side = jnp.concatenate([balance[None, :], jnp.zeros((experts - 1, rows), F32)], 0)
        d_all, balance_all = ring_gather(d_mix, side, count)
        d_all = d_all.reshape(count * rows, width)
        balance_all = balance_all[:, 0, :].reshape(-1, 1)
        raw = dot(d_all, down_pair[layer], NT)
        gate_sig = jax.nn.sigmoid(act_gate)
        swish = act_gate * gate_sig
        d_share = jnp.sum((swish * act_up * raw).reshape(-1, 2, ff), -1)
        d_logit = share_mine * (d_share - balance_all)
        d_hidden = raw * share_wide
        d_gate = (d_hidden * act_up * gate_sig * (1.0 + act_gate * (1.0 - gate_sig))).astype(BF16)
        d_up = (d_hidden * swish).astype(BF16)
        g_down = dot(weighted, d_all, TN)
        g_gate = dot(m_all, d_gate, TN)
        g_up = dot(m_all, d_up, TN)
        router_mine = lax.dynamic_slice_in_dim(routers[layer], 2 * chip, 2, 1).astype(F32)
        g_router = jnp.dot(d_logit.T, m_all.astype(F32), precision=lax.Precision.HIGHEST)
        partial = (
            dot(d_gate, gate_pair[layer], NT)
            + dot(d_up, up_pair[layer], NT)
            + d_logit[:, 0:1] * router_mine[:, 0][None, :]
            + d_logit[:, 1:2] * router_mine[:, 1][None, :]
        ).astype(BF16)
        d_x = ring_scatter(partial.reshape(count, rows, width), count)
        gain = gains_two[layer][None, :]
        d_norm = d_x * gain
        d_gain_two = jnp.sum(d_x * normed_two, 0)
        grad_mid = grad + inverse_two * (
            d_norm - normed_two * jnp.mean(d_norm * normed_two, -1, keepdims=True)
        )
        side = jnp.zeros((experts, rows), F32)
        b_all, _ = ring_gather(grad_mid.astype(BF16), side, count)
        d_query, d_kv = attend_back(
            info, query, kv, begin, w_outs[layer], att, lse, b_all,
            cosine.reshape(count, rows, LANES), sine.reshape(count, rows, LANES),
        )
        b_all = b_all.reshape(count * rows, width)
        g_out = dot(att.reshape(count * rows, GROUP * LANES), b_all, TN)
        halves = d_kv.astype(BF16).reshape(count, 2, rows, LANES).transpose(1, 0, 2, 3)
        own, other = own_and_other(halves)
        d_kv = (own.astype(F32) + swap(other).astype(F32)).reshape(count * rows, LANES)
        d_key, d_value = d_kv[:, :HD], d_kv[:, HD:]
        cos_half, sin_half = cosine[:, : HD // 2], sine[:, : HD // 2]
        low, high = d_key[:, : HD // 2], d_key[:, HD // 2 :]
        d_key = jnp.concatenate(
            [low * cos_half + high * sin_half, high * cos_half - low * sin_half], 1
        )
        d_heads = jnp.concatenate(
            [
                d_query.reshape(count * rows, GROUP * LANES),
                jnp.concatenate([d_key, d_value], 1).astype(BF16),
            ],
            1,
        )
        partial = dot(d_heads, w_heads[layer], NT).astype(BF16)
        d_x = ring_scatter(partial.reshape(count, rows, width), count)
        g_heads = dot(x_all, d_heads, TN)
        gain = gains_one[layer][None, :]
        d_norm = d_x * gain
        d_gain_one = jnp.sum(d_x * normed_one, 0)
        grad = grad_mid + inverse_one * (
            d_norm - normed_one * jnp.mean(d_norm * normed_one, -1, keepdims=True)
        )
        g_down = g_down.astype(BF16).reshape(2, ff, width)
        g_gate = g_gate.astype(BF16).reshape(width, 2, ff).transpose(1, 0, 2)
        g_up = g_up.astype(BF16).reshape(width, 2, ff).transpose(1, 0, 2)
        g_out = g_out.reshape(GROUP, LANES, width)[:, HD:].reshape(2, shard, width).astype(BF16)
        g_router = g_router.astype(BF16)
        sums = []
        for pair in (g_gate, g_up, g_down, g_out, g_router):
            own, other = own_and_other(pair)
            sums.append((own.astype(F32) + swap(other).astype(F32)).astype(BF16))
        g_heads = jnp.concatenate(
            [g_heads[:, h * LANES : h * LANES + HD] for h in range(GROUP)]
            + [g_heads[:, GROUP * LANES :]],
            1,
        )
        spread = jnp.concatenate(
            [
                g_heads.reshape(devices, shard, head_width),
                d_gain_one.reshape(devices, shard, 1),
                d_gain_two.reshape(devices, shard, 1),
            ],
            2,
        ).astype(BF16)
        sent_router = lax.all_to_all(
            sums[4].reshape(devices, shard), "fsdp", split_axis=0, concat_axis=0, tiled=True
        )
        spread = lax.all_to_all(spread, "fsdp", split_axis=0, concat_axis=0, tiled=True).astype(F32)
        gains = jnp.sum(spread[:, :, head_width:], 0)
        heads = jnp.sum(spread[:, :, :head_width].reshape(count, 2, shard, head_width), 1)
        heads = heads.transpose(1, 0, 2)
        q_part = heads[:, :, : GROUP * HD].reshape(shard, width)
        k_part = heads[:, :, GROUP * HD : (GROUP + 1) * HD].reshape(shard, KV_HEADS * HD)
        v_part = heads[:, :, (GROUP + 1) * HD :].reshape(shard, KV_HEADS * HD)
        packed = jnp.concatenate([q_part, k_part, v_part, sent_router.T.astype(F32), gains], 1)
        g_gate, g_up, g_down, g_out, packed = over_replicas(sums[:4] + [packed.astype(BF16)])
        edge_key = width + KV_HEADS * HD
        edge_value = edge_key + KV_HEADS * HD
        edge_router = edge_value + experts
        grads[layer] = (
            packed[:, edge_router],
            packed[:, :width],
            packed[:, width:edge_key],
            packed[:, edge_key:edge_value],
            g_out,
            packed[:, edge_router + 1],
            packed[:, edge_value:edge_router],
            g_gate[None],
            g_up[None],
            g_down[None],
        )
    return (activations, grad) + tuple(
        jnp.stack([grads[layer][index] for layer in range(LAYERS)]) for index in range(10)
    )


def solution(mesh):
    placed = (
        P(("rep", "fsdp"), None),
        P(("rep", "fsdp"), None),
        P(("rep", "fsdp")),
        P("rep", None),
        P(None, ("rep", "fsdp"), None),
        P(None, "fsdp"),
        P(None, "fsdp", None),
        P(None, "fsdp", None),
        P(None, "fsdp", None),
        P(None, "fsdp", None),
        P(None, "fsdp"),
        P(None, "fsdp", None),
        P(None, "fsdp", None, None),
        P(None, "fsdp", None, None),
        P(None, "fsdp", None, None),
    )
    return jax.shard_map(
        on_device,
        mesh=mesh,
        in_specs=placed,
        out_specs=(
            P(("rep", "fsdp"), None),
            P(("rep", "fsdp"), None),
            P(None, "fsdp"),
            P(None, "fsdp", None),
            P(None, "fsdp", None),
            P(None, "fsdp", None),
            P(None, "fsdp", None),
            P(None, "fsdp"),
            P(None, "fsdp", None),
            P(None, "fsdp", None, None),
            P(None, "fsdp", None, None),
            P(None, "fsdp", None, None),
        ),
        check_vma=False,
    )
```

time: 2680 us -> 1320 us (0.49)
  waiting for transfers between devices: 1520 us -> 163 us
  Pallas kernels: 0 us -> 627 us
  blocking collectives: 399 us -> 51.2 us
  local copies, waits for them, and re-layouts: 256 us -> 160 us
  matrix products: 204 us -> 116 us
  loops' own time: 43.9 us -> 0 us
  starting transfers between devices: 109 us -> 75.2 us
    pallas_call x0 -> x22, Pallas kernels: none -> 627 us  [the longest x8 265 us: ring_scatter(): pl.pallas_call(functools.partial(scatter_kernel, count), out_shape=jax.Sh...]
    all_to_all x7 -> x5, waiting for transfers between devices: 403 us -> 6.54 us  [the longest x2 6.53 us: on_device(): lax.all_to_all(spread, 'fsdp', split_axis=0, concat_axis=0, tiled=True)]
    unnamed x23 -> x0, waiting for transfers between devices: 395 us -> none
    all_gather x12 -> x0, waiting for transfers between devices: 266 us -> none  [the longest x2 82.5 us: on_device(): lax.all_gather(value_rows, 'fsdp', axis=0, tiled=True)]
    psum x1 -> x0, waiting for transfers between devices: 245 us -> none  [on_device(): lax.psum(stacked_query.astype(jnp.bfloat16), 'rep').astype(jnp.float32)]
    reduce_scatter x2 -> x0, waiting for transfers between devices: 215 us -> none  [on_device(): lax.psum_scatter(jnp.concatenate([projections, outputs, routing, jnp.sum(...]
    all_gather x2 -> x1, blocking collectives: 222 us -> 51.2 us  [on_device(): small = lax.all_gather(small, 'fsdp', axis=1, tiled=True)]
    ppermute x0 -> x28, waiting for transfers between devices: none -> 156 us  [the longest x10 156 us: over_replicas(): other = [lax.ppermute(a, 'rep', [(0, 1), (1, 0)]) for a in arrays]]
  transfers between devices with their start and end apart: 26 -> 33, of which waited for: 20 -> 7; matrix products, arithmetic and copies ran while one was open for 12% -> 21% of each run, Pallas kernels for 0% -> 19%
where the time goes in v1:
time: 1320 us
  Pallas kernels  627 us (48%)
  waiting for transfers between devices  163 us (12%)
  local copies, waits for them, and re-layouts  160 us (12%)
  other arithmetic  120 us (9%)
  matrix products  116 us (9%)
  starting transfers between devices  75.2 us (6%)
  blocking collectives  51.2 us (4%)
    pallas_call x8, Pallas kernels, ring_scatter(): pl.pallas_call(functools.partial(scatter_kernel, count), out_shape=jax.Sh...  265 us
    pallas_call x8, Pallas kernels, ring_gather(): pl.pallas_call(functools.partial(gather_kernel, count), out_shape=(jax.Sh...  245 us
    ppermute x10, waiting for transfers between devices, over_replicas(): other = [lax.ppermute(a, 'rep', [(0, 1), (1, 0)]) for a in arrays]  156 us
    dot_general x26, matrix products, dot(): lax.dot_general(left, right, (contract, ((), ())), preferred_element_type...  111 us
    pallas_call x2, Pallas kernels, attend_back(): pl.pallas_call(attend_back_kernel, grid_spec=pltpu.PrefetchScalarGridSpec...  59 us
    all_gather x1, blocking collectives, on_device(): small = lax.all_gather(small, 'fsdp', axis=1, tiled=True)  51.2 us
    pallas_call x2, Pallas kernels, attend(): pl.pallas_call(attend_kernel, grid_spec=pltpu.PrefetchScalarGridSpec(num_...  44.3 us
    ppermute x10, starting transfers between devices, over_replicas(): other = [lax.ppermute(a, 'rep', [(0, 1), (1, 0)]) for a in arrays]  41 us
  transfers between devices with their start and end apart: 33, of which 7 were waited for; matrix products, arithmetic and copies ran while one was open for 21% of the time, Pallas kernels for 19%

profile of v1, /device:TPU:0, one launch (start us, length us, event | category | flops | bytes accessed | tf_op | source)
XLA Modules:
  0.0 1315.3 jit_solution(16624504666711561708)
XLA Ops:
  7.5 7.4 all-to-all-start
  27.3 51.2 %all_gather.3 = bf16[2,1536,18]{2,0,1:T(2,128)(2,1)S(1)} all-gather(bf16[2,96,18]{2,0,1:T(2,128)(2,1)S(1)} %pad_maximum_fusion.13), channel_id=1, replica_groups=mesh['rep'=2,'fsdp'=16] {'fsdp'}, dimensions={1}, use_global_device_ids=true | all-gather | bytes 117504 | tf_op jit(solution)/shard_map/all_gather | solution.py:465
  90.9 12.1 slice_reduce_fusion.3
  105.7 37.6 %ring_gather.8 = (bf16[8,128,1536]{2,1,0:T(8,128)(2,1)}, f32[8,16,128]{2,1,0:T(8,128)}) custom-call(bf16[128,1536]{1,0:T(8,128)(2,1)} %fusion.17.x_ref, f32[16,128]{1,0:T(8,128)} %concatenate.62.side_ref), custom_call_target="tpu_custom_call" | custom-call | tf_op jit(solution)/shard_map/ring_gather/pallas_call | solution.py:129
  151.0 13.8 %slice_reduce_fusion.2 = (f32[1536]{0:T(1024)S(1)}, f32[1536]{0:T(1024)S(1)}) fusion(f32[2,1536,1]{2,0,1:T(2,128)} %get-tuple-element.211), kind=kLoop, calls=%fused_computation.101 | loop fusion | bytes 24576 | tf_op jit(solution)/shard_map/slice | solution.py:535
  168.3 5.6 maximum_select_fusion
  176.8 5.5 maximum_select_fusion.1
  185.5 6.7 maximum_select_fusion.2
  194.2 8.6 concatenate.64
  206.5 6.4 project.2
  213.0 6.0 fusion.61
  219.8 22.1 %attend.2 = (bf16[8,128,384]{2,1,0:T(8,128)(2,1)}, f32[8,384,1]{2,1,0:T(8,128)}, bf16[8,128,1536]{2,1,0:T(8,128)(2,1)}) custom-call(s32[9]{0:T(128)} %pad_add_fusion.info_ref, bf16[8,3,128,128]{3,2,1,0:T(8,128)(2,1)} %get-tuple-element.41.q_ref, bf16[2048,128]{1,0:T(8,128)(2,1)} %bitcast.384, s32[8,128,1]{2,1,0:T(8,128)} %copy.343.begin_ref, ...), custom_call_target="tpu_custom_call" | custom-call | tf_op jit(solution)/shard_map/attend/pallas_call | solution.py:315
  243.9 29.7 %ring_scatter.8 = f32[128,1536]{1,0:T(8,128)S(1)} custom-call(bf16[8,128,1536]{2,1,0:T(8,128)(2,1)S(1)} %copy-done), custom_call_target="tpu_custom_call" | custom-call | tf_op jit(solution)/shard_map/ring_scatter/pallas_call | solution.py:200
  275.4 30.2 %ring_gather.9 = (bf16[8,128,1536]{2,1,0:T(8,128)(2,1)}, f32[8,16,128]{2,1,0:T(8,128)}) custom-call(bf16[128,1536]{1,0:T(8,128)(2,1)} %copy-done.41, f32[16,128]{1,0:T(8,128)} %divide_bitcast_fusion.1.side_ref), custom_call_target="tpu_custom_call" | custom-call | tf_op jit(solution)/shard_map/ring_gather/pallas_call | solution.py:129
  306.4 6.4 fusion.74
  312.9 5.3 fusion
  322.0 29.4 %ring_scatter.9 = f32[128,1536]{1,0:T(8,128)S(1)} custom-call(bf16[8,128,1536]{2,1,0:T(8,128)(2,1)S(1)} %bitcast.350), custom_call_target="tpu_custom_call" | custom-call | tf_op jit(solution)/shard_map/ring_scatter/pallas_call | solution.py:200
  352.5 28.3 %ring_gather.10 = (bf16[8,128,1536]{2,1,0:T(8,128)(2,1)}, f32[8,16,128]{2,1,0:T(8,128)}) custom-call(bf16[128,1536]{1,0:T(8,128)(2,1)} %multiply_convert_fusion.5.x_ref, f32[16,128]{1,0:T(8,128)} %concatenate.62.side_ref), custom_call_target="tpu_custom_call" | custom-call | tf_op jit(solution)/shard_map/ring_gather/pallas_call | solution.py:129
  380.8 6.5 project.3
  393.5 22.2 %attend.3 = (bf16[8,128,384]{2,1,0:T(8,128)(2,1)}, f32[8,384,1]{2,1,0:T(8,128)}, bf16[8,128,1536]{2,1,0:T(8,128)(2,1)}) custom-call(s32[9]{0:T(128)} %pad_add_fusion.info_ref, bf16[8,3,128,128]{3,2,1,0:T(8,128)(2,1)} %get-tuple-element.47.q_ref, bf16[2048,128]{1,0:T(8,128)(2,1)} %bitcast.386, s32[8,128,1]{2,1,0:T(8,128)} %copy.343.begin_ref, ...), custom_call_target="tpu_custom_call" | custom-call | tf_op jit(solution)/shard_map/attend/pallas_call | solution.py:315
  417.6 30.5 %ring_scatter.10 = f32[128,1536]{1,0:T(8,128)S(1)} custom-call(bf16[8,128,1536]{2,1,0:T(8,128)(2,1)S(1)} %copy-done.1), custom_call_target="tpu_custom_call" | custom-call | tf_op jit(solution)/shard_map/ring_scatter/pallas_call | solution.py:200
  449.9 30.1 %ring_gather.11 = (bf16[8,128,1536]{2,1,0:T(8,128)(2,1)}, f32[8,16,128]{2,1,0:T(8,128)}) custom-call(bf16[128,1536]{1,0:T(8,128)(2,1)} %copy-done.42, f32[16,128]{1,0:T(8,128)} %divide_bitcast_fusion.side_ref), custom_call_target="tpu_custom_call" | custom-call | tf_op jit(solution)/shard_map/ring_gather/pallas_call | solution.py:129
  480.8 6.4 fusion.75
  487.3 5.3 fusion.1
  496.8 30.9 %ring_scatter.11 = f32[128,1536]{1,0:T(8,128)S(1)} custom-call(bf16[8,128,1536]{2,1,0:T(8,128)(2,1)S(1)} %bitcast.351), custom_call_target="tpu_custom_call" | custom-call | tf_op jit(solution)/shard_map/ring_scatter/pallas_call | solution.py:200
  528.5 27.4 %ring_gather.12 = (bf16[8,128,1536]{2,1,0:T(8,128)(2,1)}, f32[8,16,128]{2,1,0:T(8,128)}) custom-call(bf16[128,1536]{1,0:T(8,128)(2,1)} %x_ref, f32[16,128]{1,0:T(8,128)} %concatenate.66.side_ref), custom_call_target="tpu_custom_call" | custom-call | tf_op jit(solution)/shard_map/ring_gather/pallas_call | solution.py:129
  556.0 7.8 convolution_convert_fusion.6
  568.4 5.4 fusion.76
  586.8 6.2 add_convert_fusion.1
  593.0 28.9 %ring_scatter.12 = f32[128,1536]{1,0:T(8,128)S(1)} custom-call(bf16[8,128,1536]{2,1,0:T(8,128)(2,1)S(1)} %bitcast.347), custom_call_target="tpu_custom_call" | custom-call | tf_op jit(solution)/shard_map/ring_scatter/pallas_call | solution.py:200
  624.4 24.5 %ring_gather.13 = (bf16[8,128,1536]{2,1,0:T(8,128)(2,1)}, f32[8,16,128]{2,1,0:T(8,128)}) custom-call(bf16[128,1536]{1,0:T(8,128)(2,1)} %fusion.57.x_ref, f32[16,128]{1,0:T(8,128)} %broadcast_10_side_ref.2.side_ref), custom_call_target="tpu_custom_call" | custom-call | tf_op jit(solution)/shard_map/ring_gather/pallas_call | solution.py:129
  648.9 29.5 %attend_back.2 = (bf16[8,128,384]{2,1,0:T(8,128)(2,1)}, f32[2048,128]{1,0:T(8,128)}) custom-call(s32[9]{0:T(128)} %pad_add_fusion.info_ref, bf16[8,3,128,128]{3,2,1,0:T(8,128)(2,1)} %get-tuple-element.47.q_ref, bf16[2048,128]{1,0:T(8,128)(2,1)} %bitcast.387, s32[8,128,1]{2,1,0:T(8,128)} %copy.343.begin_ref, bf16[384,1536]{1,0:T(8,128)(2,1)} %bitcast.374, ...), custom_call_target="tpu_custom_call" | custom-call | tf_op jit(solution)/shard_map/attend_back/pallas_call | solution.py:380
  728.1 34.1 %ring_scatter.13 = f32[128,1536]{1,0:T(8,128)S(1)} custom-call(bf16[8,128,1536]{2,1,0:T(8,128)(2,1)S(1)} %bitcast.352), custom_call_target="tpu_custom_call" | custom-call | tf_op jit(solution)/shard_map/ring_scatter/pallas_call | solution.py:200
  765.4 33.9 %ring_gather.14 = (bf16[8,128,1536]{2,1,0:T(8,128)(2,1)}, f32[8,16,128]{2,1,0:T(8,128)}) custom-call(bf16[128,1536]{1,0:T(8,128)(2,1)} %get-tuple-element.161.x_ref, f32[16,128]{1,0:T(8,128)} %concatenate.68.side_ref), custom_call_target="tpu_custom_call" | custom-call | tf_op jit(solution)/shard_map/ring_gather/pallas_call | solution.py:129
  799.3 6.1 convolution_convert_fusion.7
  816.0 5.4 fusion.77
  840.3 33.1 %ring_scatter.14 = f32[128,1536]{1,0:T(8,128)S(1)} custom-call(bf16[8,128,1536]{2,1,0:T(8,128)(2,1)S(1)} %bitcast.348), custom_call_target="tpu_custom_call" | custom-call | tf_op jit(solution)/shard_map/ring_scatter/pallas_call | solution.py:200
  875.0 33.3 %ring_gather.15 = (bf16[8,128,1536]{2,1,0:T(8,128)(2,1)}, f32[8,16,128]{2,1,0:T(8,128)}) custom-call(bf16[128,1536]{1,0:T(8,128)(2,1)} %get-tuple-element.158.x_ref, f32[16,128]{1,0:T(8,128)} %broadcast_10_side_ref.2.side_ref), custom_call_target="tpu_custom_call" | custom-call | tf_op jit(solution)/shard_map/ring_gather/pallas_call | solution.py:129
  918.4 29.5 %attend_back.3 = (bf16[8,128,384]{2,1,0:T(8,128)(2,1)}, f32[2048,128]{1,0:T(8,128)}) custom-call(s32[9]{0:T(128)} %pad_add_fusion.info_ref, bf16[8,3,128,128]{3,2,1,0:T(8,128)(2,1)} %get-tuple-element.41.q_ref, bf16[2048,128]{1,0:T(8,128)(2,1)} %bitcast.385, s32[8,128,1]{2,1,0:T(8,128)} %copy.343.begin_ref, bf16[384,1536]{1,0:T(8,128)(2,1)} %bitcast.372, ...), custom_call_target="tpu_custom_call" | custom-call | tf_op jit(solution)/shard_map/attend_back/pallas_call | solution.py:380
  965.2 6.3 all-to-all-start.3
  979.2 48.5 %ring_scatter.15 = f32[128,1536]{1,0:T(8,128)S(1)} custom-call(bf16[8,128,1536]{2,1,0:T(8,128)(2,1)S(1)} %bitcast.349), custom_call_target="tpu_custom_call" | custom-call | tf_op jit(solution)/shard_map/ring_scatter/pallas_call | solution.py:200
  1034.1 29.9 %collective-permute-start.15 = (bf16[96,1536]{1,0:T(8,128)(2,1)S(1)}, bf16[96,1536]{1,0:T(8,128)(2,1)S(1)}, u32[]{:S(2)}, u32[]{:S(2)}) collective-permute-start(bf16[96,1536]{1,0:T(8,128)(2,1)S(1)} %copy-done.68), channel_id=1, source_target_pairs={{0,16},{16,0},{1,17},{17,1},{2,18},{18,2},{3,19},{19,3},{4,20},{20... | collective-permute-start | bytes 884744 | tf_op jit(solution)/shard_map/ppermute | solution.py:453
  1089.3 8.6 all-to-all-start.1
  1116.5 6.5 all-to-all-done.1
  1128.2 101.7 %collective-permute-done.11 = bf16[96,2578]{1,0:T(8,128)(2,1)} collective-permute-done((bf16[96,2578]{1,0:T(8,128)(2,1)}, bf16[96,2578]{1,0:T(8,128)(2,1)}, u32[]{:S(2)}, u32[]{:S(2)}) %collective-permute-start.11) | collective-permute-done | bytes 495008 | tf_op jit(solution)/shard_map/ppermute | solution.py:453
  1236.0 6.9 collective-permute-done.9
  1267.8 12.5 collective-permute-done.21
  1285.6 25.5 %collective-permute-done.17 = bf16[1536,512]{1,0:T(8,128)(2,1)S(1)} collective-permute-done((bf16[1536,512]{1,0:T(8,128)(2,1)S(1)}, bf16[1536,512]{1,0:T(8,128)(2,1)S(1)}, u32[]{:S(2)}, u32[]{:S(2)}) %collective-permute-start.17) | collective-permute-done | bytes 1572896 | tf_op jit(solution)/shard_map/ppermute | solution.py:453
  (531 shorter events, 316.5 us)
Async XLA Ops:
  7.5 184.7 %all-to-all-start = ((bf16[16,2,96,320]{3,2,1,0:T(8,128)(2,1)}), bf16[16,2,96,320]{3,2,1,0:T(8,128)(2,1)S(1)}, u32[]{:S(2)}, u32[]{:S(2)}) async-start(bf16[16,2,96,320]{3,2,1,0:T(8,128)(2,1)} %bitcast.376), calls=%async_computation | async-start | bytes 4718592 | tf_op jit(solution)/shard_map/all_to_all | solution.py:479
  14.9 149.9 %collective-permute-start.1 = (bf16[2,96,1536]{2,1,0:T(8,128)(2,1)}, bf16[2,96,1536]{2,1,0:T(8,128)(2,1)}, u32[]{:S(2)}, u32[]{:S(2)}) collective-permute-start(bf16[2,96,1536]{2,1,0:T(8,128)(2,1)} %param.24), channel_id=1, source_target_pairs={{0,1},{1,0},{2,3},{3,2},{4,5},{5,4},{6,7},{7,6},{8,9},{9,8},{10,11... | collective-permute-start | bytes 1769480 | tf_op jit(solution)/shard_map/ppermute | solution.py:438
  19.9 58.6 %copy-start.29 = (bf16[128,1536]{1,0:T(8,128)(2,1)S(1)}, bf16[128,1536]{1,0:T(8,128)(2,1)}, u32[]{:S(2)}) copy-start(bf16[128,1536]{1,0:T(8,128)(2,1)} %param.15) | copy-start | bytes 1179652
  19.9 148.4 %collective-permute-start.2 = (bf16[2,1536,512]{1,2,0:T(8,128)(2,1)}, bf16[2,1536,512]{1,2,0:T(8,128)(2,1)}, u32[]{:S(2)}, u32[]{:S(2)}) collective-permute-start(bf16[2,1536,512]{1,2,0:T(8,128)(2,1)} %bitcast.32), channel_id=1, source_target_pairs={{0,1},{1,0},{2,3},{3,2},{4,5},{5,4},{6,7},{7,6},{8,9},{9,8},{10,11... | collective-permute-start | bytes 9437192 | tf_op jit(solution)/shard_map/ppermute | solution.py:438
  24.8 57.2 %copy-start.106 = (s32[2,128,8]{1,2,0:T(8,128)S(1)}, s32[2,128,8]{1,2,0:T(8,128)}, u32[]{:S(2)}) copy-start(s32[2,128,8]{1,2,0:T(8,128)} %param.19) | copy-start | bytes 24580
  24.8 152.1 %collective-permute-start.3 = (bf16[2,1536,512]{1,2,0:T(8,128)(2,1)}, bf16[2,1536,512]{1,2,0:T(8,128)(2,1)}, u32[]{:S(2)}, u32[]{:S(2)}) collective-permute-start(bf16[2,1536,512]{1,2,0:T(8,128)(2,1)} %bitcast.36), channel_id=1, source_target_pairs={{0,1},{1,0},{2,3},{3,2},{4,5},{5,4},{6,7},{7,6},{8,9},{9,8},{10,11... | collective-permute-start | bytes 9437192 | tf_op jit(solution)/shard_map/ppermute | solution.py:438
  25.1 160.3 %collective-permute-start.4 = (bf16[2,512,1536]{2,1,0:T(8,128)(2,1)}, bf16[2,512,1536]{2,1,0:T(8,128)(2,1)}, u32[]{:S(2)}, u32[]{:S(2)}) collective-permute-start(bf16[2,512,1536]{2,1,0:T(8,128)(2,1)} %bitcast.398), channel_id=1, source_target_pairs={{0,1},{1,0},{2,3},{3,2},{4,5},{5,4},{6,7},{7,6},{8,9},{9,8},{10,11... | collective-permute-start | bytes 9437192 | tf_op jit(solution)/shard_map/ppermute | solution.py:438
  90.9 54.1 %copy-start.46 = (bf16[1,1536,16]{2,0,1:T(2,128)(2,1)S(1)}, bf16[1,1536,16]{2,0,1:T(2,128)(2,1)}, u32[]{:S(2)}) copy-start(bf16[1,1536,16]{2,0,1:T(2,128)(2,1)} %get-tuple-element.210) | copy-start | bytes 147460
  90.9 57.0 %copy-start.113 = (f32[128]{0:T(128)S(1)}, f32[128]{0:T(128)}, u32[]{:S(2)}) copy-start(f32[128]{0:T(128)} %compare_select_fusion) | copy-start | bytes 1540
  164.8 109.0 %copy-start.81 = (f32[1536]{0:T(1024)}, f32[1536]{0:T(1024)S(1)}, u32[]{:S(2)}) copy-start(f32[1536]{0:T(1024)S(1)} %get-tuple-element.145) | copy-start | bytes 18436
  213.0 6.0 collective-permute-start
  273.8 77.6 %copy-start.11 = (f32[128,1536]{1,0:T(8,128)}, f32[128,1536]{1,0:T(8,128)S(1)}, u32[]{:S(2)}) copy-start(f32[128,1536]{1,0:T(8,128)S(1)} %get-tuple-element.168) | copy-start | bytes 2359300
  387.3 4.3 collective-permute-start.5
  448.3 39.0 %copy-start.8 = (f32[128,1536]{1,0:T(8,128)}, f32[128,1536]{1,0:T(8,128)S(1)}, u32[]{:S(2)}) copy-start(f32[128,1536]{1,0:T(8,128)S(1)} %get-tuple-element.164) | copy-start | bytes 2359300
  680.6 42.6 %collective-permute-start.6 = (bf16[8,128,128]{2,1,0:T(8,128)(2,1)}, bf16[8,128,128]{2,1,0:T(8,128)(2,1)}, u32[]{:S(2)}, u32[]{:S(2)}) collective-permute-start(bf16[8,128,128]{2,1,0:T(8,128)(2,1)} %dynamic-slice_bitcast_fusion.5), channel_id=1, source_target_pairs={{0,1},{1,0},{2,3},{3,2},{4,5},{5,4},{6,7},{7,6},{8,9},{9,8},{10,11... | collective-permute-start | bytes 786440 | tf_op jit(solution)/shard_map/ppermute | solution.py:438
  683.3 394.4 %collective-permute-start.26 = (bf16[512,1536]{1,0:T(8,128)(2,1)}, bf16[512,1536]{1,0:T(8,128)(2,1)}, u32[]{:S(2)}, u32[]{:S(2)}) collective-permute-start(bf16[512,1536]{1,0:T(8,128)(2,1)} %dynamic-slice_bitcast_fusion), channel_id=1, source_target_pairs={{0,1},{1,0},{2,3},{3,2},{4,5},{5,4},{6,7},{7,6},{8,9},{9,8},{10,11... | collective-permute-start | bytes 4718600 | tf_op jit(solution)/shard_map/ppermute | solution.py:438
  691.1 390.0 %collective-permute-start.22 = (bf16[1536,512]{1,0:T(8,128)(2,1)}, bf16[1536,512]{1,0:T(8,128)(2,1)}, u32[]{:S(2)}, u32[]{:S(2)}) collective-permute-start(bf16[1536,512]{1,0:T(8,128)(2,1)} %bitcast.426), channel_id=1, source_target_pairs={{0,1},{1,0},{2,3},{3,2},{4,5},{5,4},{6,7},{7,6},{8,9},{9,8},{10,11... | collective-permute-start | bytes 4718600 | tf_op jit(solution)/shard_map/ppermute | solution.py:438
  695.6 7.2 collective-permute-start.10
  705.5 16.4 %all-to-all-start.4 = ((bf16[16,1,96]{2,1,0:T(2,128)(2,1)}), bf16[16,1,96]{2,1,0:T(2,128)(2,1)}, u32[]{:S(2)}, u32[]{:S(2)}) async-start(bf16[16,1,96]{2,1,0:T(2,128)(2,1)} %all_to_all.29), calls=%async_computation.4 | async-start | bytes 16384 | tf_op jit(solution)/shard_map/all_to_all | solution.py:649
  716.6 369.2 %collective-permute-start.18 = (bf16[1536,512]{1,0:T(8,128)(2,1)}, bf16[1536,512]{1,0:T(8,128)(2,1)}, u32[]{:S(2)}, u32[]{:S(2)}) collective-permute-start(bf16[1536,512]{1,0:T(8,128)(2,1)} %bitcast.427), channel_id=1, source_target_pairs={{0,1},{1,0},{2,3},{3,2},{4,5},{5,4},{6,7},{7,6},{8,9},{9,8},{10,11... | collective-permute-start | bytes 4718600 | tf_op jit(solution)/shard_map/ppermute | solution.py:438
  721.7 250.5 %collective-permute-start.14 = (bf16[96,1536]{1,0:T(8,128)(2,1)}, bf16[96,1536]{1,0:T(8,128)(2,1)}, u32[]{:S(2)}, u32[]{:S(2)}) collective-permute-start(bf16[96,1536]{1,0:T(8,128)(2,1)} %dynamic-slice_bitcast_fusion.2), channel_id=1, source_target_pairs={{0,1},{1,0},{2,3},{3,2},{4,5},{5,4},{6,7},{7,6},{8,9},{9,8},{10,11... | collective-permute-start | bytes 884744 | tf_op jit(solution)/shard_map/ppermute | solution.py:438
  834.7 115.3 %collective-permute-start.8 = (bf16[1536]{0:T(1024)(128)(2,1)S(1)}, bf16[1536]{0:T(1024)(128)(2,1)}, u32[]{:S(2)}, u32[]{:S(2)}) collective-permute-start(bf16[1536]{0:T(1024)(128)(2,1)S(1)} %fusion.46), channel_id=1, source_target_pairs={{0,1},{1,0},{2,3},{3,2},{4,5},{5,4},{6,7},{7,6},{8,9},{9,8},{10,11... | collective-permute-start | bytes 9224 | tf_op jit(solution)/shard_map/ppermute | solution.py:438
  875.0 35.5 %copy-start.69 = (bf16[384,1024]{1,0:T(8,128)(2,1)S(1)}, bf16[384,1024]{1,0:T(8,128)(2,1)}, u32[]{:S(2)}) copy-start(bf16[384,1024]{1,0:T(8,128)(2,1)} %copy.377) | copy-start | bytes 2359300
  950.0 147.9 %collective-permute-start.24 = (bf16[512,1536]{1,0:T(8,128)(2,1)}, bf16[512,1536]{1,0:T(8,128)(2,1)}, u32[]{:S(2)}, u32[]{:S(2)}) collective-permute-start(bf16[512,1536]{1,0:T(8,128)(2,1)} %dynamic-slice_bitcast_fusion.1), channel_id=1, source_target_pairs={{0,1},{1,0},{2,3},{3,2},{4,5},{5,4},{6,7},{7,6},{8,9},{9,8},{10,11... | collective-permute-start | bytes 4718600 | tf_op jit(solution)/shard_map/ppermute | solution.py:438
  951.5 13.7 %all-to-all-start.2 = ((bf16[16,1,96]{2,1,0:T(2,128)(2,1)}), bf16[16,1,96]{2,1,0:T(2,128)(2,1)S(1)}, u32[]{:S(2)}, u32[]{:S(2)}) async-start(bf16[16,1,96]{2,1,0:T(2,128)(2,1)} %all_to_all.28), calls=%async_computation.2 | async-start | bytes 16384 | tf_op jit(solution)/shard_map/all_to_all | solution.py:649
  965.2 124.0 %all-to-all-start.3 = ((bf16[16,96,322]{2,1,0:T(8,128)(2,1)}), bf16[16,96,322]{2,1,0:T(8,128)(2,1)}, u32[]{:S(2)}, u32[]{:S(2)}) async-start(bf16[16,96,322]{2,1,0:T(8,128)(2,1)} %pad_maximum_fusion.4), calls=%async_computation.3 | async-start | bytes 2359296 | tf_op jit(solution)/shard_map/all_to_all | solution.py:652
  972.2 2.6 collective-permute-start.7
  974.8 59.3 %collective-permute-start.12 = (bf16[96,1536]{1,0:T(8,128)(2,1)}, bf16[96,1536]{1,0:T(8,128)(2,1)}, u32[]{:S(2)}, u32[]{:S(2)}) collective-permute-start(bf16[96,1536]{1,0:T(8,128)(2,1)} %dynamic-slice_bitcast_fusion.3), channel_id=1, source_target_pairs={{0,1},{1,0},{2,3},{3,2},{4,5},{5,4},{6,7},{7,6},{8,9},{9,8},{10,11... | collective-permute-start | bytes 884744 | tf_op jit(solution)/shard_map/ppermute | solution.py:438
  979.1 48.6 %copy-start.30 = (bf16[128,1536]{1,0:T(8,128)(2,1)S(1)}, bf16[128,1536]{1,0:T(8,128)(2,1)}, u32[]{:S(2)}) copy-start(bf16[128,1536]{1,0:T(8,128)(2,1)} %param.15) | copy-start | bytes 1179652
  979.2 48.6 %copy-start.80 = (f32[1536]{0:T(1024)S(1)}, f32[1536]{0:T(1024)}, u32[]{:S(2)}) copy-start(f32[1536]{0:T(1024)} %copy-done.79) | copy-start | bytes 18436
  979.2 48.6 %copy-start.112 = (f32[128]{0:T(128)S(1)}, f32[128]{0:T(128)}, u32[]{:S(2)}) copy-start(f32[128]{0:T(128)} %copy-done.111) | copy-start | bytes 1540
  979.2 48.9 %copy-start.56 = (f32[128,1536]{1,0:T(8,128)S(1)}, f32[128,1536]{1,0:T(8,128)}, u32[]{:S(2)}) copy-start(f32[128,1536]{1,0:T(8,128)} %get-tuple-element.159) | copy-start | bytes 2359300
  979.2 50.1 %slice-start.1 = ((bf16[1536,512]{0,1:T(8,128)(2,1)}), bf16[1536,128]{0,1:T(8,128)(2,1)S(1)}, s32[]{:S(2)}) async-start(bf16[1536,512]{0,1:T(8,128)(2,1)} %copy-done.67), calls=%async_computation.6 | async-start | bytes 786432 | tf_op jit(solution)/shard_map/slice | solution.py:638
  1034.1 44.1 %copy-start.44 = (bf16[1024,1536]{1,0:T(8,128)(2,1)S(1)}, bf16[1024,1536]{1,0:T(8,128)(2,1)}, u32[]{:S(2)}) copy-start(bf16[1024,1536]{1,0:T(8,128)(2,1)} %convolution_convert_fusion.6) | copy-start | bytes 9437188
  1034.1 35.6 %collective-permute-start.15 = (bf16[96,1536]{1,0:T(8,128)(2,1)S(1)}, bf16[96,1536]{1,0:T(8,128)(2,1)S(1)}, u32[]{:S(2)}, u32[]{:S(2)}) collective-permute-start(bf16[96,1536]{1,0:T(8,128)(2,1)S(1)} %copy-done.68), channel_id=1, source_target_pairs={{0,16},{16,0},{1,17},{17,1},{2,18},{18,2},{3,19},{19,3},{4,20},{20... | collective-permute-start | bytes 884744 | tf_op jit(solution)/shard_map/ppermute | solution.py:453
  1069.7 6.8 collective-permute-start.13
  1076.5 26.3 %collective-permute-start.20 = (bf16[1536,512]{1,0:T(8,128)(2,1)}, bf16[1536,512]{1,0:T(8,128)(2,1)}, u32[]{:S(2)}, u32[]{:S(2)}) collective-permute-start(bf16[1536,512]{1,0:T(8,128)(2,1)} %bitcast.157), channel_id=1, source_target_pairs={{0,1},{1,0},{2,3},{3,2},{4,5},{5,4},{6,7},{7,6},{8,9},{9,8},{10,11... | collective-permute-start | bytes 4718600 | tf_op jit(solution)/shard_map/ppermute | solution.py:438
  1077.7 28.7 %collective-permute-start.16 = (bf16[1536,512]{1,0:T(8,128)(2,1)}, bf16[1536,512]{1,0:T(8,128)(2,1)}, u32[]{:S(2)}, u32[]{:S(2)}) collective-permute-start(bf16[1536,512]{1,0:T(8,128)(2,1)} %bitcast.149), channel_id=1, source_target_pairs={{0,1},{1,0},{2,3},{3,2},{4,5},{5,4},{6,7},{7,6},{8,9},{9,8},{10,11... | collective-permute-start | bytes 4718600 | tf_op jit(solution)/shard_map/ppermute | solution.py:438
  1081.1 174.1 %collective-permute-start.27 = (bf16[512,1536]{1,0:T(8,128)(2,1)}, bf16[512,1536]{1,0:T(8,128)(2,1)}, u32[]{:S(2)}, u32[]{:S(2)}) collective-permute-start(bf16[512,1536]{1,0:T(8,128)(2,1)} %fusion.4), channel_id=1, source_target_pairs={{0,16},{16,0},{1,17},{17,1},{2,18},{18,2},{3,19},{19,3},{4,20},{20... | collective-permute-start | bytes 4718600 | tf_op jit(solution)/shard_map/ppermute | solution.py:453
  1085.8 172.2 %collective-permute-start.23 = (bf16[1536,512]{1,0:T(8,128)(2,1)}, bf16[1536,512]{1,0:T(8,128)(2,1)}, u32[]{:S(2)}, u32[]{:S(2)}) collective-permute-start(bf16[1536,512]{1,0:T(8,128)(2,1)} %fusion.6), channel_id=1, source_target_pairs={{0,16},{16,0},{1,17},{17,1},{2,18},{18,2},{3,19},{19,3},{4,20},{20... | collective-permute-start | bytes 4718600 | tf_op jit(solution)/shard_map/ppermute | solution.py:453
  1089.3 33.8 %all-to-all-start.1 = ((bf16[16,96,322]{2,1,0:T(8,128)(2,1)}), bf16[16,96,322]{2,1,0:T(8,128)(2,1)}, u32[]{:S(2)}, u32[]{:S(2)}) async-start(bf16[16,96,322]{2,1,0:T(8,128)(2,1)} %pad_maximum_fusion.3), calls=%async_computation.1 | async-start | bytes 2359296 | tf_op jit(solution)/shard_map/all_to_all | solution.py:652
  1097.9 162.6 %collective-permute-start.19 = (bf16[1536,512]{1,0:T(8,128)(2,1)}, bf16[1536,512]{1,0:T(8,128)(2,1)}, u32[]{:S(2)}, u32[]{:S(2)}) collective-permute-start(bf16[1536,512]{1,0:T(8,128)(2,1)} %fusion.8), channel_id=1, source_target_pairs={{0,16},{16,0},{1,17},{17,1},{2,18},{18,2},{3,19},{19,3},{4,20},{20... | collective-permute-start | bytes 4718600 | tf_op jit(solution)/shard_map/ppermute | solution.py:453
  1102.8 159.5 %collective-permute-start.25 = (bf16[512,1536]{1,0:T(8,128)(2,1)}, bf16[512,1536]{1,0:T(8,128)(2,1)}, u32[]{:S(2)}, u32[]{:S(2)}) collective-permute-start(bf16[512,1536]{1,0:T(8,128)(2,1)} %fusion.5), channel_id=1, source_target_pairs={{0,16},{16,0},{1,17},{17,1},{2,18},{18,2},{3,19},{19,3},{4,20},{20... | collective-permute-start | bytes 4718600 | tf_op jit(solution)/shard_map/ppermute | solution.py:453
  1115.1 114.8 %collective-permute-start.11 = (bf16[96,2578]{1,0:T(8,128)(2,1)}, bf16[96,2578]{1,0:T(8,128)(2,1)}, u32[]{:S(2)}, u32[]{:S(2)}) collective-permute-start(bf16[96,2578]{1,0:T(8,128)(2,1)} %concatenate.75), channel_id=1, source_target_pairs={{0,16},{16,0},{1,17},{17,1},{2,18},{18,2},{3,19},{19,3},{4,20},{20... | collective-permute-start | bytes 1484936 | tf_op jit(solution)/shard_map/ppermute | solution.py:453
  1126.9 115.9 %copy-start.36 = (bf16[1536,512]{1,0:T(8,128)(2,1)S(1)}, bf16[1536,512]{1,0:T(8,128)(2,1)}, u32[]{:S(2)}) copy-start(bf16[1536,512]{1,0:T(8,128)(2,1)} %fusion.7) | copy-start | bytes 4718596
  1229.9 12.9 collective-permute-start.9
  1242.9 37.4 %collective-permute-start.21 = (bf16[1536,512]{1,0:T(8,128)(2,1)S(1)}, bf16[1536,512]{1,0:T(8,128)(2,1)}, u32[]{:S(2)}, u32[]{:S(2)}) collective-permute-start(bf16[1536,512]{1,0:T(8,128)(2,1)S(1)} %copy-done.36), channel_id=1, source_target_pairs={{0,16},{16,0},{1,17},{17,1},{2,18},{18,2},{3,19},{19,3},{4,20},{20... | collective-permute-start | bytes 4718600 | tf_op jit(solution)/shard_map/ppermute | solution.py:453
  1255.3 55.9 %collective-permute-start.17 = (bf16[1536,512]{1,0:T(8,128)(2,1)S(1)}, bf16[1536,512]{1,0:T(8,128)(2,1)S(1)}, u32[]{:S(2)}, u32[]{:S(2)}) collective-permute-start(bf16[1536,512]{1,0:T(8,128)(2,1)S(1)} %copy-done.35), channel_id=1, source_target_pairs={{0,16},{16,0},{1,17},{17,1},{2,18},{18,2},{3,19},{19,3},{4,20},{20... | collective-permute-start | bytes 4718600 | tf_op jit(solution)/shard_map/ppermute | solution.py:453
  (112 other events, 1191.9 us)

commit v2 on v1

v2 whole, which is shorter than its diff:
```python
import functools

import jax
import jax.numpy as jnp
from jax import lax
from jax.experimental import pallas as pl
from jax.experimental.pallas import tpu as pltpu
from jax.sharding import PartitionSpec as P

HEADS = 24
KV_HEADS = 8
HD = 64
LAYERS = 2
GROUP = HEADS // KV_HEADS
LANES = 128
EPS = 1e-06
MASKED = -1e30
MESH = pl.DeviceIdType.MESH
F32 = jnp.float32
BF16 = jnp.bfloat16


def ring_place(chip, count):
    return lax.select(lax.rem(chip, 2) == 0, chip // 2, count - 1 - chip // 2)


def ring_chip(place, count):
    return lax.select(place < count // 2, 2 * place, 2 * (count - 1 - place) + 1)


def ring_setup(count):
    me = lax.axis_index("fsdp")
    chip, core = me // 2, lax.rem(me, 2)
    place = ring_place(chip, count)

    def at(offset):
        return ring_chip(lax.rem(place + offset + 2 * count, count), count)

    near = [{"fsdp": at(1) * 2 + core}, {"fsdp": at(-1) * 2 + core}]
    return chip, at, near


def partner_of(axis):
    if axis == "rep":
        return {"rep": 1 - lax.axis_index("rep")}
    me = lax.axis_index("fsdp")
    return {"fsdp": me + 1 - 2 * lax.rem(me, 2)}


def meet(others):
    barrier = pltpu.get_barrier_semaphore()
    for other in others:
        pl.semaphore_signal(barrier, inc=1, device_id=other, device_id_type=MESH)
    pl.semaphore_wait(barrier, len(others))


def remote(src, dst, send_sem, recv_sem, device):
    return pltpu.make_async_remote_copy(
        src_ref=src,
        dst_ref=dst,
        send_sem=send_sem,
        recv_sem=recv_sem,
        device_id=device,
        device_id_type=MESH,
    )


def ring_hops(count):
    half = count // 2
    return {(0, 0): half, (1, 1): half, (0, 1): half - 1, (1, 0): half - 1}


def gather_kernel(count, axes, sided, *refs):
    riders = len(axes)
    sources = refs[: 1 + sided]
    ride_in = refs[1 + sided : 1 + sided + riders]
    rest = refs[1 + sided + riders :]
    targets, rest = rest[: 1 + sided], rest[1 + sided :]
    ride_out, rest = rest[:riders], rest[riders:]
    own_sem, send_sem, recv_sem, side_send, side_recv, ride_send, ride_recv = rest
    chip, at, near = ring_setup(count)
    x_ref, o_ref = sources[0], targets[0]
    half_rows = x_ref.shape[0] // 2
    hops = ring_hops(count)
    steps = count // 2
    meet(near + [partner_of(axis) for axis in sorted(set(axes))])
    rides = [
        remote(ride_in[i], ride_out[i], ride_send.at[i], ride_recv.at[i], partner_of(axes[i]))
        for i in range(riders)
    ]
    for ride in rides:
        ride.start()
    own = [
        pltpu.make_async_copy(sources[i], targets[i].at[chip], own_sem.at[i])
        for i in range(1 + sided)
    ]
    for copy in own:
        copy.start()

    def piece(key, step, arrived):
        direction, part = key
        moved = step + 1 if arrived else step
        block = at(-moved if direction == 0 else moved)
        rows = pl.ds(part * half_rows, half_rows)
        target = o_ref.at[block, rows]
        return remote(
            x_ref.at[rows] if step == 0 and not arrived else target,
            target,
            send_sem.at[direction, part, step],
            recv_sem.at[direction, part, step],
            near[direction],
        )

    def side_piece(direction, step, arrived):
        moved = step + 1 if arrived else step
        target = targets[1].at[at(-moved if direction == 0 else moved)]
        return remote(
            sources[1] if step == 0 and not arrived else target,
            target,
            side_send.at[direction, step],
            side_recv.at[direction, step],
            near[direction],
        )

    side_hops = (steps, steps - 1) if sided else (0, 0)
    for step in range(steps + 1):
        for direction in range(2):
            if 0 < step <= side_hops[direction]:
                side_piece(direction, step - 1, True).wait_recv()
            if step < side_hops[direction]:
                side_piece(direction, step, False).start()
        for key in hops:
            if 0 < step <= hops[key]:
                piece(key, step - 1, True).wait_recv()
            if step < hops[key]:
                piece(key, step, False).start()
    for step in range(steps):
        for direction in range(2):
            if step < side_hops[direction]:
                side_piece(direction, step, False).wait_send()
        for key in hops:
            if step < hops[key]:
                piece(key, step, False).wait_send()
    for copy in own:
        copy.wait()
    for ride in rides:
        ride.wait()


IDENTITIES = {}


def identity(*key):
    return IDENTITIES.setdefault(key, len(IDENTITIES))


def shape_of(array):
    return jax.ShapeDtypeStruct(array.shape, array.dtype)


def ring_gather(count, arrays, rides=()):
    steps = count // 2
    sided = len(arrays) - 1
    axes = tuple(axis for _, axis in rides)
    passengers = [array for array, _ in rides]
    dma = pltpu.SemaphoreType.DMA
    return pl.pallas_call(
        functools.partial(gather_kernel, count, axes, sided),
        out_shape=tuple(
            jax.ShapeDtypeStruct((count,) + a.shape, a.dtype) for a in arrays
        ) + tuple(shape_of(a) for a in passengers),
        in_specs=[pl.BlockSpec(memory_space=pl.ANY)] * (len(arrays) + len(rides)),
        out_specs=[pl.BlockSpec(memory_space=pl.ANY)] * (len(arrays) + len(rides)),
        scratch_shapes=[
            dma((2,)),
            dma((2, 2, steps)),
            dma((2, 2, steps)),
            dma((2, steps)),
            dma((2, steps)),
            dma((max(len(rides), 1),)),
            dma((max(len(rides), 1),)),
        ],
        compiler_params=pltpu.CompilerParams(
            collective_id=identity("gather", sided, axes, *(a.shape for a in passengers)),
            has_side_effects=True,
        ),
        name="ring_gather",
    )(*arrays, *passengers)


def scatter_kernel(count, axes, *refs):
    riders = len(axes)
    p_ref, ride_in, o_ref, ride_out = refs[0], refs[1 : 1 + riders], refs[1 + riders], refs[2 + riders : 2 + 2 * riders]
    land, send_sem, recv_sem, ride_send, ride_recv = refs[2 + 2 * riders :]
    chip, at, near = ring_setup(count)
    half_rows = o_ref.shape[0] // 2
    hops = ring_hops(count)
    steps = count // 2
    meet(near + [partner_of(axis) for axis in sorted(set(axes))])
    rides = [
        remote(ride_in[i], ride_out[i], ride_send.at[i], ride_recv.at[i], partner_of(axes[i]))
        for i in range(riders)
    ]
    for ride in rides:
        ride.start()

    def ahead(key, step):
        places = hops[key] - step
        return at(places if key[0] == 0 else -places)

    def piece(key, step):
        direction, part = key
        rows = pl.ds(part * half_rows, half_rows)
        return remote(
            p_ref.at[ahead(key, step), rows] if step == 0 else land.at[direction, part, step - 1],
            land.at[direction, part, step],
            send_sem.at[direction, part, step],
            recv_sem.at[direction, part, step],
            near[direction],
        )

    for step in range(steps + 1):
        for key in hops:
            direction, part = key
            rows = pl.ds(part * half_rows, half_rows)
            if 0 < step <= hops[key]:
                piece(key, step - 1).wait_recv()
                if step < hops[key]:
                    slot = land.at[direction, part, step - 1]
                    total = slot[...].astype(F32) + p_ref[ahead(key, step), rows].astype(F32)
                    slot[...] = total.astype(BF16)
            if step < hops[key]:
                piece(key, step).start()
    for part in range(2):
        rows = pl.ds(part * half_rows, half_rows)
        total = p_ref[chip, rows].astype(F32)
        for direction in range(2):
            total = total + land[direction, part, hops[direction, part] - 1].astype(F32)
        o_ref[rows, :] = total
    for step in range(steps):
        for key in hops:
            if step < hops[key]:
                piece(key, step).wait_send()
    for ride in rides:
        ride.wait()


def ring_scatter(count, partial, rides=()):
    _, rows, width = partial.shape
    steps = count // 2
    axes = tuple(axis for _, axis in rides)
    passengers = [array for array, _ in rides]
    away = [pl.BlockSpec(memory_space=pl.ANY)] * len(rides)
    here = [pl.BlockSpec(memory_space=pltpu.VMEM)]
    dma = pltpu.SemaphoreType.DMA
    return pl.pallas_call(
        functools.partial(scatter_kernel, count, axes),
        out_shape=(jax.ShapeDtypeStruct((rows, width), F32),)
        + tuple(shape_of(a) for a in passengers),
        in_specs=here + away,
        out_specs=here + away,
        scratch_shapes=[
            pltpu.VMEM((2, 2, steps, rows // 2, width), partial.dtype),
            dma((2, 2, steps)),
            dma((2, 2, steps)),
            dma((max(len(rides), 1),)),
            dma((max(len(rides), 1),)),
        ],
        compiler_params=pltpu.CompilerParams(
            collective_id=identity("scatter", axes, *(a.shape for a in passengers)),
            has_side_effects=True,
            vmem_limit_bytes=24 << 20,
        ),
        name="ring_scatter",
    )(partial, *passengers)


def setup_kernel(
    count, slab_ref, out_w_ref, small_ref, table_ref,
    heads_ref, outs_ref, smalls_ref, tables_ref,
    own_sem, slab_send, slab_recv, pass_send, pass_recv,
    small_send, small_recv, table_send, table_recv, out_send, out_recv,
):
    devices = 2 * count
    me = lax.axis_index("fsdp")
    chip, core = me // 2, lax.rem(me, 2)
    layers = slab_ref.shape[1]

    def device(offset):
        return {"fsdp": lax.rem(me + offset, devices)}

    def chip_at(offset):
        return lax.rem(chip + offset + count, count)

    partner = partner_of("fsdp")
    meet([device(offset) for offset in range(1, devices)])
    copies = [
        pltpu.make_async_copy(slab_ref.at[chip, layer], heads_ref.at[layer, me], own_sem.at[layer])
        for layer in range(layers)
    ] + [
        pltpu.make_async_copy(small_ref, smalls_ref.at[me], own_sem.at[layers]),
        pltpu.make_async_copy(table_ref, tables_ref.at[chip], own_sem.at[layers + 1]),
        pltpu.make_async_copy(out_w_ref, outs_ref.at[core], own_sem.at[layers + 2]),
    ]
    sends = [
        remote(small_ref, smalls_ref.at[me], small_send.at[offset], small_recv.at[offset], device(offset))
        for offset in range(1, devices)
    ]
    for offset in range(1, count):
        there = {"fsdp": chip_at(offset) * 2 + core}
        sends.append(
            remote(table_ref, tables_ref.at[chip], table_send.at[offset], table_recv.at[offset], there)
        )
        for layer in range(layers):
            sends.append(
                remote(
                    slab_ref.at[chip_at(offset), layer], heads_ref.at[layer, me],
                    slab_send.at[offset, layer], slab_recv.at[offset, layer], there,
                )
            )
    for layer in range(layers):
        sends.append(
            remote(
                slab_ref.at[chip, layer], heads_ref.at[layer, me],
                pass_send.at[0, layer], pass_recv.at[0, layer], partner,
            )
        )
    sends.append(remote(out_w_ref, outs_ref.at[core], out_send.at[0], out_recv.at[0], partner))
    for copy in copies + sends:
        copy.start()
    for offset in range(1, count):
        origin = chip_at(-offset) * 2 + core
        for layer in range(layers):
            slot = heads_ref.at[layer, origin]
            remote(slot, slot, slab_send.at[offset, layer], slab_recv.at[offset, layer], partner).wait_recv()
            forward = remote(slot, slot, pass_send.at[offset, layer], pass_recv.at[offset, layer], partner)
            forward.start()
    for offset in range(1, count):
        origin = chip_at(-offset)
        table = tables_ref.at[origin]
        remote(table, table, table_send.at[offset], table_recv.at[offset], partner).wait_recv()
    for offset in range(count):
        origin = chip_at(-offset) * 2 + 1 - core
        mine = chip_at(-offset) * 2 + core
        for layer in range(layers):
            slot, sent = heads_ref.at[layer, origin], heads_ref.at[layer, mine]
            if offset > 0:
                remote(sent, sent, pass_send.at[offset, layer], pass_recv.at[offset, layer], partner).wait_send()
            remote(slot, slot, pass_send.at[offset, layer], pass_recv.at[offset, layer], partner).wait_recv()
    for offset in range(1, devices):
        slot = smalls_ref.at[lax.rem(me - offset + devices, devices)]
        remote(slot, slot, small_send.at[offset], small_recv.at[offset], partner).wait_recv()
    other = outs_ref.at[1 - core]
    remote(other, other, out_send.at[0], out_recv.at[0], partner).wait_recv()
    for copy in copies:
        copy.wait()
    for send in sends:
        send.wait_send()


def exchange_weights(count, slabs, out_w, small, table):
    layers = slabs.shape[1]
    devices = 2 * count
    dma = pltpu.SemaphoreType.DMA
    anywhere = pl.BlockSpec(memory_space=pl.ANY)
    return pl.pallas_call(
        functools.partial(setup_kernel, count),
        out_shape=(
            jax.ShapeDtypeStruct((layers, devices) + slabs.shape[2:], slabs.dtype),
            jax.ShapeDtypeStruct((2,) + out_w.shape, out_w.dtype),
            jax.ShapeDtypeStruct((devices,) + small.shape, small.dtype),
            jax.ShapeDtypeStruct((count,) + table.shape, table.dtype),
        ),
        in_specs=[anywhere] * 4,
        out_specs=[anywhere] * 4,
        scratch_shapes=[
            dma((layers + 3,)),
            dma((count, layers)),
            dma((count, layers)),
            dma((count, layers)),
            dma((count, layers)),
            dma((devices,)),
            dma((devices,)),
            dma((count,)),
            dma((count,)),
            dma((1,)),
            dma((1,)),
        ],
        compiler_params=pltpu.CompilerParams(
            collective_id=identity("setup"), has_side_effects=True
        ),
        name="exchange_weights",
    )(slabs, out_w, small, table)


def finish_kernel(
    count, replicas, g_ref, o_ref, land, total, mine, peer,
    pair_send, pair_recv, part_send, part_recv, rep_send, rep_recv,
):
    me = lax.axis_index("fsdp")
    chip, core = me // 2, lax.rem(me, 2)
    partner = partner_of("fsdp")

    def chip_at(offset):
        return lax.rem(chip + offset + count, count)

    def device(offset):
        return {"fsdp": chip_at(offset) * 2 + core}

    across = [partner_of("rep")] if replicas == 2 else []
    meet([device(offset) for offset in range(1, count)] + [partner] + across)
    swap = remote(g_ref.at[1 - core], land, pair_send.at[0], pair_recv.at[0], partner)
    swap.start()
    swap.wait()
    for block in range(count):
        total[block] = (g_ref[core, block].astype(F32) + land[block].astype(F32)).astype(BF16)
    sends = [
        remote(
            total.at[chip_at(offset)], mine.at[chip],
            part_send.at[offset], part_recv.at[offset], device(offset),
        )
        for offset in range(1, count)
    ]
    for send in sends:
        send.start()
    mine[chip] = total[chip]

    def to_peer(offset):
        slot = chip_at(-offset)
        return remote(mine.at[slot], peer.at[slot], rep_send.at[offset], rep_recv.at[offset], across[0])

    for offset in range(count):
        if offset > 0:
            slot = mine.at[chip_at(-offset)]
            remote(slot, slot, part_send.at[offset], part_recv.at[offset], partner).wait_recv()
        if replicas == 2:
            to_peer(offset).start()
    for offset in range(count):
        slot = chip_at(-offset)
        if replicas == 2:
            to_peer(offset).wait()
            o_ref[slot] = mine[slot].astype(F32) + peer[slot].astype(F32)
        else:
            o_ref[slot] = mine[slot].astype(F32)
    for send in sends:
        send.wait_send()


def finish_heads(count, replicas, g):
    part = g.shape[1:]
    dma = pltpu.SemaphoreType.DMA
    here = pl.BlockSpec(memory_space=pltpu.VMEM)
    buffer = pltpu.VMEM(part, BF16)
    return pl.pallas_call(
        functools.partial(finish_kernel, count, replicas),
        out_shape=jax.ShapeDtypeStruct(part, F32),
        in_specs=[here],
        out_specs=here,
        scratch_shapes=[
            buffer, buffer, buffer, buffer,
            dma((1,)), dma((1,)), dma((count,)), dma((count,)), dma((count,)), dma((count,)),
        ],
        compiler_params=pltpu.CompilerParams(
            collective_id=identity("finish"), has_side_effects=True, vmem_limit_bytes=24 << 20
        ),
        name="finish_heads",
    )(g)


def dot(left, right, contract=((1,), (0,))):
    return lax.dot_general(left, right, (contract, ((), ())), preferred_element_type=F32)


NT = ((1,), (1,))
TN = ((0,), (0,))


def lanes_of(field):
    return lax.broadcasted_iota(jnp.int32, field.shape, 1)


def turn(field):
    return pltpu.roll(field, HD, 1)


def spin(field, cosine, sine):
    swapped = jnp.where(
        lax.rem(lanes_of(field), HD) < HD // 2,
        -pltpu.roll(field, LANES - HD // 2, 1),
        pltpu.roll(field, HD // 2, 1),
    )
    return field * cosine + swapped * sine


def project_kernel(x_ref, w_ref, cos_ref, sin_ref, q_ref, kv_ref):
    rows = dot(x_ref[...], w_ref[...])
    cosine, sine = cos_ref[...], sin_ref[...]
    first = spin(rows[:, :LANES], cosine, sine)
    second = spin(rows[:, LANES : 2 * LANES], cosine, sine)
    third = rows[:, 2 * LANES :]
    low = lanes_of(first) < HD
    kv_ref[...] = jnp.where(low, turn(second), turn(third)).astype(BF16)
    for head, field in enumerate((first, turn(first), second)):
        rounded = jnp.where(low, field, 0.0).astype(BF16).astype(F32)
        scaled = (rounded * (HD**-0.5)).astype(BF16)
        for block in range(2):
            q_ref[block, head] = scaled[block * LANES : (block + 1) * LANES]


def project(x, w, cosine, sine):
    tokens, width = x.shape
    tile = 2 * LANES
    return pl.pallas_call(
        project_kernel,
        grid=(tokens // tile,),
        out_shape=(
            jax.ShapeDtypeStruct((tokens // LANES, GROUP, LANES, LANES), BF16),
            jax.ShapeDtypeStruct((tokens, LANES), BF16),
        ),
        in_specs=[
            pl.BlockSpec((tile, width), lambda i: (i, 0)),
            pl.BlockSpec(w.shape, lambda i: (0, 0)),
            pl.BlockSpec((tile, LANES), lambda i: (i, 0)),
            pl.BlockSpec((tile, LANES), lambda i: (i, 0)),
        ],
        out_specs=[
            pl.BlockSpec((2, GROUP, LANES, LANES), lambda i: (i, 0, 0, 0)),
            pl.BlockSpec((tile, LANES), lambda i: (i, 0)),
        ],
        name="project",
    )(x, w, cosine, sine)


def allowed_keys(begin, block, chunk, core):
    shape = (GROUP * LANES, 2 * LANES)
    place = lax.broadcasted_iota(jnp.int32, shape, 1)
    shift = jnp.where(place < LANES, core, -core)
    key = chunk * 2 * LANES + place + shift * LANES
    query = block * LANES + lax.rem(lax.broadcasted_iota(jnp.int32, shape, 0), LANES)
    return (key >= begin) & (key <= query)


def fill_out_weights(w_ref, wide_ref):
    rows = w_ref.shape[0]
    wide_ref[:rows] = w_ref[...]
    wide_ref[rows:] = jnp.zeros((wide_ref.shape[0] - rows, wide_ref.shape[1]), BF16)


def attend_kernel(info_ref, q_ref, own_ref, other_ref, begin_ref, w_ref, att_ref, lse_ref, out_ref, wide_ref):
    step = pl.program_id(0)
    core = info_ref[0]
    block = 2 * step + core
    first = info_ref[1 + step] // (2 * LANES)

    @pl.when(step == 0)
    def _():
        fill_out_weights(w_ref, wide_ref)

    q = q_ref[0].reshape(GROUP * LANES, LANES)
    begin = jnp.concatenate([begin_ref[0]] * GROUP, 0)

    def one(chunk, state):
        top, total, acc = state
        keys = jnp.concatenate([own_ref[chunk], other_ref[chunk]], 0)
        allowed = allowed_keys(begin, block, chunk, core)
        scores = jnp.where(allowed, dot(q, keys, NT), MASKED)
        new_top = jnp.maximum(top, jnp.max(scores, -1, keepdims=True))
        weights = jnp.where(allowed, jnp.exp(scores - new_top), 0.0)
        shrink = jnp.exp(top - new_top)
        total = total * shrink + jnp.sum(weights, -1, keepdims=True)
        return new_top, total, acc * shrink + dot(weights.astype(BF16), keys)

    rows = GROUP * LANES
    top, total, acc = lax.fori_loop(
        first,
        step + 1,
        one,
        (jnp.full((rows, 1), MASKED, F32), jnp.zeros((rows, 1), F32), jnp.zeros((rows, LANES), F32)),
    )
    lse_ref[0] = top + jnp.log(total)
    att = acc / total
    heads = [att[h * LANES : (h + 1) * LANES] for h in range(GROUP)]
    low = lanes_of(heads[0]) < HD
    wide = jnp.concatenate(
        [jnp.where(low, turn(heads[0]), heads[1]), jnp.where(low, turn(heads[2]), 0.0)], 1
    ).astype(BF16)
    att_ref[0] = wide
    out_ref[0] = dot(wide, wide_ref[...]).astype(BF16)


def attend(info, q, own, other, begin, w):
    blocks = q.shape[0]
    width = w.shape[1]
    wide = 2 * LANES
    return pl.pallas_call(
        attend_kernel,
        grid_spec=pltpu.PrefetchScalarGridSpec(
            num_scalar_prefetch=1,
            grid=(blocks,),
            in_specs=[
                pl.BlockSpec((1, GROUP, LANES, LANES), lambda i, s: (i, 0, 0, 0)),
                pl.BlockSpec(own.shape, lambda i, s: (0, 0, 0)),
                pl.BlockSpec(own.shape, lambda i, s: (0, 0, 0)),
                pl.BlockSpec((1, LANES, 1), lambda i, s: (i, 0, 0)),
                pl.BlockSpec(w.shape, lambda i, s: (0, 0)),
            ],
            out_specs=[
                pl.BlockSpec((1, LANES, wide), lambda i, s: (i, 0, 0)),
                pl.BlockSpec((1, GROUP * LANES, 1), lambda i, s: (i, 0, 0)),
                pl.BlockSpec((1, LANES, width), lambda i, s: (i, 0, 0)),
            ],
            scratch_shapes=[pltpu.VMEM((wide, width), BF16)],
        ),
        out_shape=(
            jax.ShapeDtypeStruct((blocks, LANES, wide), BF16),
            jax.ShapeDtypeStruct((blocks, GROUP * LANES, 1), F32),
            jax.ShapeDtypeStruct((blocks, LANES, width), BF16),
        ),
        name="attend",
    )(info, q, own, other, begin, w)


def attend_back_kernel(
    info_ref, q_ref, own_ref, other_ref, begin_ref, w_ref, att_ref, lse_ref, db_ref, cos_ref, sin_ref,
    dq_ref, d_own_ref, d_other_ref, wide_ref,
):
    step = pl.program_id(0)
    core = info_ref[0]
    block = 2 * step + core
    first = info_ref[1 + step] // (2 * LANES)

    @pl.when(step == 0)
    def _():
        fill_out_weights(w_ref, wide_ref)
        d_own_ref[...] = jnp.zeros_like(d_own_ref)
        d_other_ref[...] = jnp.zeros_like(d_other_ref)

    q = q_ref[0].reshape(GROUP * LANES, LANES)
    begin = jnp.concatenate([begin_ref[0]] * GROUP, 0)

    def spread(wide):
        front, back = wide[:, :LANES], wide[:, LANES:]
        low = lanes_of(front) < HD
        parts = [jnp.where(low, 0.0, part) for part in (turn(front), front, turn(back))]
        return jnp.concatenate(parts, 0)

    datt = spread(dot(db_ref[0], wide_ref[...], NT)).astype(BF16)
    att = spread(att_ref[0].astype(F32))
    delta = jnp.sum(datt.astype(F32) * att, -1, keepdims=True)
    lse = lse_ref[0]
    both = jnp.concatenate([q, datt], 0)

    def one(chunk, acc):
        keys = jnp.concatenate([own_ref[chunk], other_ref[chunk]], 0)
        allowed = allowed_keys(begin, block, chunk, core)
        weights = jnp.where(allowed, jnp.exp(dot(q, keys, NT) - lse), 0.0)
        slope = (weights * (dot(datt, keys, NT) - delta)).astype(BF16)
        d_keys = dot(jnp.concatenate([slope, weights.astype(BF16)], 0), both, TN)
        d_own_ref[chunk] += d_keys[:LANES]
        d_other_ref[chunk] += d_keys[LANES:]
        return acc + dot(slope, keys)

    acc = lax.fori_loop(first, step + 1, one, jnp.zeros((GROUP * LANES, LANES), F32))
    heads = [acc[h * LANES : (h + 1) * LANES] * (HD**-0.5) for h in range(GROUP)]
    low = lanes_of(heads[0]) < HD
    cosine, sine = cos_ref[0], -sin_ref[0]
    front = spin(jnp.where(low, heads[0], turn(heads[1])), cosine, sine)
    back = spin(jnp.where(low, heads[2], 0.0), cosine, sine)
    dq_ref[0] = jnp.concatenate([front, back], 1).astype(BF16)


def attend_back(info, q, own, other, begin, w, att, lse, db, cosine, sine):
    blocks = q.shape[0]
    width = w.shape[1]
    wide = 2 * LANES
    return pl.pallas_call(
        attend_back_kernel,
        grid_spec=pltpu.PrefetchScalarGridSpec(
            num_scalar_prefetch=1,
            grid=(blocks,),
            in_specs=[
                pl.BlockSpec((1, GROUP, LANES, LANES), lambda i, s: (i, 0, 0, 0)),
                pl.BlockSpec(own.shape, lambda i, s: (0, 0, 0)),
                pl.BlockSpec(own.shape, lambda i, s: (0, 0, 0)),
                pl.BlockSpec((1, LANES, 1), lambda i, s: (i, 0, 0)),
                pl.BlockSpec(w.shape, lambda i, s: (0, 0)),
                pl.BlockSpec((1, LANES, wide), lambda i, s: (i, 0, 0)),
                pl.BlockSpec((1, GROUP * LANES, 1), lambda i, s: (i, 0, 0)),
                pl.BlockSpec((1, LANES, width), lambda i, s: (i, 0, 0)),
                pl.BlockSpec((1, LANES, LANES), lambda i, s: (i, 0, 0)),
                pl.BlockSpec((1, LANES, LANES), lambda i, s: (i, 0, 0)),
            ],
            out_specs=[
                pl.BlockSpec((1, LANES, wide), lambda i, s: (i, 0, 0)),
                pl.BlockSpec(own.shape, lambda i, s: (0, 0, 0)),
                pl.BlockSpec(own.shape, lambda i, s: (0, 0, 0)),
            ],
            scratch_shapes=[pltpu.VMEM((wide, width), BF16)],
        ),
        out_shape=(
            jax.ShapeDtypeStruct((blocks, LANES, wide), BF16),
            jax.ShapeDtypeStruct(own.shape, F32),
            jax.ShapeDtypeStruct(own.shape, F32),
        ),
        name="attend_back",
    )(info, q, own, other, begin, w, att, lse, db, cosine, sine)


def join_kernel(dq_ref, own_ref, got_ref, cos_ref, sin_ref, w_ref, x_ref, out_ref, g_ref):
    pair = own_ref[...] + got_ref[...].astype(F32)
    front = spin(pair, cos_ref[...], -sin_ref[...])
    low = lanes_of(pair) < HD
    middle = jnp.where(low, dq_ref[:, LANES:].astype(F32), turn(front))
    last = jnp.where(low, turn(pair), 0.0)
    rows = jnp.concatenate([dq_ref[:, :LANES], middle.astype(BF16), last.astype(BF16)], 1)
    out_ref[...] = dot(rows, w_ref[...], NT).astype(BF16)
    part = dot(x_ref[...], rows, TN)

    @pl.when(pl.program_id(0) == 0)
    def _():
        g_ref[...] = part

    @pl.when(pl.program_id(0) > 0)
    def _():
        g_ref[...] += part


def join(dq, own, got, cosine, sine, w, x):
    tokens, width = x.shape
    tile = 2 * LANES

    def rows(columns):
        return pl.BlockSpec((tile, columns), lambda i: (i, 0))

    return pl.pallas_call(
        join_kernel,
        grid=(tokens // tile,),
        out_shape=(
            jax.ShapeDtypeStruct((tokens, width), BF16),
            jax.ShapeDtypeStruct(w.shape, F32),
        ),
        in_specs=[rows(2 * LANES), rows(LANES), rows(LANES), rows(LANES), rows(LANES),
                  pl.BlockSpec(w.shape, lambda i: (0, 0)), rows(width)],
        out_specs=[rows(width), pl.BlockSpec(w.shape, lambda i: (0, 0))],
        compiler_params=pltpu.CompilerParams(vmem_limit_bytes=40 << 20),
        name="join",
    )(dq, own, got, cosine, sine, w, x)


def mix_kernel(x_ref, share_ref, *refs):
    weights, out_ref = refs[:6], refs[6]
    x = x_ref[...]
    out = None
    for e in range(2):
        gate_w, up_w, down_w = weights[3 * e : 3 * e + 3]
        act_gate, act_up = dot(x, gate_w[...]), dot(x, up_w[...])
        hidden = jax.nn.silu(act_gate) * act_up * share_ref[:, e : e + 1]
        part = dot(hidden.astype(BF16), down_w[...])
        out = part if out is None else out + part
    out_ref[...] = out.astype(BF16)


def mix(x, share, weights):
    tokens, width = x.shape
    tile = 2 * LANES

    def rows(columns):
        return pl.BlockSpec((tile, columns), lambda i: (i, 0))

    return pl.pallas_call(
        mix_kernel,
        grid=(tokens // tile,),
        out_shape=jax.ShapeDtypeStruct((tokens, width), BF16),
        in_specs=[rows(width), rows(2)]
        + [pl.BlockSpec(w.shape, lambda i: (0, 0)) for w in weights],
        out_specs=rows(width),
        compiler_params=pltpu.CompilerParams(vmem_limit_bytes=50 << 20),
        name="mix",
    )(x, share, *weights)


def mix_back_kernel(x_ref, d_ref, share_ref, balance_ref, router_ref, *refs):
    weights = refs[:6]
    out_ref, logit_ref = refs[6:8]
    grads = refs[8:]
    x, d = x_ref[...], d_ref[...]
    out = None
    for e in range(2):
        gate_w, up_w, down_w = weights[3 * e : 3 * e + 3]
        share = share_ref[:, e : e + 1]
        act_gate, act_up = dot(x, gate_w[...]), dot(x, up_w[...])
        sig = jax.nn.sigmoid(act_gate)
        swish = act_gate * sig
        hidden = swish * act_up
        raw = dot(d, down_w[...], NT)
        d_logit = share * (jnp.sum(hidden * raw, -1, keepdims=True) - balance_ref[...])
        d_hidden = raw * share
        d_gate = (d_hidden * act_up * sig * (1.0 + act_gate * (1.0 - sig))).astype(BF16)
        d_up = (d_hidden * swish).astype(BF16)
        grads[3 * e][...] = d_gate
        grads[3 * e + 1][...] = d_up
        grads[3 * e + 2][...] = (hidden * share).astype(BF16)
        logit_ref[:, e : e + 1] = d_logit
        part = dot(d_gate, gate_w[...], NT) + dot(d_up, up_w[...], NT)
        part = part + d_logit * router_ref[e : e + 1, :]
        out = part if out is None else out + part
    out_ref[...] = out.astype(BF16)


def mix_back(x, d, share, balance, router, weights):
    tokens, width = x.shape
    ff = weights[0].shape[1]
    tile = 2 * LANES

    def rows(columns):
        return pl.BlockSpec((tile, columns), lambda i: (i, 0))

    return pl.pallas_call(
        mix_back_kernel,
        grid=(tokens // tile,),
        out_shape=(
            jax.ShapeDtypeStruct((tokens, width), BF16),
            jax.ShapeDtypeStruct((tokens, 2), F32),
        ) + (jax.ShapeDtypeStruct((tokens, ff), BF16),) * 6,
        in_specs=[rows(width), rows(width), rows(2), rows(1), pl.BlockSpec(router.shape, lambda i: (0, 0))]
        + [pl.BlockSpec(w.shape, lambda i: (0, 0)) for w in weights],
        out_specs=[rows(width), rows(2)] + [rows(ff)] * 6,
        compiler_params=pltpu.CompilerParams(vmem_limit_bytes=56 << 20),
        name="mix_back",
    )(x, d, share, balance, router, *weights)


def add_kernel(layers, *refs):
    o_ref = refs[-1]
    for layer in range(layers):
        own, got = refs[2 * layer], refs[2 * layer + 1]
        o_ref[layer, 0] = own[...].astype(F32) + got[...].astype(F32)


def add_layers(pairs):
    layers = len(pairs)
    rows, columns = pairs[0][0].shape
    tile = rows // 4
    flat = [array for pair in pairs for array in pair]
    return pl.pallas_call(
        functools.partial(add_kernel, layers),
        grid=(4,),
        out_shape=jax.ShapeDtypeStruct((layers, 1, rows, columns), F32),
        in_specs=[pl.BlockSpec((tile, columns), lambda i: (i, 0))] * len(flat),
        out_specs=pl.BlockSpec((layers, 1, tile, columns), lambda i: (0, 0, i, 0)),
        name="add_layers",
    )(*flat)


def on_device(
    tokens,
    cotangent,
    positions,
    segments,
    routes,
    attn_gain,
    w_query,
    w_key,
    w_value,
    w_out,
    ffn_gain,
    router,
    w_gate,
    w_up,
    w_down,
):
    rows, width = tokens.shape
    devices = lax.axis_size("fsdp")
    replicas = lax.axis_size("rep")
    count = devices // 2
    me = lax.axis_index("fsdp")
    chip, core = me // 2, lax.rem(me, 2)
    shard = w_query.shape[1]
    experts = devices
    columns = 3 * LANES
    used = (GROUP + 2) * HD
    pairs = [(index, index ^ 1) for index in range(devices)]

    def swap(array):
        return lax.ppermute(array, "fsdp", pairs)

    small = jnp.concatenate(
        [attn_gain, ffn_gain, router.transpose(0, 2, 1).reshape(LAYERS * experts, shard)], 0
    )
    small = jnp.pad(small, ((0, 48 - small.shape[0]), (0, LANES - shard)))
    rate = jnp.exp(-jnp.log(10000.0) * jnp.arange(HD // 2, dtype=F32) / (HD // 2))
    angle = rate[:, None] * positions.astype(F32)[None, :]
    table = jnp.concatenate([jnp.cos(angle), jnp.sin(angle)], 0)
    slabs = jnp.concatenate(
        [
            w_query.reshape(LAYERS, shard, count, GROUP * HD),
            w_key.reshape(LAYERS, shard, count, HD),
            w_value.reshape(LAYERS, shard, count, HD),
            jnp.zeros((LAYERS, shard, count, columns - used), BF16),
        ],
        -1,
    ).transpose(2, 0, 1, 3)
    heads_w, outs_w, smalls, tables = exchange_weights(count, slabs, w_out, small, table)
    heads_w = heads_w.reshape(LAYERS, width, columns)
    w_heads = [heads_w[layer] for layer in range(LAYERS)]
    w_outs = [outs_w[:, layer].reshape(2 * shard, width) for layer in range(LAYERS)]
    smalls = smalls[:, : (2 + experts) * LAYERS, :shard].transpose(1, 0, 2).reshape(-1, width)
    smalls = smalls.astype(F32)
    gains_one, gains_two = smalls[:LAYERS], smalls[LAYERS : 2 * LAYERS]
    routers = smalls[2 * LAYERS :].reshape(LAYERS, experts, width)
    tables = tables.transpose(0, 2, 1).reshape(count * rows, HD)
    cosine = jnp.concatenate([tables[:, : HD // 2]] * 4, 1)
    sine = jnp.concatenate([tables[:, HD // 2 :]] * 4, 1)
    experts_w = []
    for layer in range(LAYERS):
        own = [w_gate[layer, 0], w_up[layer, 0], w_down[layer, 0]]
        experts_w.append(own + [swap(w) for w in own])
    mine = [2 * chip + core, 2 * chip + 1 - core]

    flat = segments.reshape(1, -1)
    kinds = jnp.arange(8, dtype=jnp.int32)[:, None]
    starts = jnp.sum((flat < kinds).astype(jnp.int32), 1, keepdims=True)
    begin = jnp.sum(jnp.where(flat == kinds, starts, 0), 0).reshape(count, 2, rows)
    begin = lax.dynamic_index_in_dim(begin, core, 1, False)
    info = jnp.concatenate([core[None], begin[:, 0]]).astype(jnp.int32)
    begin = begin[:, :, None]

    hidden = tokens.astype(F32)
    saved = []

    def normal(values):
        inverse = lax.rsqrt(jnp.mean(values * values, -1, keepdims=True) + EPS)
        return inverse, values * inverse

    for layer in range(LAYERS):
        inverse_one, normed_one = normal(hidden)
        x_attn = (normed_one * gains_one[layer][None, :]).astype(BF16)
        (x_all,) = ring_gather(count, [x_attn])
        x_all = x_all.reshape(count * rows, width)
        query, kv = project(x_all, w_heads[layer], cosine, sine)
        kv = kv.reshape(count, rows, LANES)
        kv_other = swap(kv)
        att, lse, partial = attend(info, query, kv, kv_other, begin, w_outs[layer])
        (added,) = ring_scatter(count, partial)
        middle = hidden + added
        inverse_two, normed_two = normal(middle)
        x_moe = (normed_two * gains_two[layer][None, :]).astype(BF16)
        logits = dot(routers[layer].astype(BF16), x_moe, NT)
        named = jnp.any(
            jnp.arange(experts, dtype=jnp.int32)[:, None, None] == routes[layer].T[None, :, :], 1
        )
        share = jax.nn.softmax(jnp.where(named, logits, -jnp.inf), axis=0)
        m_all, share_all = ring_gather(count, [x_moe, share])
        m_all = m_all.reshape(count * rows, width)
        share = jnp.stack(
            [lax.dynamic_index_in_dim(share_all, e, 1, False).reshape(-1) for e in mine], 1
        )
        partial = mix(m_all, share, experts_w[layer])
        (mixed,) = ring_scatter(count, partial.reshape(count, rows, width))
        saved.append(
            (inverse_one, normed_one, x_all, query, kv, kv_other, att, lse)
            + (inverse_two, normed_two, m_all, share, mixed)
        )
        hidden = middle + mixed
    activations = hidden.astype(BF16)

    grad = cotangent.astype(F32)
    waiting = []
    own_sums = [[None] * 4 for _ in range(LAYERS)]
    peer_sums = [[None] * 4 for _ in range(LAYERS)]
    heads_sums = [None] * LAYERS

    def send(kernel, argument, rides=()):
        taken = []
        while replicas == 2 and waiting and (not taken or taken[-1][1] == 3):
            taken.append(waiting.pop(0))
        rides = list(rides)
        more = [(own_sums[layer][index], "rep") for layer, index in taken]
        results = kernel(count, argument, rides + more)
        for place, (layer, index) in enumerate(taken):
            peer_sums[layer][index] = results[len(results) - len(taken) + place]
        return results[: len(results) - len(taken)]

    def core_sum(own, got):
        return (own + got.astype(F32)).astype(BF16)

    for layer in reversed(range(LAYERS)):
        (inverse_one, normed_one, x_all, query, kv, kv_other, att, lse) = saved[layer][:8]
        (inverse_two, normed_two, m_all, share, mixed) = saved[layer][8:]
        d_mix = grad.astype(BF16)
        balance = jnp.sum(mixed * d_mix.astype(F32), -1)
        side = jnp.broadcast_to(balance[None, :], (experts, rows))
        d_all, balance = send(ring_gather, [d_mix, side])
        d_all = d_all.reshape(count * rows, width)
        balance = balance[:, 0, :].reshape(-1, 1)
        router_mine = jnp.concatenate(
            [lax.dynamic_slice_in_dim(routers[layer], e, 1, 0) for e in mine], 0
        )
        partial, d_logit, *d_acts = mix_back(
            m_all, d_all, share, balance, router_mine, experts_w[layer]
        )
        expert_grads = [
            [
                dot(m_all, d_acts[3 * e], TN),
                dot(m_all, d_acts[3 * e + 1], TN),
                dot(d_acts[3 * e + 2], d_all, TN),
            ]
            for e in range(2)
        ]
        g_router = jnp.dot(d_logit.T, m_all.astype(F32), precision=lax.Precision.HIGHEST)
        theirs = [g.astype(BF16) for g in expert_grads[1]]
        d_x, *got = send(
            ring_scatter, partial.reshape(count, rows, width), [(g, "fsdp") for g in theirs]
        )
        for index in range(3):
            own_sums[layer][index] = core_sum(expert_grads[0][index], got[index])
            waiting.append((layer, index))
        gain = gains_two[layer][None, :]
        d_norm = d_x * gain
        d_gain_two = jnp.sum(d_x * normed_two, 0)
        grad_mid = grad + inverse_two * (
            d_norm - normed_two * jnp.mean(d_norm * normed_two, -1, keepdims=True)
        )
        (b_all,) = send(ring_gather, [grad_mid.astype(BF16)])
        d_query, d_own, d_other = attend_back(
            info, query, kv, kv_other, begin, w_outs[layer], att, lse, b_all,
            cosine.reshape(count, rows, LANES), sine.reshape(count, rows, LANES),
        )
        g_out = dot(att.reshape(count * rows, 2 * LANES), b_all.reshape(count * rows, width), TN)
        g_out = g_out[: 2 * shard].reshape(2, shard, width)
        g_out_own = lax.dynamic_index_in_dim(g_out, core, 0, False)
        g_out_other = lax.dynamic_index_in_dim(g_out, 1 - core, 0, False)
        d_got = swap(d_other.astype(BF16))
        partial, g_heads = join(
            d_query.reshape(count * rows, 2 * LANES),
            d_own.reshape(count * rows, LANES),
            d_got.reshape(count * rows, LANES),
            cosine, sine, w_heads[layer], x_all,
        )
        own_sums[layer][3] = core_sum(g_out_own, swap(g_out_other.astype(BF16)))
        waiting.append((layer, 3))
        (d_x,) = send(ring_scatter, partial.reshape(count, rows, width))
        gain = gains_one[layer][None, :]
        d_norm = d_x * gain
        d_gain_one = jnp.sum(d_x * normed_one, 0)
        grad = grad_mid + inverse_one * (
            d_norm - normed_one * jnp.mean(d_norm * normed_one, -1, keepdims=True)
        )
        g_router = jnp.where(core == 0, g_router, g_router[::-1])
        extra = jnp.concatenate(
            [g_router, d_gain_one[None, :], d_gain_two[None, :]], 0
        ).T
        heads_sums[layer] = jnp.concatenate(
            [g_heads[:, :used], extra, jnp.zeros((width, columns - used - 4), F32)], 1
        ).astype(BF16).reshape(count, 2, shard, columns)
    heads_sums = jnp.stack(heads_sums, 2).transpose(1, 0, 2, 3, 4)
    total = finish_heads(count, replicas, heads_sums)
    for layer, index in waiting:
        if replicas == 2:
            peer_sums[layer][index] = lax.ppermute(own_sums[layer][index], "rep", [(0, 1), (1, 0)])
    if replicas == 2:
        g_gate, g_up, g_down, g_out = [
            add_layers([(own_sums[layer][index], peer_sums[layer][index]) for layer in range(LAYERS)])
            for index in range(4)
        ]
    else:
        total = lax.psum(total.astype(BF16), "rep").astype(F32)
        g_gate, g_up, g_down, g_out = [
            jnp.stack(
                [lax.psum(own_sums[layer][index], "rep").astype(F32) for layer in range(LAYERS)]
            )[:, None]
            for index in range(4)
        ]
    total = total.transpose(1, 2, 0, 3)

    def part(first, last):
        return total[..., first:last].reshape(LAYERS, shard, -1)

    key_edge = GROUP * HD
    gains = jnp.sum(total[..., used + 2 : used + 4], 2)
    return (
        activations,
        grad,
        gains[..., 0],
        part(0, key_edge),
        part(key_edge, key_edge + HD),
        part(key_edge + HD, used),
        g_out[:, 0],
        gains[..., 1],
        part(used, used + 2),
        g_gate,
        g_up,
        g_down,
    )


def solution(mesh):
    placed = (
        P(("rep", "fsdp"), None),
        P(("rep", "fsdp"), None),
        P(("rep", "fsdp")),
        P("rep", None),
        P(None, ("rep", "fsdp"), None),
        P(None, "fsdp"),
        P(None, "fsdp", None),
        P(None, "fsdp", None),
        P(None, "fsdp", None),
        P(None, "fsdp", None),
        P(None, "fsdp"),
        P(None, "fsdp", None),
        P(None, "fsdp", None, None),
        P(None, "fsdp", None, None),
        P(None, "fsdp", None, None),
    )
    return jax.shard_map(
        on_device,
        mesh=mesh,
        in_specs=placed,
        out_specs=(
            P(("rep", "fsdp"), None),
            P(("rep", "fsdp"), None),
            P(None, "fsdp"),
            P(None, "fsdp", None),
            P(None, "fsdp", None),
            P(None, "fsdp", None),
            P(None, "fsdp", None),
            P(None, "fsdp"),
            P(None, "fsdp", None),
            P(None, "fsdp", None, None),
            P(None, "fsdp", None, None),
            P(None, "fsdp", None, None),
        ),
        check_vma=False,
    )
```

time: 1320 us -> 1060 us (0.80)
  Pallas kernels: 627 us -> 867 us
  waiting for transfers between devices: 163 us -> 0.45 us
  other arithmetic: 120 us -> 31.8 us
  starting transfers between devices: 75.2 us -> 3.94 us
  matrix products: 116 us -> 51.5 us
  local copies, waits for them, and re-layouts: 160 us -> 96.4 us
  blocking collectives: 51.2 us -> 0 us
    pallas_call x16 -> x28, Pallas kernels: 510 us -> 752 us  [the longest x8 281 us: ring_scatter(): pl.pallas_call(functools.partial(scatter_kernel, count, axes), out_shape=...]
    ppermute x10 -> x2, waiting for transfers between devices: 156 us -> 0.01 us  [on_device(): lax.ppermute(own_sums[layer][index], 'rep', [(0, 1), (1, 0)])]
    dot_general x26 -> x16, matrix products: 111 us -> 47.7 us  [dot(): lax.dot_general(left, right, (contract, ((), ())), preferred_element_type...]
    all_gather x1 -> x0, blocking collectives: 51.2 us -> none  [on_device(): small = lax.all_gather(small, 'fsdp', axis=1, tiled=True)]
    ppermute x10 -> x2, starting transfers between devices: 41 us -> 1.51 us  [on_device(): lax.ppermute(own_sums[layer][index], 'rep', [(0, 1), (1, 0)])]
    all_to_all x5 -> x0, starting transfers between devices: 30.4 us -> none  [the longest x2 14.9 us: on_device(): lax.all_to_all(spread, 'fsdp', split_axis=0, concat_axis=0, tiled=True)]
    another operation x18 -> x4, other arithmetic: 28.2 us -> 0.64 us  [the longest x16 26.4 us: on_device(): jnp.stack([grads[layer][index] for layer in range(LAYERS)])]
    convert_element_type x21 -> x8, other arithmetic: 36.1 us -> 9.31 us  [the longest x2 3.87 us: on_device(): d_got = swap(d_other.astype(BF16))]
  transfers between devices with their start and end apart: 33 -> 14, of which waited for: 7 -> 1; matrix products, arithmetic and copies ran while one was open for 21% -> 10% of each run, Pallas kernels for 19% -> 45%
where the time goes in v2:
time: 1060 us; the launch traced here: 1050 us
  Pallas kernels  867 us (82%)
  local copies, waits for them, and re-layouts  96.4 us (9%)
  matrix products  51.5 us (5%)
  other arithmetic  31.8 us (3%)
    pallas_call x8, Pallas kernels, ring_scatter(): pl.pallas_call(functools.partial(scatter_kernel, count, axes), out_shape=...  281 us
    pallas_call x8, Pallas kernels, ring_gather(): pl.pallas_call(functools.partial(gather_kernel, count, axes, sided), out_...  281 us
    pallas_call x2, Pallas kernels, attend_back(): pl.pallas_call(attend_back_kernel, grid_spec=pltpu.PrefetchScalarGridSpec...  59.9 us
    pallas_call x2, Pallas kernels, mix_back(): pl.pallas_call(mix_back_kernel, grid=(tokens // tile,), out_shape=(jax.Sh...  50.3 us
    dot_general x16, matrix products, dot(): lax.dot_general(left, right, (contract, ((), ())), preferred_element_type...  47.7 us
    pallas_call x2, Pallas kernels, attend(): pl.pallas_call(attend_kernel, grid_spec=pltpu.PrefetchScalarGridSpec(num_...  43.2 us
    pallas_call x1, Pallas kernels, finish_heads(): pl.pallas_call(functools.partial(finish_kernel, count, replicas), out_sha...  41.4 us
    unnamed x220, local copies, waits for them, and re-layouts  37.6 us
  transfers between devices with their start and end apart: 14, of which 1 were waited for; matrix products, arithmetic and copies ran while one was open for 10% of the time, Pallas kernels for 45%

profile of v2, /device:TPU:0, one launch (start us, length us, event | category | flops | bytes accessed | tf_op | source)
XLA Modules:
  0.0 1053.9 jit_solution(18061926703087072601)
XLA Ops:
  7.2 34.7 %exchange_weights.1 = (bf16[2,16,96,384]{3,2,1,0:T(8,128)(2,1)}, bf16[2,2,96,1536]{3,2,1,0:T(8,128)(2,1)}, bf16[16,48,128]{2,1,0:T(8,128)(2,1)}, f32[8,64,128]{2,1,0:T(8,128)}) custom-call(bf16[8,2,96,384]{3,2,1,0:T(8,128)(2,1)} %maximum_bitcast_fusion.1.slab_ref, bf16[2,96,1536]{2,1,0:T(8,128)(2,1)} %out_w_ref.1, bf16[48,128]{1,0:T(8,128)(2,1)} %fusion.34.small_ref, ...), custom_call_target="tpu_custom_call" | custom-call | tf_op jit(solution)/shard_map/exchange_weights/pallas_call | solution.py:366
  45.4 44.1 %ring_gather.8 = bf16[8,128,1536]{2,1,0:T(8,128)(2,1)} custom-call(bf16[128,1536]{1,0:T(8,128)(2,1)} %fusion.11.refs_0_), custom_call_target="tpu_custom_call" | custom-call | tf_op jit(solution)/shard_map/ring_gather/pallas_call | solution.py:167
  93.5 6.3 project.2
  99.8 3.4 slice_bitcast_fusion.2
  127.4 21.5 %attend.2 = (bf16[8,128,256]{2,1,0:T(8,128)(2,1)}, f32[8,384,1]{2,1,0:T(8,128)}, bf16[8,128,1536]{2,1,0:T(8,128)(2,1)}) custom-call(s32[9]{0:T(128)} %pad_add_fusion.info_ref, bf16[8,3,128,128]{3,2,1,0:T(8,128)(2,1)} %get-tuple-element.81.q_ref, bf16[8,128,128]{2,1,0:T(8,128)(2,1)} %bitcast.209, bf16[8,128,128]{2,1,0:T(8,128)(2,1)} %collective-permute-done.other_ref, ...), custom_call_target="tpu_custom_call" | custom-call | tf_op jit(solution)/shard_map/attend/pallas_call | solution.py:595
  150.7 33.5 %ring_scatter.8 = f32[128,1536]{1,0:T(8,128)S(1)} custom-call(bf16[8,128,1536]{2,1,0:T(8,128)(2,1)S(1)} %copy-done.18), custom_call_target="tpu_custom_call" | custom-call | tf_op jit(solution)/shard_map/ring_scatter/pallas_call | solution.py:256
  186.4 32.4 %ring_gather.9 = (bf16[8,128,1536]{2,1,0:T(8,128)(2,1)}, f32[8,16,128]{2,1,0:T(8,128)}) custom-call(bf16[128,1536]{1,0:T(8,128)(2,1)} %copy-done.64, f32[16,128]{1,0:T(8,128)} %fusion.35.refs_1_), custom_call_target="tpu_custom_call" | custom-call | tf_op jit(solution)/shard_map/ring_gather/pallas_call | solution.py:167
  221.8 15.3 %mix.2 = bf16[1024,1536]{1,0:T(8,128)(2,1)} custom-call(bf16[1024,1536]{1,0:T(8,128)(2,1)} %bitcast.172, f32[1024,2]{1,0:T(8,128)S(1)} %copy-done.14, bf16[1536,512]{1,0:T(8,128)(2,1)S(1)} %get-tuple-element.246.refs_0_, bf16[1536,512]{1,0:T(8,128)(2,1)} %get-tuple-element.244.refs_1_, bf16[512,1536]{1,0:T(8,128)(2,1)} %get-tuple-element.242.refs_2_, ...), custom_call_target="tpu_custom_call" | custom-call | tf_op jit(solution)/shard_map/mix/pallas_call | solution.py:770
  239.0 33.0 %ring_scatter.9 = f32[128,1536]{1,0:T(8,128)S(1)} custom-call(bf16[8,128,1536]{2,1,0:T(8,128)(2,1)S(1)} %bitcast.156), custom_call_target="tpu_custom_call" | custom-call | tf_op jit(solution)/shard_map/ring_scatter/pallas_call | solution.py:256
  273.2 32.6 %ring_gather.10 = bf16[8,128,1536]{2,1,0:T(8,128)(2,1)} custom-call(bf16[128,1536]{1,0:T(8,128)(2,1)} %multiply_convert_fusion.1.refs_0_), custom_call_target="tpu_custom_call" | custom-call | tf_op jit(solution)/shard_map/ring_gather/pallas_call | solution.py:167
  305.9 6.2 project.3
  314.5 21.7 %attend.3 = (bf16[8,128,256]{2,1,0:T(8,128)(2,1)}, f32[8,384,1]{2,1,0:T(8,128)}, bf16[8,128,1536]{2,1,0:T(8,128)(2,1)}) custom-call(s32[9]{0:T(128)} %pad_add_fusion.info_ref, bf16[8,3,128,128]{3,2,1,0:T(8,128)(2,1)} %get-tuple-element.87.q_ref, bf16[8,128,128]{2,1,0:T(8,128)(2,1)} %bitcast.212, bf16[8,128,128]{2,1,0:T(8,128)(2,1)} %copy-done.75, ...), custom_call_target="tpu_custom_call" | custom-call | tf_op jit(solution)/shard_map/attend/pallas_call | solution.py:595
  338.1 32.2 %ring_scatter.10 = f32[128,1536]{1,0:T(8,128)S(1)} custom-call(bf16[8,128,1536]{2,1,0:T(8,128)(2,1)S(1)} %copy-done.19), custom_call_target="tpu_custom_call" | custom-call | tf_op jit(solution)/shard_map/ring_scatter/pallas_call | solution.py:256
  372.4 32.4 %ring_gather.11 = (bf16[8,128,1536]{2,1,0:T(8,128)(2,1)}, f32[8,16,128]{2,1,0:T(8,128)}) custom-call(bf16[128,1536]{1,0:T(8,128)(2,1)} %copy-done.63, f32[16,128]{1,0:T(8,128)} %fusion.37.refs_1_), custom_call_target="tpu_custom_call" | custom-call | tf_op jit(solution)/shard_map/ring_gather/pallas_call | solution.py:167
  406.0 15.4 %mix.3 = bf16[1024,1536]{1,0:T(8,128)(2,1)} custom-call(bf16[1024,1536]{1,0:T(8,128)(2,1)} %bitcast.179, f32[1024,2]{1,0:T(8,128)S(1)} %copy.194.share_ref, bf16[1536,512]{1,0:T(8,128)(2,1)} %get-tuple-element.245.refs_0_, bf16[1536,512]{1,0:T(8,128)(2,1)S(1)} %get-tuple-element.243.refs_1_, bf16[512,1536]{1,0:T(8,128)(2,1)} %get-tuple-element.241.refs_2_, ...), custom_call_target="tpu_custom_call" | custom-call | tf_op jit(solution)/shard_map/mix/pallas_call | solution.py:770
  423.3 30.4 %ring_scatter.11 = f32[128,1536]{1,0:T(8,128)S(1)} custom-call(bf16[8,128,1536]{2,1,0:T(8,128)(2,1)S(1)} %bitcast.157), custom_call_target="tpu_custom_call" | custom-call | tf_op jit(solution)/shard_map/ring_scatter/pallas_call | solution.py:256
  454.4 30.5 %ring_gather.12 = (bf16[8,128,1536]{2,1,0:T(8,128)(2,1)}, f32[8,16,128]{2,1,0:T(8,128)}) custom-call(bf16[128,1536]{1,0:T(8,128)(2,1)} %refs_0_, f32[16,128]{1,0:T(8,128)} %broadcast_in_dim.80.refs_1_), custom_call_target="tpu_custom_call" | custom-call | tf_op jit(solution)/shard_map/ring_gather/pallas_call | solution.py:167
  486.8 25.3 %mix_back.2 = (bf16[1024,1536]{1,0:T(8,128)(2,1)}, f32[1024,2]{1,0:T(8,128)}, bf16[1024,512]{1,0:T(8,128)(2,1)}, bf16[1024,512]{1,0:T(8,128)(2,1)}, bf16[1024,51...) custom-call(bf16[1024,1536]{1,0:T(8,128)(2,1)} %bitcast.180, ...), custom_call_target="tpu_custom_call" | custom-call | tf_op jit(solution)/shard_map/mix_back/pallas_call | solution.py:818
  512.1 3.1 convolution_convert_fusion.5.refs_1_
  519.3 32.9 %ring_scatter.12 = (f32[128,1536]{1,0:T(8,128)S(1)}, bf16[1536,512]{1,0:T(8,128)(2,1)S(1)}, bf16[1536,512]{1,0:T(8,128)(2,1)S(1)}, bf16[512,1536]{1,0:T(8,128)(2,1)S(1)}) custom-call(bf16[8,128,1536]{2,1,0:T(8,128)(2,1)S(1)} %bitcast.165, bf16[1536,512]{1,0:T(8,128)(2,1)S(1)} %convolution_convert_fusion.5.refs_1_, ...), custom_call_target="tpu_custom_call" | custom-call | tf_op jit(solution)/shard_map/ring_scatter/pallas_call | solution.py:256
  555.8 3.0 fusion.refs_1_.refs_2_
  558.8 36.6 %ring_gather.13 = (bf16[8,128,1536]{2,1,0:T(8,128)(2,1)}, bf16[1536,512]{1,0:T(8,128)(2,1)}) custom-call(bf16[128,1536]{1,0:T(8,128)(2,1)} %fusion.39.refs_0_, bf16[1536,512]{1,0:T(8,128)(2,1)} %fusion.refs_1_.refs_2_), custom_call_target="tpu_custom_call" | custom-call | tf_op jit(solution)/shard_map/ring_gather/pallas_call | solution.py:167
  595.4 4.2 convolution_bitcast_fusion.1
  599.7 29.8 %attend_back.2 = (bf16[8,128,256]{2,1,0:T(8,128)(2,1)}, f32[8,128,128]{2,1,0:T(8,128)}, f32[8,128,128]{2,1,0:T(8,128)}) custom-call(s32[9]{0:T(128)} %pad_add_fusion.info_ref, bf16[8,3,128,128]{3,2,1,0:T(8,128)(2,1)} %get-tuple-element.87.q_ref, bf16[8,128,128]{2,1,0:T(8,128)(2,1)} %bitcast.213, bf16[8,128,128]{2,1,0:T(8,128)(2,1)} %copy-done.75, ...), custom_call_target="tpu_custom_call" | custom-call | tf_op jit(solution)/shard_map/attend_back/pallas_call | solution.py:676
  637.0 4.7 fusion.1.refs_1_.refs_2_
  645.6 5.5 join.2
  651.2 36.7 %ring_scatter.13 = (f32[128,1536]{1,0:T(8,128)S(1)}, bf16[1536,512]{1,0:T(8,128)(2,1)S(1)}) custom-call(bf16[8,128,1536]{2,1,0:T(8,128)(2,1)S(1)} %bitcast.163, bf16[1536,512]{1,0:T(8,128)(2,1)S(1)} %fusion.1.refs_1_.refs_2_), custom_call_target="tpu_custom_call" | custom-call | tf_op jit(solution)/shard_map/ring_scatter/pallas_call | solution.py:256
  690.4 36.3 %ring_gather.14 = (bf16[8,128,1536]{2,1,0:T(8,128)(2,1)}, f32[8,16,128]{2,1,0:T(8,128)}, bf16[512,1536]{1,0:T(8,128)(2,1)}) custom-call(bf16[128,1536]{1,0:T(8,128)(2,1)} %get-tuple-element.233.refs_0_, f32[16,128]{1,0:T(8,128)} %broadcast_in_dim.81.refs_1_, bf16[512,1536]{1,0:T(8,128)(2,1)} %fusion.2.refs_2_), custom_call_target="tpu_custom_call" | custom-call | tf_op jit(solution)/shard_map/ring_gather/pallas_call | solution.py:167
  728.5 25.0 %mix_back.3 = (bf16[1024,1536]{1,0:T(8,128)(2,1)}, f32[1024,2]{1,0:T(8,128)}, bf16[1024,512]{1,0:T(8,128)(2,1)}, bf16[1024,512]{1,0:T(8,128)(2,1)}, bf16[1024,51...) custom-call(bf16[1024,1536]{1,0:T(8,128)(2,1)} %bitcast.173, ...), custom_call_target="tpu_custom_call" | custom-call | tf_op jit(solution)/shard_map/mix_back/pallas_call | solution.py:818
  753.6 4.3 convolution_convert_fusion.2.refs_1_
  757.9 3.0 convolution_convert_fusion.1.refs_2_
  760.9 3.0 convolution_convert_fusion.refs_3_
  767.7 3.0 slice.215
  776.8 32.0 %ring_scatter.14 = (f32[128,1536]{1,0:T(8,128)S(1)}, bf16[1536,512]{1,0:T(8,128)(2,1)S(1)}, bf16[1536,512]{1,0:T(8,128)(2,1)S(1)}, bf16[512,1536]{1,0:T(8,128)(2,1)S(1)}, bf16[96,1536]{1,0:T(8,128)(2,1)S(1)}) custom-call(bf16[8,128,1536]{2,1,0:T(8,128)(2,1)S(1)} %bitcast.164, bf16[1536,512]{1,0:T(8,128)(2,1)S(1)} %copy-done.27, ...), custom_call_target="tpu_custom_call" | custom-call | tf_op jit(solution)/shard_map/ring_scatter/pallas_call | solution.py:256
  812.7 3.0 fusion.3.refs_1_.refs_0_
  815.7 36.1 %ring_gather.15 = (bf16[8,128,1536]{2,1,0:T(8,128)(2,1)}, bf16[1536,512]{1,0:T(8,128)(2,1)}) custom-call(bf16[128,1536]{1,0:T(8,128)(2,1)} %get-tuple-element.230.refs_0_, bf16[1536,512]{1,0:T(8,128)(2,1)} %fusion.3.refs_1_.refs_0_), custom_call_target="tpu_custom_call" | custom-call | tf_op jit(solution)/shard_map/ring_gather/pallas_call | solution.py:167
  851.8 4.2 convolution_bitcast_fusion
  856.0 30.1 %attend_back.3 = (bf16[8,128,256]{2,1,0:T(8,128)(2,1)}, f32[8,128,128]{2,1,0:T(8,128)}, f32[8,128,128]{2,1,0:T(8,128)}) custom-call(s32[9]{0:T(128)} %pad_add_fusion.info_ref, bf16[8,3,128,128]{3,2,1,0:T(8,128)(2,1)} %get-tuple-element.81.q_ref, bf16[8,128,128]{2,1,0:T(8,128)(2,1)} %bitcast.210, bf16[8,128,128]{2,1,0:T(8,128)(2,1)} %collective-permute-done.other_ref, ...), custom_call_target="tpu_custom_call" | custom-call | tf_op jit(solution)/shard_map/attend_back/pallas_call | solution.py:676
  890.8 5.1 fusion.5.refs_0_
  895.9 3.1 fusion.4.refs_1_.refs_0_
  899.0 6.2 add_layers.5
  910.7 5.5 join.3
  916.2 50.5 %ring_scatter.15 = (f32[128,1536]{1,0:T(8,128)S(1)}, bf16[1536,512]{1,0:T(8,128)(2,1)S(1)}) custom-call(bf16[8,128,1536]{2,1,0:T(8,128)(2,1)S(1)} %bitcast.162, bf16[1536,512]{1,0:T(8,128)(2,1)S(1)} %copy-done.13), custom_call_target="tpu_custom_call" | custom-call | tf_op jit(solution)/shard_map/ring_scatter/pallas_call | solution.py:256
  971.8 3.2 maximum_bitcast_fusion.g_ref
  974.9 41.4 %finish_heads.1 = f32[8,2,96,384]{3,2,1,0:T(8,128)S(1)} custom-call(bf16[2,8,2,96,384]{4,3,2,1,0:T(8,128)(2,1)S(1)} %maximum_bitcast_fusion.g_ref), custom_call_target="tpu_custom_call" | custom-call | tf_op jit(solution)/shard_map/finish_heads/pallas_call | solution.py:454
  1037.3 5.9 add_layers.6
  1044.0 3.5 add_layers.4
  1047.5 5.9 add_layers.7
  (370 shorter events, 133.8 us)
Async XLA Ops:
  5.7 38.6 %copy-start.54 = (bf16[128,1536]{1,0:T(8,128)(2,1)S(1)}, bf16[128,1536]{1,0:T(8,128)(2,1)}, u32[]{:S(2)}) copy-start(bf16[128,1536]{1,0:T(8,128)(2,1)} %param.15) | copy-start | bytes 1179652
  44.3 45.2 %copy-start.68 = (bf16[2,16,96,384]{3,2,1,0:T(8,128)(2,1)S(1)}, bf16[2,16,96,384]{3,2,1,0:T(8,128)(2,1)}, u32[]{:S(2)}) copy-start(bf16[2,16,96,384]{3,2,1,0:T(8,128)(2,1)} %get-tuple-element.79) | copy-start | bytes 7077892
  44.5 45.0 %copy-start.94 = (f32[128]{0:T(128)}, f32[128]{0:T(128)S(1)}, u32[]{:S(2)}) copy-start(f32[128]{0:T(128)S(1)} %add_rsqrt_fusion.3) | copy-start | bytes 1540
  99.8 27.2 %collective-permute-start = (bf16[8,128,128]{2,1,0:T(8,128)(2,1)}, bf16[8,128,128]{2,1,0:T(8,128)(2,1)}, u32[]{:S(2)}, u32[]{:S(2)}) collective-permute-start(bf16[8,128,128]{2,1,0:T(8,128)(2,1)} %bitcast.208), channel_id=1, source_target_pairs={{0,1},{1,0},{2,3},{3,2},{4,5},{5,4},{6,7},{7,6},{8,9},{9,8},{10,11... | collective-permute-start | bytes 786440 | tf_op jit(solution)/shard_map/ppermute | solution.py:885
  103.2 117.6 %copy-start.6 = (bf16[1536,512]{1,0:T(8,128)(2,1)}, bf16[1536,512]{1,0:T(8,128)(2,1)S(1)}, u32[]{:S(2)}) copy-start(bf16[1536,512]{1,0:T(8,128)(2,1)S(1)} %get-tuple-element.246.refs_0_) | copy-start | bytes 4718596
  103.2 117.5 %collective-permute-start.1 = (bf16[1536,512]{1,0:T(8,128)(2,1)S(1)}, bf16[1536,512]{1,0:T(8,128)(2,1)}, u32[]{:S(2)}, u32[]{:S(2)}) collective-permute-start(bf16[1536,512]{1,0:T(8,128)(2,1)S(1)} %get-tuple-element.246.refs_0_), channel_id=1, source_target_pairs={{0,1},{1,0},{2,3},{3,2},{4,5},{5,4},{6,7},{7,6},{8,9},{9,8},{10,11... | collective-permute-start | bytes 4718600 | tf_op jit(solution)/shard_map/ppermute | solution.py:885
  105.0 301.0 %copy-start.7 = (bf16[1536,512]{1,0:T(8,128)(2,1)}, bf16[1536,512]{1,0:T(8,128)(2,1)S(1)}, u32[]{:S(2)}) copy-start(bf16[1536,512]{1,0:T(8,128)(2,1)S(1)} %get-tuple-element.243.refs_1_) | copy-start | bytes 4718596
  105.0 115.8 %collective-permute-start.2 = (bf16[1536,512]{1,0:T(8,128)(2,1)}, bf16[1536,512]{1,0:T(8,128)(2,1)}, u32[]{:S(2)}, u32[]{:S(2)}) collective-permute-start(bf16[1536,512]{1,0:T(8,128)(2,1)} %get-tuple-element.244.refs_1_), channel_id=1, source_target_pairs={{0,1},{1,0},{2,3},{3,2},{4,5},{5,4},{6,7},{7,6},{8,9},{9,8},{10,11... | collective-permute-start | bytes 4718600 | tf_op jit(solution)/shard_map/ppermute | solution.py:885
  108.7 112.1 %collective-permute-start.3 = (bf16[512,1536]{1,0:T(8,128)(2,1)}, bf16[512,1536]{1,0:T(8,128)(2,1)}, u32[]{:S(2)}, u32[]{:S(2)}) collective-permute-start(bf16[512,1536]{1,0:T(8,128)(2,1)} %get-tuple-element.242.refs_2_), channel_id=1, source_target_pairs={{0,1},{1,0},{2,3},{3,2},{4,5},{5,4},{6,7},{7,6},{8,9},{9,8},{10,11... | collective-permute-start | bytes 4718600 | tf_op jit(solution)/shard_map/ppermute | solution.py:885
  109.0 296.9 %collective-permute-start.5 = (bf16[1536,512]{1,0:T(8,128)(2,1)}, bf16[1536,512]{1,0:T(8,128)(2,1)}, u32[]{:S(2)}, u32[]{:S(2)}) collective-permute-start(bf16[1536,512]{1,0:T(8,128)(2,1)} %get-tuple-element.245.refs_0_), channel_id=1, source_target_pairs={{0,1},{1,0},{2,3},{3,2},{4,5},{5,4},{6,7},{7,6},{8,9},{9,8},{10,11... | collective-permute-start | bytes 4718600 | tf_op jit(solution)/shard_map/ppermute | solution.py:885
  127.0 278.9 %collective-permute-start.6 = (bf16[1536,512]{1,0:T(8,128)(2,1)S(1)}, bf16[1536,512]{1,0:T(8,128)(2,1)}, u32[]{:S(2)}, u32[]{:S(2)}) collective-permute-start(bf16[1536,512]{1,0:T(8,128)(2,1)S(1)} %get-tuple-element.243.refs_1_), channel_id=1, source_target_pairs={{0,1},{1,0},{2,3},{3,2},{4,5},{5,4},{6,7},{7,6},{8,9},{9,8},{10,11... | collective-permute-start | bytes 4718600 | tf_op jit(solution)/shard_map/ppermute | solution.py:885
  220.8 185.2 %collective-permute-start.7 = (bf16[512,1536]{1,0:T(8,128)(2,1)}, bf16[512,1536]{1,0:T(8,128)(2,1)}, u32[]{:S(2)}, u32[]{:S(2)}) collective-permute-start(bf16[512,1536]{1,0:T(8,128)(2,1)} %get-tuple-element.241.refs_2_), channel_id=1, source_target_pairs={{0,1},{1,0},{2,3},{3,2},{4,5},{5,4},{6,7},{7,6},{8,9},{9,8},{10,11... | collective-permute-start | bytes 4718600 | tf_op jit(solution)/shard_map/ppermute | solution.py:885
  239.0 33.0 %copy-start.49 = (f32[128,1536]{1,0:T(8,128)S(1)}, f32[128,1536]{1,0:T(8,128)}, u32[]{:S(2)}) copy-start(f32[128,1536]{1,0:T(8,128)} %copy-done.48) | copy-start | bytes 2359300
  239.0 33.2 %copy-start.81 = (f32[1536]{0:T(1024)S(1)}, f32[1536]{0:T(1024)}, u32[]{:S(2)}) copy-start(f32[1536]{0:T(1024)} %mul.233) | copy-start | bytes 18436
  272.2 98.1 %copy-start.44 = (f32[128,1536]{1,0:T(8,128)}, f32[128,1536]{1,0:T(8,128)S(1)}, u32[]{:S(2)}) copy-start(f32[128,1536]{1,0:T(8,128)S(1)} %get-tuple-element.238) | copy-start | bytes 2359300
  305.9 6.2 copy-start.86
  305.9 6.2 copy-start.87
  305.9 6.8 copy-start.83
  305.9 6.9 copy-start.84
  305.9 6.9 copy-start.85
  312.1 1.7 collective-permute-start.4
  405.9 15.5 %copy-start.15 = (f32[1024,2]{1,0:T(8,128)}, f32[1024,2]{1,0:T(8,128)S(1)}, u32[]{:S(2)}) copy-start(f32[1024,2]{1,0:T(8,128)S(1)} %copy.194.share_ref) | copy-start | bytes 24580
  423.3 30.4 %copy-start.56 = (bf16[128,1536]{1,0:T(8,128)(2,1)S(1)}, bf16[128,1536]{1,0:T(8,128)(2,1)}, u32[]{:S(2)}) copy-start(bf16[128,1536]{1,0:T(8,128)(2,1)} %refs_0_) | copy-start | bytes 1179652
  486.8 25.3 %copy-start.42 = (bf16[8,128,1536]{2,1,0:T(8,128)(2,1)S(1)}, bf16[8,128,1536]{2,1,0:T(8,128)(2,1)}, u32[]{:S(2)}) copy-start(bf16[8,128,1536]{2,1,0:T(8,128)(2,1)} %get-tuple-element.90) | copy-start | bytes 9437188
  519.3 35.2 %copy-start.47 = (f32[128,1536]{1,0:T(8,128)S(1)}, f32[128,1536]{1,0:T(8,128)}, u32[]{:S(2)}) copy-start(f32[128,1536]{1,0:T(8,128)} %copy-done.46) | copy-start | bytes 2359300
  519.3 35.5 %copy-start.57 = (bf16[128,1536]{1,0:T(8,128)(2,1)S(1)}, bf16[128,1536]{1,0:T(8,128)(2,1)}, u32[]{:S(2)}) copy-start(bf16[128,1536]{1,0:T(8,128)(2,1)} %refs_0_) | copy-start | bytes 1179652
  631.4 13.3 %collective-permute-start.8 = (bf16[8,128,128]{2,1,0:T(8,128)(2,1)}, bf16[8,128,128]{2,1,0:T(8,128)(2,1)S(1)}, u32[]{:S(2)}, u32[]{:S(2)}) collective-permute-start(bf16[8,128,128]{2,1,0:T(8,128)(2,1)} %convert_element_type.177), channel_id=1, source_target_pairs={{0,1},{1,0},{2,3},{3,2},{4,5},{5,4},{6,7},{7,6},{8,9},{9,8},{10,11... | collective-permute-start | bytes 786440 | tf_op jit(solution)/shard_map/ppermute | solution.py:885
  634.6 136.7 %collective-permute-start.9 = (bf16[96,1536]{1,0:T(8,128)(2,1)}, bf16[96,1536]{1,0:T(8,128)(2,1)}, u32[]{:S(2)}, u32[]{:S(2)}) collective-permute-start(bf16[96,1536]{1,0:T(8,128)(2,1)} %fusion.20), channel_id=1, source_target_pairs={{0,1},{1,0},{2,3},{3,2},{4,5},{5,4},{6,7},{7,6},{8,9},{9,8},{10,11... | collective-permute-start | bytes 884744 | tf_op jit(solution)/shard_map/ppermute | solution.py:885
  641.7 9.5 copy-start.12
  651.1 36.8 %copy-start.30 = (f32[1536,384]{1,0:T(8,128)}, f32[1536,384]{1,0:T(8,128)S(1)}, u32[]{:S(2)}) copy-start(f32[1536,384]{1,0:T(8,128)S(1)} %get-tuple-element.134) | copy-start | bytes 7077892
  651.1 36.7 %copy-start.45 = (f32[128,1536]{1,0:T(8,128)S(1)}, f32[128,1536]{1,0:T(8,128)}, u32[]{:S(2)}) copy-start(f32[128,1536]{1,0:T(8,128)} %copy-done.44) | copy-start | bytes 2359300
  651.1 37.0 %copy-start.58 = (bf16[128,1536]{1,0:T(8,128)(2,1)S(1)}, bf16[128,1536]{1,0:T(8,128)(2,1)}, u32[]{:S(2)}) copy-start(bf16[128,1536]{1,0:T(8,128)(2,1)} %refs_0_) | copy-start | bytes 1179652
  728.5 25.0 %copy-start.40 = (bf16[8,128,1536]{2,1,0:T(8,128)(2,1)S(1)}, bf16[8,128,1536]{2,1,0:T(8,128)(2,1)}, u32[]{:S(2)}) copy-start(bf16[8,128,1536]{2,1,0:T(8,128)(2,1)} %get-tuple-element.85) | copy-start | bytes 9437188
  772.5 36.4 %copy-start.20 = (bf16[96,1536]{1,0:T(8,128)(2,1)}, bf16[96,1536]{1,0:T(8,128)(2,1)S(1)}, u32[]{:S(2)}) copy-start(bf16[96,1536]{1,0:T(8,128)(2,1)S(1)} %fusion.19.refs_4_.refs_2_) | copy-start | bytes 884740
  776.8 32.0 %copy-start.50 = (f32[128,1536]{1,0:T(8,128)S(1)}, f32[128,1536]{1,0:T(8,128)}, u32[]{:S(2)}) copy-start(f32[128,1536]{1,0:T(8,128)} %copy-done.48) | copy-start | bytes 2359300
  776.8 32.1 %copy-start.93 = (f32[128]{0:T(128)S(1)}, f32[128]{0:T(128)}, u32[]{:S(2)}) copy-start(f32[128]{0:T(128)} %copy-done.92) | copy-start | bytes 1540
  776.8 32.4 %copy-start.67 = (f32[128,1536]{1,0:T(8,128)S(1)}, f32[128,1536]{1,0:T(8,128)}, u32[]{:S(2)}) copy-start(f32[128,1536]{1,0:T(8,128)} %get-tuple-element.234) | copy-start | bytes 2359300
  888.0 17.2 %collective-permute-start.10 = (bf16[8,128,128]{2,1,0:T(8,128)(2,1)}, bf16[8,128,128]{2,1,0:T(8,128)(2,1)S(1)}, u32[]{:S(2)}, u32[]{:S(2)}) collective-permute-start(bf16[8,128,128]{2,1,0:T(8,128)(2,1)} %convert_element_type.194), channel_id=1, source_target_pairs={{0,1},{1,0},{2,3},{3,2},{4,5},{5,4},{6,7},{7,6},{8,9},{9,8},{10,11... | collective-permute-start | bytes 786440 | tf_op jit(solution)/shard_map/ppermute | solution.py:885
  890.3 143.1 %collective-permute-start.11 = (bf16[96,1536]{1,0:T(8,128)(2,1)}, bf16[96,1536]{1,0:T(8,128)(2,1)}, u32[]{:S(2)}, u32[]{:S(2)}) collective-permute-start(bf16[96,1536]{1,0:T(8,128)(2,1)} %fusion.21), channel_id=1, source_target_pairs={{0,1},{1,0},{2,3},{3,2},{4,5},{5,4},{6,7},{7,6},{8,9},{9,8},{10,11... | collective-permute-start | bytes 884744 | tf_op jit(solution)/shard_map/ppermute | solution.py:885
  895.9 151.6 %collective-permute-start.13 = (bf16[512,1536]{1,0:T(8,128)(2,1)}, bf16[512,1536]{1,0:T(8,128)(2,1)}, u32[]{:S(2)}, u32[]{:S(2)}) collective-permute-start(bf16[512,1536]{1,0:T(8,128)(2,1)} %fusion.5.refs_0_), channel_id=1, source_target_pairs={{0,16},{16,0},{1,17},{17,1},{2,18},{18,2},{3,19},{19,3},{4,20},{20... | collective-permute-start | bytes 4718600 | tf_op jit(solution)/shard_map/ppermute | solution.py:1060
  916.2 50.6 %copy-start.31 = (f32[1536,384]{1,0:T(8,128)}, f32[1536,384]{1,0:T(8,128)S(1)}, u32[]{:S(2)}) copy-start(f32[1536,384]{1,0:T(8,128)S(1)} %get-tuple-element.132) | copy-start | bytes 7077892
  916.2 51.7 %copy-start.55 = (bf16[128,1536]{1,0:T(8,128)(2,1)S(1)}, bf16[128,1536]{1,0:T(8,128)(2,1)}, u32[]{:S(2)}) copy-start(bf16[128,1536]{1,0:T(8,128)(2,1)} %param.15) | copy-start | bytes 1179652
  916.2 51.7 %copy-start.95 = (f32[128]{0:T(128)S(1)}, f32[128]{0:T(128)}, u32[]{:S(2)}) copy-start(f32[128]{0:T(128)} %copy-done.94) | copy-start | bytes 1540
  916.2 52.5 %copy-start.88 = (bf16[2,1536]{1,0:T(2,128)(2,1)S(1)}, bf16[2,1536]{1,0:T(2,128)(2,1)}, u32[]{:S(2)}) copy-start(bf16[2,1536]{1,0:T(2,128)(2,1)} %select_convert_fusion.1) | copy-start | bytes 18436
  1022.7 8.4 copy-start.97
  1022.7 8.4 copy-start.96
  1034.5 8.8 copy-start.72
  1034.5 9.6 collective-permute-start.12
  (74 other events, 194.6 us)

commit v3 on v2

--- a/solution.py
+++ b/solution.py
@@ -70,122 +70,249 @@
     return {(0, 0): half, (1, 1): half, (0, 1): half - 1, (1, 0): half - 1}
 
 
-def gather_kernel(count, axes, sided, *refs):
-    riders = len(axes)
-    sources = refs[: 1 + sided]
-    ride_in = refs[1 + sided : 1 + sided + riders]
-    rest = refs[1 + sided + riders :]
-    targets, rest = rest[: 1 + sided], rest[1 + sided :]
-    ride_out, rest = rest[:riders], rest[riders:]
-    own_sem, send_sem, recv_sem, side_send, side_recv, ride_send, ride_recv = rest
-    chip, at, near = ring_setup(count)
-    x_ref, o_ref = sources[0], targets[0]
-    half_rows = x_ref.shape[0] // 2
-    hops = ring_hops(count)
-    steps = count // 2
-    meet(near + [partner_of(axis) for axis in sorted(set(axes))])
+IDENTITIES = {}
+
+
+def identity(*key):
+    return IDENTITIES.setdefault(key, len(IDENTITIES))
+
+
+def shape_of(array):
+    return jax.ShapeDtypeStruct(array.shape, array.dtype)
+
+
+class Ring:
+    def __init__(self, count, rides=()):
+        self.count = count
+        self.steps = count // 2
+        self.chip, self.at, self.near = ring_setup(count)
+        self.rides = rides
+
+    def meet(self, axes):
+        meet(self.near + [partner_of(axis) for axis in sorted(set(axes))])
+
+    def gather(self, x_ref, buf, sems, side=None, first=None, second=None):
+        own_sem, send_sem, recv_sem = sems[:3]
+        half_rows = x_ref.shape[0] // 2
+        steps = self.steps
+        own = [pltpu.make_async_copy(x_ref, buf.at[self.chip], own_sem.at[0])]
+        if side is not None:
+            side_ref, side_buf = side
+            side_send, side_recv = sems[3:]
+            own.append(pltpu.make_async_copy(side_ref, side_buf.at[self.chip], own_sem.at[1]))
+        for copy in own:
+            copy.start()
+
+        def piece(key, step, block, source=None):
+            direction, part = key
+            rows = pl.ds(part * half_rows, half_rows)
+            target = buf.at[block, rows]
+            return remote(
+                target if source is None else source.at[rows],
+                target,
+                send_sem.at[direction, part, step],
+                recv_sem.at[direction, part, step],
+                self.near[direction],
+            )
+
+        def side_piece(direction, step, block, source=None):
+            target = side_buf.at[block]
+            return remote(
+                target if source is None else source,
+                target,
+                side_send.at[direction, step],
+                side_recv.at[direction, step],
+                self.near[direction],
+            )
+
+        def toward(key, places):
+            return self.at(-places if key[0] == 0 else places)
+
+        early, late = [(0, 0), (1, 1)], [(0, 1), (1, 0)]
+        if side is not None:
+            for direction in range(2):
+                side_piece(direction, 0, self.chip, side_ref).start()
+        for key in early + late:
+            piece(key, 0, self.chip, x_ref).start()
+
+        def step(s, carry):
+            if side is not None:
+                for direction in range(2):
+
+                    @pl.when(s <= steps - direction)
+                    def _():
+                        block = toward((direction, 0), s)
+                        side_piece(direction, s - 1, block).wait_recv()
+
+                        @pl.when(s < steps - direction)
+                        def _():
+                            side_piece(direction, s, block).start()
+
+            for key in early:
+                block = toward(key, s)
+                piece(key, s - 1, block).wait_recv()
+
+                @pl.when(s < steps)
+                def _():
+                    piece(key, s, block).start()
+
+            if first is not None:
+                first(s)
+
+            @pl.when(s < steps)
+            def _():
+                for key in late:
+                    block = toward(key, s)
+                    piece(key, s - 1, block).wait_recv()
+
+                    @pl.when(s < steps - 1)
+                    def _():
+                        piece(key, s, block).start()
+
+            if second is not None:
+                second(s)
+            return carry
+
+        for copy in own:
+            copy.wait()
+        lax.fori_loop(1, steps + 1, step, 0)
+
+        def drain():
+            for s in range(steps):
+                for key in early + (late if s < steps - 1 else []):
+                    piece(key, s, toward(key, s)).wait_send()
+                if side is not None:
+                    for direction in range(2):
+                        if s < steps - direction:
+                            side_piece(direction, s, toward((direction, 0), s)).wait_send()
+
+        return drain
+
+    def pair(self, s):
+        return self.at(s), self.at(lax.select(s < self.steps, -s, 0))
+
+    def scatter(self, partial, land, out_ref, sems, work=None):
+        send_sem, recv_sem = sems
+        half_rows = out_ref.shape[0] // 2
+        steps = self.steps
+        hops = ring_hops(self.count)
+
+        def ahead(key, s):
+            places = hops[key] - s
+            return self.at(places if key[0] == 0 else -places)
+
+        def piece(key, s, source):
+            direction, part = key
+            return remote(
+                source,
+                land.at[direction, part, s],
+                send_sem.at[direction, part, s],
+                recv_sem.at[direction, part, s],
+                self.near[direction],
+            )
+
+        def rows_of(key):
+            return pl.ds(key[1] * half_rows, half_rows)
+
+        for key in hops:
+            piece(key, 0, partial.at[ahead(key, 0), rows_of(key)]).start()
+
+        def step(s, carry):
+            for place, key in enumerate(hops):
+                if work is not None:
+                    work(s - 1, place)
+
+                @pl.when(s < hops[key])
+                def _():
+                    slot = land.at[key[0], key[1], s - 1]
+                    piece(key, s - 1, slot).wait_recv()
+                    mine = partial[ahead(key, s), rows_of(key)]
+                    slot[...] = (slot[...].astype(F32) + mine.astype(F32)).astype(BF16)
+                    piece(key, s, slot).start()
+
+            return carry
+
+        lax.fori_loop(1, steps + 1, step, 0)
+        for key in hops:
+            slot = land.at[key[0], key[1], hops[key] - 1]
+            piece(key, hops[key] - 1, slot).wait_recv()
+        for part in range(2):
+            rows = pl.ds(part * half_rows, half_rows)
+            total = partial[self.chip, rows].astype(F32)
+            for direction in range(2):
+                total = total + land[direction, part, hops[direction, part] - 1].astype(F32)
+            out_ref[rows, :] = total
+
+        def drain():
+            for key in hops:
+                for s in range(hops[key]):
+                    piece(key, s, land.at[key[0], key[1], s]).wait_send()
+
+        return drain
+
+
+def start_rides(axes, sources, targets, sems):
+    send_sem, recv_sem = sems
     rides = [
-        remote(ride_in[i], ride_out[i], ride_send.at[i], ride_recv.at[i], partner_of(axes[i]))
-        for i in range(riders)
+        remote(sources[i], targets[i], send_sem.at[i], recv_sem.at[i], partner_of(axis))
+        for i, axis in enumerate(axes)
     ]
     for ride in rides:
         ride.start()
-    own = [
-        pltpu.make_async_copy(sources[i], targets[i].at[chip], own_sem.at[i])
-        for i in range(1 + sided)
-    ]
-    for copy in own:
-        copy.start()
-
-    def piece(key, step, arrived):
-        direction, part = key
-        moved = step + 1 if arrived else step
-        block = at(-moved if direction == 0 else moved)
-        rows = pl.ds(part * half_rows, half_rows)
-        target = o_ref.at[block, rows]
-        return remote(
-            x_ref.at[rows] if step == 0 and not arrived else target,
-            target,
-            send_sem.at[direction, part, step],
-            recv_sem.at[direction, part, step],
-            near[direction],
-        )
-
-    def side_piece(direction, step, arrived):
-        moved = step + 1 if arrived else step
-        target = targets[1].at[at(-moved if direction == 0 else moved)]
-        return remote(
-            sources[1] if step == 0 and not arrived else target,
-            target,
-            side_send.at[direction, step],
-            side_recv.at[direction, step],
-            near[direction],
-        )
-
-    side_hops = (steps, steps - 1) if sided else (0, 0)
-    for step in range(steps + 1):
-        for direction in range(2):
-            if 0 < step <= side_hops[direction]:
-                side_piece(direction, step - 1, True).wait_recv()
-            if step < side_hops[direction]:
-                side_piece(direction, step, False).start()
-        for key in hops:
-            if 0 < step <= hops[key]:
-                piece(key, step - 1, True).wait_recv()
-            if step < hops[key]:
-                piece(key, step, False).start()
-    for step in range(steps):
-        for direction in range(2):
-            if step < side_hops[direction]:
-                side_piece(direction, step, False).wait_send()
-        for key in hops:
-            if step < hops[key]:
-                piece(key, step, False).wait_send()
-    for copy in own:
-        copy.wait()
-    for ride in rides:
-        ride.wait()
-
-
-IDENTITIES = {}
-
-
-def identity(*key):
-    return IDENTITIES.setdefault(key, len(IDENTITIES))
-
-
-def shape_of(array):
-    return jax.ShapeDtypeStruct(array.shape, array.dtype)
-
-
-def ring_gather(count, arrays, rides=()):
+    return rides
+
+
+def dmas(*shapes):
+    return [pltpu.SemaphoreType.DMA(shape) for shape in shapes]
+
+
+def gather_sems(count, sided=False):
     steps = count // 2
-    sided = len(arrays) - 1
+    shapes = [(2,), (2, 2, steps), (2, 2, steps)]
+    return dmas(*(shapes + ([(2, steps), (2, steps)] if sided else [])))
+
+
+def scatter_sems(count):
+    return dmas((2, 2, count // 2), (2, 2, count // 2))
+
+
+def ride_sems(rides):
+    return dmas((max(len(rides), 1),), (max(len(rides), 1),))
+
+
+ANYWHERE = pl.BlockSpec(memory_space=pl.ANY)
+HERE = pl.BlockSpec(memory_space=pltpu.VMEM)
+
+
+def ring_call(body, name, here, inputs, outputs, scratch, rides, megabytes):
     axes = tuple(axis for _, axis in rides)
     passengers = [array for array, _ in rides]
-    dma = pltpu.SemaphoreType.DMA
+    arrays = [array for array, _ in inputs]
     return pl.pallas_call(
-        functools.partial(gather_kernel, count, axes, sided),
-        out_shape=tuple(
-            jax.ShapeDtypeStruct((count,) + a.shape, a.dtype) for a in arrays
-        ) + tuple(shape_of(a) for a in passengers),
-        in_specs=[pl.BlockSpec(memory_space=pl.ANY)] * (len(arrays) + len(rides)),
-        out_specs=[pl.BlockSpec(memory_space=pl.ANY)] * (len(arrays) + len(rides)),
-        scratch_shapes=[
-            dma((2,)),
-            dma((2, 2, steps)),
-            dma((2, 2, steps)),
-            dma((2, steps)),
-            dma((2, steps)),
-            dma((max(len(rides), 1),)),
-            dma((max(len(rides), 1),)),
-        ],
+        functools.partial(body, axes),
+        out_shape=tuple(shape for shape, _ in outputs) + tuple(shape_of(a) for a in passengers),
+        in_specs=[spec for _, spec in inputs] + [ANYWHERE] * len(rides),
+        out_specs=[spec for _, spec in outputs] + [ANYWHERE] * len(rides),
+        scratch_shapes=list(scratch) + ride_sems(rides),
         compiler_params=pltpu.CompilerParams(
-            collective_id=identity("gather", sided, axes, *(a.shape for a in passengers)),
+            collective_id=identity(name, here, axes, *(a.shape for a in passengers)),
             has_side_effects=True,
+            vmem_limit_bytes=megabytes << 20,
         ),
-        name="ring_gather",
+        name=name,
     )(*arrays, *passengers)
+
+
+def split(refs, *sizes):
+    parts, place = [], 0
+    for size in sizes:
+        parts.append(refs[place : place + size])
+        place += size
+    return parts + [refs[place:]]
+
+
+def cells(shape, dtype):
+    return jax.ShapeDtypeStruct(shape, dtype)
 
 
 def scatter_kernel(count, axes, *refs):
@@ -492,43 +619,532 @@
     return field * cosine + swapped * sine
 
 
-def project_kernel(x_ref, w_ref, cos_ref, sin_ref, q_ref, kv_ref):
-    rows = dot(x_ref[...], w_ref[...])
-    cosine, sine = cos_ref[...], sin_ref[...]
+def project_rows(rows, cosine, sine):
     first = spin(rows[:, :LANES], cosine, sine)
     second = spin(rows[:, LANES : 2 * LANES], cosine, sine)
     third = rows[:, 2 * LANES :]
     low = lanes_of(first) < HD
-    kv_ref[...] = jnp.where(low, turn(second), turn(third)).astype(BF16)
-    for head, field in enumerate((first, turn(first), second)):
+    heads = []
+    for field in (first, turn(first), second):
         rounded = jnp.where(low, field, 0.0).astype(BF16).astype(F32)
-        scaled = (rounded * (HD**-0.5)).astype(BF16)
-        for block in range(2):
-            q_ref[block, head] = scaled[block * LANES : (block + 1) * LANES]
-
-
-def project(x, w, cosine, sine):
-    tokens, width = x.shape
-    tile = 2 * LANES
-    return pl.pallas_call(
-        project_kernel,
-        grid=(tokens // tile,),
-        out_shape=(
-            jax.ShapeDtypeStruct((tokens // LANES, GROUP, LANES, LANES), BF16),
-            jax.ShapeDtypeStruct((tokens, LANES), BF16),
-        ),
-        in_specs=[
-            pl.BlockSpec((tile, width), lambda i: (i, 0)),
-            pl.BlockSpec(w.shape, lambda i: (0, 0)),
-            pl.BlockSpec((tile, LANES), lambda i: (i, 0)),
-            pl.BlockSpec((tile, LANES), lambda i: (i, 0)),
+        heads.append((rounded * (HD**-0.5)).astype(BF16))
+    return heads, jnp.where(low, turn(second), turn(third)).astype(BF16)
+
+
+def project_kernel(count, axes, *refs):
+    inputs, ride_in, outputs, ride_out, scratch = split(refs, 4, len(axes), 4, len(axes))
+    x_ref, w_ref, cos_ref, sin_ref = inputs
+    q_ref, own_ref, other_ref, all_ref = outputs
+    buf, sems, pair_sems, out_sem, ride_sem = scratch[0], scratch[1:4], scratch[4:6], scratch[6], scratch[7:]
+    ring = Ring(count)
+    ring.meet(axes + ("fsdp",))
+    rides = start_rides(axes, ride_in, ride_out, ride_sem)
+    partner = partner_of("fsdp")
+
+    def pass_on(block):
+        return remote(
+            own_ref.at[block], other_ref.at[block], pair_sems[0].at[block], pair_sems[1].at[block], partner
+        )
+
+    def compute(s):
+        blocks = ring.pair(s)
+        rows = dot(jnp.concatenate([buf[b] for b in blocks], 0), w_ref[...])
+        cosine = jnp.concatenate([cos_ref[b] for b in blocks], 0)
+        sine = jnp.concatenate([sin_ref[b] for b in blocks], 0)
+        heads, pair = project_rows(rows, cosine, sine)
+        for place, block in enumerate(blocks):
+            here = slice(place * LANES, (place + 1) * LANES)
+            for head in range(GROUP):
+                q_ref[block, head] = heads[head][here]
+            own_ref[block] = pair[here]
+            pass_on(block).start()
+
+    def second(s):
+        @pl.when(s >= 2)
+        def _():
+            compute(s - 1)
+
+    drain = ring.gather(x_ref, buf, sems, None, None, second)
+    keep = pltpu.make_async_copy(buf, all_ref, out_sem.at[0])
+    keep.start()
+    compute(ring.steps)
+    drain()
+    for block in range(count):
+        pass_on(block).wait()
+    keep.wait()
+    for ride in rides:
+        ride.wait()
+
+
+def gather_project(count, x, w, cosine, sine, rides=()):
+    rows, width = x.shape
+    block = cells((count, rows, LANES), BF16)
+    return ring_call(
+        functools.partial(project_kernel, count),
+        "project",
+        0,
+        [(x, ANYWHERE), (w, HERE), (cosine, HERE), (sine, HERE)],
+        [
+            (cells((count, GROUP, rows, LANES), BF16), HERE),
+            (block, HERE),
+            (block, HERE),
+            (cells((count, rows, width), BF16), ANYWHERE),
         ],
-        out_specs=[
-            pl.BlockSpec((2, GROUP, LANES, LANES), lambda i: (i, 0, 0, 0)),
-            pl.BlockSpec((tile, LANES), lambda i: (i, 0)),
+        [pltpu.VMEM((count, rows, width), BF16)] + gather_sems(count) + dmas((count,), (count,), (1,)),
+        rides,
+        40,
+    )
+
+
+def column(table, block, row):
+    line = table[block, pl.ds(row, 1), :]
+    shape = (LANES, LANES)
+    same = lax.broadcasted_iota(jnp.int32, shape, 0) == lax.broadcasted_iota(jnp.int32, shape, 1)
+    return jnp.sum(jnp.where(same, jnp.broadcast_to(line, shape), 0.0), 1, keepdims=True)
+
+
+def load_experts(refs, gates, ups, downs, sem):
+    copies = []
+    for e in range(2):
+        for place, buf in enumerate((gates, ups, downs)):
+            copies.append(pltpu.make_async_copy(refs[3 * e + place], buf.at[e], sem.at[3 * e + place]))
+    for copy in copies:
+        copy.start()
+    return copies
+
+
+def expert_rows(e):
+    me = lax.axis_index("fsdp")
+    return me if e == 0 else me + 1 - 2 * lax.rem(me, 2)
+
+
+def mix_kernel(count, axes, *refs):
+    inputs, ride_in, outputs, ride_out, scratch = split(refs, 8, len(axes), 3, len(axes))
+    x_ref, side_ref = inputs[:2]
+    out_ref, all_ref, share_ref = outputs
+    buf, partial, land, acc, gates, ups, downs = scratch[:7]
+    sems, scatter_sem, load_sem, out_sem, ride_sem = split(scratch[7:], 5, 2, 1, 1)
+    ring = Ring(count)
+    ring.meet(axes)
+    rides = start_rides(axes, ride_in, ride_out, ride_sem)
+    loads = load_experts(inputs[2:], gates, ups, downs, load_sem[0])
+
+    def compute(e, s):
+        blocks = ring.pair(s)
+        x = jnp.concatenate([buf[b] for b in blocks], 0)
+        act_gate, act_up = dot(x, gates[e]), dot(x, ups[e])
+        share = jnp.concatenate([column(share_ref, b, expert_rows(e)) for b in blocks], 0)
+        hidden = jax.nn.silu(act_gate) * act_up * share
+        part = dot(hidden.astype(BF16), downs[e])
+        if e == 0:
+            acc[...] = part
+        else:
+            total = (acc[...] + part).astype(BF16)
+            for place, block in enumerate(blocks):
+                partial[block] = total[place * LANES : (place + 1) * LANES]
+
+    def at_step(e):
+        def run(s):
+            @pl.when(s >= 2)
+            def _():
+                compute(e, s - 1)
+
+        return run
+
+    for load in loads:
+        load.wait()
+    drain = ring.gather(x_ref, buf, sems, (side_ref, share_ref), at_step(0), at_step(1))
+    keep = pltpu.make_async_copy(buf, all_ref, out_sem[0].at[0])
+    keep.start()
+    compute(0, ring.steps)
+    compute(1, ring.steps)
+    finish = ring.scatter(partial, land, out_ref, scatter_sem)
+    drain()
+    finish()
+    keep.wait()
+    for ride in rides:
+        ride.wait()
+
+
+def expert_scratch(weights):
+    return [pltpu.VMEM((2,) + w.shape, BF16) for w in weights[:3]]
+
+
+def land_scratch(count, rows, width):
+    return pltpu.VMEM((2, 2, count // 2, rows // 2, width), BF16)
+
+
+def gather_mix_scatter(count, x, share, weights, rides=()):
+    rows, width = x.shape
+    everyone = pltpu.VMEM((count, rows, width), BF16)
+    return ring_call(
+        functools.partial(mix_kernel, count),
+        "mix",
+        0,
+        [(x, ANYWHERE), (share, ANYWHERE)] + [(w, ANYWHERE) for w in weights],
+        [
+            (cells((rows, width), F32), HERE),
+            (cells((count, rows, width), BF16), ANYWHERE),
+            (cells((count,) + share.shape, F32), HERE),
         ],
-        name="project",
-    )(x, w, cosine, sine)
+        [everyone, everyone, land_scratch(count, rows, width), pltpu.VMEM((2 * rows, width), F32)]
+        + expert_scratch(weights)
+        + gather_sems(count, True)
+        + scatter_sems(count)
+        + dmas((6,), (1,)),
+        rides,
+        56,
+    )
+
+
+def mix_back_kernel(count, axes, *refs):
+    inputs, ride_in, outputs, ride_out, scratch = split(refs, 11, len(axes), 5, len(axes))
+    d_ref, side_ref, m_ref, share_ref, router_ref = inputs[:5]
+    out_ref, upper_ref, lower_ref, down_ref, g_router_ref = outputs
+    buf, partial, land, acc, gates, ups, downs = scratch[:7]
+    tokens, acts, hiddens, balance_ref, wide_sum, down_sum, wide_got, down_got = scratch[7:15]
+    sems, scatter_sem, load_sem, pair_sem, out_sem, ride_sem = split(scratch[15:], 5, 2, 1, 2, 1)
+    ring = Ring(count)
+    ring.meet(axes + ("fsdp",))
+    rides = start_rides(axes, ride_in, ride_out, ride_sem)
+    loads = load_experts(inputs[5:], gates, ups, downs, load_sem[0])
+    loads.append(pltpu.make_async_copy(m_ref, tokens, load_sem[0].at[6]))
+    loads[-1].start()
+    ff = gates.shape[2]
+    g_router_ref[...] = jnp.zeros_like(g_router_ref)
+
+    def compute(e, s):
+        blocks = ring.pair(s)
+        d = jnp.concatenate([buf[b] for b in blocks], 0)
+        x = jnp.concatenate([tokens[b] for b in blocks], 0)
+        share = jnp.concatenate([column(share_ref, b, expert_rows(e)) for b in blocks], 0)
+        balance = jnp.concatenate([column(balance_ref, b, 0) for b in blocks], 0)
+        act_gate, act_up = dot(x, gates[e]), dot(x, ups[e])
+        sig = jax.nn.sigmoid(act_gate)
+        swish = act_gate * sig
+        hidden = swish * act_up
+        raw = dot(d, downs[e], NT)
+        d_logit = share * (jnp.sum(hidden * raw, -1, keepdims=True) - balance)
+        d_hidden = raw * share
+        d_gate = (d_hidden * act_up * sig * (1.0 + act_gate * (1.0 - sig))).astype(BF16)
+        d_up = (d_hidden * swish).astype(BF16)
+        weighted = (hidden * share).astype(BF16)
+        part = dot(d_gate, gates[e], NT) + dot(d_up, ups[e], NT)
+        part = part + d_logit * router_ref[e : e + 1, :]
+        g_router_ref[e : e + 1, :] += jnp.sum(d_logit * x.astype(F32), 0, keepdims=True)
+        for place, block in enumerate(blocks):
+            here = slice(place * LANES, (place + 1) * LANES)
+            acts[e, block, :, :ff] = d_gate[here]
+            acts[e, block, :, ff:] = d_up[here]
+            hiddens[e, block] = weighted[here]
+        if e == 0:
+            acc[...] = part
+        else:
+            total = (acc[...] + part).astype(BF16)
+            for place, block in enumerate(blocks):
+                partial[block] = total[place * LANES : (place + 1) * LANES]
+
+    def at_step(e):
+        def run(s):
+            @pl.when(s >= 2)
+            def _():
+                compute(e, s - 1)
+
+        return run
+
+    for load in loads:
+        load.wait()
+    drain = ring.gather(d_ref, buf, sems, (side_ref, balance_ref), at_step(0), at_step(1))
+    compute(0, ring.steps)
+    compute(1, ring.steps)
+
+    width = buf.shape[2]
+    steps = ring.steps
+    partner = partner_of("fsdp")
+    strip = 2 * LANES
+    strips = width // (2 * strip)
+
+    def half_of(half):
+        wide_rows = pl.ds(pl.multiple_of(half * (width // 2), strip), width // 2)
+        down_rows = pl.ds(pl.multiple_of(half * (ff // 2), strip), ff // 2)
+        return wide_rows, down_rows
+
+    def swap(half):
+        wide_rows, down_rows = half_of(half)
+        return [
+            remote(wide_sum.at[1, wide_rows], wide_got.at[wide_rows], pair_sem[0].at[0, half], pair_sem[1].at[0, half], partner),
+            remote(down_sum.at[1, down_rows], down_got.at[down_rows], pair_sem[0].at[1, half], pair_sem[1].at[1, half], partner),
+        ]
+
+    def store(half):
+        out = [upper_ref, lower_ref][half]
+        wide_rows, down_rows = half_of(half)
+        return [
+            pltpu.make_async_copy(wide_sum.at[0, wide_rows], out, out_sem[0].at[2 * half]),
+            pltpu.make_async_copy(down_sum.at[0, down_rows], down_ref.at[down_rows], out_sem[0].at[2 * half + 1]),
+        ]
+
+    def flat(value):
+        return value.reshape(value.shape[0] * value.shape[1], value.shape[2])
+
+    def work(s, place):
+        e = 1 - s // 2
+        half = lax.rem(s, 2)
+
+        def put(target, got, rows, value):
+            @pl.when(s < 2)
+            def _():
+                target[1, rows] = value.astype(BF16)
+
+            @pl.when(s >= 2)
+            def _():
+                target[0, rows] = (value + got[rows].astype(F32)).astype(BF16)
+
+        if place == 0:
+            for h in range(2):
+
+                @pl.when(s == 2 + h)
+                def _():
+                    for copy in swap(h):
+                        copy.wait_recv()
+
+        if place < strips:
+            rows = pl.ds(pl.multiple_of((half * strips + place) * strip, strip), strip)
+            value = dot(flat(tokens[:, :, rows]), flat(acts[e]), TN)
+            put(wide_sum, wide_got, rows, value)
+        if place == 3:
+            rows = pl.ds(pl.multiple_of(half * strip, strip), strip)
+            value = dot(flat(hiddens[e, :, :, rows]), flat(buf[...]), TN)
+            put(down_sum, down_got, rows, value)
+            for h in range(2):
+
+                @pl.when(s == h)
+                def _():
+                    for copy in swap(h):
+                        copy.start()
+
+                @pl.when(s == 2 + h)
+                def _():
+                    for copy in store(h):
+                        copy.start()
+
+    finish = ring.scatter(partial, land, out_ref, scatter_sem, work)
+    drain()
+    finish()
+    for half in range(2):
+        for copy in swap(half):
+            copy.wait_send()
+        for copy in store(half):
+            copy.wait()
+    for ride in rides:
+        ride.wait()
+
+
+def gather_mix_back_scatter(count, d, side, m_all, share, router, weights, rides=()):
+    rows, width = d.shape
+    ff = weights[0].shape[1]
+    everyone = pltpu.VMEM((count, rows, width), BF16)
+    return ring_call(
+        functools.partial(mix_back_kernel, count),
+        "mix_back",
+        0,
+        [(d, ANYWHERE), (side, ANYWHERE), (m_all, ANYWHERE), (share, HERE), (router, HERE)]
+        + [(w, ANYWHERE) for w in weights],
+        [
+            (cells((rows, width), F32), HERE),
+            (cells((width // 2, 2 * ff), BF16), ANYWHERE),
+            (cells((width // 2, 2 * ff), BF16), ANYWHERE),
+            (cells((ff, width), BF16), ANYWHERE),
+            (cells((2, width), F32), HERE),
+        ],
+        [everyone, everyone, land_scratch(count, rows, width), pltpu.VMEM((2 * rows, width), F32)]
+        + expert_scratch(weights)
+        + [
+            everyone,
+            pltpu.VMEM((2, count, rows, 2 * ff), BF16),
+            pltpu.VMEM((2, count, rows, ff), BF16),
+            pltpu.VMEM((count,) + side.shape, F32),
+            pltpu.VMEM((2, width, 2 * ff), BF16),
+            pltpu.VMEM((2, ff, width), BF16),
+            pltpu.VMEM((width, 2 * ff), BF16),
+            pltpu.VMEM((ff, width), BF16),
+        ]
+        + gather_sems(count, True)
+        + scatter_sems(count)
+        + dmas((7,), (2, 2), (2, 2), (4,)),
+        rides,
+        60,
+    )
+
+
+def branch_back_kernel(count, axes, *refs):
+    inputs, ride_in, outputs, ride_out, scratch = split(refs, 3, len(axes), 2, len(axes))
+    d_ref, w_ref, att_ref = inputs
+    datt_ref, g_ref = outputs
+    buf, wide_w, acc, mail, got = scratch[:5]
+    sems, pair_sem, ride_sem = split(scratch[5:], 3, 2)
+    ring = Ring(count)
+    ring.meet(axes + ("fsdp",))
+    rides = start_rides(axes, ride_in, ride_out, ride_sem)
+    fill_out_weights(w_ref, wide_w)
+    acc[...] = jnp.zeros_like(acc)
+
+    def compute(s):
+        blocks = ring.pair(s)
+        d = jnp.concatenate([buf[b] for b in blocks], 0)
+        att = jnp.concatenate([att_ref[b] for b in blocks], 0)
+        datt = dot(d, wide_w[...], NT).astype(BF16)
+        for place, block in enumerate(blocks):
+            datt_ref[block] = datt[place * LANES : (place + 1) * LANES]
+        acc[...] += dot(att, d, TN)
+
+    def second(s):
+        @pl.when(s >= 2)
+        def _():
+            compute(s - 1)
+
+    drain = ring.gather(d_ref, buf, sems, None, None, second)
+    compute(ring.steps)
+    shard = g_ref.shape[0]
+    core = lax.rem(lax.axis_index("fsdp"), 2)
+    mail[...] = acc[pl.ds(pl.multiple_of((1 - core) * shard, 8), shard), :].astype(BF16)
+    swap = remote(mail, got, pair_sem[0].at[0], pair_sem[1].at[0], partner_of("fsdp"))
+    swap.start()
+    drain()
+    swap.wait()
+    own = acc[pl.ds(pl.multiple_of(core * shard, 8), shard), :]
+    g_ref[...] = (own + got[...].astype(F32)).astype(BF16)
+    for ride in rides:
+        ride.wait()
+
+
+def gather_branch_back(count, d, w, att, rides=()):
+    rows, width = d.shape
+    shard = w.shape[0] // 2
+    return ring_call(
+        functools.partial(branch_back_kernel, count),
+        "branch_back",
+        0,
+        [(d, ANYWHERE), (w, HERE), (att, HERE)],
+        [
+            (cells((count, rows, 2 * LANES), BF16), HERE),
+            (cells((shard, width), BF16), HERE),
+        ],
+        [
+            pltpu.VMEM((count, rows, width), BF16),
+            pltpu.VMEM((2 * LANES, width), BF16),
+            pltpu.VMEM((2 * LANES, width), F32),
+            pltpu.VMEM((shard, width), BF16),
+            pltpu.VMEM((shard, width), BF16),
+        ]
+        + gather_sems(count)
+        + dmas((1,), (1,)),
+        rides,
+        32,
+    )
+
+
+def join_kernel(count, axes, *refs):
+    inputs, ride_in, outputs, ride_out, scratch = split(refs, 7, len(axes), 2, len(axes))
+    dq_ref, own_ref, other_ref, cos_ref, sin_ref, w_ref, x_ref = inputs
+    out_ref, g_ref = outputs
+    partial, land, rows_ref, tokens, got = scratch[:5]
+    scatter_sem, pair_sem, load_sem, ride_sem = split(scratch[5:], 2, 2, 1)
+    ring = Ring(count)
+    ring.meet(axes + ("fsdp",))
+    swap = remote(other_ref, got, pair_sem[0].at[0], pair_sem[1].at[0], partner_of("fsdp"))
+    swap.start()
+    rides = start_rides(axes, ride_in, ride_out, ride_sem)
+    load = pltpu.make_async_copy(x_ref, tokens, load_sem[0].at[0])
+    load.start()
+    swap.wait()
+
+    def compute(index, carry):
+        blocks = 2 * index, 2 * index + 1
+        rows = []
+        for b in blocks:
+            pair = own_ref[b] + got[b].astype(F32)
+            keys = spin(pair, cos_ref[b], -sin_ref[b])
+            low = lanes_of(pair) < HD
+            middle = jnp.where(low, dq_ref[b, :, LANES:].astype(F32), turn(keys))
+            last = jnp.where(low, turn(pair), 0.0)
+            rows.append(
+                jnp.concatenate([dq_ref[b, :, :LANES], middle.astype(BF16), last.astype(BF16)], 1)
+            )
+            rows_ref[b] = rows[-1]
+        total = dot(jnp.concatenate(rows, 0), w_ref[...], NT).astype(BF16)
+        for place, block in enumerate(blocks):
+            partial[block] = total[place * LANES : (place + 1) * LANES]
+        return carry
+
+    lax.fori_loop(0, count // 2, compute, 0)
+    load.wait()
+    strip = g_ref.shape[0] // ring.steps
+
+    def flat(value):
+        return value.reshape(value.shape[0] * value.shape[1], value.shape[2])
+
+    def work(s, place):
+        if place == 0:
+            rows = pl.ds(pl.multiple_of(s * strip, LANES), strip)
+            g_ref[rows] = dot(flat(tokens[:, :, rows]), flat(rows_ref[...]), TN)
+
+    finish = ring.scatter(partial, land, out_ref, scatter_sem, work)
+    finish()
+    for ride in rides:
+        ride.wait()
+
+
+def join_scatter(count, dq, own, other, cosine, sine, w, x_all, rides=()):
+    _, rows, width = x_all.shape
+    everyone = pltpu.VMEM((count, rows, width), BF16)
+    return ring_call(
+        functools.partial(join_kernel, count),
+        "join",
+        0,
+        [(dq, HERE), (own, HERE), (other, HERE), (cosine, HERE), (sine, HERE), (w, HERE), (x_all, ANYWHERE)],
+        [(cells((rows, width), F32), HERE), (cells(w.shape, F32), HERE)],
+        [
+            everyone,
+            land_scratch(count, rows, width),
+            pltpu.VMEM((count, rows, w.shape[1]), BF16),
+            everyone,
+            pltpu.VMEM(other.shape, BF16),
+        ]
+        + scatter_sems(count)
+        + dmas((1,), (1,), (1,)),
+        rides,
+        48,
+    )
+
+
+def add_wide_kernel(layers, *refs):
+    gate_ref, up_ref = refs[-2:]
+    ff = gate_ref.shape[-1]
+    for layer in range(layers):
+        for half in range(2):
+            own, got = refs[4 * layer + 2 * half : 4 * layer + 2 * half + 2]
+            total = own[...].astype(F32) + got[...].astype(F32)
+            gate_ref[layer, 0, half] = total[:, :ff]
+            up_ref[layer, 0, half] = total[:, ff:]
+
+
+def add_wide(pairs):
+    layers = len(pairs) // 2
+    rows, columns = pairs[0][0].shape
+    tile = rows // 4
+    flat = [array for pair in pairs for array in pair]
+    out = jax.ShapeDtypeStruct((layers, 1, 2, rows, columns // 2), F32)
+    gate, up = pl.pallas_call(
+        functools.partial(add_wide_kernel, layers),
+        grid=(4,),
+        out_shape=(out, out),
+        in_specs=[pl.BlockSpec((tile, columns), lambda i: (i, 0))] * len(flat),
+        out_specs=[pl.BlockSpec((layers, 1, 2, tile, columns // 2), lambda i: (0, 0, 0, i, 0))] * 2,
+        name="add_wide",
+    )(*flat)
+    shape = (layers, 1, 2 * rows, columns // 2)
+    return gate.reshape(shape), up.reshape(shape)
 
 
 def allowed_keys(begin, block, chunk, core):
@@ -621,8 +1237,8 @@
 
 
 def attend_back_kernel(
-    info_ref, q_ref, own_ref, other_ref, begin_ref, w_ref, att_ref, lse_ref, db_ref, cos_ref, sin_ref,
-    dq_ref, d_own_ref, d_other_ref, wide_ref,
+    info_ref, q_ref, own_ref, other_ref, begin_ref, att_ref, lse_ref, datt_ref, cos_ref, sin_ref,
+    dq_ref, d_own_ref, mail_ref, d_other_ref,
 ):
     step = pl.program_id(0)
     core = info_ref[0]
@@ -631,7 +1247,6 @@
 
     @pl.when(step == 0)
     def _():
-        fill_out_weights(w_ref, wide_ref)
         d_own_ref[...] = jnp.zeros_like(d_own_ref)
         d_other_ref[...] = jnp.zeros_like(d_other_ref)
 
@@ -644,7 +1259,7 @@
         parts = [jnp.where(low, 0.0, part) for part in (turn(front), front, turn(back))]
         return jnp.concatenate(parts, 0)
 
-    datt = spread(dot(db_ref[0], wide_ref[...], NT)).astype(BF16)
+    datt = spread(datt_ref[0].astype(F32)).astype(BF16)
     att = spread(att_ref[0].astype(F32))
     delta = jnp.sum(datt.astype(F32) * att, -1, keepdims=True)
     lse = lse_ref[0]
@@ -668,166 +1283,45 @@
     back = spin(jnp.where(low, heads[2], 0.0), cosine, sine)
     dq_ref[0] = jnp.concatenate([front, back], 1).astype(BF16)
 
-
-def attend_back(info, q, own, other, begin, w, att, lse, db, cosine, sine):
+    @pl.when(step == pl.num_programs(0) - 1)
+    def _():
+        mail_ref[...] = d_other_ref[...].astype(BF16)
+
+
+def attend_back(info, q, own, other, begin, att, lse, datt, cosine, sine):
     blocks = q.shape[0]
-    width = w.shape[1]
     wide = 2 * LANES
+
+    def block(*shape):
+        return pl.BlockSpec((1,) + shape, lambda i, s: (i,) + (0,) * len(shape))
+
+    whole = pl.BlockSpec(own.shape, lambda i, s: (0, 0, 0))
     return pl.pallas_call(
         attend_back_kernel,
         grid_spec=pltpu.PrefetchScalarGridSpec(
             num_scalar_prefetch=1,
             grid=(blocks,),
             in_specs=[
-                pl.BlockSpec((1, GROUP, LANES, LANES), lambda i, s: (i, 0, 0, 0)),
-                pl.BlockSpec(own.shape, lambda i, s: (0, 0, 0)),
-                pl.BlockSpec(own.shape, lambda i, s: (0, 0, 0)),
-                pl.BlockSpec((1, LANES, 1), lambda i, s: (i, 0, 0)),
-                pl.BlockSpec(w.shape, lambda i, s: (0, 0)),
-                pl.BlockSpec((1, LANES, wide), lambda i, s: (i, 0, 0)),
-                pl.BlockSpec((1, GROUP * LANES, 1), lambda i, s: (i, 0, 0)),
-                pl.BlockSpec((1, LANES, width), lambda i, s: (i, 0, 0)),
-                pl.BlockSpec((1, LANES, LANES), lambda i, s: (i, 0, 0)),
-                pl.BlockSpec((1, LANES, LANES), lambda i, s: (i, 0, 0)),
+                block(GROUP, LANES, LANES),
+                whole,
+                whole,
+                block(LANES, 1),
+                block(LANES, wide),
+                block(GROUP * LANES, 1),
+                block(LANES, wide),
+                block(LANES, LANES),
+                block(LANES, LANES),
             ],
-            out_specs=[
-                pl.BlockSpec((1, LANES, wide), lambda i, s: (i, 0, 0)),
-                pl.BlockSpec(own.shape, lambda i, s: (0, 0, 0)),
-                pl.BlockSpec(own.shape, lambda i, s: (0, 0, 0)),
-            ],
-            scratch_shapes=[pltpu.VMEM((wide, width), BF16)],
+            out_specs=[block(LANES, wide), whole, whole],
+            scratch_shapes=[pltpu.VMEM(own.shape, F32)],
         ),
         out_shape=(
             jax.ShapeDtypeStruct((blocks, LANES, wide), BF16),
             jax.ShapeDtypeStruct(own.shape, F32),
-            jax.ShapeDtypeStruct(own.shape, F32),
+            jax.ShapeDtypeStruct(own.shape, BF16),
         ),
         name="attend_back",
-    )(info, q, own, other, begin, w, att, lse, db, cosine, sine)
-
-
-def join_kernel(dq_ref, own_ref, got_ref, cos_ref, sin_ref, w_ref, x_ref, out_ref, g_ref):
-    pair = own_ref[...] + got_ref[...].astype(F32)
-    front = spin(pair, cos_ref[...], -sin_ref[...])
-    low = lanes_of(pair) < HD
-    middle = jnp.where(low, dq_ref[:, LANES:].astype(F32), turn(front))
-    last = jnp.where(low, turn(pair), 0.0)
-    rows = jnp.concatenate([dq_ref[:, :LANES], middle.astype(BF16), last.astype(BF16)], 1)
-    out_ref[...] = dot(rows, w_ref[...], NT).astype(BF16)
-    part = dot(x_ref[...], rows, TN)
-
-    @pl.when(pl.program_id(0) == 0)
-    def _():
-        g_ref[...] = part
-
-    @pl.when(pl.program_id(0) > 0)
-    def _():
-        g_ref[...] += part
-
-
-def join(dq, own, got, cosine, sine, w, x):
-    tokens, width = x.shape
-    tile = 2 * LANES
-
-    def rows(columns):
-        return pl.BlockSpec((tile, columns), lambda i: (i, 0))
-
-    return pl.pallas_call(
-        join_kernel,
-        grid=(tokens // tile,),
-        out_shape=(
-            jax.ShapeDtypeStruct((tokens, width), BF16),
-            jax.ShapeDtypeStruct(w.shape, F32),
-        ),
-        in_specs=[rows(2 * LANES), rows(LANES), rows(LANES), rows(LANES), rows(LANES),
-                  pl.BlockSpec(w.shape, lambda i: (0, 0)), rows(width)],
-        out_specs=[rows(width), pl.BlockSpec(w.shape, lambda i: (0, 0))],
-        compiler_params=pltpu.CompilerParams(vmem_limit_bytes=40 << 20),
-        name="join",
-    )(dq, own, got, cosine, sine, w, x)
-
-
-def mix_kernel(x_ref, share_ref, *refs):
-    weights, out_ref = refs[:6], refs[6]
-    x = x_ref[...]
-    out = None
-    for e in range(2):
-        gate_w, up_w, down_w = weights[3 * e : 3 * e + 3]
-        act_gate, act_up = dot(x, gate_w[...]), dot(x, up_w[...])
-        hidden = jax.nn.silu(act_gate) * act_up * share_ref[:, e : e + 1]
-        part = dot(hidden.astype(BF16), down_w[...])
-        out = part if out is None else out + part
-    out_ref[...] = out.astype(BF16)
-
-
-def mix(x, share, weights):
-    tokens, width = x.shape
-    tile = 2 * LANES
-
-    def rows(columns):
-        return pl.BlockSpec((tile, columns), lambda i: (i, 0))
-
-    return pl.pallas_call(
-        mix_kernel,
-        grid=(tokens // tile,),
-        out_shape=jax.ShapeDtypeStruct((tokens, width), BF16),
-        in_specs=[rows(width), rows(2)]
-        + [pl.BlockSpec(w.shape, lambda i: (0, 0)) for w in weights],
-        out_specs=rows(width),
-        compiler_params=pltpu.CompilerParams(vmem_limit_bytes=50 << 20),
-        name="mix",
-    )(x, share, *weights)
-
-
-def mix_back_kernel(x_ref, d_ref, share_ref, balance_ref, router_ref, *refs):
-    weights = refs[:6]
-    out_ref, logit_ref = refs[6:8]
-    grads = refs[8:]
-    x, d = x_ref[...], d_ref[...]
-    out = None
-    for e in range(2):
-        gate_w, up_w, down_w = weights[3 * e : 3 * e + 3]
-        share = share_ref[:, e : e + 1]
-        act_gate, act_up = dot(x, gate_w[...]), dot(x, up_w[...])
-        sig = jax.nn.sigmoid(act_gate)
-        swish = act_gate * sig
-        hidden = swish * act_up
-        raw = dot(d, down_w[...], NT)
-        d_logit = share * (jnp.sum(hidden * raw, -1, keepdims=True) - balance_ref[...])
-        d_hidden = raw * share
-        d_gate = (d_hidden * act_up * sig * (1.0 + act_gate * (1.0 - sig))).astype(BF16)
-        d_up = (d_hidden * swish).astype(BF16)
-        grads[3 * e][...] = d_gate
-        grads[3 * e + 1][...] = d_up
-        grads[3 * e + 2][...] = (hidden * share).astype(BF16)
-        logit_ref[:, e : e + 1] = d_logit
-        part = dot(d_gate, gate_w[...], NT) + dot(d_up, up_w[...], NT)
-        part = part + d_logit * router_ref[e : e + 1, :]
-        out = part if out is None else out + part
-    out_ref[...] = out.astype(BF16)
-
-
-def mix_back(x, d, share, balance, router, weights):
-    tokens, width = x.shape
-    ff = weights[0].shape[1]
-    tile = 2 * LANES
-
-    def rows(columns):
-        return pl.BlockSpec((tile, columns), lambda i: (i, 0))
-
-    return pl.pallas_call(
-        mix_back_kernel,
-        grid=(tokens // tile,),
-        out_shape=(
-            jax.ShapeDtypeStruct((tokens, width), BF16),
-            jax.ShapeDtypeStruct((tokens, 2), F32),
-        ) + (jax.ShapeDtypeStruct((tokens, ff), BF16),) * 6,
-        in_specs=[rows(width), rows(width), rows(2), rows(1), pl.BlockSpec(router.shape, lambda i: (0, 0))]
-        + [pl.BlockSpec(w.shape, lambda i: (0, 0)) for w in weights],
-        out_specs=[rows(width), rows(2)] + [rows(ff)] * 6,
-        compiler_params=pltpu.CompilerParams(vmem_limit_bytes=56 << 20),
-        name="mix_back",
-    )(x, d, share, balance, router, *weights)
+    )(info, q, own, other, begin, att, lse, datt, cosine, sine)
 
 
 def add_kernel(layers, *refs):
@@ -909,8 +1403,8 @@
     gains_one, gains_two = smalls[:LAYERS], smalls[LAYERS : 2 * LAYERS]
     routers = smalls[2 * LAYERS :].reshape(LAYERS, experts, width)
     tables = tables.transpose(0, 2, 1).reshape(count * rows, HD)
-    cosine = jnp.concatenate([tables[:, : HD // 2]] * 4, 1)
-    sine = jnp.concatenate([tables[:, HD // 2 :]] * 4, 1)
+    cosine = jnp.concatenate([tables[:, : HD // 2]] * 4, 1).reshape(count, rows, LANES)
+    sine = jnp.concatenate([tables[:, HD // 2 :]] * 4, 1).reshape(count, rows, LANES)
     experts_w = []
     for layer in range(LAYERS):
         own = [w_gate[layer, 0], w_up[layer, 0], w_down[layer, 0]]
@@ -935,11 +1429,7 @@
     for layer in range(LAYERS):
         inverse_one, normed_one = normal(hidden)
         x_attn = (normed_one * gains_one[layer][None, :]).astype(BF16)
-        (x_all,) = ring_gather(count, [x_attn])
-        x_all = x_all.reshape(count * rows, width)
-        query, kv = project(x_all, w_heads[layer], cosine, sine)
-        kv = kv.reshape(count, rows, LANES)
-        kv_other = swap(kv)
+        query, kv, kv_other, x_all = gather_project(count, x_attn, w_heads[layer], cosine, sine)
         att, lse, partial = attend(info, query, kv, kv_other, begin, w_outs[layer])
         (added,) = ring_scatter(count, partial)
         middle = hidden + added
@@ -950,16 +1440,10 @@
             jnp.arange(experts, dtype=jnp.int32)[:, None, None] == routes[layer].T[None, :, :], 1
         )
         share = jax.nn.softmax(jnp.where(named, logits, -jnp.inf), axis=0)
-        m_all, share_all = ring_gather(count, [x_moe, share])
-        m_all = m_all.reshape(count * rows, width)
-        share = jnp.stack(
-            [lax.dynamic_index_in_dim(share_all, e, 1, False).reshape(-1) for e in mine], 1
-        )
-        partial = mix(m_all, share, experts_w[layer])
-        (mixed,) = ring_scatter(count, partial.reshape(count, rows, width))
+        mixed, m_all, share_all = gather_mix_scatter(count, x_moe, share, experts_w[layer])
         saved.append(
             (inverse_one, normed_one, x_all, query, kv, kv_other, att, lse)
-            + (inverse_two, normed_two, m_all, share, mixed)
+            + (inverse_two, normed_two, m_all, share_all, mixed)
         )
         hidden = middle + mixed
     activations = hidden.astype(BF16)
@@ -970,76 +1454,47 @@
     peer_sums = [[None] * 4 for _ in range(LAYERS)]
     heads_sums = [None] * LAYERS
 
-    def send(kernel, argument, rides=()):
+    def send(kernel, *arguments, most=1):
         taken = []
-        while replicas == 2 and waiting and (not taken or taken[-1][1] == 3):
+        while replicas == 2 and waiting and len(taken) < most:
             taken.append(waiting.pop(0))
-        rides = list(rides)
-        more = [(own_sums[layer][index], "rep") for layer, index in taken]
-        results = kernel(count, argument, rides + more)
+        rides = [(own_sums[layer][index], "rep") for layer, index in taken]
+        results = kernel(count, *arguments, rides)
         for place, (layer, index) in enumerate(taken):
             peer_sums[layer][index] = results[len(results) - len(taken) + place]
         return results[: len(results) - len(taken)]
 
-    def core_sum(own, got):
-        return (own + got.astype(F32)).astype(BF16)
-
     for layer in reversed(range(LAYERS)):
         (inverse_one, normed_one, x_all, query, kv, kv_other, att, lse) = saved[layer][:8]
-        (inverse_two, normed_two, m_all, share, mixed) = saved[layer][8:]
+        (inverse_two, normed_two, m_all, share_all, mixed) = saved[layer][8:]
         d_mix = grad.astype(BF16)
         balance = jnp.sum(mixed * d_mix.astype(F32), -1)
-        side = jnp.broadcast_to(balance[None, :], (experts, rows))
-        d_all, balance = send(ring_gather, [d_mix, side])
-        d_all = d_all.reshape(count * rows, width)
-        balance = balance[:, 0, :].reshape(-1, 1)
+        side = jnp.broadcast_to(balance[None, :], (8, rows))
         router_mine = jnp.concatenate(
             [lax.dynamic_slice_in_dim(routers[layer], e, 1, 0) for e in mine], 0
         )
-        partial, d_logit, *d_acts = mix_back(
-            m_all, d_all, share, balance, router_mine, experts_w[layer]
+        d_x, *expert_grads, g_router = send(
+            gather_mix_back_scatter, d_mix, side, m_all, share_all, router_mine, experts_w[layer],
+            most=2,
         )
-        expert_grads = [
-            [
-                dot(m_all, d_acts[3 * e], TN),
-                dot(m_all, d_acts[3 * e + 1], TN),
-                dot(d_acts[3 * e + 2], d_all, TN),
-            ]
-            for e in range(2)
-        ]
-        g_router = jnp.dot(d_logit.T, m_all.astype(F32), precision=lax.Precision.HIGHEST)
-        theirs = [g.astype(BF16) for g in expert_grads[1]]
-        d_x, *got = send(
-            ring_scatter, partial.reshape(count, rows, width), [(g, "fsdp") for g in theirs]
-        )
-        for index in range(3):
-            own_sums[layer][index] = core_sum(expert_grads[0][index], got[index])
-            waiting.append((layer, index))
+        own_sums[layer][:3] = expert_grads
+        waiting.extend((layer, index) for index in range(3))
         gain = gains_two[layer][None, :]
         d_norm = d_x * gain
         d_gain_two = jnp.sum(d_x * normed_two, 0)
         grad_mid = grad + inverse_two * (
             d_norm - normed_two * jnp.mean(d_norm * normed_two, -1, keepdims=True)
         )
-        (b_all,) = send(ring_gather, [grad_mid.astype(BF16)])
+        datt, own_sums[layer][3] = send(
+            gather_branch_back, grad_mid.astype(BF16), w_outs[layer], att
+        )
         d_query, d_own, d_other = attend_back(
-            info, query, kv, kv_other, begin, w_outs[layer], att, lse, b_all,
-            cosine.reshape(count, rows, LANES), sine.reshape(count, rows, LANES),
+            info, query, kv, kv_other, begin, att, lse, datt, cosine, sine
         )
-        g_out = dot(att.reshape(count * rows, 2 * LANES), b_all.reshape(count * rows, width), TN)
-        g_out = g_out[: 2 * shard].reshape(2, shard, width)
-        g_out_own = lax.dynamic_index_in_dim(g_out, core, 0, False)
-        g_out_other = lax.dynamic_index_in_dim(g_out, 1 - core, 0, False)
-        d_got = swap(d_other.astype(BF16))
-        partial, g_heads = join(
-            d_query.reshape(count * rows, 2 * LANES),
-            d_own.reshape(count * rows, LANES),
-            d_got.reshape(count * rows, LANES),
-            cosine, sine, w_heads[layer], x_all,
+        d_x, g_heads = send(
+            join_scatter, d_query, d_own, d_other, cosine, sine, w_heads[layer], x_all
         )
-        own_sums[layer][3] = core_sum(g_out_own, swap(g_out_other.astype(BF16)))
         waiting.append((layer, 3))
-        (d_x,) = send(ring_scatter, partial.reshape(count, rows, width))
         gain = gains_one[layer][None, :]
         d_norm = d_x * gain
         d_gain_one = jnp.sum(d_x * normed_one, 0)
@@ -1059,18 +1514,28 @@
         if replicas == 2:
             peer_sums[layer][index] = lax.ppermute(own_sums[layer][index], "rep", [(0, 1), (1, 0)])
     if replicas == 2:
-        g_gate, g_up, g_down, g_out = [
+        g_gate, g_up = add_wide(
+            [
+                (own_sums[layer][index], peer_sums[layer][index])
+                for layer in range(LAYERS)
+                for index in range(2)
+            ]
+        )
+        g_down, g_out = [
             add_layers([(own_sums[layer][index], peer_sums[layer][index]) for layer in range(LAYERS)])
-            for index in range(4)
+            for index in (2, 3)
         ]
     else:
         total = lax.psum(total.astype(BF16), "rep").astype(F32)
-        g_gate, g_up, g_down, g_out = [
+        summed = [
             jnp.stack(
                 [lax.psum(own_sums[layer][index], "rep").astype(F32) for layer in range(LAYERS)]
             )[:, None]
             for index in range(4)
         ]
+        wide = jnp.concatenate(summed[:2], 2)
+        ff = w_gate.shape[3]
+        g_gate, g_up, g_down, g_out = wide[..., :ff], wide[..., ff:], summed[2], summed[3]
     total = total.transpose(1, 2, 0, 3)
 
     def part(first, last):

time: 1060 us -> 930 us (0.88)
  Pallas kernels: 867 us -> 809 us
  matrix products: 51.5 us -> 1.42 us
  local copies, waits for them, and re-layouts: 96.4 us -> 75.8 us
    pallas_call x8 -> x2, Pallas kernels: 281 us -> 61.1 us  [ring_scatter(): pl.pallas_call(functools.partial(scatter_kernel, count, axes), out_shape=...]
    pallas_call x16 -> x11, Pallas kernels: 385 us -> 549 us  [the longest x10 540 us: ring_call(): pl.pallas_call(functools.partial(body, axes), out_shape=tuple((shape for...]
    dot_general x16 -> x2, matrix products: 47.7 us -> 1.42 us  [dot(): lax.dot_general(left, right, (contract, ((), ())), preferred_element_type...]
    pallas_call x1, Pallas kernels: 41.4 us -> 58.4 us  [finish_heads(): pl.pallas_call(functools.partial(finish_kernel, count, replicas), out_sha...]
    pallas_call x4 -> x2, Pallas kernels: 21.5 us -> 9.42 us  [add_layers(): pl.pallas_call(functools.partial(add_kernel, layers), grid=(4,), out_shap...]
    unnamed x220 -> x162, local copies, waits for them, and re-layouts: 37.6 us -> 34.2 us
  transfers between devices with their start and end apart: 14 -> 8, of which waited for: 1 -> 0; matrix products, arithmetic and copies ran while one was open for 10% -> 6% of each run, Pallas kernels for 45% -> 40%
where the time goes in v3:
time: 930 us; the launch traced here: 919 us
  Pallas kernels  809 us (87%)
  local copies, waits for them, and re-layouts  75.8 us (8%)
  other arithmetic  27.4 us (3%)
    pallas_call x10, Pallas kernels, ring_call(): pl.pallas_call(functools.partial(body, axes), out_shape=tuple((shape for...  540 us
    pallas_call x2, Pallas kernels, ring_scatter(): pl.pallas_call(functools.partial(scatter_kernel, count, axes), out_shape=...  61.1 us
    pallas_call x1, Pallas kernels, finish_heads(): pl.pallas_call(functools.partial(finish_kernel, count, replicas), out_sha...  58.4 us
    pallas_call x2, Pallas kernels, attend_back(): pl.pallas_call(attend_back_kernel, grid_spec=pltpu.PrefetchScalarGridSpec...  52.5 us
    pallas_call x2, Pallas kernels, attend(): pl.pallas_call(attend_kernel, grid_spec=pltpu.PrefetchScalarGridSpec(num_...  43.5 us
    pallas_call x1, Pallas kernels, exchange_weights(): pl.pallas_call(functools.partial(setup_kernel, count), out_shape=(jax.Sha...  34.7 us
    unnamed x162, local copies, waits for them, and re-layouts  34.2 us
  transfers between devices with their start and end apart: 8, of which 0 were waited for; matrix products, arithmetic and copies ran while one was open for 6% of the time, Pallas kernels for 40%

profile of v3, /device:TPU:0, one launch (start us, length us, event | category | flops | bytes accessed | tf_op | source)
XLA Modules:
  0.0 918.5 jit_solution(10671961255772007182)
XLA Ops:
  0.7 3.9 slice_bitcast_fusion.2
  5.0 1.9 slice_bitcast_fusion.1
  8.1 1.8 slice_bitcast_fusion
  13.6 1.5 maximum_bitcast_fusion.1.slab_ref
  15.1 34.7 %exchange_weights.1 = (bf16[2,16,96,384]{3,2,1,0:T(8,128)(2,1)}, bf16[2,2,96,1536]{3,2,1,0:T(8,128)(2,1)}, bf16[16,48,128]{2,1,0:T(8,128)(2,1)}, f32[8,64,128]{2,1,0:T(8,128)}) custom-call(bf16[8,2,96,384]{3,2,1,0:T(8,128)(2,1)} %maximum_bitcast_fusion.1.slab_ref, bf16[2,96,1536]{2,1,0:T(8,128)(2,1)} %out_w_ref.1, bf16[48,128]{1,0:T(8,128)(2,1)} %fusion.24.small_ref, ...), custom_call_target="tpu_custom_call" | custom-call | tf_op jit(solution)/shard_map/exchange_weights/pallas_call | solution.py:493
  52.8 1.9 fusion.33
  55.9 1.4 copy.169
  58.3 2.4 fusion.34
  61.5 47.0 %project.2 = (bf16[8,3,128,128]{3,2,1,0:T(8,128)(2,1)S(1)}, bf16[8,128,128]{2,1,0:T(8,128)(2,1)S(1)}, bf16[8,128,128]{2,1,0:T(8,128)(2,1)S(1)}, bf16[8,128,1536]{2,1,0:T(8,128)(2,1)S(1)}) custom-call(bf16[128,1536]{1,0:T(8,128)(2,1)S(1)} %fusion.5.refs_0_, bf16[1536,384]{1,0:T(8,128)(2,1)S(1)} %bitcast.88, f32[8,128,128]{2,1,0:T(8,128)S(1)} %bitcast.73, ...), custom_call_target="tpu_custom_call" | custom-call | tf_op jit(solution)/shard_map/project/pallas_call | solution.py:291
  108.5 1.7 copy-done.10
  112.5 21.5 %attend.2 = (bf16[8,128,256]{2,1,0:T(8,128)(2,1)}, f32[8,384,1]{2,1,0:T(8,128)}, bf16[8,128,1536]{2,1,0:T(8,128)(2,1)}) custom-call(s32[9]{0:T(128)} %pad_add_fusion.info_ref, bf16[8,3,128,128]{3,2,1,0:T(8,128)(2,1)} %copy-done.14, bf16[8,128,128]{2,1,0:T(8,128)(2,1)} %copy-done.23, bf16[8,128,128]{2,1,0:T(8,128)(2,1)} %copy-done.24, ...), custom_call_target="tpu_custom_call" | custom-call | tf_op jit(solution)/shard_map/attend/pallas_call | solution.py:1211
  133.9 1.9 copy-done.12
  135.8 30.7 %ring_scatter.2 = f32[128,1536]{1,0:T(8,128)S(1)} custom-call(bf16[8,128,1536]{2,1,0:T(8,128)(2,1)S(1)} %copy-done.12), custom_call_target="tpu_custom_call" | custom-call | tf_op jit(solution)/shard_map/ring_scatter/pallas_call | solution.py:383
  174.2 1.4 fusion.12
  180.9 76.6 %mix.2 = (f32[128,1536]{1,0:T(8,128)}, bf16[8,128,1536]{2,1,0:T(8,128)(2,1)}, f32[8,16,128]{2,1,0:T(8,128)}) custom-call(bf16[128,1536]{1,0:T(8,128)(2,1)} %copy-done.52, f32[16,128]{1,0:T(8,128)} %fusion.25.refs_1_, bf16[1536,512]{1,0:T(8,128)(2,1)} %get-tuple-element.238.refs_2_.refs_5_, bf16[1536,512]{1,0:T(8,128)(2,1)} %get-tuple-element.236.refs_3_.refs_6_, ...), custom_call_target="tpu_custom_call" | custom-call | tf_op jit(solution)/shard_map/mix/pallas_call | solution.py:291
  257.6 1.3 multiply_reduce_fusion.8
  259.8 34.8 %project.3 = (bf16[8,3,128,128]{3,2,1,0:T(8,128)(2,1)S(1)}, bf16[8,128,128]{2,1,0:T(8,128)(2,1)S(1)}, bf16[8,128,128]{2,1,0:T(8,128)(2,1)S(1)}, bf16[8,128,1536]{2,1,0:T(8,128)(2,1)S(1)}) custom-call(bf16[128,1536]{1,0:T(8,128)(2,1)S(1)} %multiply_convert_fusion.1.refs_0_, bf16[1536,384]{1,0:T(8,128)(2,1)S(1)} %bitcast.90, f32[8,128,128]{2,1,0:T(8,128)S(1)} %bitcast.74, ...), custom_call_target="tpu_custom_call" | custom-call | tf_op jit(solution)/shard_map/project/pallas_call | solution.py:291
  294.6 1.7 copy-done.11
  298.5 22.0 %attend.3 = (bf16[8,128,256]{2,1,0:T(8,128)(2,1)}, f32[8,384,1]{2,1,0:T(8,128)}, bf16[8,128,1536]{2,1,0:T(8,128)(2,1)}) custom-call(s32[9]{0:T(128)} %pad_add_fusion.info_ref, bf16[8,3,128,128]{3,2,1,0:T(8,128)(2,1)} %copy-done.15, bf16[8,128,128]{2,1,0:T(8,128)(2,1)} %copy-done.25, bf16[8,128,128]{2,1,0:T(8,128)(2,1)} %copy-done.26, ...), custom_call_target="tpu_custom_call" | custom-call | tf_op jit(solution)/shard_map/attend/pallas_call | solution.py:1211
  320.5 1.9 copy-done.13
  322.4 30.3 %ring_scatter.3 = f32[128,1536]{1,0:T(8,128)S(1)} custom-call(bf16[8,128,1536]{2,1,0:T(8,128)(2,1)S(1)} %copy-done.13), custom_call_target="tpu_custom_call" | custom-call | tf_op jit(solution)/shard_map/ring_scatter/pallas_call | solution.py:383
  354.4 66.9 %mix.3 = (f32[128,1536]{1,0:T(8,128)}, bf16[8,128,1536]{2,1,0:T(8,128)(2,1)}, f32[8,16,128]{2,1,0:T(8,128)}) custom-call(bf16[128,1536]{1,0:T(8,128)(2,1)} %copy-done.53, f32[16,128]{1,0:T(8,128)} %fusion.27.refs_1_, bf16[1536,512]{1,0:T(8,128)(2,1)} %get-tuple-element.237.refs_2_.refs_5_, bf16[1536,512]{1,0:T(8,128)(2,1)} %get-tuple-element.235.refs_3_.refs_6_, ...), custom_call_target="tpu_custom_call" | custom-call | tf_op jit(solution)/shard_map/mix/pallas_call | solution.py:291
  423.1 81.7 %mix_back.2 = (f32[128,1536]{1,0:T(8,128)}, bf16[768,1024]{1,0:T(8,128)(2,1)}, bf16[768,1024]{1,0:T(8,128)(2,1)}, bf16[512,1536]{1,0:T(8,128)(2,1)}, f32[2,1536]{1,0:T(2,128)}) custom-call(bf16[128,1536]{1,0:T(8,128)(2,1)} %refs_0_, f32[8,128]{1,0:T(8,128)} %broadcast_in_dim.80.refs_1_, bf16[8,128,1536]{2,1,0:T(8,128)(2,1)} %get-tuple-element.82.refs_2_, ...), custom_call_target="tpu_custom_call" | custom-call | tf_op jit(solution)/shard_map/mix_back/pallas_call | solution.py:291
  504.9 1.5 multiply_reduce_fusion
  508.0 36.9 %branch_back.2 = (bf16[8,128,256]{2,1,0:T(8,128)(2,1)S(1)}, bf16[96,1536]{1,0:T(8,128)(2,1)S(1)}, bf16[768,1024]{1,0:T(8,128)(2,1)S(1)}) custom-call(bf16[128,1536]{1,0:T(8,128)(2,1)S(1)} %fusion.29.refs_0_, bf16[192,1536]{1,0:T(8,128)(2,1)S(1)} %bitcast.95, bf16[8,128,256]{2,1,0:T(8,128)(2,1)S(1)} %copy-done.17, bf16[768,1024]{1,0:T(8,128)(2,1)S(1)} %copy-done.6), custom_call_target="tpu_custom_call" | custom-call | tf_op jit(solution)/shard_map/branch_back/pallas_call | solution.py:291
  547.6 26.2 %attend_back.2 = (bf16[8,128,256]{2,1,0:T(8,128)(2,1)}, f32[8,128,128]{2,1,0:T(8,128)}, bf16[8,128,128]{2,1,0:T(8,128)(2,1)}) custom-call(s32[9]{0:T(128)} %pad_add_fusion.info_ref, bf16[8,3,128,128]{3,2,1,0:T(8,128)(2,1)} %copy-done.15, bf16[8,128,128]{2,1,0:T(8,128)(2,1)} %copy-done.25, bf16[8,128,128]{2,1,0:T(8,128)(2,1)} %copy-done.26, ...), custom_call_target="tpu_custom_call" | custom-call | tf_op jit(solution)/shard_map/attend_back/pallas_call | solution.py:1299
  576.9 38.8 %join.2 = (f32[128,1536]{1,0:T(8,128)S(1)}, f32[1536,384]{1,0:T(8,128)}, bf16[768,1024]{1,0:T(8,128)(2,1)S(1)}) custom-call(bf16[8,128,256]{2,1,0:T(8,128)(2,1)S(1)} %copy-done.29, f32[8,128,128]{2,1,0:T(8,128)S(1)} %copy-done.30, bf16[8,128,128]{2,1,0:T(8,128)(2,1)S(1)} %copy-done.35, f32[8,128,128]{2,1,0:T(8,128)S(1)} %bitcast.77, ...), custom_call_target="tpu_custom_call" | custom-call | tf_op jit(solution)/shard_map/join/pallas_call | solution.py:291
  616.0 1.3 copy-done.40
  617.6 1.4 multiply_reduce_fusion.4
  619.6 82.1 %mix_back.3 = (f32[128,1536]{1,0:T(8,128)}, bf16[768,1024]{1,0:T(8,128)(2,1)}, bf16[768,1024]{1,0:T(8,128)(2,1)}, bf16[512,1536]{1,0:T(8,128)(2,1)}, f32[2,1536]...) custom-call(bf16[128,1536]{1,0:T(8,128)(2,1)} %get-tuple-element.225.refs_0_, ...), custom_call_target="tpu_custom_call" | custom-call | tf_op jit(solution)/shard_map/mix_back/pallas_call | solution.py:291
  701.7 1.5 multiply_reduce_fusion.2
  705.2 36.4 %branch_back.3 = (bf16[8,128,256]{2,1,0:T(8,128)(2,1)S(1)}, bf16[96,1536]{1,0:T(8,128)(2,1)S(1)}, bf16[768,1024]{1,0:T(8,128)(2,1)S(1)}) custom-call(bf16[128,1536]{1,0:T(8,128)(2,1)S(1)} %get-tuple-element.222.refs_0_, bf16[192,1536]{1,0:T(8,128)(2,1)S(1)} %bitcast.93, bf16[8,128,256]{2,1,0:T(8,128)(2,1)S(1)} %copy-done.16, bf16[768,1024]{1,0:T(8,128)(2,1)S(1)} %copy-done.7), custom_call_target="tpu_custom_call" | custom-call | tf_op jit(solution)/shard_map/branch_back/pallas_call | solution.py:291
  743.6 26.2 %attend_back.3 = (bf16[8,128,256]{2,1,0:T(8,128)(2,1)}, f32[8,128,128]{2,1,0:T(8,128)}, bf16[8,128,128]{2,1,0:T(8,128)(2,1)}) custom-call(s32[9]{0:T(128)} %pad_add_fusion.info_ref, bf16[8,3,128,128]{3,2,1,0:T(8,128)(2,1)} %copy-done.14, bf16[8,128,128]{2,1,0:T(8,128)(2,1)} %copy-done.23, bf16[8,128,128]{2,1,0:T(8,128)(2,1)} %copy-done.24, ...), custom_call_target="tpu_custom_call" | custom-call | tf_op jit(solution)/shard_map/attend_back/pallas_call | solution.py:1299
  772.9 38.8 %join.3 = (f32[128,1536]{1,0:T(8,128)S(1)}, f32[1536,384]{1,0:T(8,128)}, bf16[768,1024]{1,0:T(8,128)(2,1)S(1)}) custom-call(bf16[8,128,256]{2,1,0:T(8,128)(2,1)S(1)} %copy-done.27, f32[8,128,128]{2,1,0:T(8,128)S(1)} %copy-done.28, bf16[8,128,128]{2,1,0:T(8,128)(2,1)S(1)} %copy-done.34, f32[8,128,128]{2,1,0:T(8,128)S(1)} %bitcast.78, ...), custom_call_target="tpu_custom_call" | custom-call | tf_op jit(solution)/shard_map/join/pallas_call | solution.py:291
  814.8 1.9 slice.196
  818.5 2.4 maximum_bitcast_fusion.g_ref
  820.9 58.4 %finish_heads.1 = f32[8,2,96,384]{3,2,1,0:T(8,128)S(1)} custom-call(bf16[2,8,2,96,384]{4,3,2,1,0:T(8,128)(2,1)S(1)} %maximum_bitcast_fusion.g_ref), custom_call_target="tpu_custom_call" | custom-call | tf_op jit(solution)/shard_map/finish_heads/pallas_call | solution.py:581
  879.4 2.1 copy.180
  881.5 2.7 reshape.236
  884.2 1.4 fusion.32
  885.6 2.2 copy.181
  887.8 2.0 copy.184
  889.7 2.2 copy.182
  891.9 2.0 copy.185
  895.0 2.4 fusion.9
  898.8 9.4 %add_wide.1 = (f32[2,1,2,768,512]{4,3,2,1,0:T(8,128)}, f32[2,1,2,768,512]{4,3,2,1,0:T(8,128)}) custom-call(bf16[768,1024]{1,0:T(8,128)(2,1)} %get-tuple-element.102.refs_3_.refs_0_, bf16[768,1024]{1,0:T(8,128)(2,1)} %copy-done.20, bf16[768,1024]{1,0:T(8,128)(2,1)} %get-tuple-element.108.refs_7_.refs_2_, bf16[768,1024]{1,0:T(8,128)(2,1)} %copy-done.21, ...), custom_call_target="tpu_custom_call" | custom-call | tf_op jit(solution)/shard_map/add_wide/pallas_call | solution.py:1138
  908.9 3.5 add_layers.2
  912.4 5.9 add_layers.3
  (255 shorter events, 56.3 us)
Async XLA Ops:
  0.6 4.4 copy-start.55
  4.6 176.3 %collective-permute-start = (bf16[1536,512]{1,0:T(8,128)(2,1)}, bf16[1536,512]{1,0:T(8,128)(2,1)}, u32[]{:S(2)}, u32[]{:S(2)}) collective-permute-start(bf16[1536,512]{1,0:T(8,128)(2,1)} %get-tuple-element.238.refs_2_.refs_5_), channel_id=1, source_target_pairs={{0,1},{1,0},{2,3},{3,2},{4,5},{5,4},{6,7},{7,6},{8,9},{9,8},{10,11... | collective-permute-start | bytes 4718600 | tf_op jit(solution)/shard_map/ppermute | solution.py:1379
  5.0 3.0 copy-start.56
  6.9 3.6 copy-start.63
  6.9 4.0 copy-start.64
  6.9 174.0 %collective-permute-start.1 = (bf16[1536,512]{1,0:T(8,128)(2,1)}, bf16[1536,512]{1,0:T(8,128)(2,1)}, u32[]{:S(2)}, u32[]{:S(2)}) collective-permute-start(bf16[1536,512]{1,0:T(8,128)(2,1)} %get-tuple-element.236.refs_3_.refs_6_), channel_id=1, source_target_pairs={{0,1},{1,0},{2,3},{3,2},{4,5},{5,4},{6,7},{7,6},{8,9},{9,8},{10,11... | collective-permute-start | bytes 4718600 | tf_op jit(solution)/shard_map/ppermute | solution.py:1379
  9.9 171.0 %collective-permute-start.2 = (bf16[512,1536]{1,0:T(8,128)(2,1)}, bf16[512,1536]{1,0:T(8,128)(2,1)}, u32[]{:S(2)}, u32[]{:S(2)}) collective-permute-start(bf16[512,1536]{1,0:T(8,128)(2,1)} %get-tuple-element.234.refs_4_.refs_7_), channel_id=1, source_target_pairs={{0,1},{1,0},{2,3},{3,2},{4,5},{5,4},{6,7},{7,6},{8,9},{9,8},{10,11... | collective-permute-start | bytes 4718600 | tf_op jit(solution)/shard_map/ppermute | solution.py:1379
  9.9 344.4 %collective-permute-start.3 = (bf16[1536,512]{1,0:T(8,128)(2,1)}, bf16[1536,512]{1,0:T(8,128)(2,1)}, u32[]{:S(2)}, u32[]{:S(2)}) collective-permute-start(bf16[1536,512]{1,0:T(8,128)(2,1)} %get-tuple-element.237.refs_2_.refs_5_), channel_id=1, source_target_pairs={{0,1},{1,0},{2,3},{3,2},{4,5},{5,4},{6,7},{7,6},{8,9},{9,8},{10,11... | collective-permute-start | bytes 4718600 | tf_op jit(solution)/shard_map/ppermute | solution.py:1379
  10.4 343.9 %collective-permute-start.4 = (bf16[1536,512]{1,0:T(8,128)(2,1)}, bf16[1536,512]{1,0:T(8,128)(2,1)}, u32[]{:S(2)}, u32[]{:S(2)}) collective-permute-start(bf16[1536,512]{1,0:T(8,128)(2,1)} %get-tuple-element.235.refs_3_.refs_6_), channel_id=1, source_target_pairs={{0,1},{1,0},{2,3},{3,2},{4,5},{5,4},{6,7},{7,6},{8,9},{9,8},{10,11... | collective-permute-start | bytes 4718600 | tf_op jit(solution)/shard_map/ppermute | solution.py:1379
  15.1 37.0 %copy-start.69 = (s32[1,2048]{1,0:T(1,128)S(1)}, s32[1,2048]{1,0:T(1,128)}, u32[]{:S(2)}) copy-start(s32[1,2048]{1,0:T(1,128)} %param.18) | copy-start | bytes 24580
  15.1 37.4 %copy-start.43 = (bf16[128,1536]{1,0:T(8,128)(2,1)S(1)}, bf16[128,1536]{1,0:T(8,128)(2,1)}, u32[]{:S(2)}) copy-start(bf16[128,1536]{1,0:T(8,128)(2,1)} %param.15) | copy-start | bytes 1179652
  52.7 8.6 copy-start.74
  52.8 1.9 copy-start.62
  55.8 203.9 %copy-start = (f32[1024,128]{1,0:T(8,128)}, f32[1024,128]{1,0:T(8,128)S(1)}, u32[]{:S(2)}) copy-start(f32[1024,128]{1,0:T(8,128)S(1)} %copy.168) | copy-start | bytes 1572868
  57.3 202.5 %copy-start.3 = (f32[1024,128]{1,0:T(8,128)}, f32[1024,128]{1,0:T(8,128)S(1)}, u32[]{:S(2)}) copy-start(f32[1024,128]{1,0:T(8,128)S(1)} %copy.169) | copy-start | bytes 1572868
  58.3 3.0 copy-start.44
  133.9 1.9 copy-start.12
  135.8 30.8 %copy-start.45 = (bf16[128,1536]{1,0:T(8,128)(2,1)S(1)}, bf16[128,1536]{1,0:T(8,128)(2,1)}, u32[]{:S(2)}) copy-start(bf16[128,1536]{1,0:T(8,128)(2,1)} %param.15) | copy-start | bytes 1179652
  166.6 2.2 copy-start.72
  174.2 3.9 copy-start.61
  176.9 4.1 copy-start.52
  180.9 76.7 %copy-start.41 = (f32[128,1536]{1,0:T(8,128)S(1)}, f32[128,1536]{1,0:T(8,128)}, u32[]{:S(2)}) copy-start(f32[128,1536]{1,0:T(8,128)} %get-tuple-element.232) | copy-start | bytes 2359300
  180.9 173.4 %collective-permute-start.5 = (bf16[512,1536]{1,0:T(8,128)(2,1)}, bf16[512,1536]{1,0:T(8,128)(2,1)}, u32[]{:S(2)}, u32[]{:S(2)}) collective-permute-start(bf16[512,1536]{1,0:T(8,128)(2,1)} %get-tuple-element.233.refs_4_.refs_7_), channel_id=1, source_target_pairs={{0,1},{1,0},{2,3},{3,2},{4,5},{5,4},{6,7},{7,6},{8,9},{9,8},{10,11... | collective-permute-start | bytes 4718600 | tf_op jit(solution)/shard_map/ppermute | solution.py:1379
  320.5 1.9 copy-start.13
  322.4 30.3 %copy-start.37 = (f32[128,1536]{1,0:T(8,128)S(1)}, f32[128,1536]{1,0:T(8,128)}, u32[]{:S(2)}) copy-start(f32[128,1536]{1,0:T(8,128)} %copy-done.36) | copy-start | bytes 2359300
  353.0 153.5 %copy-start.39 = (f32[128,1536]{1,0:T(8,128)}, f32[128,1536]{1,0:T(8,128)S(1)}, u32[]{:S(2)}) copy-start(f32[128,1536]{1,0:T(8,128)S(1)} %get-tuple-element.228) | copy-start | bytes 2359300
  354.3 66.9 %copy-start.49 = (bf16[128,1536]{1,0:T(8,128)(2,1)S(1)}, bf16[128,1536]{1,0:T(8,128)(2,1)}, u32[]{:S(2)}) copy-start(bf16[128,1536]{1,0:T(8,128)(2,1)} %refs_0_) | copy-start | bytes 1179652
  547.6 26.2 %copy-start.1 = (f32[1024,128]{1,0:T(8,128)S(1)}, f32[1024,128]{1,0:T(8,128)}, u32[]{:S(2)}) copy-start(f32[1024,128]{1,0:T(8,128)} %copy-done) | copy-start | bytes 1572868
  547.6 26.2 %copy-start.4 = (f32[1024,128]{1,0:T(8,128)S(1)}, f32[1024,128]{1,0:T(8,128)}, u32[]{:S(2)}) copy-start(f32[1024,128]{1,0:T(8,128)} %copy-done.3) | copy-start | bytes 1572868
  576.8 38.9 %copy-start.38 = (f32[128,1536]{1,0:T(8,128)S(1)}, f32[128,1536]{1,0:T(8,128)}, u32[]{:S(2)}) copy-start(f32[128,1536]{1,0:T(8,128)} %copy-done.36) | copy-start | bytes 2359300
  576.8 39.2 %copy-start.51 = (bf16[128,1536]{1,0:T(8,128)(2,1)S(1)}, bf16[128,1536]{1,0:T(8,128)(2,1)}, u32[]{:S(2)}) copy-start(bf16[128,1536]{1,0:T(8,128)(2,1)} %refs_0_) | copy-start | bytes 1179652
  576.9 39.2 %copy-start.54 = (f32[128,1536]{1,0:T(8,128)S(1)}, f32[128,1536]{1,0:T(8,128)}, u32[]{:S(2)}) copy-start(f32[128,1536]{1,0:T(8,128)} %get-tuple-element.76) | copy-start | bytes 2359300
  576.9 39.2 %copy-start.57 = (f32[128,1536]{1,0:T(8,128)S(1)}, f32[128,1536]{1,0:T(8,128)}, u32[]{:S(2)}) copy-start(f32[128,1536]{1,0:T(8,128)} %get-tuple-element.81) | copy-start | bytes 2359300
  615.7 3.3 copy-start.19
  615.7 1.9 copy-start.48
  619.6 82.1 %copy-start.42 = (f32[128,1536]{1,0:T(8,128)S(1)}, f32[128,1536]{1,0:T(8,128)}, u32[]{:S(2)}) copy-start(f32[128,1536]{1,0:T(8,128)} %get-tuple-element.232) | copy-start | bytes 2359300
  619.6 82.1 %copy-start.65 = (f32[1536]{0:T(1024)S(1)}, f32[1536]{0:T(1024)}, u32[]{:S(2)}) copy-start(f32[1536]{0:T(1024)} %mul.226) | copy-start | bytes 18436
  619.6 82.1 %copy-start.73 = (f32[128]{0:T(128)S(1)}, f32[128]{0:T(128)}, u32[]{:S(2)}) copy-start(f32[128]{0:T(128)} %add_rsqrt_fusion.2) | copy-start | bytes 1540
  703.3 2.0 copy-start.16
  743.6 150.3 %copy-start.33 = (bf16[96,1536]{1,0:T(8,128)(2,1)}, bf16[96,1536]{1,0:T(8,128)(2,1)S(1)}, u32[]{:S(2)}) copy-start(bf16[96,1536]{1,0:T(8,128)(2,1)S(1)} %get-tuple-element.114.refs_0_) | copy-start | bytes 884740
  743.6 26.2 %copy-start.2 = (f32[1024,128]{1,0:T(8,128)S(1)}, f32[1024,128]{1,0:T(8,128)}, u32[]{:S(2)}) copy-start(f32[1024,128]{1,0:T(8,128)} %copy-done) | copy-start | bytes 1572868
  743.6 26.3 %copy-start.5 = (f32[1024,128]{1,0:T(8,128)S(1)}, f32[1024,128]{1,0:T(8,128)}, u32[]{:S(2)}) copy-start(f32[1024,128]{1,0:T(8,128)} %copy-done.3) | copy-start | bytes 1572868
  772.9 40.0 %copy-start.46 = (bf16[128,1536]{1,0:T(8,128)(2,1)S(1)}, bf16[128,1536]{1,0:T(8,128)(2,1)}, u32[]{:S(2)}) copy-start(bf16[128,1536]{1,0:T(8,128)(2,1)} %param.15) | copy-start | bytes 1179652
  772.9 40.0 %copy-start.75 = (f32[128]{0:T(128)S(1)}, f32[128]{0:T(128)}, u32[]{:S(2)}) copy-start(f32[128]{0:T(128)} %copy-done.74) | copy-start | bytes 1540
  772.9 40.4 %copy-start.67 = (f32[2,1536]{1,0:T(2,128)S(1)}, f32[2,1536]{1,0:T(2,128)}, u32[]{:S(2)}) copy-start(f32[2,1536]{1,0:T(2,128)} %get-tuple-element.113) | copy-start | bytes 36868
  814.8 2.4 copy-start.59
  817.3 95.1 %collective-permute-start.7 = (bf16[512,1536]{1,0:T(8,128)(2,1)}, bf16[512,1536]{1,0:T(8,128)(2,1)}, u32[]{:S(2)}, u32[]{:S(2)}) collective-permute-start(bf16[512,1536]{1,0:T(8,128)(2,1)} %get-tuple-element.122.refs_0_), channel_id=1, source_target_pairs={{0,16},{16,0},{1,17},{17,1},{2,18},{18,2},{3,19},{19,3},{4,20},{20... | collective-permute-start | bytes 4718600 | tf_op jit(solution)/shard_map/ppermute | solution.py:1515
  893.9 15.0 %collective-permute-start.6 = (bf16[96,1536]{1,0:T(8,128)(2,1)S(1)}, bf16[96,1536]{1,0:T(8,128)(2,1)}, u32[]{:S(2)}, u32[]{:S(2)}) collective-permute-start(bf16[96,1536]{1,0:T(8,128)(2,1)S(1)} %get-tuple-element.114.refs_0_), channel_id=1, source_target_pairs={{0,16},{16,0},{1,17},{17,1},{2,18},{18,2},{3,19},{19,3},{4,20},{20... | collective-permute-start | bytes 884744 | tf_op jit(solution)/shard_map/ppermute | solution.py:1515
  (39 other events, 47.2 us)

commit v4 on v3

v4 whole, which is shorter than its diff:
```python
import functools

import jax
import jax.numpy as jnp
from jax import lax
from jax.experimental import pallas as pl
from jax.experimental.pallas import tpu as pltpu
from jax.sharding import PartitionSpec as P

HEADS = 24
KV_HEADS = 8
HD = 64
LAYERS = 2
GROUP = HEADS // KV_HEADS
LANES = 128
EPS = 1e-06
MASKED = -1e30
MESH = pl.DeviceIdType.MESH
F32 = jnp.float32
BF16 = jnp.bfloat16


def ring_place(chip, count):
    return lax.select(lax.rem(chip, 2) == 0, chip // 2, count - 1 - chip // 2)


def ring_chip(place, count):
    return lax.select(place < count // 2, 2 * place, 2 * (count - 1 - place) + 1)


def ring_setup(count):
    me = lax.axis_index("fsdp")
    chip, core = me // 2, lax.rem(me, 2)
    place = ring_place(chip, count)

    def at(offset):
        return ring_chip(lax.rem(place + offset + 2 * count, count), count)

    near = [{"fsdp": at(1) * 2 + core}, {"fsdp": at(-1) * 2 + core}]
    return chip, at, near


def partner_of(axis):
    if axis == "rep":
        return {"rep": 1 - lax.axis_index("rep")}
    me = lax.axis_index("fsdp")
    return {"fsdp": me + 1 - 2 * lax.rem(me, 2)}


def meet(others):
    barrier = pltpu.get_barrier_semaphore()
    for other in others:
        pl.semaphore_signal(barrier, inc=1, device_id=other, device_id_type=MESH)
    pl.semaphore_wait(barrier, len(others))


def remote(src, dst, send_sem, recv_sem, device):
    return pltpu.make_async_remote_copy(
        src_ref=src,
        dst_ref=dst,
        send_sem=send_sem,
        recv_sem=recv_sem,
        device_id=device,
        device_id_type=MESH,
    )


def ring_hops(count):
    half = count // 2
    return {(0, 0): half, (1, 1): half, (0, 1): half - 1, (1, 0): half - 1}


IDENTITIES = {}


def identity(key):
    return IDENTITIES.setdefault(key, len(IDENTITIES))


class Ring:
    def __init__(self, count, riders=()):
        self.count = count
        self.riders = riders
        self.steps = count // 2
        self.chip, self.at, self.near = ring_setup(count)

    def meet(self, partner=False):
        others = self.near + ([partner_of("fsdp")] if partner else [])
        meet(others + ([partner_of("rep")] if self.riders else []))
        for rider in self.riders:
            rider.start()

    def gather(self, x_ref, buf, sems, side=None, first=None, second=None):
        own_sem, send_sem, recv_sem = sems[:3]
        half_rows = x_ref.shape[0] // 2
        steps = self.steps
        own = [pltpu.make_async_copy(x_ref, buf.at[self.chip], own_sem.at[0])]
        if side is not None:
            side_ref, side_buf = side
            side_send, side_recv = sems[3:]
            own.append(pltpu.make_async_copy(side_ref, side_buf.at[self.chip], own_sem.at[1]))
        for copy in own:
            copy.start()

        def piece(key, step, block, source=None):
            direction, part = key
            rows = pl.ds(part * half_rows, half_rows)
            target = buf.at[block, rows]
            return remote(
                target if source is None else source.at[rows],
                target,
                send_sem.at[direction, part, step],
                recv_sem.at[direction, part, step],
                self.near[direction],
            )

        def side_piece(direction, step, block, source=None):
            target = side_buf.at[block]
            return remote(
                target if source is None else source,
                target,
                side_send.at[direction, step],
                side_recv.at[direction, step],
                self.near[direction],
            )

        def toward(key, places):
            return self.at(-places if key[0] == 0 else places)

        early, late = [(0, 0), (1, 1)], [(0, 1), (1, 0)]
        if side is not None:
            for direction in range(2):
                side_piece(direction, 0, self.chip, side_ref).start()
        for key in early + late:
            piece(key, 0, self.chip, x_ref).start()

        def step(s, carry):
            if side is not None:
                for direction in range(2):

                    @pl.when(s <= steps - direction)
                    def _():
                        block = toward((direction, 0), s)
                        side_piece(direction, s - 1, block).wait_recv()

                        @pl.when(s < steps - direction)
                        def _():
                            side_piece(direction, s, block).start()

            for key in early:
                block = toward(key, s)
                piece(key, s - 1, block).wait_recv()

                @pl.when(s < steps)
                def _():
                    piece(key, s, block).start()

            if first is not None:
                first(s)

            @pl.when(s < steps)
            def _():
                for key in late:
                    block = toward(key, s)
                    piece(key, s - 1, block).wait_recv()

                    @pl.when(s < steps - 1)
                    def _():
                        piece(key, s, block).start()

            if second is not None:
                second(s)
            return carry

        for copy in own:
            copy.wait()
        lax.fori_loop(1, steps + 1, step, 0)

        def drain():
            for s in range(steps):
                for key in early + (late if s < steps - 1 else []):
                    piece(key, s, toward(key, s)).wait_send()
                if side is not None:
                    for direction in range(2):
                        if s < steps - direction:
                            side_piece(direction, s, toward((direction, 0), s)).wait_send()

        return drain

    def pair(self, s):
        return self.at(s), self.at(-s)

    def meanwhile(self, compute, place):
        def run(s):
            @pl.when(s == 1)
            def _():
                compute(place, (self.chip,))

            @pl.when(s > 1)
            def _():
                compute(place, self.pair(s - 1))

        return run

    def scatter(self, partial, land, sems, work=None, source=None, ready=None):
        send_sem, recv_sem = sems
        source = partial if source is None else source
        half_rows = partial.shape[1] // 2
        steps = self.steps
        hops = ring_hops(self.count)

        def ahead(key, s):
            places = hops[key] - s
            return self.at(places if key[0] == 0 else -places)

        def piece(key, s, source):
            direction, part = key
            return remote(
                source,
                land.at[direction, part, s],
                send_sem.at[direction, part, s],
                recv_sem.at[direction, part, s],
                self.near[direction],
            )

        def rows_of(key):
            return pl.ds(key[1] * half_rows, half_rows)

        for key in hops:
            piece(key, 0, source.at[ahead(key, 0), rows_of(key)]).start()
        if ready is not None:
            ready()

        def step(s, carry):
            for place, key in enumerate(hops):
                if work is not None:
                    work(s - 1, place)

                @pl.when(s < hops[key])
                def _():
                    slot = land.at[key[0], key[1], s - 1]
                    piece(key, s - 1, slot).wait_recv()
                    mine = partial[ahead(key, s), rows_of(key)]
                    slot[...] = (slot[...].astype(F32) + mine.astype(F32)).astype(BF16)
                    piece(key, s, slot).start()

            return carry

        lax.fori_loop(1, steps + 1, step, 0)
        for key in hops:
            slot = land.at[key[0], key[1], hops[key] - 1]
            piece(key, hops[key] - 1, slot).wait_recv()
        halves = []
        for part in range(2):
            rows = pl.ds(part * half_rows, half_rows)
            total = partial[self.chip, rows].astype(F32)
            for direction in range(2):
                total = total + land[direction, part, hops[direction, part] - 1].astype(F32)
            halves.append(total)
        summed = jnp.concatenate(halves, 0)

        def drain():
            for key in hops:
                for s in range(hops[key]):
                    piece(key, s, land.at[key[0], key[1], s]).wait_send()

        return summed, drain


def dmas(*shapes):
    return [pltpu.SemaphoreType.DMA(shape) for shape in shapes]


def gather_sems(count, sided=False):
    steps = count // 2
    shapes = [(2,), (2, 2, steps), (2, 2, steps)]
    return dmas(*(shapes + ([(2, steps), (2, steps)] if sided else [])))


def scatter_sems(count):
    return dmas((2, 2, count // 2), (2, 2, count // 2))


ANYWHERE = pl.BlockSpec(memory_space=pl.ANY)
HERE = pl.BlockSpec(memory_space=pltpu.VMEM)


FREE = pl.CostEstimate(flops=0, bytes_accessed=0, transcendentals=0)


def ring_call(body, key, inputs, outputs, scratch, megabytes, rides=()):
    n_in, n_out, n_rides = len(inputs), len(outputs), len(rides)

    def kernel(*refs):
        ins, ride_in, outs, ride_out, rest = split(refs, n_in, n_rides, n_out, n_rides)
        riders = []
        if n_rides:
            *rest, send_sem, recv_sem = rest
            riders = [
                remote(ride_in[i], ride_out[i], send_sem.at[i], recv_sem.at[i], partner_of("rep"))
                for i in range(n_rides)
            ]
        body(riders, *ins, *outs, *rest)
        for rider in riders:
            rider.wait()

    return pl.pallas_call(
        kernel,
        out_shape=tuple(shape for shape, _ in outputs) + tuple(cells(a.shape, a.dtype) for a in rides),
        in_specs=[spec for _, spec in inputs] + [ANYWHERE] * n_rides,
        out_specs=[spec for _, spec in outputs] + [ANYWHERE] * n_rides,
        scratch_shapes=list(scratch) + (dmas((n_rides,), (n_rides,)) if n_rides else []),
        compiler_params=pltpu.CompilerParams(
            collective_id=identity(key),
            has_side_effects=True,
            vmem_limit_bytes=megabytes << 20,
        ),
        cost_estimate=FREE,
        name=key[0],
    )(*[array for array, _ in inputs], *rides)


def split(refs, *sizes):
    parts, place = [], 0
    for size in sizes:
        parts.append(refs[place : place + size])
        place += size
    return parts + [refs[place:]]


def cells(shape, dtype):
    return jax.ShapeDtypeStruct(shape, dtype)


def setup_kernel(
    count, slab_ref, out_w_ref, small_ref, table_ref,
    heads_ref, outs_ref, smalls_ref, tables_ref,
    own_sem, slab_send, slab_recv, pass_send, pass_recv,
    small_send, small_recv, table_send, table_recv, out_send, out_recv,
):
    devices = 2 * count
    me = lax.axis_index("fsdp")
    chip, core = me // 2, lax.rem(me, 2)
    layers = slab_ref.shape[1]

    def device(offset):
        return {"fsdp": lax.rem(me + offset, devices)}

    def chip_at(offset):
        return lax.rem(chip + offset + count, count)

    partner = partner_of("fsdp")
    meet([device(offset) for offset in range(1, devices)])
    copies = [
        pltpu.make_async_copy(slab_ref.at[chip, layer], heads_ref.at[layer, me], own_sem.at[layer])
        for layer in range(layers)
    ] + [
        pltpu.make_async_copy(small_ref, smalls_ref.at[me], own_sem.at[layers]),
        pltpu.make_async_copy(table_ref, tables_ref.at[chip], own_sem.at[layers + 1]),
        pltpu.make_async_copy(out_w_ref, outs_ref.at[core], own_sem.at[layers + 2]),
    ]
    sends = [
        remote(small_ref, smalls_ref.at[me], small_send.at[offset], small_recv.at[offset], device(offset))
        for offset in range(1, devices)
    ]
    for offset in range(1, count):
        there = {"fsdp": chip_at(offset) * 2 + core}
        sends.append(
            remote(table_ref, tables_ref.at[chip], table_send.at[offset], table_recv.at[offset], there)
        )
        for layer in range(layers):
            sends.append(
                remote(
                    slab_ref.at[chip_at(offset), layer], heads_ref.at[layer, me],
                    slab_send.at[offset, layer], slab_recv.at[offset, layer], there,
                )
            )
    for layer in range(layers):
        sends.append(
            remote(
                slab_ref.at[chip, layer], heads_ref.at[layer, me],
                pass_send.at[0, layer], pass_recv.at[0, layer], partner,
            )
        )
    sends.append(remote(out_w_ref, outs_ref.at[core], out_send.at[0], out_recv.at[0], partner))
    for copy in copies + sends:
        copy.start()
    for offset in range(1, count):
        origin = chip_at(-offset) * 2 + core
        for layer in range(layers):
            slot = heads_ref.at[layer, origin]
            remote(slot, slot, slab_send.at[offset, layer], slab_recv.at[offset, layer], partner).wait_recv()
            forward = remote(slot, slot, pass_send.at[offset, layer], pass_recv.at[offset, layer], partner)
            forward.start()
    for offset in range(1, count):
        origin = chip_at(-offset)
        table = tables_ref.at[origin]
        remote(table, table, table_send.at[offset], table_recv.at[offset], partner).wait_recv()
    for offset in range(count):
        origin = chip_at(-offset) * 2 + 1 - core
        mine = chip_at(-offset) * 2 + core
        for layer in range(layers):
            slot, sent = heads_ref.at[layer, origin], heads_ref.at[layer, mine]
            if offset > 0:
                remote(sent, sent, pass_send.at[offset, layer], pass_recv.at[offset, layer], partner).wait_send()
            remote(slot, slot, pass_send.at[offset, layer], pass_recv.at[offset, layer], partner).wait_recv()
    for offset in range(1, devices):
        slot = smalls_ref.at[lax.rem(me - offset + devices, devices)]
        remote(slot, slot, small_send.at[offset], small_recv.at[offset], partner).wait_recv()
    other = outs_ref.at[1 - core]
    remote(other, other, out_send.at[0], out_recv.at[0], partner).wait_recv()
    for copy in copies:
        copy.wait()
    for send in sends:
        send.wait_send()


def exchange_weights(count, slabs, out_w, small, table):
    layers = slabs.shape[1]
    devices = 2 * count
    dma = pltpu.SemaphoreType.DMA
    anywhere = pl.BlockSpec(memory_space=pl.ANY)
    return pl.pallas_call(
        functools.partial(setup_kernel, count),
        out_shape=(
            jax.ShapeDtypeStruct((layers, devices) + slabs.shape[2:], slabs.dtype),
            jax.ShapeDtypeStruct((2,) + out_w.shape, out_w.dtype),
            jax.ShapeDtypeStruct((devices,) + small.shape, small.dtype),
            jax.ShapeDtypeStruct((count,) + table.shape, table.dtype),
        ),
        in_specs=[anywhere] * 4,
        out_specs=[anywhere] * 4,
        scratch_shapes=[
            dma((layers + 3,)),
            dma((count, layers)),
            dma((count, layers)),
            dma((count, layers)),
            dma((count, layers)),
            dma((devices,)),
            dma((devices,)),
            dma((count,)),
            dma((count,)),
            dma((1,)),
            dma((1,)),
        ],
        compiler_params=pltpu.CompilerParams(
            collective_id=identity(("setup",)), has_side_effects=True
        ),
        cost_estimate=FREE,
        name="exchange_weights",
    )(slabs, out_w, small, table)


def dot(left, right, contract=((1,), (0,))):
    return lax.dot_general(left, right, (contract, ((), ())), preferred_element_type=F32)


NT = ((1,), (1,))
TN = ((0,), (0,))


def lanes_of(field):
    return lax.broadcasted_iota(jnp.int32, field.shape, 1)


def turn(field):
    return pltpu.roll(field, HD, 1)


def spin(field, cosine, sine):
    swapped = jnp.where(
        lax.rem(lanes_of(field), HD) < HD // 2,
        -pltpu.roll(field, LANES - HD // 2, 1),
        pltpu.roll(field, HD // 2, 1),
    )
    return field * cosine + swapped * sine


def project_rows(rows, cosine, sine):
    first = spin(rows[:, :LANES], cosine, sine)
    second = spin(rows[:, LANES : 2 * LANES], cosine, sine)
    third = rows[:, 2 * LANES :]
    low = lanes_of(first) < HD
    heads = []
    for field in (first, turn(first), second):
        rounded = jnp.where(low, field, 0.0).astype(BF16).astype(F32)
        heads.append((rounded * (HD**-0.5)).astype(BF16))
    return heads, jnp.where(low, turn(second), turn(third)).astype(BF16)


def angles(table):
    rows = jnp.concatenate([table, table], 0).T
    early = lax.rem(lanes_of(rows), HD) < HD // 2
    cosine = jnp.where(early, rows, pltpu.roll(rows, HD // 2, 1))
    sine = jnp.where(early, pltpu.roll(rows, LANES - HD // 2, 1), rows)
    return cosine, sine


def normal(values):
    inverse = lax.rsqrt(jnp.mean(values * values, -1, keepdims=True) + EPS)
    return inverse, values * inverse


def normal_back(d_x, values, gain):
    inverse, normed = normal(values)
    d_norm = d_x * gain
    d_values = inverse * (d_norm - normed * jnp.mean(d_norm * normed, -1, keepdims=True))
    return d_values, jnp.sum(d_x * normed, 0, keepdims=True)


def diagonal():
    shape = (LANES, LANES)
    return lax.broadcasted_iota(jnp.int32, shape, 0) == lax.broadcasted_iota(jnp.int32, shape, 1)


def as_column(line):
    return jnp.sum(jnp.where(diagonal(), jnp.broadcast_to(line, (LANES, LANES)), 0.0), 1, keepdims=True)


def as_line(column):
    return jnp.sum(jnp.where(diagonal(), jnp.broadcast_to(column, (LANES, LANES)), 0.0), 0, keepdims=True)


def flat(value):
    return value.reshape(value.shape[0] * value.shape[1], value.shape[2])


def stack(ref, blocks):
    parts = [ref[b] for b in blocks]
    return parts[0] if len(parts) == 1 else jnp.concatenate(parts, 0)


def cut(value, blocks):
    return [(b, value[i * LANES : (i + 1) * LANES]) for i, b in enumerate(blocks)]


def gain_row(params_ref, kind, layer):
    row = kind * LAYERS + layer
    return params_ref[row : row + 1, :]


def router_rows(experts, layer):
    first = 2 * LAYERS + layer * experts
    return slice(first, first + experts)


def project_kernel(count, layer, riders, *refs):
    inputs, outputs, scratch = split(refs, 3, 4)
    x_ref, w_ref, table_ref = inputs
    q_ref, own_ref, other_ref, all_ref = outputs
    buf, weights = scratch[:2]
    sems, pair_sems, out_sem, load_sem = split(scratch[2:], 3, 2, 1)
    ring = Ring(count, riders)
    load = pltpu.make_async_copy(w_ref.at[layer], weights, load_sem[0].at[0])
    load.start()
    ring.meet(True)
    partner = partner_of("fsdp")

    def pass_on(block):
        return remote(
            own_ref.at[block], other_ref.at[block], pair_sems[0].at[block], pair_sems[1].at[block], partner
        )

    def compute(place, blocks):
        rows = dot(stack(buf, blocks), weights[...])
        tables = [angles(table_ref[b]) for b in blocks]
        cosine = jnp.concatenate([t[0] for t in tables], 0)
        sine = jnp.concatenate([t[1] for t in tables], 0)
        heads, pair = project_rows(rows, cosine, sine)
        for index, head in enumerate(heads):
            for block, part in cut(head, blocks):
                q_ref[block, index] = part
        for block, part in cut(pair, blocks):
            own_ref[block] = part
            pass_on(block).start()

    def first(s):
        @pl.when(s == 1)
        def _():
            load.wait()

    drain = ring.gather(x_ref, buf, sems, None, first, ring.meanwhile(compute, 0))
    keep = pltpu.make_async_copy(buf, all_ref, out_sem[0].at[0])
    keep.start()
    compute(0, (ring.at(ring.steps),))
    drain()
    for block in range(count):
        pass_on(block).wait()
    keep.wait()


def gather_project(count, layer, x, w, tables):
    rows, width = x.shape
    block = cells((count, rows, LANES), BF16)
    return ring_call(
        functools.partial(project_kernel, count, layer),
        ("project", layer),
        [(x, ANYWHERE), (w, ANYWHERE), (tables, HERE)],
        [
            (cells((count, GROUP, rows, LANES), BF16), HERE),
            (block, HERE),
            (block, HERE),
            (cells((count, rows, width), BF16), ANYWHERE),
        ],
        [pltpu.VMEM((count, rows, width), BF16), pltpu.VMEM(w.shape[1:], BF16)]
        + gather_sems(count)
        + dmas((count,), (count,), (1,), (1,)),
        20,
    )


def route_kernel(count, layer, riders, *refs):
    inputs, outputs, scratch = split(refs, 4, 3)
    p_ref, hidden_ref, params_ref, routes_ref = inputs
    middle_ref, x_ref, share_ref = outputs
    partial, land = scratch[:2]
    sems, load_sem = split(scratch[2:], 2)
    ring = Ring(count, riders)
    load = pltpu.make_async_copy(p_ref, partial, load_sem[0].at[0])
    load.start()
    ring.meet()
    added, drain = ring.scatter(partial, land, sems, None, p_ref, load.wait)
    middle = hidden_ref[...] + added
    middle_ref[...] = middle
    x = (normal(middle)[1] * gain_row(params_ref, 1, layer)).astype(BF16)
    x_ref[...] = x
    experts = share_ref.shape[0]
    logits = dot(params_ref[router_rows(experts, layer), :].astype(BF16), x, NT)
    expert = lax.broadcasted_iota(jnp.int32, logits.shape, 0)
    named = expert < 0
    for choice in range(routes_ref.shape[1]):
        named = named | (expert == routes_ref[layer, choice : choice + 1, :])
    scores = jnp.where(named, logits, MASKED)
    weights = jnp.where(named, jnp.exp(scores - jnp.max(scores, 0, keepdims=True)), 0.0)
    share_ref[...] = weights / jnp.sum(weights, 0, keepdims=True)
    drain()


def scatter_route(count, layer, partial, hidden, params, routes):
    _, rows, width = partial.shape
    experts = 2 * count
    return ring_call(
        functools.partial(route_kernel, count, layer),
        ("route", layer),
        [(partial, ANYWHERE), (hidden, HERE), (params, HERE), (routes, HERE)],
        [
            (cells((rows, width), F32), HERE),
            (cells((rows, width), BF16), HERE),
            (cells((experts, rows), F32), HERE),
        ],
        [pltpu.VMEM(partial.shape, BF16), land_scratch(count, rows, width)]
        + scatter_sems(count)
        + dmas((1,)),
        20,
    )


def load_experts(refs, layer, gates, ups, downs, sem):
    copies = []
    for e in range(2):
        for place, buf in enumerate((gates, ups, downs)):
            source = refs[3 * e + place].at[layer, 0]
            copies.append(pltpu.make_async_copy(source, buf.at[e], sem.at[3 * e + place]))
    for copy in copies:
        copy.start()
    return copies


def expert_of(e):
    me = lax.axis_index("fsdp")
    return me if e == 0 else me + 1 - 2 * lax.rem(me, 2)


def share_of(share_ref, e, blocks):
    columns = [as_column(share_ref[b, pl.ds(expert_of(e), 1), :]) for b in blocks]
    return jnp.concatenate(columns, 0) if len(columns) > 1 else columns[0]


def after_loads(loads, run):
    def first(s):
        @pl.when(s == 1)
        def _():
            for load in loads:
                load.wait()

        run(s)

    return first


def mix_kernel(count, layer, riders, *refs):
    inputs, outputs, scratch = split(refs, 10, 5)
    x_ref, side_ref, middle_ref, params_ref = inputs[:4]
    mixed_ref, hidden_ref, next_ref, all_ref, share_ref = outputs
    buf, partial, land, acc, gates, ups, downs = scratch[:7]
    sems, scatter_sem, load_sem, out_sem = split(scratch[7:], 5, 2, 1)
    ring = Ring(count, riders)
    loads = load_experts(inputs[4:], layer, gates, ups, downs, load_sem[0])
    ring.meet()

    def compute(e, blocks):
        x = stack(buf, blocks)
        act_gate, act_up = dot(x, gates[e]), dot(x, ups[e])
        hidden = jax.nn.silu(act_gate) * act_up * share_of(share_ref, e, blocks)
        part = dot(hidden.astype(BF16), downs[e])
        if e == 0:
            acc[: x.shape[0]] = part
        else:
            total = (acc[: x.shape[0]] + part).astype(BF16)
            for block, rows in cut(total, blocks):
                partial[block] = rows

    drain = ring.gather(
        x_ref, buf, sems, (side_ref, share_ref),
        after_loads(loads, ring.meanwhile(compute, 0)), ring.meanwhile(compute, 1),
    )
    keep = pltpu.make_async_copy(buf, all_ref, out_sem[0].at[0])
    keep.start()
    for e in range(2):
        compute(e, (ring.at(ring.steps),))
    mixed, finish = ring.scatter(partial, land, scatter_sem)
    mixed_ref[...] = mixed
    hidden = middle_ref[...] + mixed
    hidden_ref[...] = hidden
    if layer + 1 < LAYERS:
        next_ref[...] = (normal(hidden)[1] * gain_row(params_ref, 0, layer + 1)).astype(BF16)
    else:
        next_ref[...] = hidden.astype(BF16)
    drain()
    finish()
    keep.wait()


def expert_scratch(weights):
    return [pltpu.VMEM((2,) + w.shape[2:], BF16) for w in weights[:3]]


def land_scratch(count, rows, width):
    return pltpu.VMEM((2, 2, count // 2, rows // 2, width), BF16)


def gather_mix_scatter(count, layer, x, share, middle, params, weights):
    rows, width = x.shape
    everyone = pltpu.VMEM((count, rows, width), BF16)
    own = cells((rows, width), F32)
    return ring_call(
        functools.partial(mix_kernel, count, layer),
        ("mix", layer),
        [(x, ANYWHERE), (share, ANYWHERE), (middle, HERE), (params, HERE)]
        + [(w, ANYWHERE) for w in weights],
        [
            (own, HERE),
            (own, HERE),
            (cells((rows, width), BF16), HERE),
            (cells((count, rows, width), BF16), ANYWHERE),
            (cells((count,) + share.shape, F32), HERE),
        ],
        [everyone, everyone, land_scratch(count, rows, width), pltpu.VMEM((2 * rows, width), F32)]
        + expert_scratch(weights)
        + gather_sems(count, True)
        + scatter_sems(count)
        + dmas((6,), (1,)),
        56,
    )


def mix_back_kernel(count, layer, riders, *refs):
    inputs, outputs, scratch = split(refs, 13, 5)
    d_ref, side_ref, m_ref, share_ref, params_ref, grad_ref, middle_ref = inputs[:7]
    mid_ref, branch_ref, gain_ref, sum_ref, g_router_ref = outputs
    buf, partial, land, acc, gates, ups, downs = scratch[:7]
    tokens, acts, hiddens, balance_ref, totals, got = scratch[7:13]
    sems, scatter_sem, load_sem, pair_sem, out_sem = split(scratch[13:], 5, 2, 1, 2)
    ring = Ring(count, riders)
    loads = load_experts(inputs[7:], layer, gates, ups, downs, load_sem[0])
    loads.append(pltpu.make_async_copy(m_ref, tokens, load_sem[0].at[6]))
    loads[-1].start()
    ring.meet(True)
    ff = gates.shape[2]
    width = buf.shape[2]
    g_router_ref[...] = jnp.zeros_like(g_router_ref)
    routers = 2 * LAYERS + layer * 2 * count

    def compute(e, blocks):
        d, x = stack(buf, blocks), stack(tokens, blocks)
        share = share_of(share_ref, e, blocks)
        balance = [as_column(balance_ref[b, 0:1, :]) for b in blocks]
        balance = jnp.concatenate(balance, 0) if len(balance) > 1 else balance[0]
        act_gate, act_up = dot(x, gates[e]), dot(x, ups[e])
        sig = jax.nn.sigmoid(act_gate)
        swish = act_gate * sig
        hidden = swish * act_up
        raw = dot(d, downs[e], NT)
        d_logit = share * (jnp.sum(hidden * raw, -1, keepdims=True) - balance)
        d_hidden = raw * share
        d_gate = (d_hidden * act_up * sig * (1.0 + act_gate * (1.0 - sig))).astype(BF16)
        d_up = (d_hidden * swish).astype(BF16)
        weighted = (hidden * share).astype(BF16)
        part = dot(d_gate, gates[e], NT) + dot(d_up, ups[e], NT)
        part = part + d_logit * params_ref[pl.ds(routers + expert_of(e), 1), :]
        g_router_ref[e : e + 1, :] += jnp.sum(d_logit * x.astype(F32), 0, keepdims=True)
        for place, block in enumerate(blocks):
            here = slice(place * LANES, (place + 1) * LANES)
            acts[e, block, :, :ff] = d_gate[here]
            acts[e, block, :, ff:] = d_up[here]
            hiddens[e, block] = weighted[here]
        if e == 0:
            acc[: x.shape[0]] = part
        else:
            total = (acc[: x.shape[0]] + part).astype(BF16)
            for block, rows in cut(total, blocks):
                partial[block] = rows

    drain = ring.gather(
        d_ref, buf, sems, (side_ref, balance_ref),
        after_loads(loads, ring.meanwhile(compute, 0)), ring.meanwhile(compute, 1),
    )
    for e in range(2):
        compute(e, (ring.at(ring.steps),))

    partner = partner_of("fsdp")
    strip = 2 * LANES
    strips = width // (2 * strip)
    groups = width // ff

    def regions(half):
        regions = [(group * width + half * (width // 2), width // 2) for group in range(2)]
        return regions + [(2 * width + group * ff + half * (ff // 2), ff // 2) for group in range(groups)]

    def swap(half):
        return [
            remote(
                totals.at[1, pl.ds(first, length)], got.at[pl.ds(first, length)],
                pair_sem[0].at[half, index], pair_sem[1].at[half, index], partner,
            )
            for index, (first, length) in enumerate(regions(half))
        ]

    def store(half):
        return [
            pltpu.make_async_copy(
                totals.at[0, pl.ds(first, length)], sum_ref.at[pl.ds(first, length)], out_sem[0].at[half, index]
            )
            for index, (first, length) in enumerate(regions(half))
        ]

    def work(s, place):
        e = 1 - s // 2
        half = lax.rem(s, 2)

        def put(first, value):
            rows = pl.ds(pl.multiple_of(first, strip), strip)

            @pl.when(s < 2)
            def _():
                totals[1, rows] = value.astype(BF16)

            @pl.when(s >= 2)
            def _():
                totals[0, rows] = (value + got[rows].astype(F32)).astype(BF16)

        if place == 0:
            for h in range(2):

                @pl.when(s == 2 + h)
                def _():
                    for copy in swap(h):
                        copy.wait_recv()

        if place < strips:
            first = (half * strips + place) * strip
            columns = pl.ds(pl.multiple_of(first, strip), strip)
            value = dot(flat(tokens[:, :, columns]), flat(acts[e]), TN)
            for group in range(2):
                put(group * width + first, value[:, group * ff : (group + 1) * ff])
        if place == 3:
            columns = pl.ds(pl.multiple_of(half * strip, strip), strip)
            value = dot(flat(hiddens[e, :, :, columns]), flat(buf[...]), TN)
            for group in range(groups):
                put(2 * width + group * ff + half * strip, value[:, group * ff : (group + 1) * ff])
            for h in range(2):

                @pl.when(s == h)
                def _():
                    for copy in swap(h):
                        copy.start()

                @pl.when(s == 2 + h)
                def _():
                    for copy in store(h):
                        copy.start()

    d_x, finish = ring.scatter(partial, land, scatter_sem, work)
    d_values, gain_ref[...] = normal_back(d_x, middle_ref[...], gain_row(params_ref, 1, layer))
    grad = grad_ref[...] + d_values
    mid_ref[...] = grad
    branch_ref[...] = grad.astype(BF16)
    drain()
    finish()
    for half in range(2):
        for copy in swap(half):
            copy.wait_send()
        for copy in store(half):
            copy.wait()


def gather_mix_back_scatter(count, layer, d, side, m_all, share, params, grad, middle, weights, rides):
    rows, width = d.shape
    ff = weights[0].shape[3]
    everyone = pltpu.VMEM((count, rows, width), BF16)
    groups = width // ff
    own = cells((rows, width), F32)
    return ring_call(
        functools.partial(mix_back_kernel, count, layer),
        ("mix_back", layer),
        [(d, ANYWHERE), (side, ANYWHERE), (m_all, ANYWHERE), (share, HERE), (params, HERE), (grad, HERE), (middle, HERE)]
        + [(w, ANYWHERE) for w in weights],
        [
            (own, HERE),
            (cells((rows, width), BF16), HERE),
            (cells((1, width), F32), HERE),
            (cells((3 * width, ff), BF16), ANYWHERE),
            (cells((2, width), F32), HERE),
        ],
        [everyone, everyone, land_scratch(count, rows, width), pltpu.VMEM((2 * rows, width), F32)]
        + expert_scratch(weights)
        + [
            everyone,
            pltpu.VMEM((2, count, rows, 2 * ff), BF16),
            pltpu.VMEM((2, count, rows, ff), BF16),
            pltpu.VMEM((count,) + side.shape, F32),
            pltpu.VMEM((2, 3 * width, ff), BF16),
            pltpu.VMEM((3 * width, ff), BF16),
        ]
        + gather_sems(count, True)
        + scatter_sems(count)
        + dmas((7,), (2, 2 + groups), (2, 2 + groups), (2, 2 + groups)),
        60,
        rides,
    )


def branch_back_kernel(count, layer, riders, *refs):
    inputs, outputs, scratch = split(refs, 3, 2)
    d_ref, w_ref, att_ref = inputs
    datt_ref, g_ref = outputs
    buf, wide_w, acc, mail, got = scratch[:5]
    sems, pair_sem, load_sem = split(scratch[5:], 3, 2)
    ring = Ring(count, riders)
    shard = g_ref.shape[0]
    loads = load_out_weights(w_ref, layer, wide_w, load_sem[0])
    ring.meet(True)
    acc[...] = jnp.zeros_like(acc)

    def compute(place, blocks):
        d = stack(buf, blocks)
        datt = dot(d, wide_w[...], NT).astype(BF16)
        for block, rows in cut(datt, blocks):
            datt_ref[block] = rows
        acc[...] += dot(stack(att_ref, blocks), d, TN)

    drain = ring.gather(
        d_ref, buf, sems, None, after_loads(loads, lambda s: None), ring.meanwhile(compute, 0)
    )
    compute(0, (ring.at(ring.steps),))
    core = lax.rem(lax.axis_index("fsdp"), 2)
    mail[...] = acc[pl.ds(pl.multiple_of((1 - core) * shard, 8), shard), :].astype(BF16)
    swap = remote(mail, got, pair_sem[0].at[0], pair_sem[1].at[0], partner_of("fsdp"))
    swap.start()
    drain()
    swap.wait()
    own = acc[pl.ds(pl.multiple_of(core * shard, 8), shard), :]
    g_ref[...] = (own + got[...].astype(F32)).astype(BF16)


def gather_branch_back(count, layer, d, w, att):
    rows, width = d.shape
    shard = w.shape[2]
    return ring_call(
        functools.partial(branch_back_kernel, count, layer),
        ("branch_back", layer),
        [(d, ANYWHERE), (w, ANYWHERE), (att, HERE)],
        [
            (cells((count, rows, 2 * LANES), BF16), HERE),
            (cells((shard, width), BF16), HERE),
        ],
        [
            pltpu.VMEM((count, rows, width), BF16),
            pltpu.VMEM((2 * LANES, width), BF16),
            pltpu.VMEM((2 * LANES, width), F32),
            pltpu.VMEM((shard, width), BF16),
            pltpu.VMEM((shard, width), BF16),
        ]
        + gather_sems(count)
        + dmas((1,), (1,), (2,)),
        20,
    )


def load_out_weights(w_ref, layer, wide_ref, sem):
    shard = w_ref.shape[2]
    copies = [
        pltpu.make_async_copy(w_ref.at[core, layer], wide_ref.at[pl.ds(core * shard, shard)], sem.at[core])
        for core in range(2)
    ]
    for copy in copies:
        copy.start()
    used = 2 * shard
    wide_ref[used:] = jnp.zeros((wide_ref.shape[0] - used, wide_ref.shape[1]), BF16)
    return copies


def join_kernel(count, layer, riders, *refs):
    inputs, outputs, scratch = split(refs, 13, 4)
    dq_ref, own_ref, other_ref, table_ref, w_ref, x_ref, params_ref, mid_ref, hidden_ref = inputs[:9]
    mixed_ref, router_ref, gain_two_ref = inputs[9:12]
    grad_ref, d_mix_ref, side_ref, g_ref = outputs
    partial, land, rows_ref, tokens, got, weights, last_ref = scratch[:7]
    scatter_sem, pair_sem, load_sem = split(scratch[7:], 2, 2)
    ring = Ring(count, riders)
    loads = [
        pltpu.make_async_copy(x_ref, tokens, load_sem[0].at[0]),
        pltpu.make_async_copy(w_ref.at[layer], weights, load_sem[0].at[1]),
    ]
    for load in loads:
        load.start()
    ring.meet(True)
    swap = remote(other_ref, got, pair_sem[0].at[0], pair_sem[1].at[0], partner_of("fsdp"))
    swap.start()
    swap.wait()
    loads[1].wait()

    def compute(index, carry):
        blocks = 2 * index, 2 * index + 1
        rows = []
        for b in blocks:
            pair = own_ref[b] + got[b].astype(F32)
            cosine, sine = angles(table_ref[b])
            keys = spin(pair, cosine, -sine)
            low = lanes_of(pair) < HD
            middle = jnp.where(low, dq_ref[b, :, LANES:].astype(F32), turn(keys))
            last = jnp.where(low, turn(pair), 0.0)
            rows.append(
                jnp.concatenate([dq_ref[b, :, :LANES], middle.astype(BF16), last.astype(BF16)], 1)
            )
            rows_ref[b] = rows[-1]
        total = dot(jnp.concatenate(rows, 0), weights[...], NT).astype(BF16)
        for block, part in cut(total, blocks):
            partial[block] = part
        return carry

    lax.fori_loop(0, count // 2, compute, 0)
    loads[0].wait()
    strip = g_ref.shape[0] // ring.steps
    tile = 2 * LANES

    def work(s, place):
        if place == 0:
            rows = pl.ds(pl.multiple_of(s * strip, LANES), strip)
            value = dot(flat(tokens[:, :, rows]), flat(rows_ref[...]), TN)
            g_ref[rows, :tile] = value[:, :tile].astype(BF16)
            last_ref[rows] = value[:, tile:]

    d_x, drain = ring.scatter(partial, land, scatter_sem, work)
    d_values, gain_one = normal_back(d_x, hidden_ref[...], gain_row(params_ref, 0, layer))
    grad = mid_ref[...] + d_values
    grad_ref[...] = grad
    d_mix = grad.astype(BF16)
    d_mix_ref[...] = d_mix
    balance = jnp.sum(mixed_ref[...] * d_mix.astype(F32), -1, keepdims=True)
    side_ref[...] = jnp.broadcast_to(as_line(balance), side_ref.shape)
    core = lax.rem(lax.axis_index("fsdp"), 2)
    routers = router_ref[...]
    first, second = routers[0:1], routers[1:2]
    lines = [
        jnp.where(core == 0, first, second),
        jnp.where(core == 0, second, first),
        gain_one,
        gain_two_ref[...],
    ]
    width = g_ref.shape[0]
    tall = jnp.concatenate(
        [jnp.zeros((HD, width), F32)] + lines + [jnp.zeros((HD - len(lines), width), F32)], 0
    )
    g_ref[:, tile:] = (last_ref[...] + tall.T).astype(BF16)
    drain()


def join_scatter(count, layer, dq, own, other, tables, w, x_all, params, mid, hidden, mixed, g_router, gain_two):
    _, rows, width = x_all.shape
    everyone = pltpu.VMEM((count, rows, width), BF16)
    here = [dq, own, other, tables]
    late = [params, mid, hidden, mixed, g_router, gain_two]
    nothing = jnp.zeros((8, LANES), F32)
    return ring_call(
        functools.partial(join_kernel, count, layer),
        ("join", layer),
        [(a, HERE) for a in here] + [(w, ANYWHERE), (x_all, ANYWHERE)] + [(a, HERE) for a in late]
        + [(nothing, HERE)],
        [
            (cells((rows, width), F32), HERE),
            (cells((rows, width), BF16), HERE),
            (cells((8, rows), F32), HERE),
            (cells(w.shape[1:], BF16), HERE),
        ],
        [
            everyone,
            land_scratch(count, rows, width),
            pltpu.VMEM((count, rows, w.shape[2]), BF16),
            everyone,
            pltpu.VMEM(other.shape, BF16),
            pltpu.VMEM(w.shape[1:], BF16),
            pltpu.VMEM((width, LANES), F32),
        ]
        + scatter_sems(count)
        + dmas((1,), (1,), (2,)),
        28,
    )


def finish_kernel(count, replicas, *refs):
    inputs, outputs, scratch = split(refs, 3, 4)
    g_ref, early_ref, early_peer_ref = inputs
    q_out, k_out, v_out, rest_out = outputs
    early, land, total, mine, peer = scratch[:5]
    pair_send, pair_recv, part_send, part_recv, rep_send, rep_recv = scratch[5:]
    me = lax.axis_index("fsdp")
    chip, core = me // 2, lax.rem(me, 2)
    partner = partner_of("fsdp")

    def chip_at(offset):
        return lax.rem(chip + offset + count, count)

    def device(offset):
        return {"fsdp": chip_at(offset) * 2 + core}

    across = [partner_of("rep")] if replicas == 2 else []
    meet([device(offset) for offset in range(1, count)] + [partner] + across)
    swaps = [remote(g_ref.at[:, 1 - core], land.at[0], pair_send.at[0], pair_recv.at[0], partner)]
    swaps[0].start()
    for block in range(count):
        for half in range(2):
            both = early_ref[block, half].astype(F32)
            if replicas == 2:
                both = both + early_peer_ref[block, half].astype(F32)
            early[half, block] = both.astype(BF16)
    swaps.append(remote(early.at[1 - core], land.at[1], pair_send.at[1], pair_recv.at[1], partner))
    swaps[1].start()
    for swap in swaps:
        swap.wait()
    for block in range(count):
        total[block, 0] = (g_ref[block, core].astype(F32) + land[0, block].astype(F32)).astype(BF16)
        total[block, 1] = (early[core, block].astype(F32) + land[1, block].astype(F32)).astype(BF16)
    sends = [
        remote(
            total.at[chip_at(offset)], mine.at[chip],
            part_send.at[offset], part_recv.at[offset], device(offset),
        )
        for offset in range(1, count)
    ]
    for send in sends:
        send.start()
    mine[chip] = total[chip]

    def to_peer(offset):
        slot = chip_at(-offset)
        return remote(mine.at[slot, 0], peer.at[slot], rep_send.at[offset], rep_recv.at[offset], across[0])

    for offset in range(count):
        if offset > 0:
            slot = mine.at[chip_at(-offset)]
            remote(slot, slot, part_send.at[offset], part_recv.at[offset], partner).wait_recv()
        if replicas == 2:
            to_peer(offset).start()
    if replicas == 2:
        for offset in range(count):
            to_peer(offset).wait()

    def tiles(block, layer):
        value = mine[block, layer].astype(F32)
        if replicas == 2 and layer == 0:
            value = value + peer[block].astype(F32)
        return [value[:, i * LANES : (i + 1) * LANES] for i in range(3)]

    for layer in range(LAYERS):
        for half in range(count // 2):
            a, b = tiles(2 * half, layer), tiles(2 * half + 1, layer)
            low = lanes_of(a[0]) < HD
            q_out[layer, :, 3 * half * LANES : 3 * (half + 1) * LANES] = jnp.concatenate(
                [a[0], jnp.where(low, a[1], turn(b[0])), jnp.where(low, turn(b[0]), turn(b[1]))], 1
            )
            here = slice(half * LANES, (half + 1) * LANES)
            k_out[layer, :, here] = jnp.where(low, turn(a[1]), b[1])
            v_out[layer, :, here] = jnp.where(low, a[2], turn(b[2]))
            rest_out[layer, 2 * half] = a[2]
            rest_out[layer, 2 * half + 1] = b[2]
    for send in sends:
        send.wait_send()


def finish_heads(count, replicas, g, early, early_peer):
    _, _, rows, columns = g.shape
    width = count * GROUP * HD
    part = (count, LAYERS, rows, columns)
    dma = pltpu.SemaphoreType.DMA
    return pl.pallas_call(
        functools.partial(finish_kernel, count, replicas),
        out_shape=(
            cells((LAYERS, rows, width), F32),
            cells((LAYERS, rows, count * HD), F32),
            cells((LAYERS, rows, count * HD), F32),
            cells((LAYERS, count, rows, LANES), F32),
        ),
        in_specs=[HERE] * 3,
        out_specs=[HERE] * 4,
        scratch_shapes=[
            pltpu.VMEM((2, count, rows, columns), BF16),
            pltpu.VMEM((2, count, rows, columns), BF16),
            pltpu.VMEM(part, BF16),
            pltpu.VMEM(part, BF16),
            pltpu.VMEM((count, rows, columns), BF16),
            dma((2,)), dma((2,)), dma((count,)), dma((count,)), dma((count,)), dma((count,)),
        ],
        compiler_params=pltpu.CompilerParams(
            collective_id=identity(("finish",)), has_side_effects=True, vmem_limit_bytes=32 << 20
        ),
        cost_estimate=FREE,
        name="finish_heads",
    )(g, early, early_peer)


def add_kernel(layers, *refs):
    out_refs = refs[-3:]
    for layer in range(layers):
        pairs = refs[layer * 10 : (layer + 1) * 10]
        sums = [pairs[i][...].astype(F32) + pairs[i + 5][...].astype(F32) for i in range(5)]
        out_refs[0][layer, 0] = sums[0]
        out_refs[1][layer, 0] = sums[1]
        out_refs[2][layer, 0] = jnp.concatenate(sums[2:], 1)


def add_experts(pairs):
    layers = len(pairs)
    rows, ff = pairs[0][0].shape
    width = rows // 3
    steps = 4
    tall, short = width // steps, ff // steps

    def at(first, length):
        return pl.BlockSpec((length, ff), lambda i: (first // length + i, 0))

    specs = [at(0, tall), at(width, tall)] + [at(2 * width + g * ff, short) for g in range(3)]
    arrays = [array for pair in pairs for array in pair for _ in range(5)]
    return pl.pallas_call(
        functools.partial(add_kernel, layers),
        grid=(steps,),
        out_shape=(
            cells((layers, 1, width, ff), F32),
            cells((layers, 1, width, ff), F32),
            cells((layers, 1, ff, width), F32),
        ),
        in_specs=specs * (2 * layers),
        out_specs=[
            pl.BlockSpec((layers, 1, tall, ff), lambda i: (0, 0, i, 0)),
            pl.BlockSpec((layers, 1, tall, ff), lambda i: (0, 0, i, 0)),
            pl.BlockSpec((layers, 1, short, width), lambda i: (0, 0, i, 0)),
        ],
        cost_estimate=FREE,
        name="add_experts",
    )(*arrays)


def allowed_keys(begin, block, chunk, core):
    shape = (GROUP * LANES, 2 * LANES)
    place = lax.broadcasted_iota(jnp.int32, shape, 1)
    shift = jnp.where(place < LANES, core, -core)
    key = chunk * 2 * LANES + place + shift * LANES
    query = block * LANES + lax.rem(lax.broadcasted_iota(jnp.int32, shape, 0), LANES)
    return (key >= begin) & (key <= query)


def attend_kernel(layer, info_ref, q_ref, own_ref, other_ref, begin_ref, w_ref, att_ref, lse_ref, out_ref, wide_ref, sem):
    step = pl.program_id(0)
    core = info_ref[0]
    block = 2 * step + core
    first = info_ref[1 + step] // (2 * LANES)

    @pl.when(step == 0)
    def _():
        for load in load_out_weights(w_ref, layer, wide_ref, sem):
            load.wait()

    q = q_ref[0].reshape(GROUP * LANES, LANES)
    begin = jnp.concatenate([begin_ref[0]] * GROUP, 0)

    def one(chunk, state):
        top, total, acc = state
        keys = jnp.concatenate([own_ref[chunk], other_ref[chunk]], 0)
        allowed = allowed_keys(begin, block, chunk, core)
        scores = jnp.where(allowed, dot(q, keys, NT), MASKED)
        new_top = jnp.maximum(top, jnp.max(scores, -1, keepdims=True))
        weights = jnp.where(allowed, jnp.exp(scores - new_top), 0.0)
        shrink = jnp.exp(top - new_top)
        total = total * shrink + jnp.sum(weights, -1, keepdims=True)
        return new_top, total, acc * shrink + dot(weights.astype(BF16), keys)

    rows = GROUP * LANES
    top, total, acc = lax.fori_loop(
        first,
        step + 1,
        one,
        (jnp.full((rows, 1), MASKED, F32), jnp.zeros((rows, 1), F32), jnp.zeros((rows, LANES), F32)),
    )
    lse_ref[0] = top + jnp.log(total)
    att = acc / total
    heads = [att[h * LANES : (h + 1) * LANES] for h in range(GROUP)]
    low = lanes_of(heads[0]) < HD
    wide = jnp.concatenate(
        [jnp.where(low, turn(heads[0]), heads[1]), jnp.where(low, turn(heads[2]), 0.0)], 1
    ).astype(BF16)
    att_ref[0] = wide
    out_ref[0] = dot(wide, wide_ref[...]).astype(BF16)


def attend(layer, info, q, own, other, begin, w):
    blocks = q.shape[0]
    width = w.shape[3]
    wide = 2 * LANES
    return pl.pallas_call(
        functools.partial(attend_kernel, layer),
        grid_spec=pltpu.PrefetchScalarGridSpec(
            num_scalar_prefetch=1,
            grid=(blocks,),
            in_specs=[
                pl.BlockSpec((1, GROUP, LANES, LANES), lambda i, s: (i, 0, 0, 0)),
                pl.BlockSpec(own.shape, lambda i, s: (0, 0, 0)),
                pl.BlockSpec(own.shape, lambda i, s: (0, 0, 0)),
                pl.BlockSpec((1, LANES, 1), lambda i, s: (i, 0, 0)),
                ANYWHERE,
            ],
            out_specs=[
                pl.BlockSpec((1, LANES, wide), lambda i, s: (i, 0, 0)),
                pl.BlockSpec((1, GROUP * LANES, 1), lambda i, s: (i, 0, 0)),
                pl.BlockSpec((1, LANES, width), lambda i, s: (i, 0, 0)),
            ],
            scratch_shapes=[pltpu.VMEM((wide, width), BF16), pltpu.SemaphoreType.DMA((2,))],
        ),
        out_shape=(
            jax.ShapeDtypeStruct((blocks, LANES, wide), BF16),
            jax.ShapeDtypeStruct((blocks, GROUP * LANES, 1), F32),
            jax.ShapeDtypeStruct((blocks, LANES, width), BF16),
        ),
        cost_estimate=FREE,
        name="attend",
    )(info, q, own, other, begin, w)


def attend_back_kernel(
    info_ref, q_ref, own_ref, other_ref, begin_ref, att_ref, lse_ref, datt_ref, table_ref,
    dq_ref, d_own_ref, mail_ref, d_other_ref,
):
    step = pl.program_id(0)
    core = info_ref[0]
    block = 2 * step + core
    first = info_ref[1 + step] // (2 * LANES)

    @pl.when(step == 0)
    def _():
        d_own_ref[...] = jnp.zeros_like(d_own_ref)
        d_other_ref[...] = jnp.zeros_like(d_other_ref)

    q = q_ref[0].reshape(GROUP * LANES, LANES)
    begin = jnp.concatenate([begin_ref[0]] * GROUP, 0)

    def spread(wide):
        front, back = wide[:, :LANES], wide[:, LANES:]
        low = lanes_of(front) < HD
        parts = [jnp.where(low, 0.0, part) for part in (turn(front), front, turn(back))]
        return jnp.concatenate(parts, 0)

    datt = spread(datt_ref[0].astype(F32)).astype(BF16)
    att = spread(att_ref[0].astype(F32))
    delta = jnp.sum(datt.astype(F32) * att, -1, keepdims=True)
    lse = lse_ref[0]
    both = jnp.concatenate([q, datt], 0)

    def one(chunk, acc):
        keys = jnp.concatenate([own_ref[chunk], other_ref[chunk]], 0)
        allowed = allowed_keys(begin, block, chunk, core)
        weights = jnp.where(allowed, jnp.exp(dot(q, keys, NT) - lse), 0.0)
        slope = (weights * (dot(datt, keys, NT) - delta)).astype(BF16)
        d_keys = dot(jnp.concatenate([slope, weights.astype(BF16)], 0), both, TN)
        d_own_ref[chunk] += d_keys[:LANES]
        d_other_ref[chunk] += d_keys[LANES:]
        return acc + dot(slope, keys)

    acc = lax.fori_loop(first, step + 1, one, jnp.zeros((GROUP * LANES, LANES), F32))
    heads = [acc[h * LANES : (h + 1) * LANES] * (HD**-0.5) for h in range(GROUP)]
    low = lanes_of(heads[0]) < HD
    cosine, sine = angles(table_ref[0])
    front = spin(jnp.where(low, heads[0], turn(heads[1])), cosine, -sine)
    back = spin(jnp.where(low, heads[2], 0.0), cosine, -sine)
    dq_ref[0] = jnp.concatenate([front, back], 1).astype(BF16)

    @pl.when(step == pl.num_programs(0) - 1)
    def _():
        mail_ref[...] = d_other_ref[...].astype(BF16)


def attend_back(info, q, own, other, begin, att, lse, datt, tables):
    blocks = q.shape[0]
    wide = 2 * LANES

    def block(*shape):
        return pl.BlockSpec((1,) + shape, lambda i, s: (i,) + (0,) * len(shape))

    whole = pl.BlockSpec(own.shape, lambda i, s: (0, 0, 0))
    return pl.pallas_call(
        attend_back_kernel,
        grid_spec=pltpu.PrefetchScalarGridSpec(
            num_scalar_prefetch=1,
            grid=(blocks,),
            in_specs=[
                block(GROUP, LANES, LANES),
                whole,
                whole,
                block(LANES, 1),
                block(LANES, wide),
                block(GROUP * LANES, 1),
                block(LANES, wide),
                block(HD, LANES),
            ],
            out_specs=[block(LANES, wide), whole, whole],
            scratch_shapes=[pltpu.VMEM(own.shape, F32)],
        ),
        out_shape=(
            jax.ShapeDtypeStruct((blocks, LANES, wide), BF16),
            jax.ShapeDtypeStruct(own.shape, F32),
            jax.ShapeDtypeStruct(own.shape, BF16),
        ),
        cost_estimate=FREE,
        name="attend_back",
    )(info, q, own, other, begin, att, lse, datt, tables)


def on_device(
    tokens,
    cotangent,
    positions,
    segments,
    routes,
    attn_gain,
    w_query,
    w_key,
    w_value,
    w_out,
    ffn_gain,
    router,
    w_gate,
    w_up,
    w_down,
):
    rows, width = tokens.shape
    devices = lax.axis_size("fsdp")
    replicas = lax.axis_size("rep")
    count = devices // 2
    me = lax.axis_index("fsdp")
    chip, core = me // 2, lax.rem(me, 2)
    shard = w_query.shape[1]
    experts = devices
    columns = 3 * LANES
    used = (GROUP + 2) * HD
    pairs = [(index, index ^ 1) for index in range(devices)]

    def swap(array):
        return lax.ppermute(array, "fsdp", pairs)

    small = jnp.concatenate(
        [attn_gain, ffn_gain, router.transpose(0, 2, 1).reshape(LAYERS * experts, shard)], 0
    )
    small = jnp.pad(small, ((0, 48 - small.shape[0]), (0, LANES - shard)))
    rate = jnp.exp(-jnp.log(10000.0) * jnp.arange(HD // 2, dtype=F32) / (HD // 2))
    angle = rate[:, None] * positions.astype(F32)[None, :]
    table = jnp.concatenate([jnp.cos(angle), jnp.sin(angle)], 0)
    slabs = jnp.concatenate(
        [
            w_query.reshape(LAYERS, shard, count, GROUP * HD),
            w_key.reshape(LAYERS, shard, count, HD),
            w_value.reshape(LAYERS, shard, count, HD),
            jnp.zeros((LAYERS, shard, count, columns - used), BF16),
        ],
        -1,
    ).transpose(2, 0, 1, 3)
    heads_w, outs_w, smalls, tables = exchange_weights(count, slabs, w_out, small, table)
    heads_w = heads_w.reshape(LAYERS, width, columns)
    params = smalls[:, : (2 + experts) * LAYERS, :shard].transpose(1, 0, 2).reshape(-1, width)
    params = params.astype(F32)
    own_w, _ = lax.optimization_barrier(([w_gate, w_up, w_down], smalls))
    experts_w = own_w + [swap(w) for w in own_w]

    flat_segments = segments.reshape(1, -1)
    kinds = jnp.arange(8, dtype=jnp.int32)[:, None]
    starts = jnp.sum((flat_segments < kinds).astype(jnp.int32), 1, keepdims=True)
    begin = jnp.sum(jnp.where(flat_segments == kinds, starts, 0), 0).reshape(count, 2, rows)
    begin = lax.dynamic_index_in_dim(begin, core, 1, False)
    info = jnp.concatenate([core[None], begin[:, 0]]).astype(jnp.int32)
    begin = begin[:, :, None]

    hidden = tokens.astype(F32)
    x_attn = (normal(hidden)[1] * params[0:1]).astype(BF16)
    chosen = routes.transpose(0, 2, 1)
    saved = []
    for layer in range(LAYERS):
        query, kv, kv_other, x_all = gather_project(count, layer, x_attn, heads_w, tables)
        att, lse, partial = attend(layer, info, query, kv, kv_other, begin, outs_w)
        middle, x_moe, share = scatter_route(count, layer, partial, hidden, params, chosen)
        mixed, after, x_attn, m_all, share_all = gather_mix_scatter(
            count, layer, x_moe, share, middle, params, experts_w
        )
        saved.append((hidden, x_all, query, kv, kv_other, att, lse, middle, mixed, m_all, share_all))
        hidden = after
    activations = x_attn

    def across(array):
        return lax.ppermute(array, "rep", [(0, 1), (1, 0)]) if replicas == 2 else array

    grad, d_mix = cotangent.astype(F32), cotangent
    balance = jnp.sum(saved[-1][8] * grad, -1)
    side = jnp.broadcast_to(balance[None, :], (8, rows))
    expert_sums = [None] * LAYERS
    out_sums = [None] * LAYERS
    for layer in reversed(range(LAYERS)):
        hidden, x_all, query, kv, kv_other, att, lse, middle, mixed, m_all, share_all = saved[layer]
        rides = [out_sums[layer + 1], early] if layer + 1 < LAYERS and replicas == 2 else []
        grad_mid, d_branch, gain_two, expert_sum, g_router, *rode = gather_mix_back_scatter(
            count, layer, d_mix, side, m_all, share_all, params, grad, middle, experts_w, rides
        )
        if layer + 1 < LAYERS:
            d_branch, expert_sums[layer + 1] = lax.optimization_barrier(
                (d_branch, expert_sums[layer + 1])
            )
        expert_sums[layer] = (expert_sum, across(expert_sum))
        datt, out_sum = gather_branch_back(count, layer, d_branch, outs_w, att)
        out_sums[layer] = out_sum
        d_query, d_own, d_other = attend_back(
            info, query, kv, kv_other, begin, att, lse, datt, tables
        )
        grad, d_mix, side, heads = join_scatter(
            count, layer, d_query, d_own, d_other, tables, heads_w, x_all, params, grad_mid, hidden,
            saved[max(layer - 1, 0)][8], g_router, gain_two,
        )
        heads = heads.reshape(count, 2, shard, columns)
        early = heads if layer > 0 else early
    g_query, g_key, g_value, rest = finish_heads(
        count, replicas, heads, early, rode[1] if rode else early
    )
    if replicas == 2:
        g_gate, g_up, g_down = add_experts(expert_sums)
        arrived = [across(out_sums[0]), rode[0]]
        g_out = jnp.stack([a.astype(F32) + b.astype(F32) for a, b in zip(out_sums, arrived)])
    else:
        g_query, g_key, g_value, rest, g_out, flat_sums = [
            lax.psum(array.astype(BF16), "rep").astype(F32)
            for array in (
                g_query, g_key, g_value, rest,
                jnp.stack(out_sums),
                jnp.stack([own for own, _ in expert_sums]),
            )
        ]
        ff = w_gate.shape[3]
        g_gate, g_up = flat_sums[:, None, :width], flat_sums[:, None, width : 2 * width]
        g_down = flat_sums[:, 2 * width :].reshape(LAYERS, width // ff, ff, ff)
        g_down = g_down.transpose(0, 2, 1, 3).reshape(LAYERS, 1, ff, width)
    rest = rest[..., HD : HD + 4]
    gains = jnp.sum(rest, 1)
    g_router = rest[..., :2].transpose(0, 2, 1, 3).reshape(LAYERS, shard, experts)
    return (
        activations,
        grad,
        gains[..., 2],
        g_query,
        g_key,
        g_value,
        g_out,
        gains[..., 3],
        g_router,
        g_gate,
        g_up,
        g_down,
    )


def solution(mesh):
    placed = (
        P(("rep", "fsdp"), None),
        P(("rep", "fsdp"), None),
        P(("rep", "fsdp")),
        P("rep", None),
        P(None, ("rep", "fsdp"), None),
        P(None, "fsdp"),
        P(None, "fsdp", None),
        P(None, "fsdp", None),
        P(None, "fsdp", None),
        P(None, "fsdp", None),
        P(None, "fsdp"),
        P(None, "fsdp", None),
        P(None, "fsdp", None, None),
        P(None, "fsdp", None, None),
        P(None, "fsdp", None, None),
    )
    return jax.shard_map(
        on_device,
        mesh=mesh,
        in_specs=placed,
        out_specs=(
            P(("rep", "fsdp"), None),
            P(("rep", "fsdp"), None),
            P(None, "fsdp"),
            P(None, "fsdp", None),
            P(None, "fsdp", None),
            P(None, "fsdp", None),
            P(None, "fsdp", None),
            P(None, "fsdp"),
            P(None, "fsdp", None),
            P(None, "fsdp", None, None),
            P(None, "fsdp", None, None),
            P(None, "fsdp", None, None),
        ),
        check_vma=False,
    )
```

time: 930 us -> 853 us (0.917)
  Pallas kernels: 809 us -> 770 us
  local copies, waits for them, and re-layouts: 75.8 us -> 54.8 us
  other arithmetic: 27.4 us -> 14.5 us
    pallas_call x1, Pallas kernels: 58.4 us -> 38.3 us  [finish_heads(): pl.pallas_call(functools.partial(finish_kernel, count, replicas), out_sha...]
    slice x18 -> x2, local copies, waits for them, and re-layouts: 20.8 us -> 0.83 us  [the longest x1 0.8 us: on_device(): gains[..., 3]]
    unnamed x162 -> x157, local copies, waits for them, and re-layouts: 34.2 us -> 48.9 us
    pallas_call x17 -> x15, Pallas kernels: 663 us -> 650 us  [the longest x12 598 us: ring_call(): pl.pallas_call(kernel, out_shape=tuple((shape for shape, _ in outputs)) +...]
  transfers between devices with their start and end apart: 8 -> 6, of which waited for: 0 -> 0; matrix products, arithmetic and copies ran while one was open for 6% -> 1% of each run, Pallas kernels for 40% -> 51%
where the time goes in v4:
time: 853 us; the launch traced here: 844 us
  Pallas kernels  770 us (90%)
  local copies, waits for them, and re-layouts  54.8 us (6%)
  other arithmetic  14.5 us (2%)
    pallas_call x12, Pallas kernels, ring_call(): pl.pallas_call(kernel, out_shape=tuple((shape for shape, _ in outputs)) +...  598 us
    unnamed x157, local copies, waits for them, and re-layouts  48.9 us
    pallas_call x2, Pallas kernels, attend_back(): pl.pallas_call(attend_back_kernel, grid_spec=pltpu.PrefetchScalarGridSpec...  46.6 us
    pallas_call x2, Pallas kernels, attend(): pl.pallas_call(functools.partial(attend_kernel, layer), grid_spec=pltpu.P...  39.2 us
    pallas_call x1, Pallas kernels, finish_heads(): pl.pallas_call(functools.partial(finish_kernel, count, replicas), out_sha...  38.3 us
    pallas_call x1, Pallas kernels, exchange_weights(): pl.pallas_call(functools.partial(setup_kernel, count), out_shape=(jax.Sha...  34.7 us
  transfers between devices with their start and end apart: 6, of which 0 were waited for; matrix products, arithmetic and copies ran while one was open for 1% of the time, Pallas kernels for 51%

profile of v4, /device:TPU:0, one launch (start us, length us, event | category | flops | bytes accessed | tf_op | source)
XLA Modules:
  0.0 843.7 jit_solution(16741692839699589600)
XLA Ops:
  0.7 1.2 copy.85
  2.1 1.1 copy.84
  5.7 1.5 maximum_bitcast_fusion.slab_ref
  7.2 34.7 %exchange_weights.1 = (bf16[2,16,96,384]{3,2,1,0:T(8,128)(2,1)}, bf16[2,2,96,1536]{3,2,1,0:T(8,128)(2,1)}, bf16[16,48,128]{2,1,0:T(8,128)(2,1)}, f32[8,64,128]{2,1,0:T(8,128)}) custom-call(bf16[8,2,96,384]{3,2,1,0:T(8,128)(2,1)} %maximum_bitcast_fusion.slab_ref, bf16[2,96,1536]{2,1,0:T(8,128)(2,1)} %out_w_ref.1, bf16[48,128]{1,0:T(8,128)(2,1)} %fusion.8.small_ref, ...), custom_call_target="tpu_custom_call" | custom-call | tf_op jit(solution)/shard_map/exchange_weights/pallas_call | solution.py:423
  44.9 1.1 copy.89.begin_ref
  47.0 2.1 convert_element_type.43.refs_5_
  50.2 46.7 %project.2 = (bf16[8,3,128,128]{3,2,1,0:T(8,128)(2,1)S(1)}, bf16[8,128,128]{2,1,0:T(8,128)(2,1)S(1)}, bf16[8,128,128]{2,1,0:T(8,128)(2,1)S(1)}, bf16[8,128,1536]{2,1,0:T(8,128)(2,1)S(1)}) custom-call(bf16[128,1536]{1,0:T(8,128)(2,1)S(1)} %multiply_convert_fusion.refs_0_, bf16[2,1536,384]{2,1,0:T(8,128)(2,1)S(1)} %bitcast.25, f32[8,64,128]{2,1,0:T(8,128)S(1)} %copy-done.7), custom_call_target="tpu_custom_call" | custom-call | tf_op jit(solution)/shard_map/project/pallas_call | solution.py:307
  96.9 1.7 copy-done.14
  101.5 19.4 %attend.2 = (bf16[8,128,256]{2,1,0:T(8,128)(2,1)}, f32[8,384,1]{2,1,0:T(8,128)}, bf16[8,128,1536]{2,1,0:T(8,128)(2,1)}) custom-call(s32[9]{0:T(128)} %pad_add_fusion.info_ref, bf16[8,3,128,128]{3,2,1,0:T(8,128)(2,1)} %copy-done.22, bf16[8,128,128]{2,1,0:T(8,128)(2,1)} %copy-done.32, bf16[8,128,128]{2,1,0:T(8,128)(2,1)} %copy-done.33, ...), custom_call_target="tpu_custom_call" | custom-call | tf_op jit(solution)/shard_map/attend/pallas_call | solution.py:1329
  121.0 1.1 copy-done.10
  122.1 1.9 copy-done.24
  124.0 34.3 %route.2 = (f32[128,1536]{1,0:T(8,128)S(1)}, bf16[128,1536]{1,0:T(8,128)(2,1)S(1)}, f32[16,128]{1,0:T(8,128)S(1)}) custom-call(bf16[8,128,1536]{2,1,0:T(8,128)(2,1)S(1)} %copy-done.24, f32[128,1536]{1,0:T(8,128)S(1)} %copy-done.10, f32[36,1536]{1,0:T(8,128)S(1)} %convert_element_type.42.refs_2_.refs_3_.refs_4_.refs_6_, s32[2,8,128]{2,1,0:T(8,128)S(1)} %bitcast.32), custom_call_target="tpu_custom_call" | custom-call | tf_op jit(solution)/shard_map/route/pallas_call | solution.py:307
  160.6 69.5 %mix.2 = (f32[128,1536]{1,0:T(8,128)}, f32[128,1536]{1,0:T(8,128)}, bf16[128,1536]{1,0:T(8,128)(2,1)}, bf16[8,128,1536]{2,1,0:T(8,128)(2,1)}, f32[8,16,128]{2,1,0:T(8,128)}) custom-call(bf16[128,1536]{1,0:T(8,128)(2,1)} %copy-done.51, f32[16,128]{1,0:T(8,128)} %copy-done.58, f32[128,1536]{1,0:T(8,128)} %copy-done.20, f32[36,1536]{1,0:T(8,128)} %copy-done.1, ...), custom_call_target="tpu_custom_call" | custom-call | tf_op jit(solution)/shard_map/mix/pallas_call | solution.py:307
  231.0 35.6 %project.3 = (bf16[8,3,128,128]{3,2,1,0:T(8,128)(2,1)S(1)}, bf16[8,128,128]{2,1,0:T(8,128)(2,1)S(1)}, bf16[8,128,128]{2,1,0:T(8,128)(2,1)S(1)}, bf16[8,128,1536]{2,1,0:T(8,128)(2,1)S(1)}) custom-call(bf16[128,1536]{1,0:T(8,128)(2,1)S(1)} %copy-done.49, bf16[2,1536,384]{2,1,0:T(8,128)(2,1)S(1)} %bitcast.26, f32[8,64,128]{2,1,0:T(8,128)S(1)} %copy-done.7), custom_call_target="tpu_custom_call" | custom-call | tf_op jit(solution)/shard_map/project/pallas_call | solution.py:307
  266.6 1.7 copy-done.16
  270.6 19.8 %attend.3 = (bf16[8,128,256]{2,1,0:T(8,128)(2,1)}, f32[8,384,1]{2,1,0:T(8,128)}, bf16[8,128,1536]{2,1,0:T(8,128)(2,1)}) custom-call(s32[9]{0:T(128)} %pad_add_fusion.info_ref, bf16[8,3,128,128]{3,2,1,0:T(8,128)(2,1)} %copy-done.23, bf16[8,128,128]{2,1,0:T(8,128)(2,1)} %copy-done.34, bf16[8,128,128]{2,1,0:T(8,128)(2,1)} %copy-done.35, ...), custom_call_target="tpu_custom_call" | custom-call | tf_op jit(solution)/shard_map/attend/pallas_call | solution.py:1329
  290.4 1.9 copy-done.25
  292.3 33.0 %route.3 = (f32[128,1536]{1,0:T(8,128)S(1)}, bf16[128,1536]{1,0:T(8,128)(2,1)S(1)}, f32[16,128]{1,0:T(8,128)S(1)}) custom-call(bf16[8,128,1536]{2,1,0:T(8,128)(2,1)S(1)} %copy-done.25, f32[128,1536]{1,0:T(8,128)S(1)} %copy-done.26, f32[36,1536]{1,0:T(8,128)S(1)} %copy-done.2, s32[2,8,128]{2,1,0:T(8,128)S(1)} %bitcast.33), custom_call_target="tpu_custom_call" | custom-call | tf_op jit(solution)/shard_map/route/pallas_call | solution.py:307
  327.5 69.4 %mix.3 = (f32[128,1536]{1,0:T(8,128)}, f32[128,1536]{1,0:T(8,128)}, bf16[128,1536]{1,0:T(8,128)(2,1)}, bf16[8,128,1536]{2,1,0:T(8,128)(2,1)}, f32[8,16,128]{2,1,0:T(8,128)}) custom-call(bf16[128,1536]{1,0:T(8,128)(2,1)} %copy-done.52, f32[16,128]{1,0:T(8,128)} %copy-done.59, f32[128,1536]{1,0:T(8,128)} %copy-done.21, f32[36,1536]{1,0:T(8,128)} %copy-done.1, ...), custom_call_target="tpu_custom_call" | custom-call | tf_op jit(solution)/shard_map/mix/pallas_call | solution.py:307
  397.0 1.3 multiply_reduce_fusion
  398.9 77.4 %mix_back.2 = (f32[128,1536]{1,0:T(8,128)}, bf16[128,1536]{1,0:T(8,128)(2,1)}, f32[1,1536]{1,0:T(1,128)}, bf16[4608,512]{1,0:T(8,128)(2,1)}, f32[2,1536]{1,0:T(2,128)}) custom-call(bf16[128,1536]{1,0:T(8,128)(2,1)} %refs_0_.1, f32[8,128]{1,0:T(8,128)} %broadcast_in_dim.37.refs_1_, bf16[8,128,1536]{2,1,0:T(8,128)(2,1)} %get-tuple-element.115.refs_2_, ...), custom_call_target="tpu_custom_call" | custom-call | tf_op jit(solution)/shard_map/mix_back/pallas_call | solution.py:307
  477.4 35.5 %branch_back.2 = (bf16[8,128,256]{2,1,0:T(8,128)(2,1)S(1)}, bf16[96,1536]{1,0:T(8,128)(2,1)S(1)}) custom-call(bf16[128,1536]{1,0:T(8,128)(2,1)S(1)} %copy-done.48, bf16[2,2,96,1536]{3,2,1,0:T(8,128)(2,1)S(1)} %copy-done.5, bf16[8,128,256]{2,1,0:T(8,128)(2,1)S(1)} %copy-done.29), custom_call_target="tpu_custom_call" | custom-call | tf_op jit(solution)/shard_map/branch_back/pallas_call | solution.py:307
  514.4 23.3 %attend_back.2 = (bf16[8,128,256]{2,1,0:T(8,128)(2,1)}, f32[8,128,128]{2,1,0:T(8,128)}, bf16[8,128,128]{2,1,0:T(8,128)(2,1)}) custom-call(s32[9]{0:T(128)} %pad_add_fusion.info_ref, bf16[8,3,128,128]{3,2,1,0:T(8,128)(2,1)} %copy-done.23, bf16[8,128,128]{2,1,0:T(8,128)(2,1)} %copy-done.34, bf16[8,128,128]{2,1,0:T(8,128)(2,1)} %copy-done.35, ...), custom_call_target="tpu_custom_call" | custom-call | tf_op jit(solution)/shard_map/attend_back/pallas_call | solution.py:1418
  537.8 1.9 copy-done.17
  539.7 1.1 copy-done.18
  540.8 1.1 copy-done.27
  542.0 1.1 copy-done.38
  543.1 1.0 copy-done.43
  544.1 1.0 copy-done.44
  546.1 39.0 %join.2 = (f32[128,1536]{1,0:T(8,128)S(1)}, bf16[128,1536]{1,0:T(8,128)(2,1)S(1)}, f32[8,128]{1,0:T(8,128)S(1)}, bf16[1536,384]{1,0:T(8,128)(2,1)S(1)}) custom-call(bf16[8,128,256]{2,1,0:T(8,128)(2,1)S(1)} %copy-done.43, f32[8,128,128]{2,1,0:T(8,128)S(1)} %copy-done.44, bf16[8,128,128]{2,1,0:T(8,128)(2,1)S(1)} %copy-done.54, f32[8,64,128]{2,1,0:T(8,128)S(1)} %copy-done.8, ...), custom_call_target="tpu_custom_call" | custom-call | tf_op jit(solution)/shard_map/join/pallas_call | solution.py:307
  585.1 1.0 copy-done.12
  588.4 82.4 %mix_back.3 = (f32[128,1536]{1,0:T(8,128)}, bf16[128,1536]{1,0:T(8,128)(2,1)}, f32[1,1536]{1,0:T(1,128)}, bf16[4608,512]{1,0:T(8,128)(2,1)}, f32[2,1536]{1,0:T(2...) custom-call(bf16[128,1536]{1,0:T(8,128)(2,1)} %copy-done.50, f32[8,128]{1,0:T(8,128)} %copy-done.62, ...), custom_call_target="tpu_custom_call" | custom-call | tf_op jit(solution)/shard_map/mix_back/pallas_call | solution.py:307
  670.7 1.0 collective-permute-start.5
  671.8 2.0 add_bitcast_fusion
  674.8 36.0 %branch_back.3 = (bf16[8,128,256]{2,1,0:T(8,128)(2,1)S(1)}, bf16[96,1536]{1,0:T(8,128)(2,1)}) custom-call(bf16[128,1536]{1,0:T(8,128)(2,1)S(1)} %copy-done.47, bf16[2,2,96,1536]{3,2,1,0:T(8,128)(2,1)S(1)} %copy-done.6, bf16[8,128,256]{2,1,0:T(8,128)(2,1)S(1)} %copy-done.28), custom_call_target="tpu_custom_call" | custom-call | tf_op jit(solution)/shard_map/branch_back/pallas_call | solution.py:307
  712.3 23.3 %attend_back.3 = (bf16[8,128,256]{2,1,0:T(8,128)(2,1)}, f32[8,128,128]{2,1,0:T(8,128)}, bf16[8,128,128]{2,1,0:T(8,128)(2,1)}) custom-call(s32[9]{0:T(128)} %pad_add_fusion.info_ref, bf16[8,3,128,128]{3,2,1,0:T(8,128)(2,1)} %copy-done.22, bf16[8,128,128]{2,1,0:T(8,128)(2,1)} %copy-done.32, bf16[8,128,128]{2,1,0:T(8,128)(2,1)} %copy-done.33, ...), custom_call_target="tpu_custom_call" | custom-call | tf_op jit(solution)/shard_map/attend_back/pallas_call | solution.py:1418
  735.6 1.1 copy-done.11
  736.8 1.9 copy-done.15
  738.7 1.1 copy-done.19
  739.8 1.1 copy-done.37
  740.9 1.0 copy-done.41
  742.0 1.0 copy-done.42
  744.0 39.7 %join.3 = (f32[128,1536]{1,0:T(8,128)S(1)}, bf16[128,1536]{1,0:T(8,128)(2,1)}, f32[8,128]{1,0:T(8,128)}, bf16[1536,384]{1,0:T(8,128)(2,1)S(1)}) custom-call(bf16[8,128,256]{2,1,0:T(8,128)(2,1)S(1)} %copy-done.41, f32[8,128,128]{2,1,0:T(8,128)S(1)} %copy-done.42, bf16[8,128,128]{2,1,0:T(8,128)(2,1)S(1)} %copy-done.53, f32[8,64,128]{2,1,0:T(8,128)S(1)} %copy-done.9, ...), custom_call_target="tpu_custom_call" | custom-call | tf_op jit(solution)/shard_map/join/pallas_call | solution.py:307
  783.7 38.3 %finish_heads.1 = (f32[2,96,1536]{2,1,0:T(8,128)S(1)}, f32[2,96,512]{2,1,0:T(8,128)S(1)}, f32[2,96,512]{2,1,0:T(8,128)S(1)}, f32[2,8,96,128]{3,2,1,0:T(8,128)S(1)}) custom-call(bf16[8,2,96,384]{3,2,1,0:T(8,128)(2,1)S(1)} %bitcast.31, bf16[8,2,96,384]{3,2,1,0:T(8,128)(2,1)S(1)} %bitcast.30, bf16[8,2,96,384]{3,2,1,0:T(8,128)(2,1)S(1)} %copy-done.30), custom_call_target="tpu_custom_call" | custom-call | tf_op jit(solution)/shard_map/finish_heads/pallas_call | solution.py:1206
  823.1 12.7 %add_experts.1 = (f32[2,1,1536,512]{3,2,1,0:T(8,128)}, f32[2,1,1536,512]{3,2,1,0:T(8,128)}, f32[2,1,512,1536]{3,2,1,0:T(8,128)}) custom-call(bf16[4608,512]{1,0:T(8,128)(2,1)} %get-tuple-element.154.refs_0_.refs_1_.refs_2_.refs_3_.refs_4_, bf16[4608,512]{1,0:T(8,128)(2,1)} %get-tuple-element.154.refs_0_.refs_1_.refs_2_.refs_3_.refs_4_, ...), custom_call_target="tpu_custom_call" | custom-call | tf_op jit(solution)/shard_map/add_experts/pallas_call | solution.py:1254
  836.9 1.1 add_bitcast_fusion.1
  838.0 1.1 pad_maximum_fusion
  840.8 1.0 copy.102
  (178 shorter events, 33.7 us)
Async XLA Ops:
  0.6 2.8 copy-start.66
  1.8 2.4 copy-start.74
  1.8 3.3 copy-start.71
  1.9 3.3 copy-start.72
  1.9 3.2 copy-start.73
  5.7 38.9 %copy-start.70 = (s32[1,2048]{1,0:T(1,128)S(1)}, s32[1,2048]{1,0:T(1,128)}, u32[]{:S(2)}) copy-start(s32[1,2048]{1,0:T(1,128)} %param.18) | copy-start | bytes 24580
  7.2 38.7 %copy-start.63 = (bf16[128,1536]{1,0:T(8,128)(2,1)S(1)}, bf16[128,1536]{1,0:T(8,128)(2,1)}, u32[]{:S(2)}) copy-start(bf16[128,1536]{1,0:T(8,128)(2,1)} %param.15) | copy-start | bytes 1179652
  41.9 118.7 %collective-permute-start = (bf16[2,1,1536,512]{3,2,1,0:T(8,128)(2,1)}, bf16[2,1,1536,512]{3,2,1,0:T(8,128)(2,1)}, u32[]{:S(2)}, u32[]{:S(2)}) collective-permute-start(bf16[2,1,1536,512]{3,2,1,0:T(8,128)(2,1)} %refs_7_.1), channel_id=1, source_target_pairs={{0,1},{1,0},{2,3},{3,2},{4,5},{5,4},{6,7},{7,6},{8,9},{9,8},{10,11... | collective-permute-start | bytes 9437192 | tf_op jit(solution)/shard_map/ppermute | solution.py:1476
  42.3 118.2 %collective-permute-start.1 = (bf16[2,1,1536,512]{3,2,1,0:T(8,128)(2,1)}, bf16[2,1,1536,512]{3,2,1,0:T(8,128)(2,1)}, u32[]{:S(2)}, u32[]{:S(2)}) collective-permute-start(bf16[2,1,1536,512]{3,2,1,0:T(8,128)(2,1)} %refs_8_.1), channel_id=1, source_target_pairs={{0,1},{1,0},{2,3},{3,2},{4,5},{5,4},{6,7},{7,6},{8,9},{9,8},{10,11... | collective-permute-start | bytes 9437192 | tf_op jit(solution)/shard_map/ppermute | solution.py:1476
  42.5 118.1 %collective-permute-start.2 = (bf16[2,1,512,1536]{3,2,1,0:T(8,128)(2,1)}, bf16[2,1,512,1536]{3,2,1,0:T(8,128)(2,1)}, u32[]{:S(2)}, u32[]{:S(2)}) collective-permute-start(bf16[2,1,512,1536]{3,2,1,0:T(8,128)(2,1)} %refs_9_.1), channel_id=1, source_target_pairs={{0,1},{1,0},{2,3},{3,2},{4,5},{5,4},{6,7},{7,6},{8,9},{9,8},{10,11... | collective-permute-start | bytes 9437192 | tf_op jit(solution)/shard_map/ppermute | solution.py:1476
  43.9 6.3 copy-start
  43.9 6.3 copy-start.7
  47.0 73.9 %copy-start.1 = (f32[36,1536]{1,0:T(8,128)}, f32[36,1536]{1,0:T(8,128)S(1)}, u32[]{:S(2)}) copy-start(f32[36,1536]{1,0:T(8,128)S(1)} %convert_element_type.42.refs_2_.refs_3_.refs_4_.refs_6_) | copy-start | bytes 663556
  49.1 51.7 %copy-start.69 = (s32[8,1,128]{2,1,0:T(1,128)S(1)}, s32[8,1,128]{2,1,0:T(1,128)}, u32[]{:S(2)}) copy-start(s32[8,1,128]{2,1,0:T(1,128)} %copy-done.68) | copy-start | bytes 12292
  50.2 70.8 %copy-start.55 = (s32[2,128,8]{1,2,0:T(8,128)S(1)}, s32[2,128,8]{1,2,0:T(8,128)}, u32[]{:S(2)}) copy-start(s32[2,128,8]{1,2,0:T(8,128)} %param.19) | copy-start | bytes 24580
  96.9 1.7 copy-start.14
  121.0 1.1 copy-start.10
  122.1 1.9 copy-start.24
  231.0 59.3 %copy-start.2 = (f32[36,1536]{1,0:T(8,128)S(1)}, f32[36,1536]{1,0:T(8,128)}, u32[]{:S(2)}) copy-start(f32[36,1536]{1,0:T(8,128)} %copy-done.1) | copy-start | bytes 663556
  266.6 1.7 copy-start.16
  270.6 19.8 %copy-start.26 = (f32[128,1536]{1,0:T(8,128)S(1)}, f32[128,1536]{1,0:T(8,128)}, u32[]{:S(2)}) copy-start(f32[128,1536]{1,0:T(8,128)} %get-tuple-element.105.refs_1_.refs_8_) | copy-start | bytes 2359300
  290.4 1.9 copy-start.25
  327.5 69.4 %copy-start.64 = (bf16[128,1536]{1,0:T(8,128)(2,1)S(1)}, bf16[128,1536]{1,0:T(8,128)(2,1)}, u32[]{:S(2)}) copy-start(bf16[128,1536]{1,0:T(8,128)(2,1)} %refs_0_.1) | copy-start | bytes 1179652
  398.9 77.5 %copy-start.5 = (bf16[2,2,96,1536]{3,2,1,0:T(8,128)(2,1)S(1)}, bf16[2,2,96,1536]{3,2,1,0:T(8,128)(2,1)}, u32[]{:S(2)}) copy-start(bf16[2,2,96,1536]{3,2,1,0:T(8,128)(2,1)} %get-tuple-element.92.w_ref.refs_1_) | copy-start | bytes 3538948
  398.9 77.5 %copy-start.29 = (bf16[8,128,256]{2,1,0:T(8,128)(2,1)S(1)}, bf16[8,128,256]{2,1,0:T(8,128)(2,1)}, u32[]{:S(2)}) copy-start(bf16[8,128,256]{2,1,0:T(8,128)(2,1)} %get-tuple-element.112.refs_2_.att_ref) | copy-start | bytes 1572868
  476.3 197.5 %collective-permute-start.3 = (bf16[4608,512]{1,0:T(8,128)(2,1)}, bf16[4608,512]{1,0:T(8,128)(2,1)}, u32[]{:S(2)}, u32[]{:S(2)}) collective-permute-start(bf16[4608,512]{1,0:T(8,128)(2,1)} %get-tuple-element.155.refs_10_.refs_11_.refs_12_.refs_13_.refs_14_), channel_id=1, source_target_pairs={{0,16},{16,0},{1,17},{17,1},{2,18},{18,2},{3,19},{19,3},{4,20},{20... | collective-permute-start | bytes 14155784 | tf_op jit(solution)/shard_map/ppermute | solution.py:1525
  514.4 23.3 %copy-start.3 = (f32[36,1536]{1,0:T(8,128)S(1)}, f32[36,1536]{1,0:T(8,128)}, u32[]{:S(2)}) copy-start(f32[36,1536]{1,0:T(8,128)} %copy-done.1) | copy-start | bytes 663556
  514.4 23.3 %copy-start.8 = (f32[8,64,128]{2,1,0:T(8,128)S(1)}, f32[8,64,128]{2,1,0:T(8,128)}, u32[]{:S(2)}) copy-start(f32[8,64,128]{2,1,0:T(8,128)} %get-tuple-element.88.refs_2_.table_ref.refs_3_) | copy-start | bytes 786436
  514.4 23.4 %copy-start.57 = (f32[2,1536]{1,0:T(2,128)S(1)}, f32[2,1536]{1,0:T(2,128)}, u32[]{:S(2)}) copy-start(f32[2,1536]{1,0:T(2,128)} %get-tuple-element.125.refs_10_) | copy-start | bytes 36868
  514.4 23.4 %copy-start.61 = (f32[1,1536]{1,0:T(1,128)S(1)}, f32[1,1536]{1,0:T(1,128)}, u32[]{:S(2)}) copy-start(f32[1,1536]{1,0:T(1,128)} %get-tuple-element.126.refs_11_) | copy-start | bytes 18436
  537.8 1.9 copy-start.17
  539.7 1.1 copy-start.18
  588.3 85.4 %copy-start.6 = (bf16[2,2,96,1536]{3,2,1,0:T(8,128)(2,1)S(1)}, bf16[2,2,96,1536]{3,2,1,0:T(8,128)(2,1)}, u32[]{:S(2)}) copy-start(bf16[2,2,96,1536]{3,2,1,0:T(8,128)(2,1)} %get-tuple-element.92.w_ref.refs_1_) | copy-start | bytes 3538948
  588.4 85.4 %copy-start.28 = (bf16[8,128,256]{2,1,0:T(8,128)(2,1)S(1)}, bf16[8,128,256]{2,1,0:T(8,128)(2,1)}, u32[]{:S(2)}) copy-start(bf16[8,128,256]{2,1,0:T(8,128)(2,1)} %get-tuple-element.110.refs_2_.att_ref) | copy-start | bytes 1572868
  670.7 152.4 %collective-permute-start.5 = (bf16[4608,512]{1,0:T(8,128)(2,1)}, bf16[4608,512]{1,0:T(8,128)(2,1)}, u32[]{:S(2)}, u32[]{:S(2)}) collective-permute-start(bf16[4608,512]{1,0:T(8,128)(2,1)} %get-tuple-element.154.refs_0_.refs_1_.refs_2_.refs_3_.refs_4_), channel_id=1, source_target_pairs={{0,16},{16,0},{1,17},{17,1},{2,18},{18,2},{3,19},{19,3},{4,20},{20... | collective-permute-start | bytes 14155784 | tf_op jit(solution)/shard_map/ppermute | solution.py:1525
  711.6 125.4 %collective-permute-start.4 = (bf16[96,1536]{1,0:T(8,128)(2,1)}, bf16[96,1536]{1,0:T(8,128)(2,1)}, u32[]{:S(2)}, u32[]{:S(2)}) collective-permute-start(bf16[96,1536]{1,0:T(8,128)(2,1)} %get-tuple-element.152), channel_id=1, source_target_pairs={{0,16},{16,0},{1,17},{17,1},{2,18},{18,2},{3,19},{19,3},{4,20},{20... | collective-permute-start | bytes 884744 | tf_op jit(solution)/shard_map/ppermute | solution.py:1525
  712.3 23.3 %copy-start.4 = (f32[36,1536]{1,0:T(8,128)S(1)}, f32[36,1536]{1,0:T(8,128)}, u32[]{:S(2)}) copy-start(f32[36,1536]{1,0:T(8,128)} %copy-done.1) | copy-start | bytes 663556
  712.3 23.3 %copy-start.9 = (f32[8,64,128]{2,1,0:T(8,128)S(1)}, f32[8,64,128]{2,1,0:T(8,128)}, u32[]{:S(2)}) copy-start(f32[8,64,128]{2,1,0:T(8,128)} %get-tuple-element.88.refs_2_.table_ref.refs_3_) | copy-start | bytes 786436
  712.3 23.3 %copy-start.56 = (f32[2,1536]{1,0:T(2,128)S(1)}, f32[2,1536]{1,0:T(2,128)}, u32[]{:S(2)}) copy-start(f32[2,1536]{1,0:T(2,128)} %get-tuple-element.143.refs_10_) | copy-start | bytes 36868
  712.3 23.4 %copy-start.60 = (f32[1,1536]{1,0:T(1,128)S(1)}, f32[1,1536]{1,0:T(1,128)}, u32[]{:S(2)}) copy-start(f32[1,1536]{1,0:T(1,128)} %get-tuple-element.144.refs_11_) | copy-start | bytes 18436
  735.6 1.1 copy-start.11
  736.8 1.9 copy-start.15
  744.0 39.7 %copy-start.13 = (bf16[1536,384]{1,0:T(8,128)(2,1)S(1)}, bf16[1536,384]{1,0:T(8,128)(2,1)}, u32[]{:S(2)}) copy-start(bf16[1536,384]{1,0:T(8,128)(2,1)} %copy-done.12) | copy-start | bytes 3538948
  744.0 39.8 %copy-start.30 = (bf16[8,2,96,384]{3,2,1,0:T(8,128)(2,1)S(1)}, bf16[8,2,96,384]{3,2,1,0:T(8,128)(2,1)}, u32[]{:S(2)}) copy-start(bf16[8,2,96,384]{3,2,1,0:T(8,128)(2,1)} %get-tuple-element.147.refs_2_) | copy-start | bytes 3538948
  783.7 38.6 %copy-start.39 = (f32[128,1536]{1,0:T(8,128)}, f32[128,1536]{1,0:T(8,128)S(1)}, u32[]{:S(2)}) copy-start(f32[128,1536]{1,0:T(8,128)S(1)} %get-tuple-element.177) | copy-start | bytes 2359300
  835.8 2.2 copy-start.65
  835.8 3.3 copy-start.67
  836.1 3.8 copy-start.40
  (33 other events, 29.2 us)

commit v5 on v4

--- a/solution.py
+++ b/solution.py
@@ -13,6 +13,7 @@
 LAYERS = 2
 GROUP = HEADS // KV_HEADS
 LANES = 128
+PAIR = 2
 EPS = 1e-06
 MASKED = -1e30
 MESH = pl.DeviceIdType.MESH
@@ -78,9 +79,9 @@
 
 
 class Ring:
-    def __init__(self, count, riders=()):
+    def __init__(self, count, traffic):
         self.count = count
-        self.riders = riders
+        self.riders, self.early, self.late = traffic
         self.steps = count // 2
         self.chip, self.at, self.near = ring_setup(count)
 
@@ -89,6 +90,12 @@
         meet(others + ([partner_of("rep")] if self.riders else []))
         for rider in self.riders:
             rider.start()
+        for copy in self.early:
+            copy.wait()
+
+    def settle(self):
+        for copy in self.late:
+            copy.wait()
 
     def gather(self, x_ref, buf, sems, side=None, first=None, second=None):
         own_sem, send_sem, recv_sem = sems[:3]
@@ -281,8 +288,10 @@
     return dmas((2, 2, count // 2), (2, 2, count // 2))
 
 
-ANYWHERE = pl.BlockSpec(memory_space=pl.ANY)
+ANYWHERE = pl.BlockSpec(memory_space=pltpu.HBM)
 HERE = pl.BlockSpec(memory_space=pltpu.VMEM)
+EARLY, LATE = "early", "late"
+OUT = "out"
 
 
 FREE = pl.CostEstimate(flops=0, bytes_accessed=0, transcendentals=0)
@@ -290,26 +299,58 @@
 
 def ring_call(body, key, inputs, outputs, scratch, megabytes, rides=()):
     n_in, n_out, n_rides = len(inputs), len(outputs), len(rides)
+    in_kinds = [kind for _, kind in inputs]
+    out_kinds = [kind for _, kind in outputs]
+    copied = [a for a, kind in inputs if kind in (EARLY, LATE)]
+    returned = [a for a, kind in outputs if kind == OUT]
+    moves = len(copied) + len(returned)
 
     def kernel(*refs):
         ins, ride_in, outs, ride_out, rest = split(refs, n_in, n_rides, n_out, n_rides)
+        rest, own, rest_sems = rest[: len(scratch)], rest[len(scratch) : len(scratch) + moves], rest[len(scratch) + moves :]
+        move_sem, rest_sems = rest_sems[0], rest_sems[1:]
         riders = []
         if n_rides:
-            *rest, send_sem, recv_sem = rest
+            send_sem, recv_sem = rest_sems
             riders = [
                 remote(ride_in[i], ride_out[i], send_sem.at[i], recv_sem.at[i], partner_of("rep"))
                 for i in range(n_rides)
             ]
-        body(riders, *ins, *outs, *rest)
+        used = 0
+        early, late, leaving = [], [], []
+        ins, outs = list(ins), list(outs)
+        for i, kind in enumerate(in_kinds):
+            if kind in (EARLY, LATE):
+                copy = pltpu.make_async_copy(ins[i], own[used], move_sem.at[used])
+                copy.start()
+                (early if kind == EARLY else late).append(copy)
+                ins[i] = own[used]
+                used += 1
+        for i, kind in enumerate(out_kinds):
+            if kind == OUT:
+                leaving.append(pltpu.make_async_copy(own[used], outs[i], move_sem.at[used]))
+                outs[i] = own[used]
+                used += 1
+        body((riders, early, late), *ins, *outs, *rest)
+        for copy in leaving:
+            copy.start()
         for rider in riders:
             rider.wait()
+        for copy in leaving:
+            copy.wait()
+
+    def spec(kind):
+        return ANYWHERE if isinstance(kind, str) else kind
 
     return pl.pallas_call(
         kernel,
         out_shape=tuple(shape for shape, _ in outputs) + tuple(cells(a.shape, a.dtype) for a in rides),
-        in_specs=[spec for _, spec in inputs] + [ANYWHERE] * n_rides,
-        out_specs=[spec for _, spec in outputs] + [ANYWHERE] * n_rides,
-        scratch_shapes=list(scratch) + (dmas((n_rides,), (n_rides,)) if n_rides else []),
+        in_specs=[spec(kind) for kind in in_kinds] + [ANYWHERE] * n_rides,
+        out_specs=[spec(kind) for kind in out_kinds] + [ANYWHERE] * n_rides,
+        scratch_shapes=list(scratch)
+        + [pltpu.VMEM(a.shape, a.dtype) for a in copied + returned]
+        + dmas((max(moves, 1),))
+        + (dmas((n_rides,), (n_rides,)) if n_rides else []),
         compiler_params=pltpu.CompilerParams(
             collective_id=identity(key),
             has_side_effects=True,
@@ -544,22 +585,26 @@
     return slice(first, first + experts)
 
 
-def project_kernel(count, layer, riders, *refs):
+def project_kernel(count, layer, traffic, *refs):
     inputs, outputs, scratch = split(refs, 3, 4)
     x_ref, w_ref, table_ref = inputs
     q_ref, own_ref, other_ref, all_ref = outputs
-    buf, weights = scratch[:2]
-    sems, pair_sems, out_sem, load_sem = split(scratch[2:], 3, 2, 1)
-    ring = Ring(count, riders)
+    buf, weights, q_buf, own_buf = scratch[:4]
+    sems, pair_sems, out_sem, load_sem = split(scratch[4:], 3, 2, 1)
+    ring = Ring(count, traffic)
     load = pltpu.make_async_copy(w_ref.at[layer], weights, load_sem[0].at[0])
     load.start()
     ring.meet(True)
     partner = partner_of("fsdp")
 
     def pass_on(block):
-        return remote(
-            own_ref.at[block], other_ref.at[block], pair_sems[0].at[block], pair_sems[1].at[block], partner
-        )
+        return [
+            remote(
+                own_buf.at[block], other_ref.at[block], pair_sems[0].at[block], pair_sems[1].at[block], partner
+            ),
+            pltpu.make_async_copy(own_buf.at[block], own_ref.at[block], out_sem[0].at[0, block]),
+            pltpu.make_async_copy(q_buf.at[block], q_ref.at[block], out_sem[0].at[1, block]),
+        ]
 
     def compute(place, blocks):
         rows = dot(stack(buf, blocks), weights[...])
@@ -569,10 +614,11 @@
         heads, pair = project_rows(rows, cosine, sine)
         for index, head in enumerate(heads):
             for block, part in cut(head, blocks):
-                q_ref[block, index] = part
+                q_buf[block, index] = part
         for block, part in cut(pair, blocks):
-            own_ref[block] = part
-            pass_on(block).start()
+            own_buf[block] = part
+            for copy in pass_on(block):
+                copy.start()
 
     def first(s):
         @pl.when(s == 1)
@@ -580,46 +626,54 @@
             load.wait()
 
     drain = ring.gather(x_ref, buf, sems, None, first, ring.meanwhile(compute, 0))
-    keep = pltpu.make_async_copy(buf, all_ref, out_sem[0].at[0])
+    keep = pltpu.make_async_copy(buf, all_ref, out_sem[0].at[2, 0])
     keep.start()
     compute(0, (ring.at(ring.steps),))
     drain()
     for block in range(count):
-        pass_on(block).wait()
+        for copy in pass_on(block):
+            copy.wait()
     keep.wait()
 
 
 def gather_project(count, layer, x, w, tables):
     rows, width = x.shape
     block = cells((count, rows, LANES), BF16)
+    queries = (count, GROUP, rows, LANES)
     return ring_call(
         functools.partial(project_kernel, count, layer),
         ("project", layer),
-        [(x, ANYWHERE), (w, ANYWHERE), (tables, HERE)],
+        [(x, ANYWHERE), (w, ANYWHERE), (tables, EARLY)],
         [
-            (cells((count, GROUP, rows, LANES), BF16), HERE),
-            (block, HERE),
-            (block, HERE),
+            (cells(queries, BF16), ANYWHERE),
+            (block, ANYWHERE),
+            (block, ANYWHERE),
             (cells((count, rows, width), BF16), ANYWHERE),
         ],
-        [pltpu.VMEM((count, rows, width), BF16), pltpu.VMEM(w.shape[1:], BF16)]
+        [
+            pltpu.VMEM((count, rows, width), BF16),
+            pltpu.VMEM(w.shape[1:], BF16),
+            pltpu.VMEM(queries, BF16),
+            pltpu.VMEM(block.shape, BF16),
+        ]
         + gather_sems(count)
-        + dmas((count,), (count,), (1,), (1,)),
+        + dmas((count,), (count,), (3, count), (1,)),
         20,
     )
 
 
-def route_kernel(count, layer, riders, *refs):
+def route_kernel(count, layer, traffic, *refs):
     inputs, outputs, scratch = split(refs, 4, 3)
     p_ref, hidden_ref, params_ref, routes_ref = inputs
     middle_ref, x_ref, share_ref = outputs
     partial, land = scratch[:2]
     sems, load_sem = split(scratch[2:], 2)
-    ring = Ring(count, riders)
+    ring = Ring(count, traffic)
     load = pltpu.make_async_copy(p_ref, partial, load_sem[0].at[0])
     load.start()
     ring.meet()
     added, drain = ring.scatter(partial, land, sems, None, p_ref, load.wait)
+    ring.settle()
     middle = hidden_ref[...] + added
     middle_ref[...] = middle
     x = (normal(middle)[1] * gain_row(params_ref, 1, layer)).astype(BF16)
@@ -642,11 +696,11 @@
     return ring_call(
         functools.partial(route_kernel, count, layer),
         ("route", layer),
-        [(partial, ANYWHERE), (hidden, HERE), (params, HERE), (routes, HERE)],
+        [(partial, ANYWHERE), (hidden, LATE), (params, LATE), (routes, LATE)],
         [
-            (cells((rows, width), F32), HERE),
-            (cells((rows, width), BF16), HERE),
-            (cells((experts, rows), F32), HERE),
+            (cells((rows, width), F32), OUT),
+            (cells((rows, width), BF16), OUT),
+            (cells((experts, rows), F32), OUT),
         ],
         [pltpu.VMEM(partial.shape, BF16), land_scratch(count, rows, width)]
         + scatter_sems(count)
@@ -688,13 +742,13 @@
     return first
 
 
-def mix_kernel(count, layer, riders, *refs):
+def mix_kernel(count, layer, traffic, *refs):
     inputs, outputs, scratch = split(refs, 10, 5)
     x_ref, side_ref, middle_ref, params_ref = inputs[:4]
     mixed_ref, hidden_ref, next_ref, all_ref, share_ref = outputs
     buf, partial, land, acc, gates, ups, downs = scratch[:7]
     sems, scatter_sem, load_sem, out_sem = split(scratch[7:], 5, 2, 1)
-    ring = Ring(count, riders)
+    ring = Ring(count, traffic)
     loads = load_experts(inputs[4:], layer, gates, ups, downs, load_sem[0])
     ring.meet()
 
@@ -719,6 +773,7 @@
     for e in range(2):
         compute(e, (ring.at(ring.steps),))
     mixed, finish = ring.scatter(partial, land, scatter_sem)
+    ring.settle()
     mixed_ref[...] = mixed
     hidden = middle_ref[...] + mixed
     hidden_ref[...] = hidden
@@ -746,14 +801,14 @@
     return ring_call(
         functools.partial(mix_kernel, count, layer),
         ("mix", layer),
-        [(x, ANYWHERE), (share, ANYWHERE), (middle, HERE), (params, HERE)]
+        [(x, ANYWHERE), (share, ANYWHERE), (middle, LATE), (params, LATE)]
         + [(w, ANYWHERE) for w in weights],
         [
-            (own, HERE),
-            (own, HERE),
-            (cells((rows, width), BF16), HERE),
+            (own, OUT),
+            (own, OUT),
+            (cells((rows, width), BF16), OUT),
             (cells((count, rows, width), BF16), ANYWHERE),
-            (cells((count,) + share.shape, F32), HERE),
+            (cells((count,) + share.shape, F32), OUT),
         ],
         [everyone, everyone, land_scratch(count, rows, width), pltpu.VMEM((2 * rows, width), F32)]
         + expert_scratch(weights)
@@ -764,14 +819,14 @@
     )
 
 
-def mix_back_kernel(count, layer, riders, *refs):
+def mix_back_kernel(count, layer, traffic, *refs):
     inputs, outputs, scratch = split(refs, 13, 5)
     d_ref, side_ref, m_ref, share_ref, params_ref, grad_ref, middle_ref = inputs[:7]
     mid_ref, branch_ref, gain_ref, sum_ref, g_router_ref = outputs
     buf, partial, land, acc, gates, ups, downs = scratch[:7]
     tokens, acts, hiddens, balance_ref, totals, got = scratch[7:13]
     sems, scatter_sem, load_sem, pair_sem, out_sem = split(scratch[13:], 5, 2, 1, 2)
-    ring = Ring(count, riders)
+    ring = Ring(count, traffic)
     loads = load_experts(inputs[7:], layer, gates, ups, downs, load_sem[0])
     loads.append(pltpu.make_async_copy(m_ref, tokens, load_sem[0].at[6]))
     loads[-1].start()
@@ -891,6 +946,7 @@
                         copy.start()
 
     d_x, finish = ring.scatter(partial, land, scatter_sem, work)
+    ring.settle()
     d_values, gain_ref[...] = normal_back(d_x, middle_ref[...], gain_row(params_ref, 1, layer))
     grad = grad_ref[...] + d_values
     mid_ref[...] = grad
@@ -913,14 +969,14 @@
     return ring_call(
         functools.partial(mix_back_kernel, count, layer),
         ("mix_back", layer),
-        [(d, ANYWHERE), (side, ANYWHERE), (m_all, ANYWHERE), (share, HERE), (params, HERE), (grad, HERE), (middle, HERE)]
+        [(d, ANYWHERE), (side, ANYWHERE), (m_all, ANYWHERE), (share, EARLY), (params, EARLY), (grad, LATE), (middle, LATE)]
         + [(w, ANYWHERE) for w in weights],
         [
-            (own, HERE),
-            (cells((rows, width), BF16), HERE),
-            (cells((1, width), F32), HERE),
+            (own, OUT),
+            (cells((rows, width), BF16), OUT),
+            (cells((1, width), F32), OUT),
             (cells((3 * width, ff), BF16), ANYWHERE),
-            (cells((2, width), F32), HERE),
+            (cells((2, width), F32), OUT),
         ],
         [everyone, everyone, land_scratch(count, rows, width), pltpu.VMEM((2 * rows, width), F32)]
         + expert_scratch(weights)
@@ -940,13 +996,13 @@
     )
 
 
-def branch_back_kernel(count, layer, riders, *refs):
+def branch_back_kernel(count, layer, traffic, *refs):
     inputs, outputs, scratch = split(refs, 3, 2)
     d_ref, w_ref, att_ref = inputs
     datt_ref, g_ref = outputs
     buf, wide_w, acc, mail, got = scratch[:5]
     sems, pair_sem, load_sem = split(scratch[5:], 3, 2)
-    ring = Ring(count, riders)
+    ring = Ring(count, traffic)
     shard = g_ref.shape[0]
     loads = load_out_weights(w_ref, layer, wide_w, load_sem[0])
     ring.meet(True)
@@ -979,10 +1035,10 @@
     return ring_call(
         functools.partial(branch_back_kernel, count, layer),
         ("branch_back", layer),
-        [(d, ANYWHERE), (w, ANYWHERE), (att, HERE)],
+        [(d, ANYWHERE), (w, ANYWHERE), (att, EARLY)],
         [
-            (cells((count, rows, 2 * LANES), BF16), HERE),
-            (cells((shard, width), BF16), HERE),
+            (cells((count, rows, 2 * LANES), BF16), OUT),
+            (cells((shard, width), BF16), OUT),
         ],
         [
             pltpu.VMEM((count, rows, width), BF16),
@@ -1010,14 +1066,14 @@
     return copies
 
 
-def join_kernel(count, layer, riders, *refs):
-    inputs, outputs, scratch = split(refs, 13, 4)
+def join_kernel(count, layer, traffic, *refs):
+    inputs, outputs, scratch = split(refs, 12, 4)
     dq_ref, own_ref, other_ref, table_ref, w_ref, x_ref, params_ref, mid_ref, hidden_ref = inputs[:9]
     mixed_ref, router_ref, gain_two_ref = inputs[9:12]
     grad_ref, d_mix_ref, side_ref, g_ref = outputs
     partial, land, rows_ref, tokens, got, weights, last_ref = scratch[:7]
     scatter_sem, pair_sem, load_sem = split(scratch[7:], 2, 2)
-    ring = Ring(count, riders)
+    ring = Ring(count, traffic)
     loads = [
         pltpu.make_async_copy(x_ref, tokens, load_sem[0].at[0]),
         pltpu.make_async_copy(w_ref.at[layer], weights, load_sem[0].at[1]),
@@ -1062,6 +1118,7 @@
             last_ref[rows] = value[:, tile:]
 
     d_x, drain = ring.scatter(partial, land, scatter_sem, work)
+    ring.settle()
     d_values, gain_one = normal_back(d_x, hidden_ref[...], gain_row(params_ref, 0, layer))
     grad = mid_ref[...] + d_values
     grad_ref[...] = grad
@@ -1089,19 +1146,17 @@
 def join_scatter(count, layer, dq, own, other, tables, w, x_all, params, mid, hidden, mixed, g_router, gain_two):
     _, rows, width = x_all.shape
     everyone = pltpu.VMEM((count, rows, width), BF16)
-    here = [dq, own, other, tables]
     late = [params, mid, hidden, mixed, g_router, gain_two]
-    nothing = jnp.zeros((8, LANES), F32)
     return ring_call(
         functools.partial(join_kernel, count, layer),
         ("join", layer),
-        [(a, HERE) for a in here] + [(w, ANYWHERE), (x_all, ANYWHERE)] + [(a, HERE) for a in late]
-        + [(nothing, HERE)],
+        [(dq, EARLY), (own, EARLY), (other, ANYWHERE), (tables, EARLY), (w, ANYWHERE), (x_all, ANYWHERE)]
+        + [(a, LATE) for a in late],
         [
-            (cells((rows, width), F32), HERE),
-            (cells((rows, width), BF16), HERE),
-            (cells((8, rows), F32), HERE),
-            (cells(w.shape[1:], BF16), HERE),
+            (cells((rows, width), F32), OUT),
+            (cells((rows, width), BF16), OUT),
+            (cells((8, rows), F32), OUT),
+            (cells(w.shape[1:], BF16), OUT),
         ],
         [
             everyone,
@@ -1270,86 +1325,125 @@
     )(*arrays)
 
 
-def allowed_keys(begin, block, chunk, core):
-    shape = (GROUP * LANES, 2 * LANES)
-    place = lax.broadcasted_iota(jnp.int32, shape, 1)
+def chunk_keys(own_ref, other_ref, chunk):
+    return jnp.concatenate([own_ref[chunk], other_ref[chunk]], 0)
+
+
+def allowed_keys(begin, query, chunk, core):
+    shape = (2 * LANES, begin.shape[1])
+    place = lax.broadcasted_iota(jnp.int32, shape, 0)
     shift = jnp.where(place < LANES, core, -core)
     key = chunk * 2 * LANES + place + shift * LANES
-    query = block * LANES + lax.rem(lax.broadcasted_iota(jnp.int32, shape, 0), LANES)
     return (key >= begin) & (key <= query)
 
 
-def attend_kernel(layer, info_ref, q_ref, own_ref, other_ref, begin_ref, w_ref, att_ref, lse_ref, out_ref, wide_ref, sem):
+def block_info(info_ref, begin_ref):
     step = pl.program_id(0)
     core = info_ref[0]
-    block = 2 * step + core
-    first = info_ref[1 + step] // (2 * LANES)
-
-    @pl.when(step == 0)
+    lane = lax.broadcasted_iota(jnp.int32, (1, LANES), 1)
+    begin, query = [], []
+    for part in range(PAIR):
+        begin += [begin_ref[part]] * GROUP
+        query += [(2 * (PAIR * step + part) + core) * LANES + lane] * GROUP
+    first = info_ref[1 + PAIR * step] // (2 * LANES)
+    return core, jnp.concatenate(begin, 1), jnp.concatenate(query, 1), first, PAIR * (step + 1)
+
+
+def chunk_keys(own_ref, other_ref, chunk):
+    return jnp.concatenate([own_ref[chunk], other_ref[chunk]], 0)
+
+
+def turn_keys(own_ref, other_ref, turned_ref):
+    for chunk in range(turned_ref.shape[0]):
+        turned_ref[chunk] = chunk_keys(own_ref, other_ref, chunk).astype(F32).T.astype(BF16)
+
+
+def by_head(field):
+    return [field[:, h * LANES : (h + 1) * LANES].T for h in range(GROUP)]
+
+
+def attend_kernel(layer, info_ref, q_ref, own_ref, other_ref, begin_ref, w_ref, att_ref, lse_ref, out_ref, wide_ref, turned_ref, score_ref, sem):
+    core, begin, query, first, last = block_info(info_ref, begin_ref)
+    width = PAIR * GROUP * LANES
+
+    @pl.when(pl.program_id(0) == 0)
     def _():
-        for load in load_out_weights(w_ref, layer, wide_ref, sem):
+        loads = load_out_weights(w_ref, layer, wide_ref, sem)
+        turn_keys(own_ref, other_ref, turned_ref)
+        for load in loads:
             load.wait()
 
-    q = q_ref[0].reshape(GROUP * LANES, LANES)
-    begin = jnp.concatenate([begin_ref[0]] * GROUP, 0)
-
-    def one(chunk, state):
-        top, total, acc = state
-        keys = jnp.concatenate([own_ref[chunk], other_ref[chunk]], 0)
-        allowed = allowed_keys(begin, block, chunk, core)
-        scores = jnp.where(allowed, dot(q, keys, NT), MASKED)
-        new_top = jnp.maximum(top, jnp.max(scores, -1, keepdims=True))
-        weights = jnp.where(allowed, jnp.exp(scores - new_top), 0.0)
-        shrink = jnp.exp(top - new_top)
-        total = total * shrink + jnp.sum(weights, -1, keepdims=True)
-        return new_top, total, acc * shrink + dot(weights.astype(BF16), keys)
-
-    rows = GROUP * LANES
-    top, total, acc = lax.fori_loop(
-        first,
-        step + 1,
-        one,
-        (jnp.full((rows, 1), MASKED, F32), jnp.zeros((rows, 1), F32), jnp.zeros((rows, LANES), F32)),
+    q = q_ref[...].reshape(width, LANES)
+
+    def score(chunk, top):
+        keys = chunk_keys(own_ref, other_ref, chunk)
+        scores = jnp.where(allowed_keys(begin, query, chunk, core), dot(keys, q, NT), MASKED)
+        score_ref[chunk] = scores
+        return jnp.maximum(top, jnp.max(scores, 0, keepdims=True))
+
+    top = lax.fori_loop(first, last, score, jnp.full((1, width), MASKED, F32))
+
+    def add(chunk, state):
+        total, acc = state
+        weights = jnp.exp(score_ref[chunk] - top)
+        total = total + jnp.sum(weights, 0, keepdims=True)
+        return total, acc + dot(turned_ref[chunk], weights.astype(BF16))
+
+    total, acc = lax.fori_loop(
+        first, last, add, (jnp.zeros((1, width), F32), jnp.zeros((LANES, width), F32))
     )
-    lse_ref[0] = top + jnp.log(total)
+    lse = top + jnp.log(total)
     att = acc / total
-    heads = [att[h * LANES : (h + 1) * LANES] for h in range(GROUP)]
-    low = lanes_of(heads[0]) < HD
-    wide = jnp.concatenate(
-        [jnp.where(low, turn(heads[0]), heads[1]), jnp.where(low, turn(heads[2]), 0.0)], 1
-    ).astype(BF16)
-    att_ref[0] = wide
-    out_ref[0] = dot(wide, wide_ref[...]).astype(BF16)
+    rows = []
+    for part in range(PAIR):
+        here = slice(part * GROUP * LANES, (part + 1) * GROUP * LANES)
+        lse_ref[part] = lse[:, here]
+        heads = by_head(att[:, here])
+        low = lanes_of(heads[0]) < HD
+        rows.append(
+            jnp.concatenate(
+                [jnp.where(low, turn(heads[0]), heads[1]), jnp.where(low, turn(heads[2]), 0.0)], 1
+            ).astype(BF16)
+        )
+        att_ref[part] = rows[-1]
+    out = dot(jnp.concatenate(rows, 0), wide_ref[...]).astype(BF16)
+    for part in range(PAIR):
+        out_ref[part] = out[part * LANES : (part + 1) * LANES]
+
+
+def blocks_of(*shape):
+    return pl.BlockSpec((PAIR,) + shape, lambda i, s: (i,) + (0,) * len(shape))
 
 
 def attend(layer, info, q, own, other, begin, w):
     blocks = q.shape[0]
     width = w.shape[3]
     wide = 2 * LANES
+    whole = pl.BlockSpec(own.shape, lambda i, s: (0, 0, 0))
     return pl.pallas_call(
         functools.partial(attend_kernel, layer),
         grid_spec=pltpu.PrefetchScalarGridSpec(
             num_scalar_prefetch=1,
-            grid=(blocks,),
+            grid=(blocks // PAIR,),
             in_specs=[
-                pl.BlockSpec((1, GROUP, LANES, LANES), lambda i, s: (i, 0, 0, 0)),
-                pl.BlockSpec(own.shape, lambda i, s: (0, 0, 0)),
-                pl.BlockSpec(own.shape, lambda i, s: (0, 0, 0)),
-                pl.BlockSpec((1, LANES, 1), lambda i, s: (i, 0, 0)),
-                ANYWHERE,
+                blocks_of(GROUP, LANES, LANES), whole, whole, blocks_of(1, LANES), ANYWHERE,
             ],
             out_specs=[
-                pl.BlockSpec((1, LANES, wide), lambda i, s: (i, 0, 0)),
-                pl.BlockSpec((1, GROUP * LANES, 1), lambda i, s: (i, 0, 0)),
-                pl.BlockSpec((1, LANES, width), lambda i, s: (i, 0, 0)),
+                blocks_of(LANES, wide), blocks_of(1, GROUP * LANES), blocks_of(LANES, width),
             ],
-            scratch_shapes=[pltpu.VMEM((wide, width), BF16), pltpu.SemaphoreType.DMA((2,))],
+            scratch_shapes=[
+                pltpu.VMEM((wide, width), BF16),
+                pltpu.VMEM((blocks, LANES, wide), BF16),
+                pltpu.VMEM((blocks, wide, PAIR * GROUP * LANES), F32),
+                pltpu.SemaphoreType.DMA((2,)),
+            ],
         ),
         out_shape=(
-            jax.ShapeDtypeStruct((blocks, LANES, wide), BF16),
-            jax.ShapeDtypeStruct((blocks, GROUP * LANES, 1), F32),
-            jax.ShapeDtypeStruct((blocks, LANES, width), BF16),
+            cells((blocks, LANES, wide), BF16),
+            cells((blocks, 1, GROUP * LANES), F32),
+            cells((blocks, LANES, width), BF16),
         ),
+        compiler_params=pltpu.CompilerParams(vmem_limit_bytes=28 << 20),
         cost_estimate=FREE,
         name="attend",
     )(info, q, own, other, begin, w)
@@ -1357,52 +1451,54 @@
 
 def attend_back_kernel(
     info_ref, q_ref, own_ref, other_ref, begin_ref, att_ref, lse_ref, datt_ref, table_ref,
-    dq_ref, d_own_ref, mail_ref, d_other_ref,
+    dq_ref, d_own_ref, mail_ref, d_other_ref, turned_ref,
 ):
-    step = pl.program_id(0)
-    core = info_ref[0]
-    block = 2 * step + core
-    first = info_ref[1 + step] // (2 * LANES)
-
-    @pl.when(step == 0)
+    core, begin, query, first, last = block_info(info_ref, begin_ref)
+    width = PAIR * GROUP * LANES
+
+    @pl.when(pl.program_id(0) == 0)
     def _():
+        turn_keys(own_ref, other_ref, turned_ref)
         d_own_ref[...] = jnp.zeros_like(d_own_ref)
         d_other_ref[...] = jnp.zeros_like(d_other_ref)
 
-    q = q_ref[0].reshape(GROUP * LANES, LANES)
-    begin = jnp.concatenate([begin_ref[0]] * GROUP, 0)
+    q = q_ref[...].reshape(width, LANES)
 
     def spread(wide):
         front, back = wide[:, :LANES], wide[:, LANES:]
         low = lanes_of(front) < HD
-        parts = [jnp.where(low, 0.0, part) for part in (turn(front), front, turn(back))]
-        return jnp.concatenate(parts, 0)
-
-    datt = spread(datt_ref[0].astype(F32)).astype(BF16)
-    att = spread(att_ref[0].astype(F32))
-    delta = jnp.sum(datt.astype(F32) * att, -1, keepdims=True)
-    lse = lse_ref[0]
+        return [jnp.where(low, 0.0, part) for part in (turn(front), front, turn(back))]
+
+    slopes, deltas = [], []
+    for part in range(PAIR):
+        for d, a in zip(spread(datt_ref[part].astype(F32)), spread(att_ref[part].astype(F32))):
+            slopes.append(d)
+            deltas.append(jnp.sum((d * a).T, 0, keepdims=True))
+    datt = jnp.concatenate(slopes, 0).astype(BF16)
+    delta = jnp.concatenate(deltas, 1)
+    lse = jnp.concatenate([lse_ref[part] for part in range(PAIR)], 1)
     both = jnp.concatenate([q, datt], 0)
 
     def one(chunk, acc):
-        keys = jnp.concatenate([own_ref[chunk], other_ref[chunk]], 0)
-        allowed = allowed_keys(begin, block, chunk, core)
-        weights = jnp.where(allowed, jnp.exp(dot(q, keys, NT) - lse), 0.0)
-        slope = (weights * (dot(datt, keys, NT) - delta)).astype(BF16)
-        d_keys = dot(jnp.concatenate([slope, weights.astype(BF16)], 0), both, TN)
+        keys = chunk_keys(own_ref, other_ref, chunk)
+        scores = jnp.where(allowed_keys(begin, query, chunk, core), dot(keys, q, NT), MASKED)
+        weights = jnp.exp(scores - lse)
+        slope = (weights * (dot(keys, datt, NT) - delta)).astype(BF16)
+        d_keys = dot(jnp.concatenate([slope, weights.astype(BF16)], 1), both)
         d_own_ref[chunk] += d_keys[:LANES]
         d_other_ref[chunk] += d_keys[LANES:]
-        return acc + dot(slope, keys)
-
-    acc = lax.fori_loop(first, step + 1, one, jnp.zeros((GROUP * LANES, LANES), F32))
-    heads = [acc[h * LANES : (h + 1) * LANES] * (HD**-0.5) for h in range(GROUP)]
-    low = lanes_of(heads[0]) < HD
-    cosine, sine = angles(table_ref[0])
-    front = spin(jnp.where(low, heads[0], turn(heads[1])), cosine, -sine)
-    back = spin(jnp.where(low, heads[2], 0.0), cosine, -sine)
-    dq_ref[0] = jnp.concatenate([front, back], 1).astype(BF16)
-
-    @pl.when(step == pl.num_programs(0) - 1)
+        return acc + dot(turned_ref[chunk], slope)
+
+    acc = lax.fori_loop(first, last, one, jnp.zeros((LANES, width), F32)) * (HD**-0.5)
+    for part in range(PAIR):
+        heads = by_head(acc[:, part * GROUP * LANES : (part + 1) * GROUP * LANES])
+        low = lanes_of(heads[0]) < HD
+        cosine, sine = angles(table_ref[part])
+        front = spin(jnp.where(low, heads[0], turn(heads[1])), cosine, -sine)
+        back = spin(jnp.where(low, heads[2], 0.0), cosine, -sine)
+        dq_ref[part] = jnp.concatenate([front, back], 1).astype(BF16)
+
+    @pl.when(pl.program_id(0) == pl.num_programs(0) - 1)
     def _():
         mail_ref[...] = d_other_ref[...].astype(BF16)
 
@@ -1410,34 +1506,31 @@
 def attend_back(info, q, own, other, begin, att, lse, datt, tables):
     blocks = q.shape[0]
     wide = 2 * LANES
-
-    def block(*shape):
-        return pl.BlockSpec((1,) + shape, lambda i, s: (i,) + (0,) * len(shape))
-
     whole = pl.BlockSpec(own.shape, lambda i, s: (0, 0, 0))
     return pl.pallas_call(
         attend_back_kernel,
         grid_spec=pltpu.PrefetchScalarGridSpec(
             num_scalar_prefetch=1,
-            grid=(blocks,),
+            grid=(blocks // PAIR,),
             in_specs=[
-                block(GROUP, LANES, LANES),
+                blocks_of(GROUP, LANES, LANES),
                 whole,
                 whole,
-                block(LANES, 1),
-                block(LANES, wide),
-                block(GROUP * LANES, 1),
-                block(LANES, wide),
-                block(HD, LANES),
+                blocks_of(1, LANES),
+                blocks_of(LANES, wide),
+                blocks_of(1, GROUP * LANES),
+                blocks_of(LANES, wide),
+                blocks_of(HD, LANES),
             ],
-            out_specs=[block(LANES, wide), whole, whole],
-            scratch_shapes=[pltpu.VMEM(own.shape, F32)],
+            out_specs=[blocks_of(LANES, wide), whole, whole],
+            scratch_shapes=[pltpu.VMEM(own.shape, F32), pltpu.VMEM((blocks, LANES, wide), BF16)],
         ),
         out_shape=(
-            jax.ShapeDtypeStruct((blocks, LANES, wide), BF16),
-            jax.ShapeDtypeStruct(own.shape, F32),
-            jax.ShapeDtypeStruct(own.shape, BF16),
+            cells((blocks, LANES, wide), BF16),
+            cells(own.shape, F32),
+            cells(own.shape, BF16),
         ),
+        compiler_params=pltpu.CompilerParams(vmem_limit_bytes=28 << 20),
         cost_estimate=FREE,
         name="attend_back",
     )(info, q, own, other, begin, att, lse, datt, tables)
@@ -1504,7 +1597,7 @@
     begin = jnp.sum(jnp.where(flat_segments == kinds, starts, 0), 0).reshape(count, 2, rows)
     begin = lax.dynamic_index_in_dim(begin, core, 1, False)
     info = jnp.concatenate([core[None], begin[:, 0]]).astype(jnp.int32)
-    begin = begin[:, :, None]
+    begin = begin[:, None, :]
 
     hidden = tokens.astype(F32)
     x_attn = (normal(hidden)[1] * params[0:1]).astype(BF16)

time: 853 us -> 817 us (0.958)
  Pallas kernels: 770 us -> 750 us
  local copies, waits for them, and re-layouts: 54.8 us -> 40.6 us
    unnamed x157 -> x147, local copies, waits for them, and re-layouts: 48.9 us -> 33.4 us
    pallas_call x2, Pallas kernels: 46.6 us -> 38 us  [attend_back(): pl.pallas_call(attend_back_kernel, grid_spec=pltpu.PrefetchScalarGridSpec...]
    pallas_call x2, Pallas kernels: 39.2 us -> 30.7 us  [attend(): pl.pallas_call(functools.partial(attend_kernel, layer), grid_spec=pltpu.P...]
where the time goes in v5:
time: 817 us; the launch traced here: 810 us
  Pallas kernels  750 us (92%)
  local copies, waits for them, and re-layouts  40.6 us (5%)
  other arithmetic  13 us (2%)
    pallas_call x12, Pallas kernels, ring_call(): pl.pallas_call(kernel, out_shape=tuple((shape for shape, _ in outputs)) +...  600 us
    pallas_call x2, Pallas kernels, attend_back(): pl.pallas_call(attend_back_kernel, grid_spec=pltpu.PrefetchScalarGridSpec...  38 us
    pallas_call x1, Pallas kernels, exchange_weights(): pl.pallas_call(functools.partial(setup_kernel, count), out_shape=(jax.Sha...  34.7 us
    pallas_call x1, Pallas kernels, finish_heads(): pl.pallas_call(functools.partial(finish_kernel, count, replicas), out_sha...  33.5 us
    unnamed x147, local copies, waits for them, and re-layouts  33.4 us
    pallas_call x2, Pallas kernels, attend(): pl.pallas_call(functools.partial(attend_kernel, layer), grid_spec=pltpu.P...  30.7 us
  transfers between devices with their start and end apart: 6, of which 0 were waited for; matrix products, arithmetic and copies ran while one was open for 1% of the time, Pallas kernels for 51%

profile of v5, /device:TPU:0, one launch (start us, length us, event | category | flops | bytes accessed | tf_op | source)
XLA Modules:
  0.0 810.3 jit_solution(14085659356918761227)
XLA Ops:
  1.4 1.1 copy.56
  2.7 1.1 copy.57
  6.3 1.5 maximum_bitcast_fusion.slab_ref
  7.8 34.7 %exchange_weights.1 = (bf16[2,16,96,384]{3,2,1,0:T(8,128)(2,1)}, bf16[2,2,96,1536]{3,2,1,0:T(8,128)(2,1)}, bf16[16,48,128]{2,1,0:T(8,128)(2,1)}, f32[8,64,128]{2,1,0:T(8,128)}) custom-call(bf16[8,2,96,384]{3,2,1,0:T(8,128)(2,1)} %maximum_bitcast_fusion.slab_ref, bf16[2,96,1536]{2,1,0:T(8,128)(2,1)} %out_w_ref.1, bf16[48,128]{1,0:T(8,128)(2,1)} %fusion.8.small_ref, ...), custom_call_target="tpu_custom_call" | custom-call | tf_op jit(solution)/shard_map/exchange_weights/pallas_call | solution.py:464
  43.5 1.0 convert_element_type.37.refs_1_.refs_8_
  44.4 2.1 convert_element_type.43.refs_5_
  47.6 1.0 slice_reduce_fusion.3
  49.0 47.2 %project.2 = (bf16[8,3,128,128]{3,2,1,0:T(8,128)(2,1)S(1)}, bf16[8,128,128]{2,1,0:T(8,128)(2,1)S(1)}, bf16[8,128,128]{2,1,0:T(8,128)(2,1)S(1)}, bf16[8,128,1536]{2,1,0:T(8,128)(2,1)S(1)}) custom-call(bf16[128,1536]{1,0:T(8,128)(2,1)S(1)} %multiply_convert_fusion.refs_0_, bf16[2,1536,384]{2,1,0:T(8,128)(2,1)S(1)} %bitcast.24, f32[8,64,128]{2,1,0:T(8,128)S(1)} %copy-done.7), custom_call_target="tpu_custom_call" | custom-call | tf_op jit(solution)/shard_map/project/pallas_call | solution.py:345
  96.2 1.7 copy-done.15
  98.4 15.4 %attend.2 = (bf16[8,128,256]{2,1,0:T(8,128)(2,1)S(1)}, f32[8,1,384]{2,1,0:T(1,128)S(1)}, bf16[8,128,1536]{2,1,0:T(8,128)(2,1)S(1)}) custom-call(s32[9]{0:T(128)S(1)} %pad_add_fusion.info_ref, bf16[8,3,128,128]{3,2,1,0:T(8,128)(2,1)S(1)} %get-tuple-element.89.q_ref, bf16[8,128,128]{2,1,0:T(8,128)(2,1)S(1)} %get-tuple-element.90.own_ref, ...), custom_call_target="tpu_custom_call" | custom-call | tf_op jit(solution)/shard_map/attend/pallas_call | solution.py:1423
  113.8 35.7 %route.2 = (f32[128,1536]{1,0:T(8,128)S(1)}, bf16[128,1536]{1,0:T(8,128)(2,1)S(1)}, f32[16,128]{1,0:T(8,128)S(1)}) custom-call(bf16[8,128,1536]{2,1,0:T(8,128)(2,1)S(1)} %get-tuple-element.93.refs_0_, f32[128,1536]{1,0:T(8,128)S(1)} %copy-done.9, f32[36,1536]{1,0:T(8,128)S(1)} %convert_element_type.42.refs_2_.refs_3_.refs_4_.refs_6_, s32[2,8,128]{2,1,0:T(8,128)S(1)} %bitcast.32), custom_call_target="tpu_custom_call" | custom-call | tf_op jit(solution)/shard_map/route/pallas_call | solution.py:345
  151.7 69.7 %mix.2 = (f32[128,1536]{1,0:T(8,128)}, f32[128,1536]{1,0:T(8,128)}, bf16[128,1536]{1,0:T(8,128)(2,1)}, bf16[8,128,1536]{2,1,0:T(8,128)(2,1)}, f32[8,16,128]{2,1,0:T(8,128)}) custom-call(bf16[128,1536]{1,0:T(8,128)(2,1)} %copy-done.49, f32[16,128]{1,0:T(8,128)} %copy-done.54, f32[128,1536]{1,0:T(8,128)} %copy-done.13, f32[36,1536]{1,0:T(8,128)} %copy-done.1, ...), custom_call_target="tpu_custom_call" | custom-call | tf_op jit(solution)/shard_map/mix/pallas_call | solution.py:345
  221.5 1.0 copy-done.47
  222.5 36.5 %project.3 = (bf16[8,3,128,128]{3,2,1,0:T(8,128)(2,1)S(1)}, bf16[8,128,128]{2,1,0:T(8,128)(2,1)S(1)}, bf16[8,128,128]{2,1,0:T(8,128)(2,1)S(1)}, bf16[8,128,1536]{2,1,0:T(8,128)(2,1)S(1)}) custom-call(bf16[128,1536]{1,0:T(8,128)(2,1)S(1)} %copy-done.47, bf16[2,1536,384]{2,1,0:T(8,128)(2,1)S(1)} %bitcast.25, f32[8,64,128]{2,1,0:T(8,128)S(1)} %copy-done.7), custom_call_target="tpu_custom_call" | custom-call | tf_op jit(solution)/shard_map/project/pallas_call | solution.py:345
  259.0 1.7 copy-done.17
  260.6 15.3 %attend.3 = (bf16[8,128,256]{2,1,0:T(8,128)(2,1)S(1)}, f32[8,1,384]{2,1,0:T(1,128)S(1)}, bf16[8,128,1536]{2,1,0:T(8,128)(2,1)S(1)}) custom-call(s32[9]{0:T(128)S(1)} %pad_add_fusion.info_ref, bf16[8,3,128,128]{3,2,1,0:T(8,128)(2,1)S(1)} %get-tuple-element.101.q_ref, bf16[8,128,128]{2,1,0:T(8,128)(2,1)S(1)} %get-tuple-element.102.own_ref, ...), custom_call_target="tpu_custom_call" | custom-call | tf_op jit(solution)/shard_map/attend/pallas_call | solution.py:1423
  275.9 34.4 %route.3 = (f32[128,1536]{1,0:T(8,128)S(1)}, bf16[128,1536]{1,0:T(8,128)(2,1)S(1)}, f32[16,128]{1,0:T(8,128)S(1)}) custom-call(bf16[8,128,1536]{2,1,0:T(8,128)(2,1)S(1)} %get-tuple-element.104.refs_0_, f32[128,1536]{1,0:T(8,128)S(1)} %copy-done.23, f32[36,1536]{1,0:T(8,128)S(1)} %copy-done.2, s32[2,8,128]{2,1,0:T(8,128)S(1)} %bitcast.33), custom_call_target="tpu_custom_call" | custom-call | tf_op jit(solution)/shard_map/route/pallas_call | solution.py:345
  312.6 69.4 %mix.3 = (f32[128,1536]{1,0:T(8,128)}, f32[128,1536]{1,0:T(8,128)}, bf16[128,1536]{1,0:T(8,128)(2,1)}, bf16[8,128,1536]{2,1,0:T(8,128)(2,1)}, f32[8,16,128]{2,1,0:T(8,128)}) custom-call(bf16[128,1536]{1,0:T(8,128)(2,1)} %copy-done.50, f32[16,128]{1,0:T(8,128)} %copy-done.55, f32[128,1536]{1,0:T(8,128)} %copy-done.14, f32[36,1536]{1,0:T(8,128)} %copy-done.1, ...), custom_call_target="tpu_custom_call" | custom-call | tf_op jit(solution)/shard_map/mix/pallas_call | solution.py:345
  382.0 1.3 multiply_reduce_fusion
  383.9 76.8 %mix_back.2 = (f32[128,1536]{1,0:T(8,128)}, bf16[128,1536]{1,0:T(8,128)(2,1)}, f32[1,1536]{1,0:T(1,128)}, bf16[4608,512]{1,0:T(8,128)(2,1)}, f32[2,1536]{1,0:T(2,128)}) custom-call(bf16[128,1536]{1,0:T(8,128)(2,1)} %refs_0_.1, f32[8,128]{1,0:T(8,128)} %broadcast_in_dim.34.refs_1_, bf16[8,128,1536]{2,1,0:T(8,128)(2,1)} %get-tuple-element.115.refs_2_, ...), custom_call_target="tpu_custom_call" | custom-call | tf_op jit(solution)/shard_map/mix_back/pallas_call | solution.py:345
  460.8 1.6 collective-permute-start.3
  462.4 1.0 copy-done.31
  463.5 1.0 copy-done.46
  464.5 35.8 %branch_back.2 = (bf16[8,128,256]{2,1,0:T(8,128)(2,1)S(1)}, bf16[96,1536]{1,0:T(8,128)(2,1)S(1)}) custom-call(bf16[128,1536]{1,0:T(8,128)(2,1)S(1)} %copy-done.46, bf16[2,2,96,1536]{3,2,1,0:T(8,128)(2,1)S(1)} %copy-done.6, bf16[8,128,256]{2,1,0:T(8,128)(2,1)S(1)} %copy-done.31), custom_call_target="tpu_custom_call" | custom-call | tf_op jit(solution)/shard_map/branch_back/pallas_call | solution.py:345
  501.0 1.0 copy-done.32
  503.0 19.0 %attend_back.2 = (bf16[8,128,256]{2,1,0:T(8,128)(2,1)S(1)}, f32[8,128,128]{2,1,0:T(8,128)S(1)}, bf16[8,128,128]{2,1,0:T(8,128)(2,1)S(1)}) custom-call(s32[9]{0:T(128)S(1)} %pad_add_fusion.info_ref, bf16[8,3,128,128]{3,2,1,0:T(8,128)(2,1)S(1)} %copy-done.22, bf16[8,128,128]{2,1,0:T(8,128)(2,1)S(1)} %get-tuple-element.102.own_ref, ...), custom_call_target="tpu_custom_call" | custom-call | tf_op jit(solution)/shard_map/attend_back/pallas_call | solution.py:1510
  522.1 1.1 copy-done.24
  523.2 1.1 copy-done.25
  524.3 1.1 copy-done.44
  525.5 40.4 %join.2 = (f32[128,1536]{1,0:T(8,128)S(1)}, bf16[128,1536]{1,0:T(8,128)(2,1)S(1)}, f32[8,128]{1,0:T(8,128)S(1)}, bf16[1536,384]{1,0:T(8,128)(2,1)S(1)}) custom-call(bf16[8,128,256]{2,1,0:T(8,128)(2,1)S(1)} %get-tuple-element.119.refs_0_, f32[8,128,128]{2,1,0:T(8,128)S(1)} %get-tuple-element.120.refs_1_, bf16[8,128,128]{2,1,0:T(8,128)(2,1)S(1)} %get-tuple-element.121.refs_2_, ...), custom_call_target="tpu_custom_call" | custom-call | tf_op jit(solution)/shard_map/join/pallas_call | solution.py:345
  565.9 1.0 copy-done.11
  569.1 78.0 %mix_back.3 = (f32[128,1536]{1,0:T(8,128)}, bf16[128,1536]{1,0:T(8,128)(2,1)}, f32[1,1536]{1,0:T(1,128)}, bf16[4608,512]{1,0:T(8,128)(2,1)}, f32[2,1536]{1,0:T(2...) custom-call(bf16[128,1536]{1,0:T(8,128)(2,1)} %copy-done.48, f32[8,128]{1,0:T(8,128)} %copy-done.58, ...), custom_call_target="tpu_custom_call" | custom-call | tf_op jit(solution)/shard_map/mix_back/pallas_call | solution.py:345
  647.8 1.9 add_bitcast_fusion
  649.8 1.0 copy-done.28
  650.8 1.0 copy-done.45
  651.8 35.6 %branch_back.3 = (bf16[8,128,256]{2,1,0:T(8,128)(2,1)S(1)}, bf16[96,1536]{1,0:T(8,128)(2,1)}) custom-call(bf16[128,1536]{1,0:T(8,128)(2,1)S(1)} %copy-done.45, bf16[2,2,96,1536]{3,2,1,0:T(8,128)(2,1)S(1)} %copy-done.6, bf16[8,128,256]{2,1,0:T(8,128)(2,1)S(1)} %copy-done.28), custom_call_target="tpu_custom_call" | custom-call | tf_op jit(solution)/shard_map/branch_back/pallas_call | solution.py:345
  687.4 1.7 collective-permute-start.4
  689.1 1.0 copy-done.29
  692.0 19.0 %attend_back.3 = (bf16[8,128,256]{2,1,0:T(8,128)(2,1)S(1)}, f32[8,128,128]{2,1,0:T(8,128)S(1)}, bf16[8,128,128]{2,1,0:T(8,128)(2,1)S(1)}) custom-call(s32[9]{0:T(128)S(1)} %pad_add_fusion.info_ref, bf16[8,3,128,128]{3,2,1,0:T(8,128)(2,1)S(1)} %copy-done.20, bf16[8,128,128]{2,1,0:T(8,128)(2,1)S(1)} %copy-done.37, bf16[8,128,128]{2,1,0:T(8,128)(2,1)S(1)} %copy-done.39, ...), custom_call_target="tpu_custom_call" | custom-call | tf_op jit(solution)/shard_map/attend_back/pallas_call | solution.py:1510
  711.1 1.1 copy-done.43
  712.2 40.7 %join.3 = (f32[128,1536]{1,0:T(8,128)S(1)}, bf16[128,1536]{1,0:T(8,128)(2,1)}, f32[8,128]{1,0:T(8,128)}, bf16[1536,384]{1,0:T(8,128)(2,1)S(1)}) custom-call(bf16[8,128,256]{2,1,0:T(8,128)(2,1)S(1)} %get-tuple-element.138.refs_0_, f32[8,128,128]{2,1,0:T(8,128)S(1)} %get-tuple-element.139.refs_1_, bf16[8,128,128]{2,1,0:T(8,128)(2,1)S(1)} %get-tuple-element.140.refs_2_, ...), custom_call_target="tpu_custom_call" | custom-call | tf_op jit(solution)/shard_map/join/pallas_call | solution.py:345
  753.0 33.5 %finish_heads.1 = (f32[2,96,1536]{2,1,0:T(8,128)S(1)}, f32[2,96,512]{2,1,0:T(8,128)S(1)}, f32[2,96,512]{2,1,0:T(8,128)S(1)}, f32[2,8,96,128]{3,2,1,0:T(8,128)S(1)}) custom-call(bf16[8,2,96,384]{3,2,1,0:T(8,128)(2,1)S(1)} %bitcast.30, bf16[8,2,96,384]{3,2,1,0:T(8,128)(2,1)S(1)} %bitcast.29, bf16[8,2,96,384]{3,2,1,0:T(8,128)(2,1)S(1)} %copy-done.33), custom_call_target="tpu_custom_call" | custom-call | tf_op jit(solution)/shard_map/finish_heads/pallas_call | solution.py:1261
  786.5 1.2 slice_bitcast_fusion
  787.7 2.0 copy.62
  789.7 12.7 %add_experts.1 = (f32[2,1,1536,512]{3,2,1,0:T(8,128)}, f32[2,1,1536,512]{3,2,1,0:T(8,128)}, f32[2,1,512,1536]{3,2,1,0:T(8,128)}) custom-call(bf16[4608,512]{1,0:T(8,128)(2,1)} %get-tuple-element.154.refs_0_.refs_1_.refs_2_.refs_3_.refs_4_, bf16[4608,512]{1,0:T(8,128)(2,1)} %get-tuple-element.154.refs_0_.refs_1_.refs_2_.refs_3_.refs_4_, ...), custom_call_target="tpu_custom_call" | custom-call | tf_op jit(solution)/shard_map/add_experts/pallas_call | solution.py:1309
  803.5 1.1 add_bitcast_fusion.1
  804.6 1.1 pad_maximum_fusion
  807.3 1.0 copy.70
  (166 shorter events, 22.0 us)
Async XLA Ops:
  0.6 3.4 copy-start.63
  2.5 3.2 copy-start.67
  2.5 3.2 copy-start.68
  2.5 3.2 copy-start.69
  5.0 38.5 %copy-start.59 = (bf16[128,1536]{1,0:T(8,128)(2,1)S(1)}, bf16[128,1536]{1,0:T(8,128)(2,1)}, u32[]{:S(2)}) copy-start(bf16[128,1536]{1,0:T(8,128)(2,1)} %param.15) | copy-start | bytes 1179652
  42.5 4.0 copy-start.65
  42.5 109.2 %collective-permute-start = (bf16[2,1,1536,512]{3,2,1,0:T(8,128)(2,1)}, bf16[2,1,1536,512]{3,2,1,0:T(8,128)(2,1)}, u32[]{:S(2)}, u32[]{:S(2)}) collective-permute-start(bf16[2,1,1536,512]{3,2,1,0:T(8,128)(2,1)} %refs_7_.1), channel_id=1, source_target_pairs={{0,1},{1,0},{2,3},{3,2},{4,5},{5,4},{6,7},{7,6},{8,9},{9,8},{10,11... | collective-permute-start | bytes 9437192 | tf_op jit(solution)/shard_map/ppermute | solution.py:1569
  43.0 108.8 %collective-permute-start.1 = (bf16[2,1,1536,512]{3,2,1,0:T(8,128)(2,1)}, bf16[2,1,1536,512]{3,2,1,0:T(8,128)(2,1)}, u32[]{:S(2)}, u32[]{:S(2)}) collective-permute-start(bf16[2,1,1536,512]{3,2,1,0:T(8,128)(2,1)} %refs_8_.1), channel_id=1, source_target_pairs={{0,1},{1,0},{2,3},{3,2},{4,5},{5,4},{6,7},{7,6},{8,9},{9,8},{10,11... | collective-permute-start | bytes 9437192 | tf_op jit(solution)/shard_map/ppermute | solution.py:1569
  43.1 108.6 %collective-permute-start.2 = (bf16[2,1,512,1536]{3,2,1,0:T(8,128)(2,1)}, bf16[2,1,512,1536]{3,2,1,0:T(8,128)(2,1)}, u32[]{:S(2)}, u32[]{:S(2)}) collective-permute-start(bf16[2,1,512,1536]{3,2,1,0:T(8,128)(2,1)} %refs_9_.1), channel_id=1, source_target_pairs={{0,1},{1,0},{2,3},{3,2},{4,5},{5,4},{6,7},{7,6},{8,9},{9,8},{10,11... | collective-permute-start | bytes 9437192 | tf_op jit(solution)/shard_map/ppermute | solution.py:1569
  43.5 5.5 copy-start
  43.5 5.5 copy-start.7
  47.5 66.3 %copy-start.1 = (f32[36,1536]{1,0:T(8,128)}, f32[36,1536]{1,0:T(8,128)S(1)}, u32[]{:S(2)}) copy-start(f32[36,1536]{1,0:T(8,128)S(1)} %convert_element_type.42.refs_2_.refs_3_.refs_4_.refs_6_) | copy-start | bytes 663556
  47.5 50.4 %copy-start.66 = (s32[1,2048]{1,0:T(1,128)S(1)}, s32[1,2048]{1,0:T(1,128)}, u32[]{:S(2)}) copy-start(s32[1,2048]{1,0:T(1,128)} %param.18) | copy-start | bytes 24580
  48.6 49.8 %copy-start.5 = (bf16[2,2,96,1536]{3,2,1,0:T(8,128)(2,1)S(1)}, bf16[2,2,96,1536]{3,2,1,0:T(8,128)(2,1)}, u32[]{:S(2)}) copy-start(bf16[2,2,96,1536]{3,2,1,0:T(8,128)(2,1)} %get-tuple-element.92.w_ref.refs_1_) | copy-start | bytes 3538948
  49.0 64.8 %copy-start.9 = (f32[128,1536]{1,0:T(8,128)S(1)}, f32[128,1536]{1,0:T(8,128)}, u32[]{:S(2)}) copy-start(f32[128,1536]{1,0:T(8,128)} %convert_element_type.37.refs_1_.refs_8_) | copy-start | bytes 2359300
  49.0 64.8 %copy-start.51 = (s32[2,128,8]{1,2,0:T(8,128)S(1)}, s32[2,128,8]{1,2,0:T(8,128)}, u32[]{:S(2)}) copy-start(s32[2,128,8]{1,2,0:T(8,128)} %param.19) | copy-start | bytes 24580
  97.9 15.9 %copy-start.36 = (bf16[8,128,128]{2,1,0:T(8,128)(2,1)}, bf16[8,128,128]{2,1,0:T(8,128)(2,1)S(1)}, u32[]{:S(2)}) copy-start(bf16[8,128,128]{2,1,0:T(8,128)(2,1)S(1)} %get-tuple-element.90.own_ref) | copy-start | bytes 786436
  97.9 15.9 %copy-start.38 = (bf16[8,128,128]{2,1,0:T(8,128)(2,1)}, bf16[8,128,128]{2,1,0:T(8,128)(2,1)S(1)}, u32[]{:S(2)}) copy-start(bf16[8,128,128]{2,1,0:T(8,128)(2,1)S(1)} %get-tuple-element.91.other_ref) | copy-start | bytes 786436
  97.9 51.6 %copy-start.19 = (bf16[8,3,128,128]{3,2,1,0:T(8,128)(2,1)}, bf16[8,3,128,128]{3,2,1,0:T(8,128)(2,1)S(1)}, u32[]{:S(2)}) copy-start(bf16[8,3,128,128]{3,2,1,0:T(8,128)(2,1)S(1)} %get-tuple-element.89.q_ref) | copy-start | bytes 2359300
  113.8 38.0 %copy-start.27 = (bf16[8,128,256]{2,1,0:T(8,128)(2,1)}, bf16[8,128,256]{2,1,0:T(8,128)(2,1)S(1)}, u32[]{:S(2)}) copy-start(bf16[8,128,256]{2,1,0:T(8,128)(2,1)S(1)} %get-tuple-element.110.refs_2_.att_ref) | copy-start | bytes 1572868
  222.5 53.5 %copy-start.2 = (f32[36,1536]{1,0:T(8,128)S(1)}, f32[36,1536]{1,0:T(8,128)}, u32[]{:S(2)}) copy-start(f32[36,1536]{1,0:T(8,128)} %copy-done.1) | copy-start | bytes 663556
  222.5 53.5 %copy-start.23 = (f32[128,1536]{1,0:T(8,128)S(1)}, f32[128,1536]{1,0:T(8,128)}, u32[]{:S(2)}) copy-start(f32[128,1536]{1,0:T(8,128)} %get-tuple-element.105.refs_1_.refs_8_) | copy-start | bytes 2359300
  260.6 49.7 %copy-start.21 = (bf16[8,3,128,128]{3,2,1,0:T(8,128)(2,1)}, bf16[8,3,128,128]{3,2,1,0:T(8,128)(2,1)S(1)}, u32[]{:S(2)}) copy-start(bf16[8,3,128,128]{3,2,1,0:T(8,128)(2,1)S(1)} %get-tuple-element.101.q_ref) | copy-start | bytes 2359300
  260.6 49.7 %copy-start.40 = (bf16[8,128,128]{2,1,0:T(8,128)(2,1)}, bf16[8,128,128]{2,1,0:T(8,128)(2,1)S(1)}, u32[]{:S(2)}) copy-start(bf16[8,128,128]{2,1,0:T(8,128)(2,1)S(1)} %get-tuple-element.103.other_ref) | copy-start | bytes 786436
  275.9 36.7 %copy-start.30 = (bf16[8,128,256]{2,1,0:T(8,128)(2,1)}, bf16[8,128,256]{2,1,0:T(8,128)(2,1)S(1)}, u32[]{:S(2)}) copy-start(bf16[8,128,256]{2,1,0:T(8,128)(2,1)S(1)} %get-tuple-element.112.refs_2_.att_ref) | copy-start | bytes 1572868
  312.6 69.4 %copy-start.60 = (bf16[128,1536]{1,0:T(8,128)(2,1)S(1)}, bf16[128,1536]{1,0:T(8,128)(2,1)}, u32[]{:S(2)}) copy-start(bf16[128,1536]{1,0:T(8,128)(2,1)} %refs_0_.1) | copy-start | bytes 1179652
  383.9 78.5 %copy-start.6 = (bf16[2,2,96,1536]{3,2,1,0:T(8,128)(2,1)S(1)}, bf16[2,2,96,1536]{3,2,1,0:T(8,128)(2,1)}, u32[]{:S(2)}) copy-start(bf16[2,2,96,1536]{3,2,1,0:T(8,128)(2,1)} %get-tuple-element.92.w_ref.refs_1_) | copy-start | bytes 3538948
  383.9 117.1 %copy-start.8 = (f32[8,64,128]{2,1,0:T(8,128)S(1)}, f32[8,64,128]{2,1,0:T(8,128)}, u32[]{:S(2)}) copy-start(f32[8,64,128]{2,1,0:T(8,128)} %get-tuple-element.88.refs_2_.table_ref.refs_3_) | copy-start | bytes 786436
  460.8 40.2 %copy-start.22 = (bf16[8,3,128,128]{3,2,1,0:T(8,128)(2,1)S(1)}, bf16[8,3,128,128]{3,2,1,0:T(8,128)(2,1)}, u32[]{:S(2)}) copy-start(bf16[8,3,128,128]{3,2,1,0:T(8,128)(2,1)} %copy-done.21) | copy-start | bytes 2359300
  460.8 189.0 %collective-permute-start.3 = (bf16[4608,512]{1,0:T(8,128)(2,1)}, bf16[4608,512]{1,0:T(8,128)(2,1)}, u32[]{:S(2)}, u32[]{:S(2)}) collective-permute-start(bf16[4608,512]{1,0:T(8,128)(2,1)} %get-tuple-element.155.refs_10_.refs_11_.refs_12_.refs_13_.refs_14_), channel_id=1, source_target_pairs={{0,16},{16,0},{1,17},{17,1},{2,18},{18,2},{3,19},{19,3},{4,20},{20... | collective-permute-start | bytes 14155784 | tf_op jit(solution)/shard_map/ppermute | solution.py:1618
  464.5 57.6 %copy-start.3 = (f32[36,1536]{1,0:T(8,128)S(1)}, f32[36,1536]{1,0:T(8,128)}, u32[]{:S(2)}) copy-start(f32[36,1536]{1,0:T(8,128)} %copy-done.1) | copy-start | bytes 663556
  464.5 57.6 %copy-start.18 = (bf16[8,128,1536]{2,1,0:T(8,128)(2,1)S(1)}, bf16[8,128,1536]{2,1,0:T(8,128)(2,1)}, u32[]{:S(2)}) copy-start(bf16[8,128,1536]{2,1,0:T(8,128)(2,1)} %copy-done.17) | copy-start | bytes 9437188
  503.0 19.1 %copy-start.53 = (f32[2,1536]{1,0:T(2,128)S(1)}, f32[2,1536]{1,0:T(2,128)}, u32[]{:S(2)}) copy-start(f32[2,1536]{1,0:T(2,128)} %get-tuple-element.125.refs_10_) | copy-start | bytes 36868
  503.0 19.1 %copy-start.57 = (f32[1,1536]{1,0:T(1,128)S(1)}, f32[1,1536]{1,0:T(1,128)}, u32[]{:S(2)}) copy-start(f32[1,1536]{1,0:T(1,128)} %get-tuple-element.126.refs_11_) | copy-start | bytes 18436
  569.1 78.7 %copy-start.35 = (bf16[96,1536]{1,0:T(8,128)(2,1)S(1)}, bf16[96,1536]{1,0:T(8,128)(2,1)}, u32[]{:S(2)}) copy-start(bf16[96,1536]{1,0:T(8,128)(2,1)} %copy-done.34) | copy-start | bytes 884740
  647.1 41.9 %copy-start.20 = (bf16[8,3,128,128]{3,2,1,0:T(8,128)(2,1)S(1)}, bf16[8,3,128,128]{3,2,1,0:T(8,128)(2,1)}, u32[]{:S(2)}) copy-start(bf16[8,3,128,128]{3,2,1,0:T(8,128)(2,1)} %copy-done.19) | copy-start | bytes 2359300
  647.1 142.6 %collective-permute-start.5 = (bf16[4608,512]{1,0:T(8,128)(2,1)}, bf16[4608,512]{1,0:T(8,128)(2,1)}, u32[]{:S(2)}, u32[]{:S(2)}) collective-permute-start(bf16[4608,512]{1,0:T(8,128)(2,1)} %get-tuple-element.154.refs_0_.refs_1_.refs_2_.refs_3_.refs_4_), channel_id=1, source_target_pairs={{0,16},{16,0},{1,17},{17,1},{2,18},{18,2},{3,19},{19,3},{4,20},{20... | collective-permute-start | bytes 14155784 | tf_op jit(solution)/shard_map/ppermute | solution.py:1618
  647.8 63.2 %copy-start.26 = (f32[128,1536]{1,0:T(8,128)S(1)}, f32[128,1536]{1,0:T(8,128)}, u32[]{:S(2)}) copy-start(f32[128,1536]{1,0:T(8,128)} %get-tuple-element.124.refs_9_) | copy-start | bytes 2359300
  651.8 59.3 %copy-start.4 = (f32[36,1536]{1,0:T(8,128)S(1)}, f32[36,1536]{1,0:T(8,128)}, u32[]{:S(2)}) copy-start(f32[36,1536]{1,0:T(8,128)} %copy-done.1) | copy-start | bytes 663556
  651.8 59.3 %copy-start.10 = (f32[128,1536]{1,0:T(8,128)S(1)}, f32[128,1536]{1,0:T(8,128)}, u32[]{:S(2)}) copy-start(f32[128,1536]{1,0:T(8,128)} %convert_element_type.37.refs_1_.refs_8_) | copy-start | bytes 2359300
  651.8 59.3 %copy-start.16 = (bf16[8,128,1536]{2,1,0:T(8,128)(2,1)S(1)}, bf16[8,128,1536]{2,1,0:T(8,128)(2,1)}, u32[]{:S(2)}) copy-start(bf16[8,128,1536]{2,1,0:T(8,128)(2,1)} %copy-done.15) | copy-start | bytes 9437188
  687.4 116.0 %collective-permute-start.4 = (bf16[96,1536]{1,0:T(8,128)(2,1)}, bf16[96,1536]{1,0:T(8,128)(2,1)}, u32[]{:S(2)}, u32[]{:S(2)}) collective-permute-start(bf16[96,1536]{1,0:T(8,128)(2,1)} %get-tuple-element.152), channel_id=1, source_target_pairs={{0,16},{16,0},{1,17},{17,1},{2,18},{18,2},{3,19},{19,3},{4,20},{20... | collective-permute-start | bytes 884744 | tf_op jit(solution)/shard_map/ppermute | solution.py:1618
  692.0 19.1 %copy-start.52 = (f32[2,1536]{1,0:T(2,128)S(1)}, f32[2,1536]{1,0:T(2,128)}, u32[]{:S(2)}) copy-start(f32[2,1536]{1,0:T(2,128)} %get-tuple-element.143.refs_10_) | copy-start | bytes 36868
  692.0 19.1 %copy-start.56 = (f32[1,1536]{1,0:T(1,128)S(1)}, f32[1,1536]{1,0:T(1,128)}, u32[]{:S(2)}) copy-start(f32[1,1536]{1,0:T(1,128)} %get-tuple-element.144.refs_11_) | copy-start | bytes 18436
  712.2 40.7 %copy-start.12 = (bf16[1536,384]{1,0:T(8,128)(2,1)S(1)}, bf16[1536,384]{1,0:T(8,128)(2,1)}, u32[]{:S(2)}) copy-start(bf16[1536,384]{1,0:T(8,128)(2,1)} %copy-done.11) | copy-start | bytes 3538948
  712.2 40.7 %copy-start.33 = (bf16[8,2,96,384]{3,2,1,0:T(8,128)(2,1)S(1)}, bf16[8,2,96,384]{3,2,1,0:T(8,128)(2,1)}, u32[]{:S(2)}) copy-start(bf16[8,2,96,384]{3,2,1,0:T(8,128)(2,1)} %get-tuple-element.147.refs_2_) | copy-start | bytes 3538948
  802.4 2.2 copy-start.61
  802.4 3.3 copy-start.64
  (28 other events, 27.0 us)

commit v6 on v5

--- a/solution.py
+++ b/solution.py
@@ -13,7 +13,6 @@
 LAYERS = 2
 GROUP = HEADS // KV_HEADS
 LANES = 128
-PAIR = 2
 EPS = 1e-06
 MASKED = -1e30
 MESH = pl.DeviceIdType.MESH
@@ -81,7 +80,7 @@
 class Ring:
     def __init__(self, count, traffic):
         self.count = count
-        self.riders, self.early, self.late = traffic
+        self.riders, self.early, self.late, self.soon = traffic
         self.steps = count // 2
         self.chip, self.at, self.near = ring_setup(count)
 
@@ -96,6 +95,10 @@
     def settle(self):
         for copy in self.late:
             copy.wait()
+
+    def depart(self):
+        for copy in self.soon:
+            copy.start()
 
     def gather(self, x_ref, buf, sems, side=None, first=None, second=None):
         own_sem, send_sem, recv_sem = sems[:3]
@@ -209,9 +212,8 @@
 
         return run
 
-    def scatter(self, partial, land, sems, work=None, source=None, ready=None):
+    def scatter(self, partial, land, sems, work=None, between=None):
         send_sem, recv_sem = sems
-        source = partial if source is None else source
         half_rows = partial.shape[1] // 2
         steps = self.steps
         hops = ring_hops(self.count)
@@ -233,10 +235,10 @@
         def rows_of(key):
             return pl.ds(key[1] * half_rows, half_rows)
 
-        for key in hops:
-            piece(key, 0, source.at[ahead(key, 0), rows_of(key)]).start()
-        if ready is not None:
-            ready()
+        for place, key in enumerate(hops):
+            if place == 2 and between is not None:
+                between()
+            piece(key, 0, partial.at[ahead(key, 0), rows_of(key)]).start()
 
         def step(s, carry):
             for place, key in enumerate(hops):
@@ -291,7 +293,7 @@
 ANYWHERE = pl.BlockSpec(memory_space=pltpu.HBM)
 HERE = pl.BlockSpec(memory_space=pltpu.VMEM)
 EARLY, LATE = "early", "late"
-OUT = "out"
+OUT, SOON = "out", "soon"
 
 
 FREE = pl.CostEstimate(flops=0, bytes_accessed=0, transcendentals=0)
@@ -302,7 +304,7 @@
     in_kinds = [kind for _, kind in inputs]
     out_kinds = [kind for _, kind in outputs]
     copied = [a for a, kind in inputs if kind in (EARLY, LATE)]
-    returned = [a for a, kind in outputs if kind == OUT]
+    returned = [a for a, kind in outputs if kind in (OUT, SOON)]
     moves = len(copied) + len(returned)
 
     def kernel(*refs):
@@ -317,7 +319,7 @@
                 for i in range(n_rides)
             ]
         used = 0
-        early, late, leaving = [], [], []
+        early, late, leaving, soon = [], [], [], []
         ins, outs = list(ins), list(outs)
         for i, kind in enumerate(in_kinds):
             if kind in (EARLY, LATE):
@@ -327,16 +329,17 @@
                 ins[i] = own[used]
                 used += 1
         for i, kind in enumerate(out_kinds):
-            if kind == OUT:
-                leaving.append(pltpu.make_async_copy(own[used], outs[i], move_sem.at[used]))
+            if kind in (OUT, SOON):
+                copy = pltpu.make_async_copy(own[used], outs[i], move_sem.at[used])
+                (leaving if kind == OUT else soon).append(copy)
                 outs[i] = own[used]
                 used += 1
-        body((riders, early, late), *ins, *outs, *rest)
+        body((riders, early, late, soon), *ins, *outs, *rest)
         for copy in leaving:
             copy.start()
         for rider in riders:
             rider.wait()
-        for copy in leaving:
+        for copy in leaving + soon:
             copy.wait()
 
     def spec(kind):
@@ -485,7 +488,7 @@
             dma((1,)),
         ],
         compiler_params=pltpu.CompilerParams(
-            collective_id=identity(("setup",)), has_side_effects=True
+            collective_id=identity(("setup",)), has_side_effects=True, vmem_limit_bytes=60 << 20
         ),
         cost_estimate=FREE,
         name="exchange_weights",
@@ -585,28 +588,63 @@
     return slice(first, first + experts)
 
 
-def project_kernel(count, layer, traffic, *refs):
-    inputs, outputs, scratch = split(refs, 3, 4)
-    x_ref, w_ref, table_ref = inputs
-    q_ref, own_ref, other_ref, all_ref = outputs
-    buf, weights, q_buf, own_buf = scratch[:4]
-    sems, pair_sems, out_sem, load_sem = split(scratch[4:], 3, 2, 1)
+def allowed_keys(begin, query, chunk, core):
+    shape = (2 * LANES, begin.shape[1])
+    place = lax.broadcasted_iota(jnp.int32, shape, 0)
+    shift = jnp.where(place < LANES, core, -core)
+    key = chunk * 2 * LANES + place + shift * LANES
+    return (key >= begin) & (key <= query)
+
+
+def query_rows(begin_ref, blocks, core):
+    lane = lax.broadcasted_iota(jnp.int32, (1, LANES), 1)
+    begin, query = [], []
+    for block in blocks:
+        begin += [begin_ref[block]] * GROUP
+        query += [(2 * block + core) * LANES + lane] * GROUP
+    return jnp.concatenate(begin, 1), jnp.concatenate(query, 1)
+
+
+def chunk_keys(own_ref, other_ref, chunk):
+    return jnp.concatenate([own_ref[chunk], other_ref[chunk]], 0)
+
+
+def turn_keys(own_ref, other_ref, turned_ref):
+    def one(chunk, carry):
+        turned_ref[chunk] = chunk_keys(own_ref, other_ref, chunk).astype(F32).T.astype(BF16)
+        return carry
+
+    lax.fori_loop(0, turned_ref.shape[0], one, 0)
+
+
+def by_head(field):
+    return [field[:, h * LANES : (h + 1) * LANES].T for h in range(GROUP)]
+
+
+def last_chunk(blocks):
+    return blocks[0] if len(blocks) == 1 else jnp.maximum(*blocks)
+
+
+def attend_kernel(count, layer, traffic, *refs):
+    inputs, outputs, scratch = split(refs, 8, 9)
+    x_ref, w_ref, w_out_ref, table_ref, begin_ref, hidden_ref, params_ref, routes_ref = inputs
+    q_ref, own_ref, other_ref, all_ref, att_ref, lse_ref, middle_ref, x_out_ref, share_ref = outputs
+    buf, weights, wide_w, turned_ref, score_ref, partial, land = scratch[:7]
+    sems, pair_sems, scatter_sem, out_sem, load_sem = split(scratch[7:], 3, 2, 2, 1)
     ring = Ring(count, traffic)
-    load = pltpu.make_async_copy(w_ref.at[layer], weights, load_sem[0].at[0])
-    load.start()
+    loads = [pltpu.make_async_copy(w_ref.at[layer], weights, load_sem[0].at[2])]
+    loads[0].start()
+    loads += load_out_weights(w_out_ref, layer, wide_w, load_sem[0])
     ring.meet(True)
     partner = partner_of("fsdp")
+    core = lax.rem(lax.axis_index("fsdp"), 2)
 
     def pass_on(block):
-        return [
-            remote(
-                own_buf.at[block], other_ref.at[block], pair_sems[0].at[block], pair_sems[1].at[block], partner
-            ),
-            pltpu.make_async_copy(own_buf.at[block], own_ref.at[block], out_sem[0].at[0, block]),
-            pltpu.make_async_copy(q_buf.at[block], q_ref.at[block], out_sem[0].at[1, block]),
-        ]
-
-    def compute(place, blocks):
+        return remote(
+            own_ref.at[block], other_ref.at[block], pair_sems[0].at[block], pair_sems[1].at[block], partner
+        )
+
+    def project(place, blocks):
         rows = dot(stack(buf, blocks), weights[...])
         tables = [angles(table_ref[b]) for b in blocks]
         cosine = jnp.concatenate([t[0] for t in tables], 0)
@@ -614,70 +652,85 @@
         heads, pair = project_rows(rows, cosine, sine)
         for index, head in enumerate(heads):
             for block, part in cut(head, blocks):
-                q_buf[block, index] = part
+                q_ref[block, index] = part
         for block, part in cut(pair, blocks):
-            own_buf[block] = part
-            for copy in pass_on(block):
-                copy.start()
-
-    def first(s):
-        @pl.when(s == 1)
-        def _():
-            load.wait()
-
-    drain = ring.gather(x_ref, buf, sems, None, first, ring.meanwhile(compute, 0))
-    keep = pltpu.make_async_copy(buf, all_ref, out_sem[0].at[2, 0])
+            own_ref[block] = part
+            pass_on(block).start()
+
+    drain = ring.gather(
+        x_ref, buf, sems, None, after_loads(loads, lambda s: None), ring.meanwhile(project, 0)
+    )
+    keep = pltpu.make_async_copy(buf, all_ref, out_sem[0].at[0])
     keep.start()
-    compute(0, (ring.at(ring.steps),))
-    drain()
+    project(0, (ring.at(ring.steps),))
     for block in range(count):
-        for copy in pass_on(block):
-            copy.wait()
-    keep.wait()
-
-
-def gather_project(count, layer, x, w, tables):
-    rows, width = x.shape
-    block = cells((count, rows, LANES), BF16)
-    queries = (count, GROUP, rows, LANES)
-    return ring_call(
-        functools.partial(project_kernel, count, layer),
-        ("project", layer),
-        [(x, ANYWHERE), (w, ANYWHERE), (tables, EARLY)],
-        [
-            (cells(queries, BF16), ANYWHERE),
-            (block, ANYWHERE),
-            (block, ANYWHERE),
-            (cells((count, rows, width), BF16), ANYWHERE),
-        ],
-        [
-            pltpu.VMEM((count, rows, width), BF16),
-            pltpu.VMEM(w.shape[1:], BF16),
-            pltpu.VMEM(queries, BF16),
-            pltpu.VMEM(block.shape, BF16),
-        ]
-        + gather_sems(count)
-        + dmas((count,), (count,), (3, count), (1,)),
-        20,
-    )
-
-
-def route_kernel(count, layer, traffic, *refs):
-    inputs, outputs, scratch = split(refs, 4, 3)
-    p_ref, hidden_ref, params_ref, routes_ref = inputs
-    middle_ref, x_ref, share_ref = outputs
-    partial, land = scratch[:2]
-    sems, load_sem = split(scratch[2:], 2)
-    ring = Ring(count, traffic)
-    load = pltpu.make_async_copy(p_ref, partial, load_sem[0].at[0])
-    load.start()
-    ring.meet()
-    added, drain = ring.scatter(partial, land, sems, None, p_ref, load.wait)
+        pass_on(block).wait()
+    ring.depart()
+    turn_keys(own_ref, other_ref, turned_ref)
+
+    def attend(blocks):
+        width = len(blocks) * GROUP * LANES
+        q = jnp.concatenate([q_ref[b].reshape(GROUP * LANES, LANES) for b in blocks], 0)
+        begin, query = query_rows(begin_ref, blocks, core)
+        end = last_chunk(blocks) + 1
+
+        def score(chunk, top):
+            keys = chunk_keys(own_ref, other_ref, chunk)
+            scores = jnp.where(allowed_keys(begin, query, chunk, core), dot(keys, q, NT), MASKED)
+            score_ref[chunk, :, :width] = scores
+            return jnp.maximum(top, jnp.max(scores, 0, keepdims=True))
+
+        top = lax.fori_loop(0, end, score, jnp.full((1, width), MASKED, F32))
+
+        def add(chunk, state):
+            total, acc = state
+            weights = jnp.exp(score_ref[chunk, :, :width] - top)
+            total = total + jnp.sum(weights, 0, keepdims=True)
+            return total, acc + dot(turned_ref[chunk], weights.astype(BF16))
+
+        total, acc = lax.fori_loop(
+            0, end, add, (jnp.zeros((1, width), F32), jnp.zeros((LANES, width), F32))
+        )
+        lse = top + jnp.log(total)
+        att = acc / total
+        rows = []
+        for place, block in enumerate(blocks):
+            here = slice(place * GROUP * LANES, (place + 1) * GROUP * LANES)
+            lse_ref[block] = lse[:, here]
+            heads = by_head(att[:, here])
+            low = lanes_of(heads[0]) < HD
+            rows.append(
+                jnp.concatenate(
+                    [jnp.where(low, turn(heads[0]), heads[1]), jnp.where(low, turn(heads[2]), 0.0)], 1
+                ).astype(BF16)
+            )
+            att_ref[block] = rows[-1]
+        out = dot(jnp.concatenate(rows, 0) if len(rows) > 1 else rows[0], wide_w[...]).astype(BF16)
+        for block, part in cut(out, blocks):
+            partial[block] = part
+
+    attend((ring.at(ring.steps),))
+
+    def between():
+        attend(ring.pair(ring.steps - 1))
+
+    def work(s, place):
+        if place == 2:
+
+            @pl.when(s < ring.steps - 2)
+            def _():
+                attend(ring.pair(ring.steps - 2 - s))
+
+            @pl.when(s == ring.steps - 2)
+            def _():
+                attend((ring.chip,))
+
+    added, finish = ring.scatter(partial, land, scatter_sem, work, between)
     ring.settle()
     middle = hidden_ref[...] + added
     middle_ref[...] = middle
     x = (normal(middle)[1] * gain_row(params_ref, 1, layer)).astype(BF16)
-    x_ref[...] = x
+    x_out_ref[...] = x
     experts = share_ref.shape[0]
     logits = dot(params_ref[router_rows(experts, layer), :].astype(BF16), x, NT)
     expert = lax.broadcasted_iota(jnp.int32, logits.shape, 0)
@@ -685,27 +738,50 @@
     for choice in range(routes_ref.shape[1]):
         named = named | (expert == routes_ref[layer, choice : choice + 1, :])
     scores = jnp.where(named, logits, MASKED)
-    weights = jnp.where(named, jnp.exp(scores - jnp.max(scores, 0, keepdims=True)), 0.0)
-    share_ref[...] = weights / jnp.sum(weights, 0, keepdims=True)
+    weighted = jnp.where(named, jnp.exp(scores - jnp.max(scores, 0, keepdims=True)), 0.0)
+    share_ref[...] = weighted / jnp.sum(weighted, 0, keepdims=True)
     drain()
-
-
-def scatter_route(count, layer, partial, hidden, params, routes):
-    _, rows, width = partial.shape
-    experts = 2 * count
+    finish()
+    keep.wait()
+
+
+def gather_attend_scatter(count, layer, x, w, w_out, tables, begin, hidden, params, routes):
+    rows, width = x.shape
+    block = cells((count, rows, LANES), BF16)
+    everyone = pltpu.VMEM((count, rows, width), BF16)
+    wide = 2 * LANES
     return ring_call(
-        functools.partial(route_kernel, count, layer),
-        ("route", layer),
-        [(partial, ANYWHERE), (hidden, LATE), (params, LATE), (routes, LATE)],
+        functools.partial(attend_kernel, count, layer),
+        ("attend", layer),
         [
+            (x, ANYWHERE), (w, ANYWHERE), (w_out, ANYWHERE), (tables, EARLY), (begin, EARLY),
+            (hidden, LATE), (params, LATE), (routes, LATE),
+        ],
+        [
+            (cells((count, GROUP, rows, LANES), BF16), SOON),
+            (block, SOON),
+            (block, SOON),
+            (cells((count, rows, width), BF16), ANYWHERE),
+            (cells((count, rows, wide), BF16), OUT),
+            (cells((count, 1, GROUP * rows), F32), OUT),
             (cells((rows, width), F32), OUT),
             (cells((rows, width), BF16), OUT),
-            (cells((experts, rows), F32), OUT),
+            (cells((2 * count, rows), F32), OUT),
         ],
-        [pltpu.VMEM(partial.shape, BF16), land_scratch(count, rows, width)]
+        [
+            everyone,
+            pltpu.VMEM(w.shape[1:], BF16),
+            pltpu.VMEM((wide, width), BF16),
+            pltpu.VMEM((count, LANES, wide), BF16),
+            pltpu.VMEM((count, wide, 2 * GROUP * LANES), F32),
+            everyone,
+            land_scratch(count, rows, width),
+        ]
+        + gather_sems(count)
+        + dmas((count,), (count,))
         + scatter_sems(count)
-        + dmas((1,)),
-        20,
+        + dmas((1,), (3,)),
+        60,
     )
 
 
@@ -815,7 +891,7 @@
         + gather_sems(count, True)
         + scatter_sems(count)
         + dmas((6,), (1,)),
-        56,
+        60,
     )
 
 
@@ -996,63 +1072,6 @@
     )
 
 
-def branch_back_kernel(count, layer, traffic, *refs):
-    inputs, outputs, scratch = split(refs, 3, 2)
-    d_ref, w_ref, att_ref = inputs
-    datt_ref, g_ref = outputs
-    buf, wide_w, acc, mail, got = scratch[:5]
-    sems, pair_sem, load_sem = split(scratch[5:], 3, 2)
-    ring = Ring(count, traffic)
-    shard = g_ref.shape[0]
-    loads = load_out_weights(w_ref, layer, wide_w, load_sem[0])
-    ring.meet(True)
-    acc[...] = jnp.zeros_like(acc)
-
-    def compute(place, blocks):
-        d = stack(buf, blocks)
-        datt = dot(d, wide_w[...], NT).astype(BF16)
-        for block, rows in cut(datt, blocks):
-            datt_ref[block] = rows
-        acc[...] += dot(stack(att_ref, blocks), d, TN)
-
-    drain = ring.gather(
-        d_ref, buf, sems, None, after_loads(loads, lambda s: None), ring.meanwhile(compute, 0)
-    )
-    compute(0, (ring.at(ring.steps),))
-    core = lax.rem(lax.axis_index("fsdp"), 2)
-    mail[...] = acc[pl.ds(pl.multiple_of((1 - core) * shard, 8), shard), :].astype(BF16)
-    swap = remote(mail, got, pair_sem[0].at[0], pair_sem[1].at[0], partner_of("fsdp"))
-    swap.start()
-    drain()
-    swap.wait()
-    own = acc[pl.ds(pl.multiple_of(core * shard, 8), shard), :]
-    g_ref[...] = (own + got[...].astype(F32)).astype(BF16)
-
-
-def gather_branch_back(count, layer, d, w, att):
-    rows, width = d.shape
-    shard = w.shape[2]
-    return ring_call(
-        functools.partial(branch_back_kernel, count, layer),
-        ("branch_back", layer),
-        [(d, ANYWHERE), (w, ANYWHERE), (att, EARLY)],
-        [
-            (cells((count, rows, 2 * LANES), BF16), OUT),
-            (cells((shard, width), BF16), OUT),
-        ],
-        [
-            pltpu.VMEM((count, rows, width), BF16),
-            pltpu.VMEM((2 * LANES, width), BF16),
-            pltpu.VMEM((2 * LANES, width), F32),
-            pltpu.VMEM((shard, width), BF16),
-            pltpu.VMEM((shard, width), BF16),
-        ]
-        + gather_sems(count)
-        + dmas((1,), (1,), (2,)),
-        20,
-    )
-
-
 def load_out_weights(w_ref, layer, wide_ref, sem):
     shard = w_ref.shape[2]
     copies = [
@@ -1066,31 +1085,102 @@
     return copies
 
 
-def join_kernel(count, layer, traffic, *refs):
-    inputs, outputs, scratch = split(refs, 12, 4)
-    dq_ref, own_ref, other_ref, table_ref, w_ref, x_ref, params_ref, mid_ref, hidden_ref = inputs[:9]
-    mixed_ref, router_ref, gain_two_ref = inputs[9:12]
-    grad_ref, d_mix_ref, side_ref, g_ref = outputs
-    partial, land, rows_ref, tokens, got, weights, last_ref = scratch[:7]
-    scatter_sem, pair_sem, load_sem = split(scratch[7:], 2, 2)
+def attend_back_kernel(count, layer, traffic, *refs):
+    inputs, outputs, scratch = split(refs, 17, 5)
+    d_ref, w_out_ref, w_ref, x_ref, att_ref, q_ref, own_ref, other_ref, begin_ref, lse_ref, table_ref = inputs[:11]
+    params_ref, mid_ref, hidden_ref, mixed_ref, router_ref, gain_two_ref = inputs[11:]
+    g_out_ref, grad_ref, d_mix_ref, side_ref, g_ref = outputs
+    buf, wide_w, g_acc, out_mail, out_got, turned_ref, d_own, d_other, mail, got, dq_ref = scratch[:11]
+    partial, land, rows_ref, tokens, weights, last_ref = scratch[11:17]
+    sems, scatter_sem, pair_sem, load_sem = split(scratch[17:], 3, 2, 2)
     ring = Ring(count, traffic)
-    loads = [
-        pltpu.make_async_copy(x_ref, tokens, load_sem[0].at[0]),
-        pltpu.make_async_copy(w_ref.at[layer], weights, load_sem[0].at[1]),
+    shard = g_out_ref.shape[0]
+    loads = load_out_weights(w_out_ref, layer, wide_w, load_sem[0])
+    later = [
+        pltpu.make_async_copy(x_ref, tokens, load_sem[0].at[2]),
+        pltpu.make_async_copy(w_ref.at[layer], weights, load_sem[0].at[3]),
     ]
-    for load in loads:
+    for load in later:
         load.start()
     ring.meet(True)
-    swap = remote(other_ref, got, pair_sem[0].at[0], pair_sem[1].at[0], partner_of("fsdp"))
-    swap.start()
-    swap.wait()
-    loads[1].wait()
-
-    def compute(index, carry):
-        blocks = 2 * index, 2 * index + 1
+    core = lax.rem(lax.axis_index("fsdp"), 2)
+    width = GROUP * LANES
+
+    def spread(wide):
+        front, back = wide[:, :LANES], wide[:, LANES:]
+        low = lanes_of(front) < HD
+        return [jnp.where(low, 0.0, part) for part in (turn(front), front, turn(back))]
+
+    def compute(block):
+        d = buf[block]
+        wide = dot(d, wide_w[...], NT).astype(BF16)
+        g_acc[...] += dot(att_ref[block], d, TN)
+        slopes, deltas = [], []
+        for piece, a in zip(spread(wide.astype(F32)), spread(att_ref[block].astype(F32))):
+            slopes.append(piece)
+            deltas.append(jnp.sum((piece * a).T, 0, keepdims=True))
+        datt = jnp.concatenate(slopes, 0).astype(BF16)
+        delta = jnp.concatenate(deltas, 1)
+        q = q_ref[block].reshape(width, LANES)
+        both = jnp.concatenate([q, datt], 0)
+        begin, query = query_rows(begin_ref, (block,), core)
+        lse = lse_ref[block]
+
+        def one(chunk, acc):
+            keys = chunk_keys(own_ref, other_ref, chunk)
+            scores = jnp.where(allowed_keys(begin, query, chunk, core), dot(keys, q, NT), MASKED)
+            weight = jnp.exp(scores - lse)
+            slope = (weight * (dot(keys, datt, NT) - delta)).astype(BF16)
+            d_keys = dot(jnp.concatenate([slope, weight.astype(BF16)], 1), both)
+            d_own[chunk] += d_keys[:LANES]
+            d_other[chunk] += d_keys[LANES:]
+            return acc + dot(turned_ref[chunk], slope)
+
+        acc = lax.fori_loop(0, block + 1, one, jnp.zeros((LANES, width), F32)) * (HD**-0.5)
+        heads = by_head(acc)
+        low = lanes_of(heads[0]) < HD
+        cosine, sine = angles(table_ref[block])
+        front = spin(jnp.where(low, heads[0], turn(heads[1])), cosine, -sine)
+        back = spin(jnp.where(low, heads[2], 0.0), cosine, -sine)
+        dq_ref[block] = jnp.concatenate([front, back], 1).astype(BF16)
+
+    def first(s):
+        @pl.when(s == 1)
+        def _():
+            for load in loads:
+                load.wait()
+            turn_keys(own_ref, other_ref, turned_ref)
+            g_acc[...] = jnp.zeros_like(g_acc)
+            d_own[...] = jnp.zeros_like(d_own)
+            d_other[...] = jnp.zeros_like(d_other)
+
+        @pl.when(s > 1)
+        def _():
+            compute(ring.at(s - 1))
+
+    def second(s):
+        compute(ring.at(1 - s))
+
+    drain = ring.gather(d_ref, buf, sems, None, first, second)
+    compute(ring.at(ring.steps))
+    partner = partner_of("fsdp")
+    mail[...] = d_other[...].astype(BF16)
+    out_mail[...] = g_acc[pl.ds(pl.multiple_of((1 - core) * shard, 8), shard), :].astype(BF16)
+    swaps = [
+        remote(mail, got, pair_sem[0].at[0], pair_sem[1].at[0], partner),
+        remote(out_mail, out_got, pair_sem[0].at[1], pair_sem[1].at[1], partner),
+    ]
+    for swap in swaps:
+        swap.start()
+    for load in later:
+        load.wait()
+    drain()
+    swaps[0].wait()
+
+    def join(blocks):
         rows = []
         for b in blocks:
-            pair = own_ref[b] + got[b].astype(F32)
+            pair = d_own[b] + got[b].astype(F32)
             cosine, sine = angles(table_ref[b])
             keys = spin(pair, cosine, -sine)
             low = lanes_of(pair) < HD
@@ -1103,12 +1193,17 @@
         total = dot(jnp.concatenate(rows, 0), weights[...], NT).astype(BF16)
         for block, part in cut(total, blocks):
             partial[block] = part
-        return carry
-
-    lax.fori_loop(0, count // 2, compute, 0)
-    loads[0].wait()
+
+    join((ring.at(ring.steps), ring.chip))
     strip = g_ref.shape[0] // ring.steps
     tile = 2 * LANES
+
+    def between():
+        def one(index, carry):
+            join(ring.pair(ring.steps - 1 - index))
+            return carry
+
+        lax.fori_loop(0, ring.steps - 1, one, 0)
 
     def work(s, place):
         if place == 0:
@@ -1117,7 +1212,10 @@
             g_ref[rows, :tile] = value[:, :tile].astype(BF16)
             last_ref[rows] = value[:, tile:]
 
-    d_x, drain = ring.scatter(partial, land, scatter_sem, work)
+    d_x, finish = ring.scatter(partial, land, scatter_sem, work, between)
+    swaps[1].wait()
+    own = g_acc[pl.ds(pl.multiple_of(core * shard, 8), shard), :]
+    g_out_ref[...] = (own + out_got[...].astype(F32)).astype(BF16)
     ring.settle()
     d_values, gain_one = normal_back(d_x, hidden_ref[...], gain_row(params_ref, 0, layer))
     grad = mid_ref[...] + d_values
@@ -1126,33 +1224,36 @@
     d_mix_ref[...] = d_mix
     balance = jnp.sum(mixed_ref[...] * d_mix.astype(F32), -1, keepdims=True)
     side_ref[...] = jnp.broadcast_to(as_line(balance), side_ref.shape)
-    core = lax.rem(lax.axis_index("fsdp"), 2)
     routers = router_ref[...]
-    first, second = routers[0:1], routers[1:2]
     lines = [
-        jnp.where(core == 0, first, second),
-        jnp.where(core == 0, second, first),
+        jnp.where(core == 0, routers[0:1], routers[1:2]),
+        jnp.where(core == 0, routers[1:2], routers[0:1]),
         gain_one,
         gain_two_ref[...],
     ]
-    width = g_ref.shape[0]
+    features = g_ref.shape[0]
     tall = jnp.concatenate(
-        [jnp.zeros((HD, width), F32)] + lines + [jnp.zeros((HD - len(lines), width), F32)], 0
+        [jnp.zeros((HD, features), F32)] + lines + [jnp.zeros((HD - len(lines), features), F32)], 0
     )
     g_ref[:, tile:] = (last_ref[...] + tall.T).astype(BF16)
-    drain()
-
-
-def join_scatter(count, layer, dq, own, other, tables, w, x_all, params, mid, hidden, mixed, g_router, gain_two):
+    finish()
+
+
+def gather_attend_back_scatter(
+    count, layer, d, w_out, w, x_all, att, q, own, other, begin, lse, tables, late, rides=()
+):
     _, rows, width = x_all.shape
+    shard = w_out.shape[2]
+    columns = w.shape[2]
     everyone = pltpu.VMEM((count, rows, width), BF16)
-    late = [params, mid, hidden, mixed, g_router, gain_two]
+    early = [att, q, own, other, begin, lse, tables]
+    pairs = cells((count, rows, LANES), BF16)
     return ring_call(
-        functools.partial(join_kernel, count, layer),
-        ("join", layer),
-        [(dq, EARLY), (own, EARLY), (other, ANYWHERE), (tables, EARLY), (w, ANYWHERE), (x_all, ANYWHERE)]
-        + [(a, LATE) for a in late],
+        functools.partial(attend_back_kernel, count, layer),
+        ("attend_back", layer),
+        [(a, ANYWHERE) for a in (d, w_out, w, x_all)] + [(a, EARLY) for a in early] + [(a, LATE) for a in late],
         [
+            (cells((shard, width), BF16), OUT),
             (cells((rows, width), F32), OUT),
             (cells((rows, width), BF16), OUT),
             (cells((8, rows), F32), OUT),
@@ -1160,16 +1261,28 @@
         ],
         [
             everyone,
+            pltpu.VMEM((2 * LANES, width), BF16),
+            pltpu.VMEM((2 * LANES, width), F32),
+            pltpu.VMEM((shard, width), BF16),
+            pltpu.VMEM((shard, width), BF16),
+            pltpu.VMEM((count, LANES, 2 * LANES), BF16),
+            pltpu.VMEM(pairs.shape, F32),
+            pltpu.VMEM(pairs.shape, F32),
+            pltpu.VMEM(pairs.shape, BF16),
+            pltpu.VMEM(pairs.shape, BF16),
+            pltpu.VMEM((count, rows, 2 * LANES), BF16),
+            everyone,
             land_scratch(count, rows, width),
-            pltpu.VMEM((count, rows, w.shape[2]), BF16),
+            pltpu.VMEM((count, rows, columns), BF16),
             everyone,
-            pltpu.VMEM(other.shape, BF16),
             pltpu.VMEM(w.shape[1:], BF16),
             pltpu.VMEM((width, LANES), F32),
         ]
+        + gather_sems(count)
         + scatter_sems(count)
-        + dmas((1,), (1,), (2,)),
-        28,
+        + dmas((2,), (2,), (4,)),
+        60,
+        rides,
     )
 
 
@@ -1277,7 +1390,7 @@
             dma((2,)), dma((2,)), dma((count,)), dma((count,)), dma((count,)), dma((count,)),
         ],
         compiler_params=pltpu.CompilerParams(
-            collective_id=identity(("finish",)), has_side_effects=True, vmem_limit_bytes=32 << 20
+            collective_id=identity(("finish",)), has_side_effects=True, vmem_limit_bytes=60 << 20
         ),
         cost_estimate=FREE,
         name="finish_heads",
@@ -1327,213 +1440,6 @@
 
 def chunk_keys(own_ref, other_ref, chunk):
     return jnp.concatenate([own_ref[chunk], other_ref[chunk]], 0)
-
-
-def allowed_keys(begin, query, chunk, core):
-    shape = (2 * LANES, begin.shape[1])
-    place = lax.broadcasted_iota(jnp.int32, shape, 0)
-    shift = jnp.where(place < LANES, core, -core)
-    key = chunk * 2 * LANES + place + shift * LANES
-    return (key >= begin) & (key <= query)
-
-
-def block_info(info_ref, begin_ref):
-    step = pl.program_id(0)
-    core = info_ref[0]
-    lane = lax.broadcasted_iota(jnp.int32, (1, LANES), 1)
-    begin, query = [], []
-    for part in range(PAIR):
-        begin += [begin_ref[part]] * GROUP
-        query += [(2 * (PAIR * step + part) + core) * LANES + lane] * GROUP
-    first = info_ref[1 + PAIR * step] // (2 * LANES)
-    return core, jnp.concatenate(begin, 1), jnp.concatenate(query, 1), first, PAIR * (step + 1)
-
-
-def chunk_keys(own_ref, other_ref, chunk):
-    return jnp.concatenate([own_ref[chunk], other_ref[chunk]], 0)
-
-
-def turn_keys(own_ref, other_ref, turned_ref):
-    for chunk in range(turned_ref.shape[0]):
-        turned_ref[chunk] = chunk_keys(own_ref, other_ref, chunk).astype(F32).T.astype(BF16)
-
-
-def by_head(field):
-    return [field[:, h * LANES : (h + 1) * LANES].T for h in range(GROUP)]
-
-
-def attend_kernel(layer, info_ref, q_ref, own_ref, other_ref, begin_ref, w_ref, att_ref, lse_ref, out_ref, wide_ref, turned_ref, score_ref, sem):
-    core, begin, query, first, last = block_info(info_ref, begin_ref)
-    width = PAIR * GROUP * LANES
-
-    @pl.when(pl.program_id(0) == 0)
-    def _():
-        loads = load_out_weights(w_ref, layer, wide_ref, sem)
-        turn_keys(own_ref, other_ref, turned_ref)
-        for load in loads:
-            load.wait()
-
-    q = q_ref[...].reshape(width, LANES)
-
-    def score(chunk, top):
-        keys = chunk_keys(own_ref, other_ref, chunk)
-        scores = jnp.where(allowed_keys(begin, query, chunk, core), dot(keys, q, NT), MASKED)
-        score_ref[chunk] = scores
-        return jnp.maximum(top, jnp.max(scores, 0, keepdims=True))
-
-    top = lax.fori_loop(first, last, score, jnp.full((1, width), MASKED, F32))
-
-    def add(chunk, state):
-        total, acc = state
-        weights = jnp.exp(score_ref[chunk] - top)
-        total = total + jnp.sum(weights, 0, keepdims=True)
-        return total, acc + dot(turned_ref[chunk], weights.astype(BF16))
-
-    total, acc = lax.fori_loop(
-        first, last, add, (jnp.zeros((1, width), F32), jnp.zeros((LANES, width), F32))
-    )
-    lse = top + jnp.log(total)
-    att = acc / total
-    rows = []
-    for part in range(PAIR):
-        here = slice(part * GROUP * LANES, (part + 1) * GROUP * LANES)
-        lse_ref[part] = lse[:, here]
-        heads = by_head(att[:, here])
-        low = lanes_of(heads[0]) < HD
-        rows.append(
-            jnp.concatenate(
-                [jnp.where(low, turn(heads[0]), heads[1]), jnp.where(low, turn(heads[2]), 0.0)], 1
-            ).astype(BF16)
-        )
-        att_ref[part] = rows[-1]
-    out = dot(jnp.concatenate(rows, 0), wide_ref[...]).astype(BF16)
-    for part in range(PAIR):
-        out_ref[part] = out[part * LANES : (part + 1) * LANES]
-
-
-def blocks_of(*shape):
-    return pl.BlockSpec((PAIR,) + shape, lambda i, s: (i,) + (0,) * len(shape))
-
-
-def attend(layer, info, q, own, other, begin, w):
-    blocks = q.shape[0]
-    width = w.shape[3]
-    wide = 2 * LANES
-    whole = pl.BlockSpec(own.shape, lambda i, s: (0, 0, 0))
-    return pl.pallas_call(
-        functools.partial(attend_kernel, layer),
-        grid_spec=pltpu.PrefetchScalarGridSpec(
-            num_scalar_prefetch=1,
-            grid=(blocks // PAIR,),
-            in_specs=[
-                blocks_of(GROUP, LANES, LANES), whole, whole, blocks_of(1, LANES), ANYWHERE,
-            ],
-            out_specs=[
-                blocks_of(LANES, wide), blocks_of(1, GROUP * LANES), blocks_of(LANES, width),
-            ],
-            scratch_shapes=[
-                pltpu.VMEM((wide, width), BF16),
-                pltpu.VMEM((blocks, LANES, wide), BF16),
-                pltpu.VMEM((blocks, wide, PAIR * GROUP * LANES), F32),
-                pltpu.SemaphoreType.DMA((2,)),
-            ],
-        ),
-        out_shape=(
-            cells((blocks, LANES, wide), BF16),
-            cells((blocks, 1, GROUP * LANES), F32),
-            cells((blocks, LANES, width), BF16),
-        ),
-        compiler_params=pltpu.CompilerParams(vmem_limit_bytes=28 << 20),
-        cost_estimate=FREE,
-        name="attend",
-    )(info, q, own, other, begin, w)
-
-
-def attend_back_kernel(
-    info_ref, q_ref, own_ref, other_ref, begin_ref, att_ref, lse_ref, datt_ref, table_ref,
-    dq_ref, d_own_ref, mail_ref, d_other_ref, turned_ref,
-):
-    core, begin, query, first, last = block_info(info_ref, begin_ref)
-    width = PAIR * GROUP * LANES
-
-    @pl.when(pl.program_id(0) == 0)
-    def _():
-        turn_keys(own_ref, other_ref, turned_ref)
-        d_own_ref[...] = jnp.zeros_like(d_own_ref)
-        d_other_ref[...] = jnp.zeros_like(d_other_ref)
-
-    q = q_ref[...].reshape(width, LANES)
-
-    def spread(wide):
-        front, back = wide[:, :LANES], wide[:, LANES:]
-        low = lanes_of(front) < HD
-        return [jnp.where(low, 0.0, part) for part in (turn(front), front, turn(back))]
-
-    slopes, deltas = [], []
-    for part in range(PAIR):
-        for d, a in zip(spread(datt_ref[part].astype(F32)), spread(att_ref[part].astype(F32))):
-            slopes.append(d)
-            deltas.append(jnp.sum((d * a).T, 0, keepdims=True))
-    datt = jnp.concatenate(slopes, 0).astype(BF16)
-    delta = jnp.concatenate(deltas, 1)
-    lse = jnp.concatenate([lse_ref[part] for part in range(PAIR)], 1)
-    both = jnp.concatenate([q, datt], 0)
-
-    def one(chunk, acc):
-        keys = chunk_keys(own_ref, other_ref, chunk)
-        scores = jnp.where(allowed_keys(begin, query, chunk, core), dot(keys, q, NT), MASKED)
-        weights = jnp.exp(scores - lse)
-        slope = (weights * (dot(keys, datt, NT) - delta)).astype(BF16)
-        d_keys = dot(jnp.concatenate([slope, weights.astype(BF16)], 1), both)
-        d_own_ref[chunk] += d_keys[:LANES]
-        d_other_ref[chunk] += d_keys[LANES:]
-        return acc + dot(turned_ref[chunk], slope)
-
-    acc = lax.fori_loop(first, last, one, jnp.zeros((LANES, width), F32)) * (HD**-0.5)
-    for part in range(PAIR):
-        heads = by_head(acc[:, part * GROUP * LANES : (part + 1) * GROUP * LANES])
-        low = lanes_of(heads[0]) < HD
-        cosine, sine = angles(table_ref[part])
-        front = spin(jnp.where(low, heads[0], turn(heads[1])), cosine, -sine)
-        back = spin(jnp.where(low, heads[2], 0.0), cosine, -sine)
-        dq_ref[part] = jnp.concatenate([front, back], 1).astype(BF16)
-
-    @pl.when(pl.program_id(0) == pl.num_programs(0) - 1)
-    def _():
-        mail_ref[...] = d_other_ref[...].astype(BF16)
-
-
-def attend_back(info, q, own, other, begin, att, lse, datt, tables):
-    blocks = q.shape[0]
-    wide = 2 * LANES
-    whole = pl.BlockSpec(own.shape, lambda i, s: (0, 0, 0))
-    return pl.pallas_call(
-        attend_back_kernel,
-        grid_spec=pltpu.PrefetchScalarGridSpec(
-            num_scalar_prefetch=1,
-            grid=(blocks // PAIR,),
-            in_specs=[
-                blocks_of(GROUP, LANES, LANES),
-                whole,
-                whole,
-                blocks_of(1, LANES),
-                blocks_of(LANES, wide),
-                blocks_of(1, GROUP * LANES),
-                blocks_of(LANES, wide),
-                blocks_of(HD, LANES),
-            ],
-            out_specs=[blocks_of(LANES, wide), whole, whole],
-            scratch_shapes=[pltpu.VMEM(own.shape, F32), pltpu.VMEM((blocks, LANES, wide), BF16)],
-        ),
-        out_shape=(
-            cells((blocks, LANES, wide), BF16),
-            cells(own.shape, F32),
-            cells(own.shape, BF16),
-        ),
-        compiler_params=pltpu.CompilerParams(vmem_limit_bytes=28 << 20),
-        cost_estimate=FREE,
-        name="attend_back",
-    )(info, q, own, other, begin, att, lse, datt, tables)
 
 
 def on_device(
@@ -1595,18 +1501,16 @@
     kinds = jnp.arange(8, dtype=jnp.int32)[:, None]
     starts = jnp.sum((flat_segments < kinds).astype(jnp.int32), 1, keepdims=True)
     begin = jnp.sum(jnp.where(flat_segments == kinds, starts, 0), 0).reshape(count, 2, rows)
-    begin = lax.dynamic_index_in_dim(begin, core, 1, False)
-    info = jnp.concatenate([core[None], begin[:, 0]]).astype(jnp.int32)
-    begin = begin[:, None, :]
+    begin = lax.dynamic_index_in_dim(begin, core, 1, True)
 
     hidden = tokens.astype(F32)
     x_attn = (normal(hidden)[1] * params[0:1]).astype(BF16)
     chosen = routes.transpose(0, 2, 1)
     saved = []
     for layer in range(LAYERS):
-        query, kv, kv_other, x_all = gather_project(count, layer, x_attn, heads_w, tables)
-        att, lse, partial = attend(layer, info, query, kv, kv_other, begin, outs_w)
-        middle, x_moe, share = scatter_route(count, layer, partial, hidden, params, chosen)
+        query, kv, kv_other, x_all, att, lse, middle, x_moe, share = gather_attend_scatter(
+            count, layer, x_attn, heads_w, outs_w, tables, begin, hidden, params, chosen
+        )
         mixed, after, x_attn, m_all, share_all = gather_mix_scatter(
             count, layer, x_moe, share, middle, params, experts_w
         )
@@ -1633,15 +1537,11 @@
                 (d_branch, expert_sums[layer + 1])
             )
         expert_sums[layer] = (expert_sum, across(expert_sum))
-        datt, out_sum = gather_branch_back(count, layer, d_branch, outs_w, att)
+        out_sum, grad, d_mix, side, heads = gather_attend_back_scatter(
+            count, layer, d_branch, outs_w, heads_w, x_all, att, query, kv, kv_other, begin, lse, tables,
+            [params, grad_mid, hidden, saved[max(layer - 1, 0)][8], g_router, gain_two],
+        )
         out_sums[layer] = out_sum
-        d_query, d_own, d_other = attend_back(
-            info, query, kv, kv_other, begin, att, lse, datt, tables
-        )
-        grad, d_mix, side, heads = join_scatter(
-            count, layer, d_query, d_own, d_other, tables, heads_w, x_all, params, grad_mid, hidden,
-            saved[max(layer - 1, 0)][8], g_router, gain_two,
-        )
         heads = heads.reshape(count, 2, shard, columns)
         early = heads if layer > 0 else early
     g_query, g_key, g_value, rest = finish_heads(

time: 817 us -> 759 us (0.929)
  Pallas kernels: 750 us -> 711 us
  local copies, waits for them, and re-layouts: 40.6 us -> 18.9 us
    pallas_call x4 -> x0, Pallas kernels: 68.7 us -> none  [the longest x2 38 us: attend_back(): pl.pallas_call(attend_back_kernel, grid_spec=pltpu.PrefetchScalarGridSpec...]
    unnamed x147 -> x39, local copies, waits for them, and re-layouts: 33.4 us -> 7.1 us
    pallas_call x12 -> x8, Pallas kernels: 600 us -> 627 us  [ring_call(): pl.pallas_call(kernel, out_shape=tuple((shape for shape, _ in outputs)) +...]
  transfers between devices with their start and end apart: 6 -> 6, of which waited for: 0 -> 0; matrix products, arithmetic and copies ran while one was open for 1% -> 2% of each run, Pallas kernels for 51% -> 51%
where the time goes in v6:
time: 759 us; the launch traced here: 750 us
  Pallas kernels  711 us (94%)
  local copies, waits for them, and re-layouts  18.9 us (2%)
  other arithmetic  13.6 us (2%)
    pallas_call x8, Pallas kernels, ring_call(): pl.pallas_call(kernel, out_shape=tuple((shape for shape, _ in outputs)) +...  627 us
    pallas_call x1, Pallas kernels, finish_heads(): pl.pallas_call(functools.partial(finish_kernel, count, replicas), out_sha...  36.9 us
    pallas_call x1, Pallas kernels, exchange_weights(): pl.pallas_call(functools.partial(setup_kernel, count), out_shape=(jax.Sha...  34.7 us
  transfers between devices with their start and end apart: 6, of which 0 were waited for; matrix products, arithmetic and copies ran while one was open for 2% of the time, Pallas kernels for 51%

profile of v6, /device:TPU:0, one launch (start us, length us, event | category | flops | bytes accessed | tf_op | source)
XLA Modules:
  0.0 749.8 jit_solution(1117687421665754778)
XLA Ops:
  0.7 0.7 convert_element_type.37
  1.4 1.1 copy.49
  2.5 0.9 copy.52
  3.4 1.1 copy.50
  4.5 0.9 copy.53
  5.5 0.6 reshape.71
  6.1 0.2 copy.51
  6.5 0.6 pad_maximum_fusion.1.table_ref
  7.1 1.5 fusion.8.small_ref
  8.6 2.6 maximum_bitcast_fusion.slab_ref
  11.2 34.7 %exchange_weights.1 = (bf16[2,16,96,384]{3,2,1,0:T(8,128)(2,1)}, bf16[2,2,96,1536]{3,2,1,0:T(8,128)(2,1)}, bf16[16,48,128]{2,1,0:T(8,128)(2,1)}, f32[8,64,128]{2,1,0:T(8,128)}) custom-call(bf16[8,2,96,384]{3,2,1,0:T(8,128)(2,1)} %maximum_bitcast_fusion.slab_ref, bf16[2,96,1536]{2,1,0:T(8,128)(2,1)} %out_w_ref.1, bf16[48,128]{1,0:T(8,128)(2,1)} %fusion.8.small_ref, ...), custom_call_target="tpu_custom_call" | custom-call | tf_op jit(solution)/shard_map/exchange_weights/pallas_call | solution.py:467
  45.9 0.4 collective-permute-start
  46.5 0.4 collective-permute-start.2
  46.9 1.0 convert_element_type.36.refs_5_.refs_13_
  47.8 2.0 convert_element_type.43.refs_5_
  49.8 0.7 copy-done.4
  50.6 0.8 copy.54
  51.3 1.8 convert_element_type.42.refs_6_.refs_3_.refs_4_.refs_11_
  53.1 1.5 slice_reduce_fusion.3
  54.6 0.8 mul.46
  55.6 0.6 constant_dynamic-slice_fusion.refs_4_.refs_8_
  56.4 0.9 multiply_convert_fusion.refs_0_
  57.3 86.0 %attend.2 = (bf16[8,3,128,128]{3,2,1,0:T(8,128)(2,1)}, bf16[8,128,128]{2,1,0:T(8,128)(2,1)}, bf16[8,128,128]{2,1,0:T(8,128)(2,1)}, bf16[8,128,1536]{2,1,0:T(8,12...) custom-call(bf16[128,1536]{1,0:T(8,128)(2,1)} %multiply_convert_fusi, ...), custom_call_target="tpu_custom_call" | custom-call | tf_op jit(solution)/shard_map/attend/pallas_call | solution.py:348
  143.3 70.2 %mix.2 = (f32[128,1536]{1,0:T(8,128)}, f32[128,1536]{1,0:T(8,128)}, bf16[128,1536]{1,0:T(8,128)(2,1)}, bf16[8,128,1536]{2,1,0:T(8,128)(2,1)}, f32[8,16,128]{2,1,0:T(8,128)}) custom-call(bf16[128,1536]{1,0:T(8,128)(2,1)} %get-tuple-element.80.refs_0_, f32[16,128]{1,0:T(8,128)} %get-tuple-element.81.refs_1_, f32[128,1536]{1,0:T(8,128)} %get-tuple-element.82.refs_2_.refs_6_, ...), custom_call_target="tpu_custom_call" | custom-call | tf_op jit(solution)/shard_map/mix/pallas_call | solution.py:348
  213.6 74.8 %attend.3 = (bf16[8,3,128,128]{3,2,1,0:T(8,128)(2,1)}, bf16[8,128,128]{2,1,0:T(8,128)(2,1)}, bf16[8,128,128]{2,1,0:T(8,128)(2,1)}, bf16[8,128,1536]{2,1,0:T(8,12...) custom-call(bf16[128,1536]{1,0:T(8,128)(2,1)} %get-tuple-element.86., ...), custom_call_target="tpu_custom_call" | custom-call | tf_op jit(solution)/shard_map/attend/pallas_call | solution.py:348
  288.4 70.7 %mix.3 = (f32[128,1536]{1,0:T(8,128)}, f32[128,1536]{1,0:T(8,128)}, bf16[128,1536]{1,0:T(8,128)(2,1)}, bf16[8,128,1536]{2,1,0:T(8,128)(2,1)}, f32[8,16,128]{2,1,0:T(8,128)}) custom-call(bf16[128,1536]{1,0:T(8,128)(2,1)} %get-tuple-element.88.refs_0_, f32[16,128]{1,0:T(8,128)} %get-tuple-element.89.refs_1_, f32[128,1536]{1,0:T(8,128)} %get-tuple-element.90.refs_2_.refs_6_, ...), custom_call_target="tpu_custom_call" | custom-call | tf_op jit(solution)/shard_map/mix/pallas_call | solution.py:348
  359.1 1.3 multiply_reduce_fusion
  360.4 0.6 broadcast_in_dim.29.refs_1_
  361.0 76.9 %mix_back.2 = (f32[128,1536]{1,0:T(8,128)}, bf16[128,1536]{1,0:T(8,128)(2,1)}, f32[1,1536]{1,0:T(1,128)}, bf16[4608,512]{1,0:T(8,128)(2,1)}, f32[2,1536]{1,0:T(2,128)}) custom-call(bf16[128,1536]{1,0:T(8,128)(2,1)} %refs_0_.1, f32[8,128]{1,0:T(8,128)} %broadcast_in_dim.29.refs_1_, bf16[8,128,1536]{2,1,0:T(8,128)(2,1)} %get-tuple-element.93.refs_2_, ...), custom_call_target="tpu_custom_call" | custom-call | tf_op jit(solution)/shard_map/mix_back/pallas_call | solution.py:348
  437.9 1.7 collective-permute-start.3
  439.7 84.7 %attend_back.2 = (bf16[96,1536]{1,0:T(8,128)(2,1)}, f32[128,1536]{1,0:T(8,128)}, bf16[128,1536]{1,0:T(8,128)(2,1)}, f32[8,128]{1,0:T(8,128)}, bf16[1536,384]{1,0:T(8,128)(2,1)}) custom-call(bf16[128,1536]{1,0:T(8,128)(2,1)} %get-tuple-element.95.refs_0_, bf16[2,2,96,1536]{3,2,1,0:T(8,128)(2,1)} %get-tuple-element.78.refs_2_.refs_1_, ...), custom_call_target="tpu_custom_call" | custom-call | tf_op jit(solution)/shard_map/attend_back/pallas_call | solution.py:348
  524.4 78.3 %mix_back.3 = (f32[128,1536]{1,0:T(8,128)}, bf16[128,1536]{1,0:T(8,128)(2,1)}, f32[1,1536]{1,0:T(1,128)}, bf16[4608,512]{1,0:T(8,128)(2,1)}, f32[2,1536]{1,0:T(2...) custom-call(bf16[128,1536]{1,0:T(8,128)(2,1)} %get-tuple-element.106.refs_0_, ...), custom_call_target="tpu_custom_call" | custom-call | tf_op jit(solution)/shard_map/mix_back/pallas_call | solution.py:348
  602.8 0.4 collective-permute-start.5
  603.2 1.0 add_bitcast_fusion
  604.2 84.8 %attend_back.3 = (bf16[96,1536]{1,0:T(8,128)(2,1)}, f32[128,1536]{1,0:T(8,128)}, bf16[128,1536]{1,0:T(8,128)(2,1)}, f32[8,128]{1,0:T(8,128)}, bf16[1536,384]{1,0:T(8,128)(2,1)}) custom-call(bf16[128,1536]{1,0:T(8,128)(2,1)} %get-tuple-element.115.refs_0_, bf16[2,2,96,1536]{3,2,1,0:T(8,128)(2,1)} %get-tuple-element.78.refs_2_.refs_1_, ...), custom_call_target="tpu_custom_call" | custom-call | tf_op jit(solution)/shard_map/attend_back/pallas_call | solution.py:348
  689.0 1.7 collective-permute-start.4
  690.7 36.9 %finish_heads.1 = (f32[2,96,1536]{2,1,0:T(8,128)}, f32[2,96,512]{2,1,0:T(8,128)}, f32[2,96,512]{2,1,0:T(8,128)}, f32[2,8,96,128]{3,2,1,0:T(8,128)}) custom-call(bf16[8,2,96,384]{3,2,1,0:T(8,128)(2,1)} %bitcast.28, bf16[8,2,96,384]{3,2,1,0:T(8,128)(2,1)} %bitcast.27, bf16[8,2,96,384]{3,2,1,0:T(8,128)(2,1)} %get-tuple-element.127.refs_2_), custom_call_target="tpu_custom_call" | custom-call | tf_op jit(solution)/shard_map/finish_heads/pallas_call | solution.py:1374
  727.6 1.4 slice_bitcast_fusion
  729.0 0.9 copy.55
  729.9 12.9 %add_experts.1 = (f32[2,1,1536,512]{3,2,1,0:T(8,128)}, f32[2,1,1536,512]{3,2,1,0:T(8,128)}, f32[2,1,512,1536]{3,2,1,0:T(8,128)}) custom-call(bf16[4608,512]{1,0:T(8,128)(2,1)} %get-tuple-element.134.refs_0_.refs_1_.refs_2_.refs_3_.refs_4_, bf16[4608,512]{1,0:T(8,128)(2,1)} %get-tuple-element.134.refs_0_.refs_1_.refs_2_.refs_3_.refs_4_, ...), custom_call_target="tpu_custom_call" | custom-call | tf_op jit(solution)/shard_map/add_experts/pallas_call | solution.py:1422
  742.8 0.3 slice_reduce_fusion
  743.1 0.8 slice_reduce_fusion.1
  744.0 1.1 pad_maximum_fusion
  745.1 0.7 copy.61
  745.9 0.9 copy.62
  746.7 1.0 copy.63
  747.8 0.7 copy.64
  748.5 0.7 copy.65
  (48 shorter events, 0.9 us)
Async XLA Ops:
  0.6 4.8 copy-start.8
  2.5 4.6 copy-start.15
  6.2 39.7 %copy-start = (bf16[2,1,1536,512]{3,2,1,0:T(8,128)(2,1)S(1)}, bf16[2,1,1536,512]{3,2,1,0:T(8,128)(2,1)}, u32[]{:S(2)}) copy-start(bf16[2,1,1536,512]{3,2,1,0:T(8,128)(2,1)} %refs_7_.1) | copy-start | bytes 9437188
  6.3 40.5 %copy-start.1 = (bf16[128,1536]{1,0:T(8,128)(2,1)S(1)}, bf16[128,1536]{1,0:T(8,128)(2,1)}, u32[]{:S(2)}) copy-start(bf16[128,1536]{1,0:T(8,128)(2,1)} %param.15) | copy-start | bytes 1179652
  45.9 9.4 %copy-start.14 = (s32[1,2048]{1,0:T(1,128)S(1)}, s32[1,2048]{1,0:T(1,128)}, u32[]{:S(2)}) copy-start(s32[1,2048]{1,0:T(1,128)} %param.18) | copy-start | bytes 24580
  45.9 97.4 %collective-permute-start = (bf16[2,1,1536,512]{3,2,1,0:T(8,128)(2,1)S(1)}, bf16[2,1,1536,512]{3,2,1,0:T(8,128)(2,1)}, u32[]{:S(2)}, u32[]{:S(2)}) collective-permute-start(bf16[2,1,1536,512]{3,2,1,0:T(8,128)(2,1)S(1)} %copy-done), channel_id=1, source_target_pairs={{0,1},{1,0},{2,3},{3,2},{4,5},{5,4},{6,7},{7,6},{8,9},{9,8},{10,11... | collective-permute-start | bytes 9437192 | tf_op jit(solution)/shard_map/ppermute | solution.py:1475
  46.4 96.9 %collective-permute-start.1 = (bf16[2,1,1536,512]{3,2,1,0:T(8,128)(2,1)}, bf16[2,1,1536,512]{3,2,1,0:T(8,128)(2,1)}, u32[]{:S(2)}, u32[]{:S(2)}) collective-permute-start(bf16[2,1,1536,512]{3,2,1,0:T(8,128)(2,1)} %refs_8_.1), channel_id=1, source_target_pairs={{0,1},{1,0},{2,3},{3,2},{4,5},{5,4},{6,7},{7,6},{8,9},{9,8},{10,11... | collective-permute-start | bytes 9437192 | tf_op jit(solution)/shard_map/ppermute | solution.py:1475
  46.5 96.8 %collective-permute-start.2 = (bf16[2,1,512,1536]{3,2,1,0:T(8,128)(2,1)}, bf16[2,1,512,1536]{3,2,1,0:T(8,128)(2,1)}, u32[]{:S(2)}, u32[]{:S(2)}) collective-permute-start(bf16[2,1,512,1536]{3,2,1,0:T(8,128)(2,1)} %refs_9_.1), channel_id=1, source_target_pairs={{0,1},{1,0},{2,3},{3,2},{4,5},{5,4},{6,7},{7,6},{8,9},{9,8},{10,11... | collective-permute-start | bytes 9437192 | tf_op jit(solution)/shard_map/ppermute | solution.py:1475
  46.9 2.9 copy-start.13
  49.8 0.7 copy-start.4
  288.4 70.7 %copy-start.2 = (bf16[128,1536]{1,0:T(8,128)(2,1)S(1)}, bf16[128,1536]{1,0:T(8,128)(2,1)}, u32[]{:S(2)}) copy-start(bf16[128,1536]{1,0:T(8,128)(2,1)} %refs_0_.1) | copy-start | bytes 1179652
  437.9 166.3 %collective-permute-start.3 = (bf16[4608,512]{1,0:T(8,128)(2,1)}, bf16[4608,512]{1,0:T(8,128)(2,1)}, u32[]{:S(2)}, u32[]{:S(2)}) collective-permute-start(bf16[4608,512]{1,0:T(8,128)(2,1)} %get-tuple-element.135.refs_10_.refs_11_.refs_12_.refs_13_.refs_14_), channel_id=1, source_target_pairs={{0,16},{16,0},{1,17},{17,1},{2,18},{18,2},{3,19},{19,3},{4,20},{20... | collective-permute-start | bytes 14155784 | tf_op jit(solution)/shard_map/ppermute | solution.py:1522
  524.4 78.8 %copy-start.6 = (bf16[96,1536]{1,0:T(8,128)(2,1)S(1)}, bf16[96,1536]{1,0:T(8,128)(2,1)}, u32[]{:S(2)}) copy-start(bf16[96,1536]{1,0:T(8,128)(2,1)} %get-tuple-element.111.refs_13_) | copy-start | bytes 884740
  602.8 127.1 %collective-permute-start.5 = (bf16[4608,512]{1,0:T(8,128)(2,1)}, bf16[4608,512]{1,0:T(8,128)(2,1)}, u32[]{:S(2)}, u32[]{:S(2)}) collective-permute-start(bf16[4608,512]{1,0:T(8,128)(2,1)} %get-tuple-element.134.refs_0_.refs_1_.refs_2_.refs_3_.refs_4_), channel_id=1, source_target_pairs={{0,16},{16,0},{1,17},{17,1},{2,18},{18,2},{3,19},{19,3},{4,20},{20... | collective-permute-start | bytes 14155784 | tf_op jit(solution)/shard_map/ppermute | solution.py:1522
  689.0 54.9 %collective-permute-start.4 = (bf16[96,1536]{1,0:T(8,128)(2,1)}, bf16[96,1536]{1,0:T(8,128)(2,1)S(1)}, u32[]{:S(2)}, u32[]{:S(2)}) collective-permute-start(bf16[96,1536]{1,0:T(8,128)(2,1)} %get-tuple-element.132), channel_id=1, source_target_pairs={{0,16},{16,0},{1,17},{17,1},{2,18},{18,2},{3,19},{19,3},{4,20},{20... | collective-permute-start | bytes 884744 | tf_op jit(solution)/shard_map/ppermute | solution.py:1522
  729.9 12.9 %copy-start.3 = (f32[2,8,96,128]{3,2,1,0:T(8,128)S(1)}, f32[2,8,96,128]{3,2,1,0:T(8,128)}, u32[]{:S(2)}) copy-start(f32[2,8,96,128]{3,2,1,0:T(8,128)} %get-tuple-element.128) | copy-start | bytes 2359300
  729.9 14.1 %copy-start.12 = (bf16[96,1536]{1,0:T(8,128)(2,1)S(1)}, bf16[96,1536]{1,0:T(8,128)(2,1)}, u32[]{:S(2)}) copy-start(bf16[96,1536]{1,0:T(8,128)(2,1)} %get-tuple-element.132) | copy-start | bytes 884740
  742.8 2.3 copy-start.9
  743.1 2.8 copy-start.7
  744.0 2.7 copy-start.5
  745.1 2.7 copy-start.11
  745.9 2.6 copy-start.10

commit v7 on v6

--- a/solution.py
+++ b/solution.py
@@ -13,6 +13,7 @@
 LAYERS = 2
 GROUP = HEADS // KV_HEADS
 LANES = 128
+SPAN = 2
 EPS = 1e-06
 MASKED = -1e30
 MESH = pl.DeviceIdType.MESH
@@ -144,7 +145,16 @@
         for key in early + late:
             piece(key, 0, self.chip, x_ref).start()
 
-        def step(s, carry):
+        def take(keys, s, last):
+            for key in keys:
+                block = toward(key, s)
+                piece(key, s - 1, block).wait_recv()
+
+                @pl.when(s < last)
+                def _():
+                    piece(key, s, block).start()
+
+        def take_side(s):
             if side is not None:
                 for direction in range(2):
 
@@ -157,34 +167,20 @@
                         def _():
                             side_piece(direction, s, block).start()
 
-            for key in early:
-                block = toward(key, s)
-                piece(key, s - 1, block).wait_recv()
-
-                @pl.when(s < steps)
-                def _():
-                    piece(key, s, block).start()
-
-            if first is not None:
-                first(s)
-
-            @pl.when(s < steps)
-            def _():
-                for key in late:
-                    block = toward(key, s)
-                    piece(key, s - 1, block).wait_recv()
-
-                    @pl.when(s < steps - 1)
-                    def _():
-                        piece(key, s, block).start()
-
-            if second is not None:
-                second(s)
+        def step(s, carry):
+            take_side(s)
+            take(early, s, steps)
+            first(s)
+            take(late, s, steps - 1)
+            second(s)
             return carry
 
         for copy in own:
             copy.wait()
-        lax.fori_loop(1, steps + 1, step, 0)
+        lax.fori_loop(1, steps, step, 0)
+        first(steps)
+        take_side(steps)
+        take(early, steps, steps)
 
         def drain():
             for s in range(steps):
@@ -200,17 +196,18 @@
     def pair(self, s):
         return self.at(s), self.at(-s)
 
-    def meanwhile(self, compute, place):
-        def run(s):
+    def meanwhile(self, compute):
+        def first(s):
             @pl.when(s == 1)
             def _():
-                compute(place, (self.chip,))
+                for part in range(2):
+                    compute(part, (self.chip,))
 
             @pl.when(s > 1)
             def _():
-                compute(place, self.pair(s - 1))
-
-        return run
+                compute(1, self.pair(s - 1))
+
+        return first, lambda s: compute(0, self.pair(s))
 
     def scatter(self, partial, land, sems, work=None, between=None):
         send_sem, recv_sem = sems
@@ -589,10 +586,13 @@
 
 
 def allowed_keys(begin, query, chunk, core):
-    shape = (2 * LANES, begin.shape[1])
-    place = lax.broadcasted_iota(jnp.int32, shape, 0)
-    shift = jnp.where(place < LANES, core, -core)
-    key = chunk * 2 * LANES + place + shift * LANES
+    half = SPAN * LANES
+    shape = (2 * half, begin.shape[1])
+    place = lax.broadcasted_iota(jnp.int32, (2 * half, 1), 0)
+    inner = lax.rem(place, half)
+    whose = jnp.where(place < half, core, 1 - core)
+    key = chunk * 2 * half + inner // LANES * (2 * LANES) + whose * LANES + lax.rem(inner, LANES)
+    key = jnp.broadcast_to(key, shape)
     return (key >= begin) & (key <= query)
 
 
@@ -606,7 +606,8 @@
 
 
 def chunk_keys(own_ref, other_ref, chunk):
-    return jnp.concatenate([own_ref[chunk], other_ref[chunk]], 0)
+    chips = pl.ds(chunk * SPAN, SPAN)
+    return jnp.concatenate([flat(own_ref[chips]), flat(other_ref[chips])], 0)
 
 
 def turn_keys(own_ref, other_ref, turned_ref):
@@ -621,8 +622,9 @@
     return [field[:, h * LANES : (h + 1) * LANES].T for h in range(GROUP)]
 
 
-def last_chunk(blocks):
-    return blocks[0] if len(blocks) == 1 else jnp.maximum(*blocks)
+def chunks_of(blocks):
+    last = blocks[0] if len(blocks) == 1 else jnp.maximum(*blocks)
+    return last // SPAN + 1
 
 
 def attend_kernel(count, layer, traffic, *refs):
@@ -644,7 +646,7 @@
             own_ref.at[block], other_ref.at[block], pair_sems[0].at[block], pair_sems[1].at[block], partner
         )
 
-    def project(place, blocks):
+    def project(blocks):
         rows = dot(stack(buf, blocks), weights[...])
         tables = [angles(table_ref[b]) for b in blocks]
         cosine = jnp.concatenate([t[0] for t in tables], 0)
@@ -657,12 +659,17 @@
             own_ref[block] = part
             pass_on(block).start()
 
-    drain = ring.gather(
-        x_ref, buf, sems, None, after_loads(loads, lambda s: None), ring.meanwhile(project, 0)
-    )
+    def first(s):
+        @pl.when(s == 1)
+        def _():
+            for load in loads:
+                load.wait()
+            project((ring.chip,))
+
+    drain = ring.gather(x_ref, buf, sems, None, first, lambda s: project(ring.pair(s)))
     keep = pltpu.make_async_copy(buf, all_ref, out_sem[0].at[0])
     keep.start()
-    project(0, (ring.at(ring.steps),))
+    project((ring.at(ring.steps),))
     for block in range(count):
         pass_on(block).wait()
     ring.depart()
@@ -672,7 +679,7 @@
         width = len(blocks) * GROUP * LANES
         q = jnp.concatenate([q_ref[b].reshape(GROUP * LANES, LANES) for b in blocks], 0)
         begin, query = query_rows(begin_ref, blocks, core)
-        end = last_chunk(blocks) + 1
+        end = chunks_of(blocks)
 
         def score(chunk, top):
             keys = chunk_keys(own_ref, other_ref, chunk)
@@ -772,8 +779,8 @@
             everyone,
             pltpu.VMEM(w.shape[1:], BF16),
             pltpu.VMEM((wide, width), BF16),
-            pltpu.VMEM((count, LANES, wide), BF16),
-            pltpu.VMEM((count, wide, 2 * GROUP * LANES), F32),
+            pltpu.VMEM((count // SPAN, LANES, SPAN * wide), BF16),
+            pltpu.VMEM((count // SPAN, SPAN * wide, 2 * GROUP * LANES), F32),
             everyone,
             land_scratch(count, rows, width),
         ]
@@ -840,10 +847,8 @@
             for block, rows in cut(total, blocks):
                 partial[block] = rows
 
-    drain = ring.gather(
-        x_ref, buf, sems, (side_ref, share_ref),
-        after_loads(loads, ring.meanwhile(compute, 0)), ring.meanwhile(compute, 1),
-    )
+    first, second = ring.meanwhile(compute)
+    drain = ring.gather(x_ref, buf, sems, (side_ref, share_ref), after_loads(loads, first), second)
     keep = pltpu.make_async_copy(buf, all_ref, out_sem[0].at[0])
     keep.start()
     for e in range(2):
@@ -942,10 +947,8 @@
             for block, rows in cut(total, blocks):
                 partial[block] = rows
 
-    drain = ring.gather(
-        d_ref, buf, sems, (side_ref, balance_ref),
-        after_loads(loads, ring.meanwhile(compute, 0)), ring.meanwhile(compute, 1),
-    )
+    first, second = ring.meanwhile(compute)
+    drain = ring.gather(d_ref, buf, sems, (side_ref, balance_ref), after_loads(loads, first), second)
     for e in range(2):
         compute(e, (ring.at(ring.steps),))
 
@@ -1132,11 +1135,13 @@
             weight = jnp.exp(scores - lse)
             slope = (weight * (dot(keys, datt, NT) - delta)).astype(BF16)
             d_keys = dot(jnp.concatenate([slope, weight.astype(BF16)], 1), both)
-            d_own[chunk] += d_keys[:LANES]
-            d_other[chunk] += d_keys[LANES:]
+            half = SPAN * LANES
+            chips = pl.ds(chunk * SPAN, SPAN)
+            d_own[chips] += d_keys[:half].reshape(SPAN, LANES, LANES)
+            d_other[chips] += d_keys[half:].reshape(SPAN, LANES, LANES)
             return acc + dot(turned_ref[chunk], slope)
 
-        acc = lax.fori_loop(0, block + 1, one, jnp.zeros((LANES, width), F32)) * (HD**-0.5)
+        acc = lax.fori_loop(0, chunks_of((block,)), one, jnp.zeros((LANES, width), F32)) * (HD**-0.5)
         heads = by_head(acc)
         low = lanes_of(heads[0]) < HD
         cosine, sine = angles(table_ref[block])
@@ -1154,12 +1159,10 @@
             d_own[...] = jnp.zeros_like(d_own)
             d_other[...] = jnp.zeros_like(d_other)
 
-        @pl.when(s > 1)
-        def _():
-            compute(ring.at(s - 1))
+        compute(ring.at(1 - s))
 
     def second(s):
-        compute(ring.at(1 - s))
+        compute(ring.at(s))
 
     drain = ring.gather(d_ref, buf, sems, None, first, second)
     compute(ring.at(ring.steps))
@@ -1265,7 +1268,7 @@
             pltpu.VMEM((2 * LANES, width), F32),
             pltpu.VMEM((shard, width), BF16),
             pltpu.VMEM((shard, width), BF16),
-            pltpu.VMEM((count, LANES, 2 * LANES), BF16),
+            pltpu.VMEM((count // SPAN, LANES, SPAN * 2 * LANES), BF16),
             pltpu.VMEM(pairs.shape, F32),
             pltpu.VMEM(pairs.shape, F32),
             pltpu.VMEM(pairs.shape, BF16),
@@ -1287,11 +1290,11 @@
 
 
 def finish_kernel(count, replicas, *refs):
-    inputs, outputs, scratch = split(refs, 3, 4)
+    inputs, outputs, scratch = split(refs, 3, 2)
     g_ref, early_ref, early_peer_ref = inputs
-    q_out, k_out, v_out, rest_out = outputs
-    early, land, total, mine, peer = scratch[:5]
-    pair_send, pair_recv, part_send, part_recv, rep_send, rep_recv = scratch[5:]
+    mine, peer = outputs
+    early, land, total = scratch[:3]
+    pair_send, pair_recv, part_send, part_recv, rep_send, rep_recv = scratch[3:]
     me = lax.axis_index("fsdp")
     chip, core = me // 2, lax.rem(me, 2)
     partner = partner_of("fsdp")
@@ -1312,6 +1315,8 @@
             if replicas == 2:
                 both = both + early_peer_ref[block, half].astype(F32)
             early[half, block] = both.astype(BF16)
+    if replicas != 2:
+        peer[...] = jnp.zeros_like(peer)
     swaps.append(remote(early.at[1 - core], land.at[1], pair_send.at[1], pair_recv.at[1], partner))
     swaps[1].start()
     for swap in swaps:
@@ -1344,49 +1349,23 @@
         for offset in range(count):
             to_peer(offset).wait()
 
-    def tiles(block, layer):
-        value = mine[block, layer].astype(F32)
-        if replicas == 2 and layer == 0:
-            value = value + peer[block].astype(F32)
-        return [value[:, i * LANES : (i + 1) * LANES] for i in range(3)]
-
-    for layer in range(LAYERS):
-        for half in range(count // 2):
-            a, b = tiles(2 * half, layer), tiles(2 * half + 1, layer)
-            low = lanes_of(a[0]) < HD
-            q_out[layer, :, 3 * half * LANES : 3 * (half + 1) * LANES] = jnp.concatenate(
-                [a[0], jnp.where(low, a[1], turn(b[0])), jnp.where(low, turn(b[0]), turn(b[1]))], 1
-            )
-            here = slice(half * LANES, (half + 1) * LANES)
-            k_out[layer, :, here] = jnp.where(low, turn(a[1]), b[1])
-            v_out[layer, :, here] = jnp.where(low, a[2], turn(b[2]))
-            rest_out[layer, 2 * half] = a[2]
-            rest_out[layer, 2 * half + 1] = b[2]
     for send in sends:
         send.wait_send()
 
 
 def finish_heads(count, replicas, g, early, early_peer):
     _, _, rows, columns = g.shape
-    width = count * GROUP * HD
     part = (count, LAYERS, rows, columns)
     dma = pltpu.SemaphoreType.DMA
     return pl.pallas_call(
         functools.partial(finish_kernel, count, replicas),
-        out_shape=(
-            cells((LAYERS, rows, width), F32),
-            cells((LAYERS, rows, count * HD), F32),
-            cells((LAYERS, rows, count * HD), F32),
-            cells((LAYERS, count, rows, LANES), F32),
-        ),
+        out_shape=(cells(part, BF16), cells((count, rows, columns), BF16)),
         in_specs=[HERE] * 3,
-        out_specs=[HERE] * 4,
+        out_specs=[HERE] * 2,
         scratch_shapes=[
             pltpu.VMEM((2, count, rows, columns), BF16),
             pltpu.VMEM((2, count, rows, columns), BF16),
             pltpu.VMEM(part, BF16),
-            pltpu.VMEM(part, BF16),
-            pltpu.VMEM((count, rows, columns), BF16),
             dma((2,)), dma((2,)), dma((count,)), dma((count,)), dma((count,)), dma((count,)),
         ],
         compiler_params=pltpu.CompilerParams(
@@ -1397,49 +1376,88 @@
     )(g, early, early_peer)
 
 
-def add_kernel(layers, *refs):
-    out_refs = refs[-3:]
-    for layer in range(layers):
-        pairs = refs[layer * 10 : (layer + 1) * 10]
-        sums = [pairs[i][...].astype(F32) + pairs[i + 5][...].astype(F32) for i in range(5)]
-        out_refs[0][layer, 0] = sums[0]
-        out_refs[1][layer, 0] = sums[1]
-        out_refs[2][layer, 0] = jnp.concatenate(sums[2:], 1)
-
-
-def add_experts(pairs):
-    layers = len(pairs)
-    rows, ff = pairs[0][0].shape
-    width = rows // 3
+def close_kernel(layers, count, *refs):
+    n_experts = 0 if len(refs) == 2 * layers + 7 else 10 * layers
+    inputs, heads_in, experts_in, outputs = split(refs, 2 * layers, 2, n_experts)
+    mine, peer = heads_in
+    out_ref, q_out, k_out, v_out, rest_out = outputs[:5]
+
+    @pl.when(pl.program_id(0) == 0)
+    def _():
+        for layer in range(layers):
+            own, got = inputs[2 * layer : 2 * layer + 2]
+            out_ref[layer] = own[...].astype(F32) + got[...].astype(F32)
+
+            def tiles(block):
+                value = mine[block, layer].astype(F32)
+                if layer == 0:
+                    value = value + peer[block].astype(F32)
+                return [value[:, i * LANES : (i + 1) * LANES] for i in range(3)]
+
+            for half in range(count // 2):
+                a, b = tiles(2 * half), tiles(2 * half + 1)
+                low = lanes_of(a[0]) < HD
+                q_out[layer, :, 3 * half * LANES : 3 * (half + 1) * LANES] = jnp.concatenate(
+                    [a[0], jnp.where(low, a[1], turn(b[0])), jnp.where(low, turn(b[0]), turn(b[1]))], 1
+                )
+                here = slice(half * LANES, (half + 1) * LANES)
+                k_out[layer, :, here] = jnp.where(low, turn(a[1]), b[1])
+                v_out[layer, :, here] = jnp.where(low, a[2], turn(b[2]))
+                rest_out[layer, 2 * half] = a[2]
+                rest_out[layer, 2 * half + 1] = b[2]
+
+    if experts_in:
+        expert_refs = outputs[5:]
+        for layer in range(layers):
+            pairs = experts_in[layer * 10 : (layer + 1) * 10]
+            sums = [pairs[i][...].astype(F32) + pairs[i + 5][...].astype(F32) for i in range(5)]
+            expert_refs[0][layer, 0] = sums[0]
+            expert_refs[1][layer, 0] = sums[1]
+            expert_refs[2][layer, 0] = jnp.concatenate(sums[2:], 1)
+
+
+def close(count, outs, mine, peer, experts):
+    layers = len(outs)
+    shard, width = outs[0][0].shape
     steps = 4
-    tall, short = width // steps, ff // steps
-
-    def at(first, length):
-        return pl.BlockSpec((length, ff), lambda i: (first // length + i, 0))
-
-    specs = [at(0, tall), at(width, tall)] + [at(2 * width + g * ff, short) for g in range(3)]
-    arrays = [array for pair in pairs for array in pair for _ in range(5)]
+
+    def whole(shape):
+        return pl.BlockSpec(shape, lambda i: (0,) * len(shape))
+
+    arrays = [array for pair in outs for array in pair] + [mine, peer]
+    specs = [whole(a.shape) for a in arrays]
+    shapes = [
+        (layers, shard, width),
+        (layers, shard, count * GROUP * HD),
+        (layers, shard, count * HD),
+        (layers, shard, count * HD),
+        (layers, count, shard, LANES),
+    ]
+    out_specs = [whole(shape) for shape in shapes]
+    if experts:
+        rows, ff = experts[0][0].shape
+        tall, short = width // steps, ff // steps
+        groups = (rows - 2 * width) // ff
+
+        def at(first, length):
+            return pl.BlockSpec((length, ff), lambda i: (first // length + i, 0))
+
+        parts = [at(0, tall), at(width, tall)] + [at(2 * width + g * ff, short) for g in range(groups)]
+        arrays += [array for pair in experts for array in pair for _ in parts]
+        specs += parts * (2 * layers)
+        shapes += [(layers, 1, width, ff), (layers, 1, width, ff), (layers, 1, ff, width)]
+        tile = pl.BlockSpec((layers, 1, tall, ff), lambda i: (0, 0, i, 0))
+        out_specs += [tile, tile, pl.BlockSpec((layers, 1, short, width), lambda i: (0, 0, i, 0))]
     return pl.pallas_call(
-        functools.partial(add_kernel, layers),
-        grid=(steps,),
-        out_shape=(
-            cells((layers, 1, width, ff), F32),
-            cells((layers, 1, width, ff), F32),
-            cells((layers, 1, ff, width), F32),
-        ),
-        in_specs=specs * (2 * layers),
-        out_specs=[
-            pl.BlockSpec((layers, 1, tall, ff), lambda i: (0, 0, i, 0)),
-            pl.BlockSpec((layers, 1, tall, ff), lambda i: (0, 0, i, 0)),
-            pl.BlockSpec((layers, 1, short, width), lambda i: (0, 0, i, 0)),
-        ],
+        functools.partial(close_kernel, layers, count),
+        grid=(steps if experts else 1,),
+        out_shape=tuple(cells(shape, F32) for shape in shapes),
+        in_specs=specs,
+        out_specs=out_specs,
+        compiler_params=pltpu.CompilerParams(vmem_limit_bytes=60 << 20),
         cost_estimate=FREE,
-        name="add_experts",
+        name="close",
     )(*arrays)
-
-
-def chunk_keys(own_ref, other_ref, chunk):
-    return jnp.concatenate([own_ref[chunk], other_ref[chunk]], 0)
 
 
 def on_device(
@@ -1544,21 +1562,18 @@
         out_sums[layer] = out_sum
         heads = heads.reshape(count, 2, shard, columns)
         early = heads if layer > 0 else early
-    g_query, g_key, g_value, rest = finish_heads(
-        count, replicas, heads, early, rode[1] if rode else early
-    )
+    arrived, peer = finish_heads(count, replicas, heads, early, rode[1] if rode else early)
     if replicas == 2:
-        g_gate, g_up, g_down = add_experts(expert_sums)
-        arrived = [across(out_sums[0]), rode[0]]
-        g_out = jnp.stack([a.astype(F32) + b.astype(F32) for a, b in zip(out_sums, arrived)])
+        outs = list(zip(out_sums, [across(out_sums[0]), rode[0]]))
+        g_out, g_query, g_key, g_value, rest, g_gate, g_up, g_down = close(
+            count, outs, arrived, peer, expert_sums
+        )
     else:
-        g_query, g_key, g_value, rest, g_out, flat_sums = [
+        outs = [(own, jnp.zeros_like(own)) for own in out_sums]
+        summed = close(count, outs, arrived, peer, [])
+        g_out, g_query, g_key, g_value, rest, flat_sums = [
             lax.psum(array.astype(BF16), "rep").astype(F32)
-            for array in (
-                g_query, g_key, g_value, rest,
-                jnp.stack(out_sums),
-                jnp.stack([own for own, _ in expert_sums]),
-            )
+            for array in (*summed, jnp.stack([own for own, _ in expert_sums]))
         ]
         ff = w_gate.shape[3]
         g_gate, g_up = flat_sums[:, None, :width], flat_sums[:, None, width : 2 * width]

time: 759 us -> 728 us (0.959)
  Pallas kernels: 711 us -> 686 us
    pallas_call x8, Pallas kernels: 627 us -> 594 us  [ring_call(): pl.pallas_call(kernel, out_shape=tuple((shape for shape, _ in outputs)) +...]
  transfers between devices with their start and end apart: 6 -> 6, of which waited for: 0 -> 0; matrix products, arithmetic and copies ran while one was open for 2% -> 1% of each run, Pallas kernels for 51% -> 50%
where the time goes in v7:
time: 728 us; the launch traced here: 722 us
  Pallas kernels  686 us (94%)
  local copies, waits for them, and re-layouts  17.1 us (2%)
  other arithmetic  12.6 us (2%)
    pallas_call x8, Pallas kernels, ring_call(): pl.pallas_call(kernel, out_shape=tuple((shape for shape, _ in outputs)) +...  594 us
    pallas_call x1, Pallas kernels, finish_heads(): pl.pallas_call(functools.partial(finish_kernel, count, replicas), out_sha...  42.1 us
    pallas_call x1, Pallas kernels, exchange_weights(): pl.pallas_call(functools.partial(setup_kernel, count), out_shape=(jax.Sha...  34.7 us
    pallas_call x1, Pallas kernels, close(): pl.pallas_call(functools.partial(close_kernel, layers, count), grid=(step...  15.2 us
  transfers between devices with their start and end apart: 6, of which 0 were waited for; matrix products, arithmetic and copies ran while one was open for 1% of the time, Pallas kernels for 50%

profile of v7, /device:TPU:0, one launch (start us, length us, event | category | flops | bytes accessed | tf_op | source)
XLA Modules:
  0.0 722.1 jit_solution(960333908577752013)
XLA Ops:
  0.7 0.7 convert_element_type.25
  1.4 1.1 copy.49
  2.5 0.9 copy.52
  3.4 1.1 copy.50
  4.5 0.9 copy.53
  5.5 0.6 reshape.71
  6.1 0.2 copy.51
  6.4 0.1 multiply_cosine_fusion
  6.5 0.6 pad_maximum_fusion.table_ref
  7.1 1.5 fusion.8.small_ref
  8.6 2.6 maximum_bitcast_fusion.slab_ref
  11.2 34.7 %exchange_weights.1 = (bf16[2,16,96,384]{3,2,1,0:T(8,128)(2,1)}, bf16[2,2,96,1536]{3,2,1,0:T(8,128)(2,1)}, bf16[16,48,128]{2,1,0:T(8,128)(2,1)}, f32[8,64,128]{2,1,0:T(8,128)}) custom-call(bf16[8,2,96,384]{3,2,1,0:T(8,128)(2,1)} %maximum_bitcast_fusion.slab_ref, bf16[2,96,1536]{2,1,0:T(8,128)(2,1)} %out_w_ref.1, bf16[48,128]{1,0:T(8,128)(2,1)} %fusion.8.small_ref, ...), custom_call_target="tpu_custom_call" | custom-call | tf_op jit(solution)/shard_map/exchange_weights/pallas_call | solution.py:464
  45.9 0.4 collective-permute-start
  46.4 0.1 collective-permute-start.1
  46.5 0.4 collective-permute-start.2
  46.9 1.0 convert_element_type.24.refs_5_.refs_13_
  47.8 2.0 convert_element_type.31.refs_5_
  49.8 0.7 copy-done.3
  50.6 0.8 copy.54
  51.3 1.8 convert_element_type.30.refs_6_.refs_3_.refs_4_.refs_11_
  53.1 1.5 slice_reduce_fusion.3
  54.6 0.8 mul.46
  55.3 0.1 convert_reduce_fusion
  55.6 0.6 constant_dynamic-slice_fusion.refs_4_.refs_8_
  56.2 0.2 multiply_reduce_fusion.1
  56.4 0.9 multiply_convert_fusion.refs_0_
  57.3 82.6 %attend.2 = (bf16[8,3,128,128]{3,2,1,0:T(8,128)(2,1)}, bf16[8,128,128]{2,1,0:T(8,128)(2,1)}, bf16[8,128,128]{2,1,0:T(8,128)(2,1)}, bf16[8,128,1536]{2,1,0:T(8,12...) custom-call(bf16[128,1536]{1,0:T(8,128)(2,1)} %multiply_convert_fusi, ...), custom_call_target="tpu_custom_call" | custom-call | tf_op jit(solution)/shard_map/attend/pallas_call | solution.py:345
  139.9 68.1 %mix.2 = (f32[128,1536]{1,0:T(8,128)}, f32[128,1536]{1,0:T(8,128)}, bf16[128,1536]{1,0:T(8,128)(2,1)}, bf16[8,128,1536]{2,1,0:T(8,128)(2,1)}, f32[8,16,128]{2,1,0:T(8,128)}) custom-call(bf16[128,1536]{1,0:T(8,128)(2,1)} %get-tuple-element.83.refs_0_, f32[16,128]{1,0:T(8,128)} %get-tuple-element.84.refs_1_, f32[128,1536]{1,0:T(8,128)} %get-tuple-element.85.refs_2_.refs_6_, ...), custom_call_target="tpu_custom_call" | custom-call | tf_op jit(solution)/shard_map/mix/pallas_call | solution.py:345
  208.0 71.5 %attend.3 = (bf16[8,3,128,128]{3,2,1,0:T(8,128)(2,1)}, bf16[8,128,128]{2,1,0:T(8,128)(2,1)}, bf16[8,128,128]{2,1,0:T(8,128)(2,1)}, bf16[8,128,1536]{2,1,0:T(8,12...) custom-call(bf16[128,1536]{1,0:T(8,128)(2,1)} %get-tuple-element.89., ...), custom_call_target="tpu_custom_call" | custom-call | tf_op jit(solution)/shard_map/attend/pallas_call | solution.py:345
  279.5 67.0 %mix.3 = (f32[128,1536]{1,0:T(8,128)}, f32[128,1536]{1,0:T(8,128)}, bf16[128,1536]{1,0:T(8,128)(2,1)}, bf16[8,128,1536]{2,1,0:T(8,128)(2,1)}, f32[8,16,128]{2,1,0:T(8,128)}) custom-call(bf16[128,1536]{1,0:T(8,128)(2,1)} %get-tuple-element.91.refs_0_, f32[16,128]{1,0:T(8,128)} %get-tuple-element.92.refs_1_, f32[128,1536]{1,0:T(8,128)} %get-tuple-element.93.refs_2_.refs_6_, ...), custom_call_target="tpu_custom_call" | custom-call | tf_op jit(solution)/shard_map/mix/pallas_call | solution.py:345
  346.5 1.3 multiply_reduce_fusion
  347.8 0.6 broadcast_in_dim.29.refs_1_
  348.4 72.0 %mix_back.2 = (f32[128,1536]{1,0:T(8,128)}, bf16[128,1536]{1,0:T(8,128)(2,1)}, f32[1,1536]{1,0:T(1,128)}, bf16[4608,512]{1,0:T(8,128)(2,1)}, f32[2,1536]{1,0:T(2,128)}) custom-call(bf16[128,1536]{1,0:T(8,128)(2,1)} %refs_0_.1, f32[8,128]{1,0:T(8,128)} %broadcast_in_dim.29.refs_1_, bf16[8,128,1536]{2,1,0:T(8,128)(2,1)} %get-tuple-element.96.refs_2_, ...), custom_call_target="tpu_custom_call" | custom-call | tf_op jit(solution)/shard_map/mix_back/pallas_call | solution.py:345
  420.4 1.6 collective-permute-start.3
  422.0 79.6 %attend_back.2 = (bf16[96,1536]{1,0:T(8,128)(2,1)}, f32[128,1536]{1,0:T(8,128)}, bf16[128,1536]{1,0:T(8,128)(2,1)}, f32[8,128]{1,0:T(8,128)}, bf16[1536,384]{1,0:T(8,128)(2,1)}) custom-call(bf16[128,1536]{1,0:T(8,128)(2,1)} %get-tuple-element.98.refs_0_, bf16[2,2,96,1536]{3,2,1,0:T(8,128)(2,1)} %get-tuple-element.81.refs_2_.refs_1_, ...), custom_call_target="tpu_custom_call" | custom-call | tf_op jit(solution)/shard_map/attend_back/pallas_call | solution.py:345
  501.6 74.8 %mix_back.3 = (f32[128,1536]{1,0:T(8,128)}, bf16[128,1536]{1,0:T(8,128)(2,1)}, f32[1,1536]{1,0:T(1,128)}, bf16[4608,512]{1,0:T(8,128)(2,1)}, f32[2,1536]{1,0:T(2...) custom-call(bf16[128,1536]{1,0:T(8,128)(2,1)} %get-tuple-element.109.refs_0_, ...), custom_call_target="tpu_custom_call" | custom-call | tf_op jit(solution)/shard_map/mix_back/pallas_call | solution.py:345
  576.4 0.5 collective-permute-start.5
  576.9 78.7 %attend_back.3 = (bf16[96,1536]{1,0:T(8,128)(2,1)}, f32[128,1536]{1,0:T(8,128)}, bf16[128,1536]{1,0:T(8,128)(2,1)}, f32[8,128]{1,0:T(8,128)}, bf16[1536,384]{1,0:T(8,128)(2,1)}) custom-call(bf16[128,1536]{1,0:T(8,128)(2,1)} %get-tuple-element.118.refs_0_, bf16[2,2,96,1536]{3,2,1,0:T(8,128)(2,1)} %get-tuple-element.81.refs_2_.refs_1_, ...), custom_call_target="tpu_custom_call" | custom-call | tf_op jit(solution)/shard_map/attend_back/pallas_call | solution.py:345
  655.6 1.7 collective-permute-start.4
  657.3 42.1 %finish_heads.1 = (bf16[8,2,96,384]{3,2,1,0:T(8,128)(2,1)}, bf16[8,96,384]{2,1,0:T(8,128)(2,1)}) custom-call(bf16[8,2,96,384]{3,2,1,0:T(8,128)(2,1)} %bitcast.24, bf16[8,2,96,384]{3,2,1,0:T(8,128)(2,1)} %bitcast.23, bf16[8,2,96,384]{3,2,1,0:T(8,128)(2,1)} %get-tuple-element.132.refs_2_), custom_call_target="tpu_custom_call" | custom-call | tf_op jit(solution)/shard_map/finish_heads/pallas_call | solution.py:1360
  699.5 0.7 copy-done.7
  700.2 15.2 %close.1 = (f32[2,96,1536]{2,1,0:T(8,128)}, f32[2,96,1536]{2,1,0:T(8,128)}, f32[2,96,512]{2,1,0:T(8,128)}, f32[2,96,512]{2,1,0:T(8,128)}, f32[2,8,96,128]{3,2,1,...) custom-call(bf16[96,1536]{1,0:T(8,128)(2,1)} %get-tuple-element.129.refs_0_, ...), custom_call_target="tpu_custom_call" | custom-call | tf_op jit(solution)/shard_map/close/pallas_call | solution.py:1451
  715.4 1.5 slice_reduce_fusion
  716.9 1.4 slice_bitcast_fusion
  718.3 0.8 slice_reduce_fusion.1
  719.1 0.9 copy.55
  720.0 0.7 copy.58
  720.8 0.9 copy.59
  (32 shorter events, 0.3 us)
Async XLA Ops:
  0.6 4.8 copy-start.5
  2.5 4.6 copy-start.10
  6.2 39.7 %copy-start = (bf16[2,1,1536,512]{3,2,1,0:T(8,128)(2,1)S(1)}, bf16[2,1,1536,512]{3,2,1,0:T(8,128)(2,1)}, u32[]{:S(2)}) copy-start(bf16[2,1,1536,512]{3,2,1,0:T(8,128)(2,1)} %refs_7_.1) | copy-start | bytes 9437188
  6.3 40.5 %copy-start.1 = (bf16[128,1536]{1,0:T(8,128)(2,1)S(1)}, bf16[128,1536]{1,0:T(8,128)(2,1)}, u32[]{:S(2)}) copy-start(bf16[128,1536]{1,0:T(8,128)(2,1)} %param.15) | copy-start | bytes 1179652
  45.9 9.4 %copy-start.9 = (s32[1,2048]{1,0:T(1,128)S(1)}, s32[1,2048]{1,0:T(1,128)}, u32[]{:S(2)}) copy-start(s32[1,2048]{1,0:T(1,128)} %param.18) | copy-start | bytes 24580
  45.9 93.9 %collective-permute-start = (bf16[2,1,1536,512]{3,2,1,0:T(8,128)(2,1)S(1)}, bf16[2,1,1536,512]{3,2,1,0:T(8,128)(2,1)}, u32[]{:S(2)}, u32[]{:S(2)}) collective-permute-start(bf16[2,1,1536,512]{3,2,1,0:T(8,128)(2,1)S(1)} %copy-done), channel_id=1, source_target_pairs={{0,1},{1,0},{2,3},{3,2},{4,5},{5,4},{6,7},{7,6},{8,9},{9,8},{10,11... | collective-permute-start | bytes 9437192 | tf_op jit(solution)/shard_map/ppermute | solution.py:1493
  46.4 93.5 %collective-permute-start.1 = (bf16[2,1,1536,512]{3,2,1,0:T(8,128)(2,1)}, bf16[2,1,1536,512]{3,2,1,0:T(8,128)(2,1)}, u32[]{:S(2)}, u32[]{:S(2)}) collective-permute-start(bf16[2,1,1536,512]{3,2,1,0:T(8,128)(2,1)} %refs_8_.1), channel_id=1, source_target_pairs={{0,1},{1,0},{2,3},{3,2},{4,5},{5,4},{6,7},{7,6},{8,9},{9,8},{10,11... | collective-permute-start | bytes 9437192 | tf_op jit(solution)/shard_map/ppermute | solution.py:1493
  46.5 93.4 %collective-permute-start.2 = (bf16[2,1,512,1536]{3,2,1,0:T(8,128)(2,1)}, bf16[2,1,512,1536]{3,2,1,0:T(8,128)(2,1)}, u32[]{:S(2)}, u32[]{:S(2)}) collective-permute-start(bf16[2,1,512,1536]{3,2,1,0:T(8,128)(2,1)} %refs_9_.1), channel_id=1, source_target_pairs={{0,1},{1,0},{2,3},{3,2},{4,5},{5,4},{6,7},{7,6},{8,9},{9,8},{10,11... | collective-permute-start | bytes 9437192 | tf_op jit(solution)/shard_map/ppermute | solution.py:1493
  46.9 2.9 copy-start.8
  49.8 0.7 copy-start.3
  279.5 67.0 %copy-start.2 = (bf16[128,1536]{1,0:T(8,128)(2,1)S(1)}, bf16[128,1536]{1,0:T(8,128)(2,1)}, u32[]{:S(2)}) copy-start(bf16[128,1536]{1,0:T(8,128)(2,1)} %refs_0_.1) | copy-start | bytes 1179652
  420.4 156.5 %collective-permute-start.3 = (bf16[4608,512]{1,0:T(8,128)(2,1)}, bf16[4608,512]{1,0:T(8,128)(2,1)}, u32[]{:S(2)}, u32[]{:S(2)}) collective-permute-start(bf16[4608,512]{1,0:T(8,128)(2,1)} %get-tuple-element.136.refs_16_.refs_17_.refs_18_.refs_19_.refs_20_), channel_id=1, source_target_pairs={{0,16},{16,0},{1,17},{17,1},{2,18},{18,2},{3,19},{19,3},{4,20},{20... | collective-permute-start | bytes 14155784 | tf_op jit(solution)/shard_map/ppermute | solution.py:1540
  576.4 123.0 %collective-permute-start.5 = (bf16[4608,512]{1,0:T(8,128)(2,1)}, bf16[4608,512]{1,0:T(8,128)(2,1)}, u32[]{:S(2)}, u32[]{:S(2)}) collective-permute-start(bf16[4608,512]{1,0:T(8,128)(2,1)} %get-tuple-element.135.refs_6_.refs_7_.refs_8_.refs_9_.refs_10_), channel_id=1, source_target_pairs={{0,16},{16,0},{1,17},{17,1},{2,18},{18,2},{3,19},{19,3},{4,20},{20... | collective-permute-start | bytes 14155784 | tf_op jit(solution)/shard_map/ppermute | solution.py:1540
  655.6 43.8 %collective-permute-start.4 = (bf16[96,1536]{1,0:T(8,128)(2,1)}, bf16[96,1536]{1,0:T(8,128)(2,1)S(1)}, u32[]{:S(2)}, u32[]{:S(2)}) collective-permute-start(bf16[96,1536]{1,0:T(8,128)(2,1)} %get-tuple-element.129.refs_0_), channel_id=1, source_target_pairs={{0,16},{16,0},{1,17},{17,1},{2,18},{18,2},{3,19},{19,3},{4,20},{20... | collective-permute-start | bytes 884744 | tf_op jit(solution)/shard_map/ppermute | solution.py:1540
  699.4 0.7 copy-start.7
  715.4 4.6 copy-start.6
  715.4 5.4 copy-start.4

commit v8 on v7

--- a/solution.py
+++ b/solution.py
@@ -85,8 +85,8 @@
         self.steps = count // 2
         self.chip, self.at, self.near = ring_setup(count)
 
-    def meet(self, partner=False):
-        others = self.near + ([partner_of("fsdp")] if partner else [])
+    def meet(self, partner=False, everyone=None):
+        others = everyone or self.near + ([partner_of("fsdp")] if partner else [])
         meet(others + ([partner_of("rep")] if self.riders else []))
         for rider in self.riders:
             rider.start()
@@ -196,18 +196,25 @@
     def pair(self, s):
         return self.at(s), self.at(-s)
 
-    def meanwhile(self, compute):
+    def meanwhile(self, compute, ready):
         def first(s):
             @pl.when(s == 1)
             def _():
-                for part in range(2):
-                    compute(part, (self.chip,))
+                compute(0, (self.chip,))
 
             @pl.when(s > 1)
             def _():
                 compute(1, self.pair(s - 1))
 
-        return first, lambda s: compute(0, self.pair(s))
+        def second(s):
+            @pl.when(s == 1)
+            def _():
+                ready()
+                compute(1, (self.chip,))
+
+            compute(0, self.pair(s))
+
+        return first, second
 
     def scatter(self, partial, land, sems, work=None, between=None):
         send_sem, recv_sem = sems
@@ -373,125 +380,6 @@
     return jax.ShapeDtypeStruct(shape, dtype)
 
 
-def setup_kernel(
-    count, slab_ref, out_w_ref, small_ref, table_ref,
-    heads_ref, outs_ref, smalls_ref, tables_ref,
-    own_sem, slab_send, slab_recv, pass_send, pass_recv,
-    small_send, small_recv, table_send, table_recv, out_send, out_recv,
-):
-    devices = 2 * count
-    me = lax.axis_index("fsdp")
-    chip, core = me // 2, lax.rem(me, 2)
-    layers = slab_ref.shape[1]
-
-    def device(offset):
-        return {"fsdp": lax.rem(me + offset, devices)}
-
-    def chip_at(offset):
-        return lax.rem(chip + offset + count, count)
-
-    partner = partner_of("fsdp")
-    meet([device(offset) for offset in range(1, devices)])
-    copies = [
-        pltpu.make_async_copy(slab_ref.at[chip, layer], heads_ref.at[layer, me], own_sem.at[layer])
-        for layer in range(layers)
-    ] + [
-        pltpu.make_async_copy(small_ref, smalls_ref.at[me], own_sem.at[layers]),
-        pltpu.make_async_copy(table_ref, tables_ref.at[chip], own_sem.at[layers + 1]),
-        pltpu.make_async_copy(out_w_ref, outs_ref.at[core], own_sem.at[layers + 2]),
-    ]
-    sends = [
-        remote(small_ref, smalls_ref.at[me], small_send.at[offset], small_recv.at[offset], device(offset))
-        for offset in range(1, devices)
-    ]
-    for offset in range(1, count):
-        there = {"fsdp": chip_at(offset) * 2 + core}
-        sends.append(
-            remote(table_ref, tables_ref.at[chip], table_send.at[offset], table_recv.at[offset], there)
-        )
-        for layer in range(layers):
-            sends.append(
-                remote(
-                    slab_ref.at[chip_at(offset), layer], heads_ref.at[layer, me],
-                    slab_send.at[offset, layer], slab_recv.at[offset, layer], there,
-                )
-            )
-    for layer in range(layers):
-        sends.append(
-            remote(
-                slab_ref.at[chip, layer], heads_ref.at[layer, me],
-                pass_send.at[0, layer], pass_recv.at[0, layer], partner,
-            )
-        )
-    sends.append(remote(out_w_ref, outs_ref.at[core], out_send.at[0], out_recv.at[0], partner))
-    for copy in copies + sends:
-        copy.start()
-    for offset in range(1, count):
-        origin = chip_at(-offset) * 2 + core
-        for layer in range(layers):
-            slot = heads_ref.at[layer, origin]
-            remote(slot, slot, slab_send.at[offset, layer], slab_recv.at[offset, layer], partner).wait_recv()
-            forward = remote(slot, slot, pass_send.at[offset, layer], pass_recv.at[offset, layer], partner)
-            forward.start()
-    for offset in range(1, count):
-        origin = chip_at(-offset)
-        table = tables_ref.at[origin]
-        remote(table, table, table_send.at[offset], table_recv.at[offset], partner).wait_recv()
-    for offset in range(count):
-        origin = chip_at(-offset) * 2 + 1 - core
-        mine = chip_at(-offset) * 2 + core
-        for layer in range(layers):
-            slot, sent = heads_ref.at[layer, origin], heads_ref.at[layer, mine]
-            if offset > 0:
-                remote(sent, sent, pass_send.at[offset, layer], pass_recv.at[offset, layer], partner).wait_send()
-            remote(slot, slot, pass_send.at[offset, layer], pass_recv.at[offset, layer], partner).wait_recv()
-    for offset in range(1, devices):
-        slot = smalls_ref.at[lax.rem(me - offset + devices, devices)]
-        remote(slot, slot, small_send.at[offset], small_recv.at[offset], partner).wait_recv()
-    other = outs_ref.at[1 - core]
-    remote(other, other, out_send.at[0], out_recv.at[0], partner).wait_recv()
-    for copy in copies:
-        copy.wait()
-    for send in sends:
-        send.wait_send()
-
-
-def exchange_weights(count, slabs, out_w, small, table):
-    layers = slabs.shape[1]
-    devices = 2 * count
-    dma = pltpu.SemaphoreType.DMA
-    anywhere = pl.BlockSpec(memory_space=pl.ANY)
-    return pl.pallas_call(
-        functools.partial(setup_kernel, count),
-        out_shape=(
-            jax.ShapeDtypeStruct((layers, devices) + slabs.shape[2:], slabs.dtype),
-            jax.ShapeDtypeStruct((2,) + out_w.shape, out_w.dtype),
-            jax.ShapeDtypeStruct((devices,) + small.shape, small.dtype),
-            jax.ShapeDtypeStruct((count,) + table.shape, table.dtype),
-        ),
-        in_specs=[anywhere] * 4,
-        out_specs=[anywhere] * 4,
-        scratch_shapes=[
-            dma((layers + 3,)),
-            dma((count, layers)),
-            dma((count, layers)),
-            dma((count, layers)),
-            dma((count, layers)),
-            dma((devices,)),
-            dma((devices,)),
-            dma((count,)),
-            dma((count,)),
-            dma((1,)),
-            dma((1,)),
-        ],
-        compiler_params=pltpu.CompilerParams(
-            collective_id=identity(("setup",)), has_side_effects=True, vmem_limit_bytes=60 << 20
-        ),
-        cost_estimate=FREE,
-        name="exchange_weights",
-    )(slabs, out_w, small, table)
-
-
 def dot(left, right, contract=((1,), (0,))):
     return lax.dot_general(left, right, (contract, ((), ())), preferred_element_type=F32)
 
@@ -627,17 +515,165 @@
     return last // SPAN + 1
 
 
+class Opening:
+    def __init__(self, count, inputs, outputs, scratch):
+        self.tokens_ref, *self.projections, self.out_w_ref, self.small_ref, self.table_ref = inputs
+        self.heads_ref, self.outs_ref, self.tables_ref, self.params_ref = outputs
+        (self.x_ref, self.slab_ref, self.smalls, self.weights, self.own_sem, self.slab_sem, self.pass_sem, self.small_sem,
+         self.table_sem, self.out_sem) = scratch
+        self.count = count
+        self.devices = 2 * count
+        self.me = lax.axis_index("fsdp")
+        self.chip, self.core = self.me // 2, lax.rem(self.me, 2)
+        self.partner = partner_of("fsdp")
+
+    def device(self, offset):
+        return {"fsdp": lax.rem(self.me + offset, self.devices)}
+
+    def chip_at(self, offset):
+        return lax.rem(self.chip + offset + self.count, self.count)
+
+    def everyone(self):
+        return [self.device(offset) for offset in range(1, self.devices)]
+
+    def home(self, layer, origin):
+        shard = self.slab_ref.shape[2]
+        rows = pl.ds(pl.multiple_of(origin * shard, shard), shard)
+        return self.weights.at[rows] if layer == 0 else self.heads_ref.at[layer, rows]
+
+    def across(self, layer, offset, source=None, target=None):
+        slot = self.home(layer, self.me) if source is None else source
+        target = slot if target is None else target
+        there = {"fsdp": self.chip_at(offset) * 2 + self.core}
+        return remote(slot, target, self.slab_sem.at[0, offset, layer], self.slab_sem.at[1, offset, layer], there)
+
+    def beside(self, layer, offset, slot, source=None):
+        return remote(
+            slot if source is None else source, slot,
+            self.pass_sem.at[0, offset, layer], self.pass_sem.at[1, offset, layer], self.partner,
+        )
+
+    def small_to(self, offset, slot, source=None):
+        return remote(
+            slot if source is None else source, slot,
+            self.small_sem.at[0, offset], self.small_sem.at[1, offset], self.device(offset),
+        )
+
+    def table_to(self, offset, slot, source=None):
+        there = {"fsdp": self.chip_at(offset) * 2 + self.core}
+        return remote(
+            slot if source is None else source, slot,
+            self.table_sem.at[0, offset], self.table_sem.at[1, offset], there,
+        )
+
+    def out_to(self, slot, source):
+        return remote(source, slot, self.out_sem.at[0], self.out_sem.at[1], self.partner)
+
+    def divide(self):
+        for layer in range(LAYERS):
+            query, key, value = [ref[layer].astype(F32) for ref in self.projections]
+            for half in range(self.count // 2):
+                first = 3 * half * LANES
+                t = [query[:, first + i * LANES : first + (i + 1) * LANES] for i in range(3)]
+                k, v = [a[:, half * LANES : (half + 1) * LANES] for a in (key, value)]
+                low = lanes_of(k) < HD
+                even = [t[0], jnp.where(low, t[1], turn(k)), jnp.where(low, v, 0.0)]
+                odd = [
+                    jnp.where(low, turn(t[1]), turn(t[2])),
+                    jnp.where(low, turn(t[2]), k),
+                    jnp.where(low, turn(v), 0.0),
+                ]
+                for place, tiles in enumerate((even, odd)):
+                    self.slab_ref[2 * half + place, layer] = jnp.concatenate(tiles, 1).astype(BF16)
+
+    def start(self):
+        me, chip = self.me, self.chip
+        self.divide()
+        self.copies = [
+            pltpu.make_async_copy(self.small_ref, self.smalls.at[me], self.own_sem.at[0]),
+            pltpu.make_async_copy(self.table_ref, self.tables_ref.at[chip], self.own_sem.at[1]),
+            pltpu.make_async_copy(self.out_w_ref, self.outs_ref.at[self.core], self.own_sem.at[2]),
+        ] + [
+            pltpu.make_async_copy(self.slab_ref.at[chip, layer], self.home(layer, me), self.own_sem.at[3 + layer])
+            for layer in range(LAYERS)
+        ]
+        self.sends = [
+            self.small_to(offset, self.smalls.at[me], self.small_ref) for offset in range(1, self.devices)
+        ]
+        for offset in range(1, self.count):
+            self.sends.append(self.table_to(offset, self.tables_ref.at[chip], self.table_ref))
+        for layer in range(LAYERS):
+            for offset in range(1, self.count):
+                slab = self.slab_ref.at[self.chip_at(offset), layer]
+                self.sends.append(self.across(layer, offset, slab, self.home(layer, me)))
+            self.sends.append(self.beside(layer, 0, self.home(layer, me), self.slab_ref.at[chip, layer]))
+        self.sends.append(self.out_to(self.outs_ref.at[self.core], self.out_w_ref))
+        for copy in self.copies + self.sends:
+            copy.start()
+
+    def parameters(self):
+        for offset in range(1, self.devices):
+            origin = lax.rem(self.me - offset + self.devices, self.devices)
+            self.small_to(offset, self.smalls.at[origin]).wait_recv()
+        self.copies[0].wait()
+        shard = self.slab_ref.shape[2]
+        width = self.params_ref.shape[1]
+        shape = (LANES, width)
+        feature = lax.broadcasted_iota(jnp.int32, shape, 1)
+        spread = (lax.rem(feature, shard) == lax.broadcasted_iota(jnp.int32, shape, 0)).astype(F32).astype(BF16)
+        owner = lax.broadcasted_iota(jnp.int32, self.params_ref.shape, 1) // shard
+        self.params_ref[...] = jnp.zeros_like(self.params_ref)
+
+        def one(device, carry):
+            rows = dot(self.smalls[device], spread)
+            self.params_ref[...] += jnp.where(owner == device, rows, 0.0)
+            return carry
+
+        lax.fori_loop(0, self.devices, one, 0)
+        normed = normal(self.tokens_ref[...].astype(F32))[1]
+        self.x_ref[...] = (normed * gain_row(self.params_ref, 0, 0)).astype(BF16)
+
+    def forward(self, layer):
+        for offset in range(1, self.count):
+            slot = self.home(layer, self.chip_at(-offset) * 2 + self.core)
+            self.across(layer, offset, slot).wait_recv()
+            self.beside(layer, offset, slot).start()
+
+    def arrived(self, layer):
+        self.copies[3 + layer].wait()
+        for offset in range(self.count):
+            slot = self.home(layer, self.chip_at(-offset) * 2 + 1 - self.core)
+            self.beside(layer, offset, slot).wait_recv()
+
+    def rest(self):
+        for offset in range(1, self.count):
+            self.table_to(offset, self.tables_ref.at[self.chip_at(-offset)]).wait_recv()
+        for copy in self.copies[1:3]:
+            copy.wait()
+        other = self.outs_ref.at[1 - self.core]
+        self.out_to(other, other).wait_recv()
+
+    def drain(self):
+        for send in self.sends:
+            send.wait_send()
+        for layer in range(LAYERS):
+            for offset in range(1, self.count):
+                slot = self.home(layer, self.chip_at(-offset) * 2 + self.core)
+                self.beside(layer, offset, slot).wait_send()
+
+
 def attend_kernel(count, layer, traffic, *refs):
-    inputs, outputs, scratch = split(refs, 8, 9)
-    x_ref, w_ref, w_out_ref, table_ref, begin_ref, hidden_ref, params_ref, routes_ref = inputs
-    q_ref, own_ref, other_ref, all_ref, att_ref, lse_ref, middle_ref, x_out_ref, share_ref = outputs
+    if layer == 0:
+        inputs, outputs, scratch = split(refs, 9, 13)
+        begin_ref, routes_ref = inputs[7:]
+        hidden_ref, table_ref, params_ref = inputs[0], outputs[11], outputs[12]
+    else:
+        inputs, outputs, scratch = split(refs, 8, 9)
+        x_ref, w_ref, w_out_ref, table_ref, begin_ref, hidden_ref, params_ref, routes_ref = inputs
+    q_ref, own_ref, other_ref, all_ref, att_ref, lse_ref, middle_ref, x_out_ref, share_ref = outputs[:9]
     buf, weights, wide_w, turned_ref, score_ref, partial, land = scratch[:7]
-    sems, pair_sems, scatter_sem, out_sem, load_sem = split(scratch[7:], 3, 2, 2, 1)
+    sems, pair_sems, scatter_sem, out_sem, load_sem, more = split(scratch[7:], 3, 2, 2, 1, 1)
     ring = Ring(count, traffic)
-    loads = [pltpu.make_async_copy(w_ref.at[layer], weights, load_sem[0].at[2])]
-    loads[0].start()
-    loads += load_out_weights(w_out_ref, layer, wide_w, load_sem[0])
-    ring.meet(True)
     partner = partner_of("fsdp")
     core = lax.rem(lax.axis_index("fsdp"), 2)
 
@@ -659,17 +695,46 @@
             own_ref[block] = part
             pass_on(block).start()
 
-    def first(s):
-        @pl.when(s == 1)
-        def _():
-            for load in loads:
-                load.wait()
-            project((ring.chip,))
-
-    drain = ring.gather(x_ref, buf, sems, None, first, lambda s: project(ring.pair(s)))
-    keep = pltpu.make_async_copy(buf, all_ref, out_sem[0].at[0])
-    keep.start()
-    project((ring.at(ring.steps),))
+    if layer == 0:
+        more = scratch[7 + 9 :]
+        opening = Opening(count, inputs[:7], outputs[9:], [*more[:3], weights, *more[3:]])
+        ring.meet(True, opening.everyone())
+        opening.start()
+        opening.parameters()
+        drain = ring.gather(opening.x_ref, buf, sems, None, lambda s: None, lambda s: None)
+        keep = [pltpu.make_async_copy(buf, all_ref, out_sem[0].at[0])]
+        keep[0].start()
+        opening.forward(0)
+        opening.rest()
+        loads = load_out_weights(outputs[10], layer, wide_w, load_sem[0])
+        opening.arrived(0)
+        keep.append(pltpu.make_async_copy(weights, outputs[9].at[0], out_sem[0].at[1]))
+        keep[1].start()
+
+        def both(index, carry):
+            project((2 * index, 2 * index + 1))
+            return carry
+
+        lax.fori_loop(0, count // 2, both, 0)
+        for load in loads:
+            load.wait()
+    else:
+        loads = [pltpu.make_async_copy(w_ref.at[layer], weights, load_sem[0].at[2])]
+        loads[0].start()
+        loads += load_out_weights(w_out_ref, layer, wide_w, load_sem[0])
+        ring.meet(True)
+
+        def first(s):
+            @pl.when(s == 1)
+            def _():
+                for load in loads:
+                    load.wait()
+                project((ring.chip,))
+
+        drain = ring.gather(x_ref, buf, sems, None, first, lambda s: project(ring.pair(s)))
+        keep = [pltpu.make_async_copy(buf, all_ref, out_sem[0].at[0])]
+        keep[0].start()
+        project((ring.at(ring.steps),))
     for block in range(count):
         pass_on(block).wait()
     ring.depart()
@@ -719,6 +784,9 @@
     attend((ring.at(ring.steps),))
 
     def between():
+        if layer == 0:
+            for later in range(1, LAYERS):
+                opening.forward(later)
         attend(ring.pair(ring.steps - 1))
 
     def work(s, place):
@@ -734,7 +802,7 @@
 
     added, finish = ring.scatter(partial, land, scatter_sem, work, between)
     ring.settle()
-    middle = hidden_ref[...] + added
+    middle = hidden_ref[...].astype(F32) + added
     middle_ref[...] = middle
     x = (normal(middle)[1] * gain_row(params_ref, 1, layer)).astype(BF16)
     x_out_ref[...] = x
@@ -749,21 +817,23 @@
     share_ref[...] = weighted / jnp.sum(weighted, 0, keepdims=True)
     drain()
     finish()
-    keep.wait()
-
-
-def gather_attend_scatter(count, layer, x, w, w_out, tables, begin, hidden, params, routes):
-    rows, width = x.shape
+    for copy in keep:
+        copy.wait()
+    if layer == 0:
+        for later in range(1, LAYERS):
+            opening.arrived(later)
+        opening.drain()
+
+
+def gather_attend_scatter(count, layer, inputs, rows, width, columns, extra=()):
     block = cells((count, rows, LANES), BF16)
     everyone = pltpu.VMEM((count, rows, width), BF16)
     wide = 2 * LANES
+    more_outputs, more_scratch = extra if extra else ([], [])
     return ring_call(
         functools.partial(attend_kernel, count, layer),
         ("attend", layer),
-        [
-            (x, ANYWHERE), (w, ANYWHERE), (w_out, ANYWHERE), (tables, EARLY), (begin, EARLY),
-            (hidden, LATE), (params, LATE), (routes, LATE),
-        ],
+        inputs,
         [
             (cells((count, GROUP, rows, LANES), BF16), SOON),
             (block, SOON),
@@ -774,10 +844,11 @@
             (cells((rows, width), F32), OUT),
             (cells((rows, width), BF16), OUT),
             (cells((2 * count, rows), F32), OUT),
-        ],
+        ]
+        + more_outputs,
         [
             everyone,
-            pltpu.VMEM(w.shape[1:], BF16),
+            pltpu.VMEM((width, columns), BF16),
             pltpu.VMEM((wide, width), BF16),
             pltpu.VMEM((count // SPAN, LANES, SPAN * wide), BF16),
             pltpu.VMEM((count // SPAN, SPAN * wide, 2 * GROUP * LANES), F32),
@@ -787,17 +858,49 @@
         + gather_sems(count)
         + dmas((count,), (count,))
         + scatter_sems(count)
-        + dmas((1,), (3,)),
+        + dmas((2,), (3,))
+        + more_scratch,
         60,
     )
 
 
-def load_experts(refs, layer, gates, ups, downs, sem):
-    copies = []
-    for e in range(2):
-        for place, buf in enumerate((gates, ups, downs)):
-            source = refs[3 * e + place].at[layer, 0]
-            copies.append(pltpu.make_async_copy(source, buf.at[e], sem.at[3 * e + place]))
+def open_attend_scatter(count, columns, tokens, projections, out_w, small, table, begin, routes):
+    rows, width = tokens.shape
+    layers, shard, _ = out_w.shape
+    devices = 2 * count
+    outputs = [
+        (cells((layers, width, columns), BF16), ANYWHERE),
+        (cells((2,) + out_w.shape, BF16), ANYWHERE),
+        (cells((count,) + table.shape, F32), OUT),
+        (cells((small.shape[0], width), F32), OUT),
+    ]
+    scratch = [
+        pltpu.VMEM((rows, width), BF16),
+        pltpu.VMEM((count, layers, shard, columns), BF16),
+        pltpu.VMEM((devices,) + small.shape, BF16),
+    ] + dmas(
+        (3 + layers,), (2, count, layers), (2, count, layers), (2, devices), (2, count), (2,)
+    )
+    inputs = [(a, EARLY) for a in (tokens, *projections)] + [(a, ANYWHERE) for a in (out_w, small, table)]
+    inputs += [(begin, EARLY), (routes, LATE)]
+    return gather_attend_scatter(count, 0, inputs, rows, width, columns, (outputs, scratch))
+
+
+def load_experts(refs, layer, bufs, sem):
+    copies = [
+        pltpu.make_async_copy(ref.at[layer, 0], buf.at[0], sem.at[place])
+        for place, (ref, buf) in enumerate(zip(refs, bufs))
+    ]
+    for copy in copies:
+        copy.start()
+    return copies
+
+
+def lend_experts(refs, layer, bufs, sems):
+    copies = [
+        remote(ref.at[layer, 0], buf.at[1], sems[0].at[place], sems[1].at[place], partner_of("fsdp"))
+        for place, (ref, buf) in enumerate(zip(refs, bufs))
+    ]
     for copy in copies:
         copy.start()
     return copies
@@ -826,14 +929,20 @@
 
 
 def mix_kernel(count, layer, traffic, *refs):
-    inputs, outputs, scratch = split(refs, 10, 5)
+    last = layer + 1 == LAYERS
+    inputs, outputs, scratch = split(refs, 7 + last, 5 + last)
     x_ref, side_ref, middle_ref, params_ref = inputs[:4]
-    mixed_ref, hidden_ref, next_ref, all_ref, share_ref = outputs
+    mixed_ref, hidden_ref, next_ref, all_ref, share_ref = outputs[:5]
     buf, partial, land, acc, gates, ups, downs = scratch[:7]
-    sems, scatter_sem, load_sem, out_sem = split(scratch[7:], 5, 2, 1)
+    sems, scatter_sem, load_sem, lend_sem, out_sem = split(scratch[7:], 5, 2, 1, 2)
     ring = Ring(count, traffic)
-    loads = load_experts(inputs[4:], layer, gates, ups, downs, load_sem[0])
-    ring.meet()
+    loads = load_experts(inputs[4:7], layer, (gates, ups, downs), load_sem[0])
+    ring.meet(True)
+    lent = lend_experts(inputs[4:7], layer, (gates, ups, downs), lend_sem)
+
+    def ready():
+        for copy in lent:
+            copy.wait()
 
     def compute(e, blocks):
         x = stack(buf, blocks)
@@ -847,7 +956,7 @@
             for block, rows in cut(total, blocks):
                 partial[block] = rows
 
-    first, second = ring.meanwhile(compute)
+    first, second = ring.meanwhile(compute, ready)
     drain = ring.gather(x_ref, buf, sems, (side_ref, share_ref), after_loads(loads, first), second)
     keep = pltpu.make_async_copy(buf, all_ref, out_sem[0].at[0])
     keep.start()
@@ -862,20 +971,22 @@
         next_ref[...] = (normal(hidden)[1] * gain_row(params_ref, 0, layer + 1)).astype(BF16)
     else:
         next_ref[...] = hidden.astype(BF16)
+        balance = jnp.sum(mixed * inputs[7][...].astype(F32), -1, keepdims=True)
+        outputs[5][...] = jnp.broadcast_to(as_line(balance), outputs[5].shape)
     drain()
     finish()
     keep.wait()
 
 
 def expert_scratch(weights):
-    return [pltpu.VMEM((2,) + w.shape[2:], BF16) for w in weights[:3]]
+    return [pltpu.VMEM((2,) + w.shape[2:], BF16) for w in weights]
 
 
 def land_scratch(count, rows, width):
     return pltpu.VMEM((2, 2, count // 2, rows // 2, width), BF16)
 
 
-def gather_mix_scatter(count, layer, x, share, middle, params, weights):
+def gather_mix_scatter(count, layer, x, share, middle, params, weights, cotangent):
     rows, width = x.shape
     everyone = pltpu.VMEM((count, rows, width), BF16)
     own = cells((rows, width), F32)
@@ -883,35 +994,43 @@
         functools.partial(mix_kernel, count, layer),
         ("mix", layer),
         [(x, ANYWHERE), (share, ANYWHERE), (middle, LATE), (params, LATE)]
-        + [(w, ANYWHERE) for w in weights],
+        + [(w, ANYWHERE) for w in weights]
+        + ([(cotangent, LATE)] if layer + 1 == LAYERS else []),
         [
             (own, OUT),
             (own, OUT),
             (cells((rows, width), BF16), OUT),
             (cells((count, rows, width), BF16), ANYWHERE),
             (cells((count,) + share.shape, F32), OUT),
-        ],
+        ]
+        + ([(cells((8, rows), F32), OUT)] if layer + 1 == LAYERS else []),
         [everyone, everyone, land_scratch(count, rows, width), pltpu.VMEM((2 * rows, width), F32)]
         + expert_scratch(weights)
         + gather_sems(count, True)
         + scatter_sems(count)
-        + dmas((6,), (1,)),
+        + dmas((3,), (3,), (3,), (1,)),
         60,
     )
 
 
 def mix_back_kernel(count, layer, traffic, *refs):
-    inputs, outputs, scratch = split(refs, 13, 5)
+    inputs, outputs, scratch = split(refs, 10, 5)
     d_ref, side_ref, m_ref, share_ref, params_ref, grad_ref, middle_ref = inputs[:7]
     mid_ref, branch_ref, gain_ref, sum_ref, g_router_ref = outputs
     buf, partial, land, acc, gates, ups, downs = scratch[:7]
     tokens, acts, hiddens, balance_ref, totals, got = scratch[7:13]
-    sems, scatter_sem, load_sem, pair_sem, out_sem = split(scratch[13:], 5, 2, 1, 2)
+    sems, scatter_sem, load_sem, pair_sem, lend_sem, out_sem = split(scratch[13:], 5, 2, 1, 2, 2)
     ring = Ring(count, traffic)
-    loads = load_experts(inputs[7:], layer, gates, ups, downs, load_sem[0])
-    loads.append(pltpu.make_async_copy(m_ref, tokens, load_sem[0].at[6]))
+    loads = load_experts(inputs[7:], layer, (gates, ups, downs), load_sem[0])
+    loads.append(pltpu.make_async_copy(m_ref, tokens, load_sem[0].at[3]))
     loads[-1].start()
     ring.meet(True)
+    lent = lend_experts(inputs[7:], layer, (gates, ups, downs), lend_sem)
+
+    def ready():
+        for copy in lent:
+            copy.wait()
+
     ff = gates.shape[2]
     width = buf.shape[2]
     g_router_ref[...] = jnp.zeros_like(g_router_ref)
@@ -947,7 +1066,7 @@
             for block, rows in cut(total, blocks):
                 partial[block] = rows
 
-    first, second = ring.meanwhile(compute)
+    first, second = ring.meanwhile(compute, ready)
     drain = ring.gather(d_ref, buf, sems, (side_ref, balance_ref), after_loads(loads, first), second)
     for e in range(2):
         compute(e, (ring.at(ring.steps),))
@@ -1027,7 +1146,7 @@
     d_x, finish = ring.scatter(partial, land, scatter_sem, work)
     ring.settle()
     d_values, gain_ref[...] = normal_back(d_x, middle_ref[...], gain_row(params_ref, 1, layer))
-    grad = grad_ref[...] + d_values
+    grad = grad_ref[...].astype(F32) + d_values
     mid_ref[...] = grad
     branch_ref[...] = grad.astype(BF16)
     drain()
@@ -1069,7 +1188,7 @@
         ]
         + gather_sems(count, True)
         + scatter_sems(count)
-        + dmas((7,), (2, 2 + groups), (2, 2 + groups), (2, 2 + groups)),
+        + dmas((4,), (2, 2 + groups), (2, 2 + groups), (3,), (3,), (2, 2 + groups)),
         60,
         rides,
     )
@@ -1220,7 +1339,7 @@
     own = g_acc[pl.ds(pl.multiple_of(core * shard, 8), shard), :]
     g_out_ref[...] = (own + out_got[...].astype(F32)).astype(BF16)
     ring.settle()
-    d_values, gain_one = normal_back(d_x, hidden_ref[...], gain_row(params_ref, 0, layer))
+    d_values, gain_one = normal_back(d_x, hidden_ref[...].astype(F32), gain_row(params_ref, 0, layer))
     grad = mid_ref[...] + d_values
     grad_ref[...] = grad
     d_mix = grad.astype(BF16)
@@ -1487,10 +1606,6 @@
     experts = devices
     columns = 3 * LANES
     used = (GROUP + 2) * HD
-    pairs = [(index, index ^ 1) for index in range(devices)]
-
-    def swap(array):
-        return lax.ppermute(array, "fsdp", pairs)
 
     small = jnp.concatenate(
         [attn_gain, ffn_gain, router.transpose(0, 2, 1).reshape(LAYERS * experts, shard)], 0
@@ -1499,21 +1614,7 @@
     rate = jnp.exp(-jnp.log(10000.0) * jnp.arange(HD // 2, dtype=F32) / (HD // 2))
     angle = rate[:, None] * positions.astype(F32)[None, :]
     table = jnp.concatenate([jnp.cos(angle), jnp.sin(angle)], 0)
-    slabs = jnp.concatenate(
-        [
-            w_query.reshape(LAYERS, shard, count, GROUP * HD),
-            w_key.reshape(LAYERS, shard, count, HD),
-            w_value.reshape(LAYERS, shard, count, HD),
-            jnp.zeros((LAYERS, shard, count, columns - used), BF16),
-        ],
-        -1,
-    ).transpose(2, 0, 1, 3)
-    heads_w, outs_w, smalls, tables = exchange_weights(count, slabs, w_out, small, table)
-    heads_w = heads_w.reshape(LAYERS, width, columns)
-    params = smalls[:, : (2 + experts) * LAYERS, :shard].transpose(1, 0, 2).reshape(-1, width)
-    params = params.astype(F32)
-    own_w, _ = lax.optimization_barrier(([w_gate, w_up, w_down], smalls))
-    experts_w = own_w + [swap(w) for w in own_w]
+    experts_w = [w_gate, w_up, w_down]
 
     flat_segments = segments.reshape(1, -1)
     kinds = jnp.arange(8, dtype=jnp.int32)[:, None]
@@ -1521,16 +1622,29 @@
     begin = jnp.sum(jnp.where(flat_segments == kinds, starts, 0), 0).reshape(count, 2, rows)
     begin = lax.dynamic_index_in_dim(begin, core, 1, True)
 
-    hidden = tokens.astype(F32)
-    x_attn = (normal(hidden)[1] * params[0:1]).astype(BF16)
     chosen = routes.transpose(0, 2, 1)
+    hidden = tokens
     saved = []
     for layer in range(LAYERS):
-        query, kv, kv_other, x_all, att, lse, middle, x_moe, share = gather_attend_scatter(
-            count, layer, x_attn, heads_w, outs_w, tables, begin, hidden, params, chosen
-        )
-        mixed, after, x_attn, m_all, share_all = gather_mix_scatter(
-            count, layer, x_moe, share, middle, params, experts_w
+        if layer == 0:
+            *results, heads_w, outs_w, tables, params = open_attend_scatter(
+                count, columns, tokens, [w_query, w_key, w_value], w_out, small, table, begin, chosen
+            )
+        else:
+            results = gather_attend_scatter(
+                count,
+                layer,
+                [
+                    (x_attn, ANYWHERE), (heads_w, ANYWHERE), (outs_w, ANYWHERE), (tables, EARLY),
+                    (begin, EARLY), (hidden, LATE), (params, LATE), (chosen, LATE),
+                ],
+                rows,
+                width,
+                columns,
+            )
+        query, kv, kv_other, x_all, att, lse, middle, x_moe, share = results
+        mixed, after, x_attn, m_all, share_all, *side = gather_mix_scatter(
+            count, layer, x_moe, share, middle, params, experts_w, cotangent
         )
         saved.append((hidden, x_all, query, kv, kv_other, att, lse, middle, mixed, m_all, share_all))
         hidden = after
@@ -1539,9 +1653,8 @@
     def across(array):
         return lax.ppermute(array, "rep", [(0, 1), (1, 0)]) if replicas == 2 else array
 
-    grad, d_mix = cotangent.astype(F32), cotangent
-    balance = jnp.sum(saved[-1][8] * grad, -1)
-    side = jnp.broadcast_to(balance[None, :], (8, rows))
+    grad = d_mix = cotangent
+    (side,) = side
     expert_sums = [None] * LAYERS
     out_sums = [None] * LAYERS
     for layer in reversed(range(LAYERS)):

time: 728 us -> 706 us (0.970)
  local copies, waits for them, and re-layouts: 17.1 us -> 6.03 us
    pallas_call x1 -> x0, Pallas kernels: 34.7 us -> none  [exchange_weights(): pl.pallas_call(functools.partial(setup_kernel, count), out_shape=(jax.Sha...]
    pallas_call x8, Pallas kernels: 594 us -> 628 us  [ring_call(): pl.pallas_call(kernel, out_shape=tuple((shape for shape, _ in outputs)) +...]
  transfers between devices with their start and end apart: 6 -> 3, of which waited for: 0 -> 0; matrix products, arithmetic and copies ran while one was open for 1% -> 0% of each run, Pallas kernels for 50% -> 39%
where the time goes in v8:
time: 706 us; the launch traced here: 702 us
  Pallas kernels  685 us (97%)
    pallas_call x8, Pallas kernels, ring_call(): pl.pallas_call(kernel, out_shape=tuple((shape for shape, _ in outputs)) +...  628 us
    pallas_call x1, Pallas kernels, finish_heads(): pl.pallas_call(functools.partial(finish_kernel, count, replicas), out_sha...  42.1 us
    pallas_call x1, Pallas kernels, close(): pl.pallas_call(functools.partial(close_kernel, layers, count), grid=(step...  15.2 us
  transfers between devices with their start and end apart: 3, of which 0 were waited for; matrix products, arithmetic and copies ran while one was open for 0% of the time, Pallas kernels for 39%

profile of v8, /device:TPU:0, one launch (start us, length us, event | category | flops | bytes accessed | tf_op | source)
XLA Modules:
  0.0 702.3 jit_solution(8741411403978973562)
XLA Ops:
  0.7 0.7 convert_element_type.8
  1.3 0.8 convert_reduce_fusion
  2.2 0.8 select_reduce_fusion
  2.9 0.6 constant_dynamic-slice_fusion.refs_7_.refs_4_.refs_8_
  3.6 0.1 multiply_cosine_fusion
  3.7 0.6 pad_maximum_fusion.refs_6_
  4.3 1.3 fusion.8.refs_5_
  5.6 116.6 %attend.2 = (bf16[8,3,128,128]{3,2,1,0:T(8,128)(2,1)}, bf16[8,128,128]{2,1,0:T(8,128)(2,1)}, bf16[8,128,128]{2,1,0:T(8,128)(2,1)}, bf16[8,128,1536]{2,1,0:T(8,12...) custom-call(bf16[128,1536]{1,0:T(8,128)(2,1)} %refs_13_.1, ...), custom_call_target="tpu_custom_call" | custom-call | tf_op jit(solution)/shard_map/attend/pallas_call | solution.py:352
  122.3 67.8 %mix.2 = (f32[128,1536]{1,0:T(8,128)}, f32[128,1536]{1,0:T(8,128)}, bf16[128,1536]{1,0:T(8,128)(2,1)}, bf16[8,128,1536]{2,1,0:T(8,128)(2,1)}, f32[8,16,128]{2,1,0:T(8,128)}) custom-call(bf16[128,1536]{1,0:T(8,128)(2,1)} %get-tuple-element.76.refs_0_, f32[16,128]{1,0:T(8,128)} %get-tuple-element.77.refs_1_, f32[128,1536]{1,0:T(8,128)} %get-tuple-element.78.refs_2_.refs_6_, ...), custom_call_target="tpu_custom_call" | custom-call | tf_op jit(solution)/shard_map/mix/pallas_call | solution.py:352
  190.1 71.4 %attend.3 = (bf16[8,3,128,128]{3,2,1,0:T(8,128)(2,1)}, bf16[8,128,128]{2,1,0:T(8,128)(2,1)}, bf16[8,128,128]{2,1,0:T(8,128)(2,1)}, bf16[8,128,1536]{2,1,0:T(8,12...) custom-call(bf16[128,1536]{1,0:T(8,128)(2,1)} %get-tuple-element.80., ...), custom_call_target="tpu_custom_call" | custom-call | tf_op jit(solution)/shard_map/attend/pallas_call | solution.py:352
  261.5 68.1 %mix.3 = (f32[128,1536]{1,0:T(8,128)}, f32[128,1536]{1,0:T(8,128)}, bf16[128,1536]{1,0:T(8,128)(2,1)}, bf16[8,128,1536]{2,1,0:T(8,128)(2,1)}, f32[8,16,128]{2,1,0:T(8,128)}, /*index=5*/f32[8,128]{1,0:T(8,128)}) custom-call(bf16[128,1536]{1,0:T(8,128)(2,1)} %get-tuple-element.85.refs_0_, f32[16,128]{1,0:T(8,128)} %get-tuple-element.86.refs_1_, ...), custom_call_target="tpu_custom_call" | custom-call | tf_op jit(solution)/shard_map/mix/pallas_call | solution.py:352
  329.6 73.3 %mix_back.2 = (f32[128,1536]{1,0:T(8,128)}, bf16[128,1536]{1,0:T(8,128)(2,1)}, f32[1,1536]{1,0:T(1,128)}, bf16[4608,512]{1,0:T(8,128)(2,1)}, f32[2,1536]{1,0:T(2,128)}) custom-call(bf16[128,1536]{1,0:T(8,128)(2,1)} %refs_5_.5, f32[8,128]{1,0:T(8,128)} %get-tuple-element.89.refs_1_, bf16[8,128,1536]{2,1,0:T(8,128)(2,1)} %get-tuple-element.90.refs_2_, ...), custom_call_target="tpu_custom_call" | custom-call | tf_op jit(solution)/shard_map/mix_back/pallas_call | solution.py:352
  402.9 1.7 collective-permute-start
  404.6 78.7 %attend_back.2 = (bf16[96,1536]{1,0:T(8,128)(2,1)}, f32[128,1536]{1,0:T(8,128)}, bf16[128,1536]{1,0:T(8,128)(2,1)}, f32[8,128]{1,0:T(8,128)}, bf16[1536,384]{1,0:T(8,128)(2,1)}) custom-call(bf16[128,1536]{1,0:T(8,128)(2,1)} %get-tuple-element.92.refs_0_, bf16[2,2,96,1536]{3,2,1,0:T(8,128)(2,1)} %get-tuple-element.82.refs_2_.refs_1_, ...), custom_call_target="tpu_custom_call" | custom-call | tf_op jit(solution)/shard_map/attend_back/pallas_call | solution.py:352
  483.3 73.5 %mix_back.3 = (f32[128,1536]{1,0:T(8,128)}, bf16[128,1536]{1,0:T(8,128)(2,1)}, f32[1,1536]{1,0:T(1,128)}, bf16[4608,512]{1,0:T(8,128)(2,1)}, f32[2,1536]{1,0:T(2...) custom-call(bf16[128,1536]{1,0:T(8,128)(2,1)} %get-tuple-element.103.refs_0_, ...), custom_call_target="tpu_custom_call" | custom-call | tf_op jit(solution)/shard_map/mix_back/pallas_call | solution.py:352
  556.8 0.7 collective-permute-start.2
  557.5 0.0 collective-permute-done.refs_21_.refs_22_.refs_23_.refs_24_.refs_25_
  557.5 78.7 %attend_back.3 = (bf16[96,1536]{1,0:T(8,128)(2,1)}, f32[128,1536]{1,0:T(8,128)}, bf16[128,1536]{1,0:T(8,128)(2,1)}, f32[8,128]{1,0:T(8,128)}, bf16[1536,384]{1,0:T(8,128)(2,1)}) custom-call(bf16[128,1536]{1,0:T(8,128)(2,1)} %get-tuple-element.112.refs_0_, bf16[2,2,96,1536]{3,2,1,0:T(8,128)(2,1)} %get-tuple-element.82.refs_2_.refs_1_, ...), custom_call_target="tpu_custom_call" | custom-call | tf_op jit(solution)/shard_map/attend_back/pallas_call | solution.py:352
  636.2 1.4 collective-permute-start.1
  637.7 42.1 %finish_heads.1 = (bf16[8,2,96,384]{3,2,1,0:T(8,128)(2,1)}, bf16[8,96,384]{2,1,0:T(8,128)(2,1)}) custom-call(bf16[8,2,96,384]{3,2,1,0:T(8,128)(2,1)} %bitcast.13, bf16[8,2,96,384]{3,2,1,0:T(8,128)(2,1)} %bitcast.12, bf16[8,2,96,384]{3,2,1,0:T(8,128)(2,1)} %get-tuple-element.126.refs_2_), custom_call_target="tpu_custom_call" | custom-call | tf_op jit(solution)/shard_map/finish_heads/pallas_call | solution.py:1479
  679.8 0.0 collective-permute-done.2.refs_11_.refs_12_.refs_13_.refs_14_.refs_15_
  679.8 0.0 collective-permute-done.1.refs_1_
  679.8 0.0 copy-start.2
  679.8 0.7 copy-done.2
  680.5 15.2 %close.1 = (f32[2,96,1536]{2,1,0:T(8,128)}, f32[2,96,1536]{2,1,0:T(8,128)}, f32[2,96,512]{2,1,0:T(8,128)}, f32[2,96,512]{2,1,0:T(8,128)}, f32[2,8,96,128]{3,2,1,...) custom-call(bf16[96,1536]{1,0:T(8,128)(2,1)} %get-tuple-element.123.refs_0_, ...), custom_call_target="tpu_custom_call" | custom-call | tf_op jit(solution)/shard_map/close/pallas_call | solution.py:1570
  695.7 0.0 copy-start.1
  695.7 0.0 copy-start
  695.7 1.5 slice_reduce_fusion
  697.3 1.4 slice_bitcast_fusion
  698.7 0.8 slice_reduce_fusion.1
  699.5 0.9 copy.30
  700.3 0.0 copy-done.1
  700.3 0.7 copy.33
  701.1 0.0 copy-done
  701.1 0.9 copy.34
  (1 shorter events, 0.0 us)
Async XLA Ops:
  402.9 154.6 %collective-permute-start = (bf16[4608,512]{1,0:T(8,128)(2,1)}, bf16[4608,512]{1,0:T(8,128)(2,1)}, u32[]{:S(2)}, u32[]{:S(2)}) collective-permute-start(bf16[4608,512]{1,0:T(8,128)(2,1)} %get-tuple-element.130.refs_16_.refs_17_.refs_18_.refs_19_.refs_20_), channel_id=1, source_target_pairs={{0,16},{16,0},{1,17},{17,1},{2,18},{18,2},{3,19},{19,3},{4,20},{20... | collective-permute-start | bytes 14155784 | tf_op jit(solution)/shard_map/ppermute | solution.py:1654
  556.8 123.0 %collective-permute-start.2 = (bf16[4608,512]{1,0:T(8,128)(2,1)}, bf16[4608,512]{1,0:T(8,128)(2,1)}, u32[]{:S(2)}, u32[]{:S(2)}) collective-permute-start(bf16[4608,512]{1,0:T(8,128)(2,1)} %get-tuple-element.129.refs_6_.refs_7_.refs_8_.refs_9_.refs_10_), channel_id=1, source_target_pairs={{0,16},{16,0},{1,17},{17,1},{2,18},{18,2},{3,19},{19,3},{4,20},{20... | collective-permute-start | bytes 14155784 | tf_op jit(solution)/shard_map/ppermute | solution.py:1654
  636.2 43.5 %collective-permute-start.1 = (bf16[96,1536]{1,0:T(8,128)(2,1)}, bf16[96,1536]{1,0:T(8,128)(2,1)S(1)}, u32[]{:S(2)}, u32[]{:S(2)}) collective-permute-start(bf16[96,1536]{1,0:T(8,128)(2,1)} %get-tuple-element.123.refs_0_), channel_id=1, source_target_pairs={{0,16},{16,0},{1,17},{17,1},{2,18},{18,2},{3,19},{19,3},{4,20},{20... | collective-permute-start | bytes 884744 | tf_op jit(solution)/shard_map/ppermute | solution.py:1654
  679.8 0.7 copy-start.2
  695.7 4.6 copy-start.1
  695.7 5.4 copy-start

commit v9 on v8

--- a/solution.py
+++ b/solution.py
@@ -701,21 +701,42 @@
         ring.meet(True, opening.everyone())
         opening.start()
         opening.parameters()
-        drain = ring.gather(opening.x_ref, buf, sems, None, lambda s: None, lambda s: None)
-        keep = [pltpu.make_async_copy(buf, all_ref, out_sem[0].at[0])]
+        loads = load_out_weights(outputs[10], layer, wide_w, load_sem[0], False)
+        keep = [
+            pltpu.make_async_copy(buf, all_ref, out_sem[0].at[0]),
+            pltpu.make_async_copy(weights, outputs[9].at[0], out_sem[0].at[1]),
+        ]
+
+        def first(s):
+            @pl.when(s == ring.steps - 1)
+            def _():
+                opening.rest()
+                for load in loads:
+                    load.start()
+                opening.arrived(0)
+                keep[1].start()
+                project((ring.chip,))
+
+            @pl.when(s == ring.steps)
+            def _():
+                project(ring.pair(ring.steps - 1))
+
+        def second(s):
+            @pl.when(s == ring.steps - 2)
+            def _():
+                opening.forward(0)
+
+            @pl.when(s == ring.steps - 1)
+            def _():
+                def one(index, carry):
+                    project(ring.pair(index))
+                    return carry
+
+                lax.fori_loop(1, ring.steps - 1, one, 0)
+
+        drain = ring.gather(opening.x_ref, buf, sems, None, first, second)
         keep[0].start()
-        opening.forward(0)
-        opening.rest()
-        loads = load_out_weights(outputs[10], layer, wide_w, load_sem[0])
-        opening.arrived(0)
-        keep.append(pltpu.make_async_copy(weights, outputs[9].at[0], out_sem[0].at[1]))
-        keep[1].start()
-
-        def both(index, carry):
-            project((2 * index, 2 * index + 1))
-            return carry
-
-        lax.fori_loop(0, count // 2, both, 0)
+        project((ring.at(ring.steps),))
         for load in loads:
             load.wait()
     else:
@@ -1194,13 +1215,13 @@
     )
 
 
-def load_out_weights(w_ref, layer, wide_ref, sem):
+def load_out_weights(w_ref, layer, wide_ref, sem, start=True):
     shard = w_ref.shape[2]
     copies = [
         pltpu.make_async_copy(w_ref.at[core, layer], wide_ref.at[pl.ds(core * shard, shard)], sem.at[core])
         for core in range(2)
     ]
-    for copy in copies:
+    for copy in copies if start else []:
         copy.start()
     used = 2 * shard
     wide_ref[used:] = jnp.zeros((wide_ref.shape[0] - used, wide_ref.shape[1]), BF16)
@@ -1496,10 +1517,12 @@
 
 
 def close_kernel(layers, count, *refs):
-    n_experts = 0 if len(refs) == 2 * layers + 7 else 10 * layers
-    inputs, heads_in, experts_in, outputs = split(refs, 2 * layers, 2, n_experts)
+    n_experts = 0 if len(refs) == 2 * layers + 13 else 10 * layers
+    inputs, heads_in, rows_in, experts_in, outputs = split(refs, 2 * layers, 2, 2, n_experts)
     mine, peer = heads_in
-    out_ref, q_out, k_out, v_out, rest_out = outputs[:5]
+    out_ref, q_out, k_out, v_out, router_out, gain_one_out, gain_two_out = outputs[:7]
+    for source, target in zip(rows_in, outputs[7:9]):
+        target[...] = source[...]
 
     @pl.when(pl.program_id(0) == 0)
     def _():
@@ -1513,20 +1536,31 @@
                     value = value + peer[block].astype(F32)
                 return [value[:, i * LANES : (i + 1) * LANES] for i in range(3)]
 
+            shard = mine.shape[2]
+            gains = jnp.zeros((shard, LANES), F32)
+            routers = jnp.zeros((shard, LANES), F32)
             for half in range(count // 2):
                 a, b = tiles(2 * half), tiles(2 * half + 1)
                 low = lanes_of(a[0]) < HD
+                for chip, tile in ((2 * half, a[2]), (2 * half + 1, b[2])):
+                    gains = gains + tile
+                    moved = pltpu.roll(tile, (2 * chip - HD) % LANES, 1)
+                    lane = lanes_of(moved)
+                    routers = jnp.where((lane >= 2 * chip) & (lane < 2 * chip + 2), moved, routers)
                 q_out[layer, :, 3 * half * LANES : 3 * (half + 1) * LANES] = jnp.concatenate(
                     [a[0], jnp.where(low, a[1], turn(b[0])), jnp.where(low, turn(b[0]), turn(b[1]))], 1
                 )
                 here = slice(half * LANES, (half + 1) * LANES)
                 k_out[layer, :, here] = jnp.where(low, turn(a[1]), b[1])
                 v_out[layer, :, here] = jnp.where(low, a[2], turn(b[2]))
-                rest_out[layer, 2 * half] = a[2]
-                rest_out[layer, 2 * half + 1] = b[2]
+
+            router_out[layer] = routers[:, : 2 * count]
+            tall = jnp.concatenate([gains, jnp.zeros((LANES - shard, LANES), F32)], 0).T
+            gain_one_out[layer : layer + 1, :] = tall[HD + 2 : HD + 3, :shard]
+            gain_two_out[layer : layer + 1, :] = tall[HD + 3 : HD + 4, :shard]
 
     if experts_in:
-        expert_refs = outputs[5:]
+        expert_refs = outputs[9:]
         for layer in range(layers):
             pairs = experts_in[layer * 10 : (layer + 1) * 10]
             sums = [pairs[i][...].astype(F32) + pairs[i + 5][...].astype(F32) for i in range(5)]
@@ -1535,7 +1569,7 @@
             expert_refs[2][layer, 0] = jnp.concatenate(sums[2:], 1)
 
 
-def close(count, outs, mine, peer, experts):
+def close(count, outs, mine, peer, rows_out, experts):
     layers = len(outs)
     shard, width = outs[0][0].shape
     steps = 4
@@ -1550,9 +1584,18 @@
         (layers, shard, count * GROUP * HD),
         (layers, shard, count * HD),
         (layers, shard, count * HD),
-        (layers, count, shard, LANES),
+        (layers, shard, 2 * count),
+        (layers, shard),
+        (layers, shard),
     ]
     out_specs = [whole(shape) for shape in shapes]
+    shapes = [cells(shape, F32) for shape in shapes] + [cells(a.shape, a.dtype) for a in rows_out]
+    parts = [
+        pl.BlockSpec((a.shape[0] // (steps if experts else 1), a.shape[1]), lambda i: (i, 0)) for a in rows_out
+    ]
+    arrays += rows_out
+    specs += parts
+    out_specs += parts
     if experts:
         rows, ff = experts[0][0].shape
         tall, short = width // steps, ff // steps
@@ -1564,13 +1607,13 @@
         parts = [at(0, tall), at(width, tall)] + [at(2 * width + g * ff, short) for g in range(groups)]
         arrays += [array for pair in experts for array in pair for _ in parts]
         specs += parts * (2 * layers)
-        shapes += [(layers, 1, width, ff), (layers, 1, width, ff), (layers, 1, ff, width)]
+        shapes += [cells((layers, 1, width, ff), F32)] * 2 + [cells((layers, 1, ff, width), F32)]
         tile = pl.BlockSpec((layers, 1, tall, ff), lambda i: (0, 0, i, 0))
         out_specs += [tile, tile, pl.BlockSpec((layers, 1, short, width), lambda i: (0, 0, i, 0))]
     return pl.pallas_call(
         functools.partial(close_kernel, layers, count),
         grid=(steps if experts else 1,),
-        out_shape=tuple(cells(shape, F32) for shape in shapes),
+        out_shape=tuple(shapes),
         in_specs=specs,
         out_specs=out_specs,
         compiler_params=pltpu.CompilerParams(vmem_limit_bytes=60 << 20),
@@ -1678,32 +1721,29 @@
     arrived, peer = finish_heads(count, replicas, heads, early, rode[1] if rode else early)
     if replicas == 2:
         outs = list(zip(out_sums, [across(out_sums[0]), rode[0]]))
-        g_out, g_query, g_key, g_value, rest, g_gate, g_up, g_down = close(
-            count, outs, arrived, peer, expert_sums
+        *results, g_gate, g_up, g_down = close(
+            count, outs, arrived, peer, [activations, grad], expert_sums
         )
     else:
         outs = [(own, jnp.zeros_like(own)) for own in out_sums]
-        summed = close(count, outs, arrived, peer, [])
-        g_out, g_query, g_key, g_value, rest, flat_sums = [
-            lax.psum(array.astype(BF16), "rep").astype(F32)
-            for array in (*summed, jnp.stack([own for own, _ in expert_sums]))
-        ]
+        results = close(count, outs, arrived, peer, [activations, grad], [])
+        sums = (*results[:7], jnp.stack([own for own, _ in expert_sums]))
+        *summed, flat_sums = [lax.psum(array.astype(BF16), "rep").astype(F32) for array in sums]
+        results = summed + list(results[7:])
         ff = w_gate.shape[3]
         g_gate, g_up = flat_sums[:, None, :width], flat_sums[:, None, width : 2 * width]
         g_down = flat_sums[:, 2 * width :].reshape(LAYERS, width // ff, ff, ff)
         g_down = g_down.transpose(0, 2, 1, 3).reshape(LAYERS, 1, ff, width)
-    rest = rest[..., HD : HD + 4]
-    gains = jnp.sum(rest, 1)
-    g_router = rest[..., :2].transpose(0, 2, 1, 3).reshape(LAYERS, shard, experts)
+    g_out, g_query, g_key, g_value, g_router, gain_one, gain_two, activations, grad = results
     return (
         activations,
         grad,
-        gains[..., 2],
+        gain_one,
         g_query,
         g_key,
         g_value,
         g_out,
-        gains[..., 3],
+        gain_two,
         g_router,
         g_gate,
         g_up,

time: 706 us -> 699 us (0.990)
  no operation moved by 1% of the time
where the time goes in v9:
time: 699 us; the launch traced here: 694 us
  Pallas kernels  681 us (97%)
    pallas_call x8, Pallas kernels, ring_call(): pl.pallas_call(kernel, out_shape=tuple((shape for shape, _ in outputs)) +...  624 us
    pallas_call x1, Pallas kernels, finish_heads(): pl.pallas_call(functools.partial(finish_kernel, count, replicas), out_sha...  42.1 us
    pallas_call x1, Pallas kernels, close(): pl.pallas_call(functools.partial(close_kernel, layers, count), grid=(step...  15.6 us
  transfers between devices with their start and end apart: 3, of which 0 were waited for; matrix products, arithmetic and copies ran while one was open for 0% of the time, Pallas kernels for 39%

profile of v9, /device:TPU:0, one launch (start us, length us, event | category | flops | bytes accessed | tf_op | source)
XLA Modules:
  0.0 693.6 jit_solution(8034298564728070063)
XLA Ops:
  0.7 0.7 convert_element_type.8
  1.3 0.8 convert_reduce_fusion
  2.2 0.8 select_reduce_fusion
  2.9 0.6 constant_dynamic-slice_fusion.refs_7_.refs_4_.refs_8_
  3.6 0.1 multiply_cosine_fusion
  3.7 0.6 pad_maximum_fusion.refs_6_
  4.3 1.3 fusion.8.refs_5_
  5.6 112.5 %attend.2 = (bf16[8,3,128,128]{3,2,1,0:T(8,128)(2,1)}, bf16[8,128,128]{2,1,0:T(8,128)(2,1)}, bf16[8,128,128]{2,1,0:T(8,128)(2,1)}, bf16[8,128,1536]{2,1,0:T(8,12...) custom-call(bf16[128,1536]{1,0:T(8,128)(2,1)} %refs_13_.1, ...), custom_call_target="tpu_custom_call" | custom-call | tf_op jit(solution)/shard_map/attend/pallas_call | solution.py:352
  118.1 67.8 %mix.2 = (f32[128,1536]{1,0:T(8,128)}, f32[128,1536]{1,0:T(8,128)}, bf16[128,1536]{1,0:T(8,128)(2,1)}, bf16[8,128,1536]{2,1,0:T(8,128)(2,1)}, f32[8,16,128]{2,1,0:T(8,128)}) custom-call(bf16[128,1536]{1,0:T(8,128)(2,1)} %get-tuple-element.80.refs_0_, f32[16,128]{1,0:T(8,128)} %get-tuple-element.81.refs_1_, f32[128,1536]{1,0:T(8,128)} %get-tuple-element.82.refs_2_.refs_6_, ...), custom_call_target="tpu_custom_call" | custom-call | tf_op jit(solution)/shard_map/mix/pallas_call | solution.py:352
  185.9 71.4 %attend.3 = (bf16[8,3,128,128]{3,2,1,0:T(8,128)(2,1)}, bf16[8,128,128]{2,1,0:T(8,128)(2,1)}, bf16[8,128,128]{2,1,0:T(8,128)(2,1)}, bf16[8,128,1536]{2,1,0:T(8,12...) custom-call(bf16[128,1536]{1,0:T(8,128)(2,1)} %get-tuple-element.84., ...), custom_call_target="tpu_custom_call" | custom-call | tf_op jit(solution)/shard_map/attend/pallas_call | solution.py:352
  257.3 67.8 %mix.3 = (f32[128,1536]{1,0:T(8,128)}, f32[128,1536]{1,0:T(8,128)}, bf16[128,1536]{1,0:T(8,128)(2,1)}, bf16[8,128,1536]{2,1,0:T(8,128)(2,1)}, f32[8,16,128]{2,1,0:T(8,128)}, /*index=5*/f32[8,128]{1,0:T(8,128)}) custom-call(bf16[128,1536]{1,0:T(8,128)(2,1)} %get-tuple-element.89.refs_0_, f32[16,128]{1,0:T(8,128)} %get-tuple-element.90.refs_1_, ...), custom_call_target="tpu_custom_call" | custom-call | tf_op jit(solution)/shard_map/mix/pallas_call | solution.py:352
  325.1 73.3 %mix_back.2 = (f32[128,1536]{1,0:T(8,128)}, bf16[128,1536]{1,0:T(8,128)(2,1)}, f32[1,1536]{1,0:T(1,128)}, bf16[4608,512]{1,0:T(8,128)(2,1)}, f32[2,1536]{1,0:T(2,128)}) custom-call(bf16[128,1536]{1,0:T(8,128)(2,1)} %refs_5_.5, f32[8,128]{1,0:T(8,128)} %get-tuple-element.92.refs_1_, bf16[8,128,1536]{2,1,0:T(8,128)(2,1)} %get-tuple-element.93.refs_2_, ...), custom_call_target="tpu_custom_call" | custom-call | tf_op jit(solution)/shard_map/mix_back/pallas_call | solution.py:352
  398.4 1.6 collective-permute-start
  400.0 78.7 %attend_back.2 = (bf16[96,1536]{1,0:T(8,128)(2,1)}, f32[128,1536]{1,0:T(8,128)}, bf16[128,1536]{1,0:T(8,128)(2,1)}, f32[8,128]{1,0:T(8,128)}, bf16[1536,384]{1,0:T(8,128)(2,1)}) custom-call(bf16[128,1536]{1,0:T(8,128)(2,1)} %get-tuple-element.95.refs_0_, bf16[2,2,96,1536]{3,2,1,0:T(8,128)(2,1)} %get-tuple-element.86.refs_2_.refs_1_, ...), custom_call_target="tpu_custom_call" | custom-call | tf_op jit(solution)/shard_map/attend_back/pallas_call | solution.py:352
  478.7 73.4 %mix_back.3 = (f32[128,1536]{1,0:T(8,128)}, bf16[128,1536]{1,0:T(8,128)(2,1)}, f32[1,1536]{1,0:T(1,128)}, bf16[4608,512]{1,0:T(8,128)(2,1)}, f32[2,1536]{1,0:T(2...) custom-call(bf16[128,1536]{1,0:T(8,128)(2,1)} %get-tuple-element.106.refs_0_, ...), custom_call_target="tpu_custom_call" | custom-call | tf_op jit(solution)/shard_map/mix_back/pallas_call | solution.py:352
  552.1 0.7 collective-permute-start.2
  552.9 0.0 collective-permute-done.refs_23_.refs_24_.refs_25_.refs_26_.refs_27_
  552.9 78.7 %attend_back.3 = (bf16[96,1536]{1,0:T(8,128)(2,1)}, f32[128,1536]{1,0:T(8,128)}, bf16[128,1536]{1,0:T(8,128)(2,1)}, f32[8,128]{1,0:T(8,128)}, bf16[1536,384]{1,0:T(8,128)(2,1)}) custom-call(bf16[128,1536]{1,0:T(8,128)(2,1)} %get-tuple-element.115.refs_0_, bf16[2,2,96,1536]{3,2,1,0:T(8,128)(2,1)} %get-tuple-element.86.refs_2_.refs_1_, ...), custom_call_target="tpu_custom_call" | custom-call | tf_op jit(solution)/shard_map/attend_back/pallas_call | solution.py:352
  631.6 1.4 collective-permute-start.1
  633.0 42.1 %finish_heads.1 = (bf16[8,2,96,384]{3,2,1,0:T(8,128)(2,1)}, bf16[8,96,384]{2,1,0:T(8,128)(2,1)}) custom-call(bf16[8,2,96,384]{3,2,1,0:T(8,128)(2,1)} %bitcast.10, bf16[8,2,96,384]{3,2,1,0:T(8,128)(2,1)} %bitcast.9, bf16[8,2,96,384]{3,2,1,0:T(8,128)(2,1)} %get-tuple-element.128.refs_2_), custom_call_target="tpu_custom_call" | custom-call | tf_op jit(solution)/shard_map/finish_heads/pallas_call | solution.py:1500
  675.1 0.0 collective-permute-done.2.refs_13_.refs_14_.refs_15_.refs_16_.refs_17_
  675.1 0.0 collective-permute-done.1.refs_1_
  675.1 0.0 copy-start
  675.2 0.7 copy-done
  675.9 15.6 %close.1 = (f32[2,96,1536]{2,1,0:T(8,128)}, f32[2,96,1536]{2,1,0:T(8,128)}, f32[2,96,512]{2,1,0:T(8,128)}, f32[2,96,512]{2,1,0:T(8,128)}, f32[2,96,16]{2,1,0:T(8...) custom-call(bf16[96,1536]{1,0:T(8,128)(2,1)} %get-tuple-element.125., ...), custom_call_target="tpu_custom_call" | custom-call | tf_op jit(solution)/shard_map/close/pallas_call | solution.py:1613
  691.5 1.6 copy.28
  (1 shorter events, 0.0 us)
Async XLA Ops:
  398.4 154.4 %collective-permute-start = (bf16[4608,512]{1,0:T(8,128)(2,1)}, bf16[4608,512]{1,0:T(8,128)(2,1)}, u32[]{:S(2)}, u32[]{:S(2)}) collective-permute-start(bf16[4608,512]{1,0:T(8,128)(2,1)} %get-tuple-element.134.refs_18_.refs_19_.refs_20_.refs_21_.refs_22_), channel_id=1, source_target_pairs={{0,16},{16,0},{1,17},{17,1},{2,18},{18,2},{3,19},{19,3},{4,20},{20... | collective-permute-start | bytes 14155784 | tf_op jit(solution)/shard_map/ppermute | solution.py:1697
  552.1 123.0 %collective-permute-start.2 = (bf16[4608,512]{1,0:T(8,128)(2,1)}, bf16[4608,512]{1,0:T(8,128)(2,1)}, u32[]{:S(2)}, u32[]{:S(2)}) collective-permute-start(bf16[4608,512]{1,0:T(8,128)(2,1)} %get-tuple-element.133.refs_8_.refs_9_.refs_10_.refs_11_.refs_12_), channel_id=1, source_target_pairs={{0,16},{16,0},{1,17},{17,1},{2,18},{18,2},{3,19},{19,3},{4,20},{20... | collective-permute-start | bytes 14155784 | tf_op jit(solution)/shard_map/ppermute | solution.py:1697
  631.6 43.5 %collective-permute-start.1 = (bf16[96,1536]{1,0:T(8,128)(2,1)}, bf16[96,1536]{1,0:T(8,128)(2,1)S(1)}, u32[]{:S(2)}, u32[]{:S(2)}) collective-permute-start(bf16[96,1536]{1,0:T(8,128)(2,1)} %get-tuple-element.125.refs_0_), channel_id=1, source_target_pairs={{0,16},{16,0},{1,17},{17,1},{2,18},{18,2},{3,19},{19,3},{4,20},{20... | collective-permute-start | bytes 884744 | tf_op jit(solution)/shard_map/ppermute | solution.py:1697
  675.1 0.7 copy-start

commit v10 on v9

--- a/solution.py
+++ b/solution.py
@@ -85,9 +85,9 @@
         self.steps = count // 2
         self.chip, self.at, self.near = ring_setup(count)
 
-    def meet(self, partner=False, everyone=None):
+    def meet(self, partner=False, everyone=None, across=False):
         others = everyone or self.near + ([partner_of("fsdp")] if partner else [])
-        meet(others + ([partner_of("rep")] if self.riders else []))
+        meet(others + ([partner_of("rep")] if self.riders or across else []))
         for rider in self.riders:
             rider.start()
         for copy in self.early:
@@ -662,18 +662,15 @@
                 self.beside(layer, offset, slot).wait_send()
 
 
-def attend_kernel(count, layer, traffic, *refs):
+def attend_part(ring, count, layer, inputs, outputs, scratch, midway):
     if layer == 0:
-        inputs, outputs, scratch = split(refs, 9, 13)
         begin_ref, routes_ref = inputs[7:]
         hidden_ref, table_ref, params_ref = inputs[0], outputs[11], outputs[12]
     else:
-        inputs, outputs, scratch = split(refs, 8, 9)
         x_ref, w_ref, w_out_ref, table_ref, begin_ref, hidden_ref, params_ref, routes_ref = inputs
     q_ref, own_ref, other_ref, all_ref, att_ref, lse_ref, middle_ref, x_out_ref, share_ref = outputs[:9]
     buf, weights, wide_w, turned_ref, score_ref, partial, land = scratch[:7]
-    sems, pair_sems, scatter_sem, out_sem, load_sem, more = split(scratch[7:], 3, 2, 2, 1, 1)
-    ring = Ring(count, traffic)
+    sems, pair_sems, scatter_sem, out_sem, load_sem, more = split(scratch[7:], 3, 2, 2, 1, 1)[:5] + [scratch[16:]]
     partner = partner_of("fsdp")
     core = lax.rem(lax.axis_index("fsdp"), 2)
 
@@ -696,7 +693,6 @@
             pass_on(block).start()
 
     if layer == 0:
-        more = scratch[7 + 9 :]
         opening = Opening(count, inputs[:7], outputs[9:], [*more[:3], weights, *more[3:]])
         ring.meet(True, opening.everyone())
         opening.start()
@@ -759,6 +755,7 @@
     for block in range(count):
         pass_on(block).wait()
     ring.depart()
+    midway()
     turn_keys(own_ref, other_ref, turned_ref)
 
     def attend(blocks):
@@ -836,56 +833,49 @@
     scores = jnp.where(named, logits, MASKED)
     weighted = jnp.where(named, jnp.exp(scores - jnp.max(scores, 0, keepdims=True)), 0.0)
     share_ref[...] = weighted / jnp.sum(weighted, 0, keepdims=True)
-    drain()
-    finish()
-    for copy in keep:
-        copy.wait()
-    if layer == 0:
-        for later in range(1, LAYERS):
-            opening.arrived(later)
-        opening.drain()
-
-
-def gather_attend_scatter(count, layer, inputs, rows, width, columns, extra=()):
+
+    def end():
+        drain()
+        finish()
+        for copy in keep:
+            copy.wait()
+        if layer == 0:
+            for later in range(1, LAYERS):
+                opening.arrived(later)
+            opening.drain()
+
+    return end
+
+
+def attend_shapes(count, rows, width, columns, extra):
     block = cells((count, rows, LANES), BF16)
     everyone = pltpu.VMEM((count, rows, width), BF16)
     wide = 2 * LANES
-    more_outputs, more_scratch = extra if extra else ([], [])
-    return ring_call(
-        functools.partial(attend_kernel, count, layer),
-        ("attend", layer),
-        inputs,
-        [
-            (cells((count, GROUP, rows, LANES), BF16), SOON),
-            (block, SOON),
-            (block, SOON),
-            (cells((count, rows, width), BF16), ANYWHERE),
-            (cells((count, rows, wide), BF16), OUT),
-            (cells((count, 1, GROUP * rows), F32), OUT),
-            (cells((rows, width), F32), OUT),
-            (cells((rows, width), BF16), OUT),
-            (cells((2 * count, rows), F32), OUT),
-        ]
-        + more_outputs,
-        [
-            everyone,
-            pltpu.VMEM((width, columns), BF16),
-            pltpu.VMEM((wide, width), BF16),
-            pltpu.VMEM((count // SPAN, LANES, SPAN * wide), BF16),
-            pltpu.VMEM((count // SPAN, SPAN * wide, 2 * GROUP * LANES), F32),
-            everyone,
-            land_scratch(count, rows, width),
-        ]
-        + gather_sems(count)
-        + dmas((count,), (count,))
-        + scatter_sems(count)
-        + dmas((2,), (3,))
-        + more_scratch,
-        60,
-    )
-
-
-def open_attend_scatter(count, columns, tokens, projections, out_w, small, table, begin, routes):
+    outputs = [
+        (cells((count, GROUP, rows, LANES), BF16), SOON),
+        (block, SOON),
+        (block, SOON),
+        (cells((count, rows, width), BF16), ANYWHERE),
+        (cells((count, rows, wide), BF16), OUT),
+        (cells((count, 1, GROUP * rows), F32), OUT),
+        (cells((rows, width), F32), OUT),
+        (cells((rows, width), BF16), OUT),
+        (cells((2 * count, rows), F32), OUT),
+    ]
+    scratch = [
+        everyone,
+        pltpu.VMEM((width, columns), BF16),
+        pltpu.VMEM((wide, width), BF16),
+        pltpu.VMEM((count // SPAN, LANES, SPAN * wide), BF16),
+        pltpu.VMEM((count // SPAN, SPAN * wide, 2 * GROUP * LANES), F32),
+        everyone,
+        land_scratch(count, rows, width),
+    ]
+    scratch += gather_sems(count) + dmas((count,), (count,)) + scatter_sems(count) + dmas((2,), (3,))
+    return outputs + extra[0], scratch + extra[1]
+
+
+def opening_shapes(count, tokens, columns, out_w, small, table):
     rows, width = tokens.shape
     layers, shard, _ = out_w.shape
     devices = 2 * count
@@ -899,12 +889,8 @@
         pltpu.VMEM((rows, width), BF16),
         pltpu.VMEM((count, layers, shard, columns), BF16),
         pltpu.VMEM((devices,) + small.shape, BF16),
-    ] + dmas(
-        (3 + layers,), (2, count, layers), (2, count, layers), (2, devices), (2, count), (2,)
-    )
-    inputs = [(a, EARLY) for a in (tokens, *projections)] + [(a, ANYWHERE) for a in (out_w, small, table)]
-    inputs += [(begin, EARLY), (routes, LATE)]
-    return gather_attend_scatter(count, 0, inputs, rows, width, columns, (outputs, scratch))
+    ] + dmas((3 + layers,), (2, count, layers), (2, count, layers), (2, devices), (2, count), (2,))
+    return outputs, scratch
 
 
 def load_experts(refs, layer, bufs, sem):
@@ -949,17 +935,11 @@
     return first
 
 
-def mix_kernel(count, layer, traffic, *refs):
-    last = layer + 1 == LAYERS
-    inputs, outputs, scratch = split(refs, 7 + last, 5 + last)
-    x_ref, side_ref, middle_ref, params_ref = inputs[:4]
+def mix_part(ring, count, layer, given, cotangent, outputs, scratch, loads, lent):
+    x_ref, side_ref, middle_ref, params_ref = given
     mixed_ref, hidden_ref, next_ref, all_ref, share_ref = outputs[:5]
     buf, partial, land, acc, gates, ups, downs = scratch[:7]
-    sems, scatter_sem, load_sem, lend_sem, out_sem = split(scratch[7:], 5, 2, 1, 2)
-    ring = Ring(count, traffic)
-    loads = load_experts(inputs[4:7], layer, (gates, ups, downs), load_sem[0])
-    ring.meet(True)
-    lent = lend_experts(inputs[4:7], layer, (gates, ups, downs), lend_sem)
+    sems, scatter_sem, out_sem = split(scratch[7:], 5, 2)
 
     def ready():
         for copy in lent:
@@ -984,7 +964,6 @@
     for e in range(2):
         compute(e, (ring.at(ring.steps),))
     mixed, finish = ring.scatter(partial, land, scatter_sem)
-    ring.settle()
     mixed_ref[...] = mixed
     hidden = middle_ref[...] + mixed
     hidden_ref[...] = hidden
@@ -992,11 +971,15 @@
         next_ref[...] = (normal(hidden)[1] * gain_row(params_ref, 0, layer + 1)).astype(BF16)
     else:
         next_ref[...] = hidden.astype(BF16)
-        balance = jnp.sum(mixed * inputs[7][...].astype(F32), -1, keepdims=True)
+        balance = jnp.sum(mixed * cotangent[0][...].astype(F32), -1, keepdims=True)
         outputs[5][...] = jnp.broadcast_to(as_line(balance), outputs[5].shape)
-    drain()
-    finish()
-    keep.wait()
+
+    def end():
+        drain()
+        finish()
+        keep.wait()
+
+    return end
 
 
 def expert_scratch(weights):
@@ -1007,45 +990,72 @@
     return pltpu.VMEM((2, 2, count // 2, rows // 2, width), BF16)
 
 
-def gather_mix_scatter(count, layer, x, share, middle, params, weights, cotangent):
-    rows, width = x.shape
+def mix_shapes(count, layer, rows, width, weights):
     everyone = pltpu.VMEM((count, rows, width), BF16)
     own = cells((rows, width), F32)
+    outputs = [
+        (own, OUT),
+        (own, OUT),
+        (cells((rows, width), BF16), OUT),
+        (cells((count, rows, width), BF16), ANYWHERE),
+        (cells((count, 2 * count, rows), F32), OUT),
+    ]
+    if layer + 1 == LAYERS:
+        outputs.append((cells((8, rows), F32), OUT))
+    scratch = [everyone, everyone, land_scratch(count, rows, width), pltpu.VMEM((2 * rows, width), F32)]
+    scratch += expert_scratch(weights) + gather_sems(count, True) + scatter_sems(count) + dmas((1,))
+    return outputs, scratch
+
+
+def forward_kernel(count, layer, sizes, traffic, *refs):
+    last = layer + 1 == LAYERS
+    attend_in, weights, cotangent, attend_out, mix_out, scratch = split(
+        refs, sizes[0], 3, int(last), sizes[1], sizes[2]
+    )
+    attend_scratch, mix_scratch, sems = split(scratch, sizes[3], sizes[4])
+    bufs = mix_scratch[4:7]
+    ring = Ring(count, traffic)
+    loads = load_experts(weights, layer, bufs, sems[0])
+    lent = []
+    attend_end = attend_part(
+        ring, count, layer, attend_in, attend_out, attend_scratch,
+        lambda: lent.extend(lend_experts(weights, layer, bufs, sems[1:])),
+    )
+    params_ref = attend_out[12] if layer == 0 else attend_in[6]
+    given = (attend_out[7], attend_out[8], attend_out[6], params_ref)
+    mix_end = mix_part(ring, count, layer, given, cotangent, mix_out, mix_scratch, loads, lent)
+    attend_end()
+    mix_end()
+
+
+def forward(count, layer, inputs, rows, width, columns, weights, cotangent, extra=([], [])):
+    last = layer + 1 == LAYERS
+    attend_out, attend_scratch = attend_shapes(count, rows, width, columns, extra)
+    mix_out, mix_scratch = mix_shapes(count, layer, rows, width, weights)
+    sizes = [len(part) for part in (inputs, attend_out, mix_out, attend_scratch, mix_scratch)]
     return ring_call(
-        functools.partial(mix_kernel, count, layer),
-        ("mix", layer),
-        [(x, ANYWHERE), (share, ANYWHERE), (middle, LATE), (params, LATE)]
-        + [(w, ANYWHERE) for w in weights]
-        + ([(cotangent, LATE)] if layer + 1 == LAYERS else []),
-        [
-            (own, OUT),
-            (own, OUT),
-            (cells((rows, width), BF16), OUT),
-            (cells((count, rows, width), BF16), ANYWHERE),
-            (cells((count,) + share.shape, F32), OUT),
-        ]
-        + ([(cells((8, rows), F32), OUT)] if layer + 1 == LAYERS else []),
-        [everyone, everyone, land_scratch(count, rows, width), pltpu.VMEM((2 * rows, width), F32)]
-        + expert_scratch(weights)
-        + gather_sems(count, True)
-        + scatter_sems(count)
-        + dmas((3,), (3,), (3,), (1,)),
+        functools.partial(forward_kernel, count, layer, sizes),
+        ("forward", layer),
+        inputs + [(w, ANYWHERE) for w in weights] + ([(cotangent, LATE)] if last else []),
+        attend_out + mix_out,
+        attend_scratch + mix_scratch + dmas((3,), (3,), (3,)),
         60,
     )
 
 
-def mix_back_kernel(count, layer, traffic, *refs):
-    inputs, outputs, scratch = split(refs, 10, 5)
+def mix_back_kernel(count, layer, replicas, traffic, *refs):
+    crossing = replicas == 2
+    inputs, outputs, scratch = split(refs, 10, 6 + crossing)
     d_ref, side_ref, m_ref, share_ref, params_ref, grad_ref, middle_ref = inputs[:7]
-    mid_ref, branch_ref, gain_ref, sum_ref, g_router_ref = outputs
+    mid_ref, branch_ref, gain_ref, part_ref, sum_ref, g_router_ref = outputs[:6]
     buf, partial, land, acc, gates, ups, downs = scratch[:7]
     tokens, acts, hiddens, balance_ref, totals, got = scratch[7:13]
-    sems, scatter_sem, load_sem, pair_sem, lend_sem, out_sem = split(scratch[13:], 5, 2, 1, 2, 2)
+    sems, scatter_sem, load_sem, pair_sem, lend_sem, cross_sem, out_sem = split(scratch[13:], 5, 2, 1, 2, 2, 2)
     ring = Ring(count, traffic)
     loads = load_experts(inputs[7:], layer, (gates, ups, downs), load_sem[0])
     loads.append(pltpu.make_async_copy(m_ref, tokens, load_sem[0].at[3]))
     loads[-1].start()
-    ring.meet(True)
+    ring.meet(True, None, crossing)
     lent = lend_experts(inputs[7:], layer, (gates, ups, downs), lend_sem)
 
     def ready():
@@ -1110,13 +1120,26 @@
             for index, (first, length) in enumerate(regions(half))
         ]
 
+    apart = width // 2
+
     def store(half):
         return [
             pltpu.make_async_copy(
-                totals.at[0, pl.ds(first, length)], sum_ref.at[pl.ds(first, length)], out_sem[0].at[half, index]
+                totals.at[0, pl.ds(first, length)],
+                sum_ref.at[pl.ds(first - apart, length)] if first else part_ref,
+                out_sem[0].at[half, index],
             )
             for index, (first, length) in enumerate(regions(half))
         ]
+
+    crossings = []
+    if crossing:
+        crossings.append(
+            remote(
+                totals.at[0, pl.ds(0, apart)], outputs[6],
+                cross_sem[0].at[0], cross_sem[1].at[0], partner_of("rep"),
+            )
+        )
 
     def work(s, place):
         e = 1 - s // 2
@@ -1161,7 +1184,7 @@
 
                 @pl.when(s == 2 + h)
                 def _():
-                    for copy in store(h):
+                    for copy in store(h) + (crossings if h == 0 else []):
                         copy.start()
 
     d_x, finish = ring.scatter(partial, land, scatter_sem, work)
@@ -1172,6 +1195,8 @@
     branch_ref[...] = grad.astype(BF16)
     drain()
     finish()
+    for copy in crossings:
+        copy.wait()
     for half in range(2):
         for copy in swap(half):
             copy.wait_send()
@@ -1179,14 +1204,14 @@
             copy.wait()
 
 
-def gather_mix_back_scatter(count, layer, d, side, m_all, share, params, grad, middle, weights, rides):
+def gather_mix_back_scatter(count, layer, replicas, d, side, m_all, share, params, grad, middle, weights, rides):
     rows, width = d.shape
     ff = weights[0].shape[3]
     everyone = pltpu.VMEM((count, rows, width), BF16)
     groups = width // ff
     own = cells((rows, width), F32)
     return ring_call(
-        functools.partial(mix_back_kernel, count, layer),
+        functools.partial(mix_back_kernel, count, layer, replicas),
         ("mix_back", layer),
         [(d, ANYWHERE), (side, ANYWHERE), (m_all, ANYWHERE), (share, EARLY), (params, EARLY), (grad, LATE), (middle, LATE)]
         + [(w, ANYWHERE) for w in weights],
@@ -1194,9 +1219,11 @@
             (own, OUT),
             (cells((rows, width), BF16), OUT),
             (cells((1, width), F32), OUT),
-            (cells((3 * width, ff), BF16), ANYWHERE),
+            (cells((width // 2, ff), BF16), ANYWHERE),
+            (cells((3 * width - width // 2, ff), BF16), ANYWHERE),
             (cells((2, width), F32), OUT),
-        ],
+        ]
+        + ([(cells((width // 2, ff), BF16), ANYWHERE)] if replicas == 2 else []),
         [everyone, everyone, land_scratch(count, rows, width), pltpu.VMEM((2 * rows, width), F32)]
         + expert_scratch(weights)
         + [
@@ -1209,7 +1236,7 @@
         ]
         + gather_sems(count, True)
         + scatter_sems(count)
-        + dmas((4,), (2, 2 + groups), (2, 2 + groups), (3,), (3,), (2, 2 + groups)),
+        + dmas((4,), (2, 2 + groups), (2, 2 + groups), (3,), (3,), (1,), (1,), (2, 2 + groups)),
         60,
         rides,
     )
@@ -1431,10 +1458,15 @@
 
 def finish_kernel(count, replicas, *refs):
     inputs, outputs, scratch = split(refs, 3, 2)
-    g_ref, early_ref, early_peer_ref = inputs
     mine, peer = outputs
-    early, land, total = scratch[:3]
-    pair_send, pair_recv, part_send, part_recv, rep_send, rep_recv = scratch[3:]
+    g_ref, early_ref, early_peer_ref, early, land, total = scratch[:6]
+    pair_send, pair_recv, part_send, part_recv, rep_send, rep_recv, load_sem = scratch[6:]
+    loads = [
+        pltpu.make_async_copy(source, target, load_sem.at[i])
+        for i, (source, target) in enumerate(zip(inputs, scratch))
+    ]
+    for load in loads:
+        load.start()
     me = lax.axis_index("fsdp")
     chip, core = me // 2, lax.rem(me, 2)
     partner = partner_of("fsdp")
@@ -1447,44 +1479,48 @@
 
     across = [partner_of("rep")] if replicas == 2 else []
     meet([device(offset) for offset in range(1, count)] + [partner] + across)
-    swaps = [remote(g_ref.at[:, 1 - core], land.at[0], pair_send.at[0], pair_recv.at[0], partner)]
+    swaps = [remote(inputs[0].at[:, 1 - core], land.at[0], pair_send.at[0], pair_recv.at[0], partner)]
     swaps[0].start()
+    for load in loads:
+        load.wait()
     for block in range(count):
-        for half in range(2):
-            both = early_ref[block, half].astype(F32)
-            if replicas == 2:
-                both = both + early_peer_ref[block, half].astype(F32)
-            early[half, block] = both.astype(BF16)
+        both = early_ref[block, 1 - core].astype(F32)
+        if replicas == 2:
+            both = both + early_peer_ref[block, 1 - core].astype(F32)
+        early[block] = both.astype(BF16)
+    swaps.append(remote(early, land.at[1], pair_send.at[1], pair_recv.at[1], partner))
+    swaps[1].start()
     if replicas != 2:
         peer[...] = jnp.zeros_like(peer)
-    swaps.append(remote(early.at[1 - core], land.at[1], pair_send.at[1], pair_recv.at[1], partner))
-    swaps[1].start()
-    for swap in swaps:
-        swap.wait()
-    for block in range(count):
-        total[block, 0] = (g_ref[block, core].astype(F32) + land[0, block].astype(F32)).astype(BF16)
-        total[block, 1] = (early[core, block].astype(F32) + land[1, block].astype(F32)).astype(BF16)
-    sends = [
-        remote(
-            total.at[chip_at(offset)], mine.at[chip],
-            part_send.at[offset], part_recv.at[offset], device(offset),
-        )
-        for offset in range(1, count)
-    ]
-    for send in sends:
-        send.start()
-    mine[chip] = total[chip]
+    sends = []
+    for layer in range(2):
+        swaps[layer].wait()
+        for block in range(count):
+            own = (g_ref, early_ref)[layer][block, core].astype(F32)
+            if layer == 1 and replicas == 2:
+                own = own + early_peer_ref[block, core].astype(F32)
+            total[layer, block] = (own + land[layer, block].astype(F32)).astype(BF16)
+        for offset in range(1, count):
+            sends.append(
+                remote(
+                    total.at[layer, chip_at(offset)], mine.at[layer, chip],
+                    part_send.at[layer, offset], part_recv.at[layer, offset], device(offset),
+                )
+            )
+            sends[-1].start()
+        mine[layer, chip] = total[layer, chip]
 
     def to_peer(offset):
         slot = chip_at(-offset)
-        return remote(mine.at[slot, 0], peer.at[slot], rep_send.at[offset], rep_recv.at[offset], across[0])
-
-    for offset in range(count):
-        if offset > 0:
-            slot = mine.at[chip_at(-offset)]
-            remote(slot, slot, part_send.at[offset], part_recv.at[offset], partner).wait_recv()
-        if replicas == 2:
-            to_peer(offset).start()
+        return remote(mine.at[0, slot], peer.at[slot], rep_send.at[offset], rep_recv.at[offset], across[0])
+
+    for layer in range(2):
+        for offset in range(count):
+            if offset > 0:
+                slot = mine.at[layer, chip_at(-offset)]
+                remote(slot, slot, part_send.at[layer, offset], part_recv.at[layer, offset], partner).wait_recv()
+            if layer == 0 and replicas == 2:
+                to_peer(offset).start()
     if replicas == 2:
         for offset in range(count):
             to_peer(offset).wait()
@@ -1495,18 +1531,21 @@
 
 def finish_heads(count, replicas, g, early, early_peer):
     _, _, rows, columns = g.shape
-    part = (count, LAYERS, rows, columns)
+    part = (LAYERS, count, rows, columns)
     dma = pltpu.SemaphoreType.DMA
     return pl.pallas_call(
         functools.partial(finish_kernel, count, replicas),
         out_shape=(cells(part, BF16), cells((count, rows, columns), BF16)),
-        in_specs=[HERE] * 3,
+        in_specs=[ANYWHERE] * 3,
         out_specs=[HERE] * 2,
         scratch_shapes=[
-            pltpu.VMEM((2, count, rows, columns), BF16),
-            pltpu.VMEM((2, count, rows, columns), BF16),
+            pltpu.VMEM(g.shape, BF16),
+            pltpu.VMEM(g.shape, BF16),
+            pltpu.VMEM(g.shape, BF16),
+            pltpu.VMEM((count, rows, columns), BF16),
             pltpu.VMEM(part, BF16),
-            dma((2,)), dma((2,)), dma((count,)), dma((count,)), dma((count,)), dma((count,)),
+            pltpu.VMEM(part, BF16),
+            dma((2,)), dma((2,)), dma((2, count)), dma((2, count)), dma((count,)), dma((count,)), dma((3,)),
         ],
         compiler_params=pltpu.CompilerParams(
             collective_id=identity(("finish",)), has_side_effects=True, vmem_limit_bytes=60 << 20
@@ -1517,7 +1556,7 @@
 
 
 def close_kernel(layers, count, *refs):
-    n_experts = 0 if len(refs) == 2 * layers + 13 else 10 * layers
+    n_experts = 0 if len(refs) == 2 * layers + 13 else 12 * layers
     inputs, heads_in, rows_in, experts_in, outputs = split(refs, 2 * layers, 2, 2, n_experts)
     mine, peer = heads_in
     out_ref, q_out, k_out, v_out, router_out, gain_one_out, gain_two_out = outputs[:7]
@@ -1531,7 +1570,7 @@
             out_ref[layer] = own[...].astype(F32) + got[...].astype(F32)
 
             def tiles(block):
-                value = mine[block, layer].astype(F32)
+                value = mine[layer, block].astype(F32)
                 if layer == 0:
                     value = value + peer[block].astype(F32)
                 return [value[:, i * LANES : (i + 1) * LANES] for i in range(3)]
@@ -1562,11 +1601,12 @@
     if experts_in:
         expert_refs = outputs[9:]
         for layer in range(layers):
-            pairs = experts_in[layer * 10 : (layer + 1) * 10]
-            sums = [pairs[i][...].astype(F32) + pairs[i + 5][...].astype(F32) for i in range(5)]
-            expert_refs[0][layer, 0] = sums[0]
-            expert_refs[1][layer, 0] = sums[1]
-            expert_refs[2][layer, 0] = jnp.concatenate(sums[2:], 1)
+            pairs = experts_in[layer * 12 : (layer + 1) * 12]
+            sums = [pairs[i][...].astype(F32) + pairs[i + 6][...].astype(F32) for i in range(6)]
+            early = pl.program_id(0) < pl.num_programs(0) // 2
+            expert_refs[0][layer, 0] = jnp.where(early, sums[0], sums[1])
+            expert_refs[1][layer, 0] = sums[2]
+            expert_refs[2][layer, 0] = jnp.concatenate(sums[3:], 1)
 
 
 def close(count, outs, mine, peer, rows_out, experts):
@@ -1597,15 +1637,23 @@
     specs += parts
     out_specs += parts
     if experts:
-        rows, ff = experts[0][0].shape
+        (_, _), (rest, _) = experts[0]
+        rows, ff = rest.shape
         tall, short = width // steps, ff // steps
-        groups = (rows - 2 * width) // ff
+        apart = width // 2
+        groups = (rows + apart - 2 * width) // ff
 
         def at(first, length):
-            return pl.BlockSpec((length, ff), lambda i: (first // length + i, 0))
-
-        parts = [at(0, tall), at(width, tall)] + [at(2 * width + g * ff, short) for g in range(groups)]
-        arrays += [array for pair in experts for array in pair for _ in parts]
+            return pl.BlockSpec((length, ff), lambda i: ((first - apart) // length + i, 0))
+
+        parts = [
+            pl.BlockSpec((tall, ff), lambda i: (jnp.minimum(i, steps // 2 - 1), 0)),
+            pl.BlockSpec((tall, ff), lambda i: (jnp.maximum(i - steps // 2, 0), 0)),
+            at(width, tall),
+        ] + [at(2 * width + g * ff, short) for g in range(groups)]
+        for front, back in experts:
+            for own, other in zip(front, back):
+                arrays += [own] + [other] * (len(parts) - 1)
         specs += parts * (2 * layers)
         shapes += [cells((layers, 1, width, ff), F32)] * 2 + [cells((layers, 1, ff, width), F32)]
         tile = pl.BlockSpec((layers, 1, tall, ff), lambda i: (0, 0, i, 0))
@@ -1670,25 +1718,19 @@
     saved = []
     for layer in range(LAYERS):
         if layer == 0:
-            *results, heads_w, outs_w, tables, params = open_attend_scatter(
-                count, columns, tokens, [w_query, w_key, w_value], w_out, small, table, begin, chosen
-            )
+            projections = [w_query, w_key, w_value]
+            inputs = [(a, EARLY) for a in (tokens, *projections)]
+            inputs += [(a, ANYWHERE) for a in (w_out, small, table)] + [(begin, EARLY), (chosen, LATE)]
+            extra = opening_shapes(count, tokens, columns, w_out, small, table)
         else:
-            results = gather_attend_scatter(
-                count,
-                layer,
-                [
-                    (x_attn, ANYWHERE), (heads_w, ANYWHERE), (outs_w, ANYWHERE), (tables, EARLY),
-                    (begin, EARLY), (hidden, LATE), (params, LATE), (chosen, LATE),
-                ],
-                rows,
-                width,
-                columns,
-            )
-        query, kv, kv_other, x_all, att, lse, middle, x_moe, share = results
-        mixed, after, x_attn, m_all, share_all, *side = gather_mix_scatter(
-            count, layer, x_moe, share, middle, params, experts_w, cotangent
-        )
+            inputs = [(a, ANYWHERE) for a in (x_attn, heads_w, outs_w)] + [(tables, EARLY), (begin, EARLY)]
+            inputs += [(hidden, LATE), (params, LATE), (chosen, LATE)]
+            extra = [], []
+        results = forward(count, layer, inputs, rows, width, columns, experts_w, cotangent, extra)
+        query, kv, kv_other, x_all, att, lse, middle, _, _ = results[:9]
+        if layer == 0:
+            heads_w, outs_w, tables, params = results[9:13]
+        mixed, after, x_attn, m_all, share_all, *side = results[9 + len(extra[0]) :]
         saved.append((hidden, x_all, query, kv, kv_other, att, lse, middle, mixed, m_all, share_all))
         hidden = after
     activations = x_attn
@@ -1703,14 +1745,15 @@
     for layer in reversed(range(LAYERS)):
         hidden, x_all, query, kv, kv_other, att, lse, middle, mixed, m_all, share_all = saved[layer]
         rides = [out_sums[layer + 1], early] if layer + 1 < LAYERS and replicas == 2 else []
-        grad_mid, d_branch, gain_two, expert_sum, g_router, *rode = gather_mix_back_scatter(
-            count, layer, d_mix, side, m_all, share_all, params, grad, middle, experts_w, rides
+        grad_mid, d_branch, gain_two, front, expert_sum, g_router, *rode = gather_mix_back_scatter(
+            count, layer, replicas, d_mix, side, m_all, share_all, params, grad, middle, experts_w, rides
         )
         if layer + 1 < LAYERS:
             d_branch, expert_sums[layer + 1] = lax.optimization_barrier(
                 (d_branch, expert_sums[layer + 1])
             )
-        expert_sums[layer] = (expert_sum, across(expert_sum))
+        peer_front = rode.pop(0) if replicas == 2 else front
+        expert_sums[layer] = ((front, peer_front), (expert_sum, across(expert_sum)))
         out_sum, grad, d_mix, side, heads = gather_attend_back_scatter(
             count, layer, d_branch, outs_w, heads_w, x_all, att, query, kv, kv_other, begin, lse, tables,
             [params, grad_mid, hidden, saved[max(layer - 1, 0)][8], g_router, gain_two],
@@ -1727,7 +1770,7 @@
     else:
         outs = [(own, jnp.zeros_like(own)) for own in out_sums]
         results = close(count, outs, arrived, peer, [activations, grad], [])
-        sums = (*results[:7], jnp.stack([own for own, _ in expert_sums]))
+        sums = (*results[:7], jnp.stack([jnp.concatenate([a, b]) for (a, _), (b, _) in expert_sums]))
         *summed, flat_sums = [lax.psum(array.astype(BF16), "rep").astype(F32) for array in sums]
         results = summed + list(results[7:])
         ff = w_gate.shape[3]

time: 699 us -> 705 us (level)
    pallas_call x8 -> x6, Pallas kernels: 624 us -> 640 us  [ring_call(): pl.pallas_call(kernel, out_shape=tuple((shape for shape, _ in outputs)) +...]
    pallas_call x1, Pallas kernels: 42.1 us -> 29.8 us  [finish_heads(): pl.pallas_call(functools.partial(finish_kernel, count, replicas), out_sha...]
where the time goes in v10:
time: 705 us; the launch traced here: 698 us
  Pallas kernels  687 us (97%)
    pallas_call x6, Pallas kernels, ring_call(): pl.pallas_call(kernel, out_shape=tuple((shape for shape, _ in outputs)) +...  640 us
    pallas_call x1, Pallas kernels, finish_heads(): pl.pallas_call(functools.partial(finish_kernel, count, replicas), out_sha...  29.8 us
    pallas_call x1, Pallas kernels, close(): pl.pallas_call(functools.partial(close_kernel, layers, count), grid=(step...  16.9 us
  transfers between devices with their start and end apart: 3, of which 0 were waited for; matrix products, arithmetic and copies ran while one was open for 0% of the time, Pallas kernels for 39%

profile of v10, /device:TPU:0, one launch (start us, length us, event | category | flops | bytes accessed | tf_op | source)
XLA Modules:
  0.0 698.4 jit_solution(7181128453861109567)
XLA Ops:
  0.7 0.7 convert_element_type.8
  1.3 0.8 convert_reduce_fusion
  2.2 0.8 select_reduce_fusion
  2.9 0.6 constant_dynamic-slice_fusion.refs_7_.refs_4_.refs_8_
  3.6 0.1 multiply_cosine_fusion
  3.7 0.6 pad_maximum_fusion.refs_6_
  4.3 1.3 fusion.8.refs_5_
  5.6 178.8 %forward.2 = (bf16[8,3,128,128]{3,2,1,0:T(8,128)(2,1)}, bf16[8,128,128]{2,1,0:T(8,128)(2,1)}, bf16[8,128,128]{2,1,0:T(8,128)(2,1)}, bf16[8,128,1536]{2,1,0:T(8,1...) custom-call(bf16[128,1536]{1,0:T(8,128)(2,1)} %refs_13_.1, ...), custom_call_target="tpu_custom_call" | custom-call | tf_op jit(solution)/shard_map/forward/pallas_call | solution.py:352
  184.4 137.7 %forward.3 = (bf16[8,3,128,128]{3,2,1,0:T(8,128)(2,1)}, bf16[8,128,128]{2,1,0:T(8,128)(2,1)}, bf16[8,128,128]{2,1,0:T(8,128)(2,1)}, bf16[8,128,1536]{2,1,0:T(8,1...) custom-call(bf16[128,1536]{1,0:T(8,128)(2,1)} %get-tuple-element.82., ...), custom_call_target="tpu_custom_call" | custom-call | tf_op jit(solution)/shard_map/forward/pallas_call | solution.py:352
  322.1 82.8 %mix_back.2 = (f32[128,1536]{1,0:T(8,128)}, bf16[128,1536]{1,0:T(8,128)(2,1)}, f32[1,1536]{1,0:T(1,128)}, bf16[768,512]{1,0:T(8,128)(2,1)}, bf16[3840,512]{1,0:T...) custom-call(bf16[128,1536]{1,0:T(8,128)(2,1)} %refs_5_.1, f32[8,128]{1,0:T(8,128)} %get-tuple-element.88.refs_1_, ...), custom_call_target="tpu_custom_call" | custom-call | tf_op jit(solution)/shard_map/mix_back/pallas_call | solution.py:352
  404.9 0.7 collective-permute-start
  405.6 78.7 %attend_back.2 = (bf16[96,1536]{1,0:T(8,128)(2,1)}, f32[128,1536]{1,0:T(8,128)}, bf16[128,1536]{1,0:T(8,128)(2,1)}, f32[8,128]{1,0:T(8,128)}, bf16[1536,384]{1,0:T(8,128)(2,1)}) custom-call(bf16[128,1536]{1,0:T(8,128)(2,1)} %get-tuple-element.92.refs_0_, bf16[2,2,96,1536]{3,2,1,0:T(8,128)(2,1)} %get-tuple-element.84.refs_2_.refs_1_, ...), custom_call_target="tpu_custom_call" | custom-call | tf_op jit(solution)/shard_map/attend_back/pallas_call | solution.py:352
  484.3 83.0 %mix_back.3 = (f32[128,1536]{1,0:T(8,128)}, bf16[128,1536]{1,0:T(8,128)(2,1)}, f32[1,1536]{1,0:T(1,128)}, bf16[768,512]{1,0:T(8,128)(2,1)}, bf16[3840,512]{1,0:T...) custom-call(bf16[128,1536]{1,0:T(8,128)(2,1)} %get-tuple-element.103, ...), custom_call_target="tpu_custom_call" | custom-call | tf_op jit(solution)/shard_map/mix_back/pallas_call | solution.py:352
  567.3 0.7 collective-permute-start.2
  568.0 0.0 collective-permute-done.refs_27_.refs_28_.refs_29_.refs_30_.refs_31_
  568.0 0.0 copy-start
  568.0 79.4 %attend_back.3 = (bf16[96,1536]{1,0:T(8,128)(2,1)}, f32[128,1536]{1,0:T(8,128)}, bf16[128,1536]{1,0:T(8,128)(2,1)}, f32[8,128]{1,0:T(8,128)}, bf16[1536,384]{1,0:T(8,128)(2,1)}) custom-call(bf16[128,1536]{1,0:T(8,128)(2,1)} %get-tuple-element.115.refs_0_, bf16[2,2,96,1536]{3,2,1,0:T(8,128)(2,1)} %get-tuple-element.84.refs_2_.refs_1_, ...), custom_call_target="tpu_custom_call" | custom-call | tf_op jit(solution)/shard_map/attend_back/pallas_call | solution.py:352
  647.4 0.0 copy-done
  647.4 1.5 collective-permute-start.1
  648.9 29.8 %finish_heads.1 = (bf16[2,8,96,384]{3,2,1,0:T(8,128)(2,1)}, bf16[8,96,384]{2,1,0:T(8,128)(2,1)}) custom-call(bf16[8,2,96,384]{3,2,1,0:T(8,128)(2,1)} %bitcast.10, bf16[8,2,96,384]{3,2,1,0:T(8,128)(2,1)} %bitcast.9, bf16[8,2,96,384]{3,2,1,0:T(8,128)(2,1)} %get-tuple-element.128.refs_2_), custom_call_target="tpu_custom_call" | custom-call | tf_op jit(solution)/shard_map/finish_heads/pallas_call | solution.py:1536
  678.7 0.0 collective-permute-done.2.refs_15_.refs_16_.refs_17_.refs_18_.refs_19_
  678.7 0.0 collective-permute-done.1.refs_1_
  678.7 0.0 copy-start.1
  678.7 0.7 copy-done.1
  679.4 16.9 %close.1 = (f32[2,96,1536]{2,1,0:T(8,128)}, f32[2,96,1536]{2,1,0:T(8,128)}, f32[2,96,512]{2,1,0:T(8,128)}, f32[2,96,512]{2,1,0:T(8,128)}, f32[2,96,16]{2,1,0:T(8...) custom-call(bf16[96,1536]{1,0:T(8,128)(2,1)} %get-tuple-element.125., ...), custom_call_target="tpu_custom_call" | custom-call | tf_op jit(solution)/shard_map/close/pallas_call | solution.py:1661
  696.3 1.6 copy.28
  (1 shorter events, 0.0 us)
Async XLA Ops:
  404.9 163.1 %collective-permute-start = (bf16[3840,512]{1,0:T(8,128)(2,1)}, bf16[3840,512]{1,0:T(8,128)(2,1)S(1)}, u32[]{:S(2)}, u32[]{:S(2)}) collective-permute-start(bf16[3840,512]{1,0:T(8,128)(2,1)} %get-tuple-element.137.refs_21_.refs_22_.refs_23_.refs_24_.refs_25_), channel_id=1, source_target_pairs={{0,16},{16,0},{1,17},{17,1},{2,18},{18,2},{3,19},{19,3},{4,20},{20... | collective-permute-start | bytes 11796488 | tf_op jit(solution)/shard_map/ppermute | solution.py:1739
  567.3 111.4 %collective-permute-start.2 = (bf16[3840,512]{1,0:T(8,128)(2,1)}, bf16[3840,512]{1,0:T(8,128)(2,1)}, u32[]{:S(2)}, u32[]{:S(2)}) collective-permute-start(bf16[3840,512]{1,0:T(8,128)(2,1)} %get-tuple-element.134.refs_9_.refs_10_.refs_11_.refs_12_.refs_13_), channel_id=1, source_target_pairs={{0,16},{16,0},{1,17},{17,1},{2,18},{18,2},{3,19},{19,3},{4,20},{20... | collective-permute-start | bytes 11796488 | tf_op jit(solution)/shard_map/ppermute | solution.py:1739
  568.0 79.4 %copy-start = (bf16[3840,512]{1,0:T(8,128)(2,1)}, bf16[3840,512]{1,0:T(8,128)(2,1)S(1)}, u32[]{:S(2)}) copy-start(bf16[3840,512]{1,0:T(8,128)(2,1)S(1)} %collective-permute-done.refs_27_.refs_28_.refs_29_.refs_30_.refs_31_) | copy-start | bytes 11796484
  647.4 31.3 %collective-permute-start.1 = (bf16[96,1536]{1,0:T(8,128)(2,1)}, bf16[96,1536]{1,0:T(8,128)(2,1)S(1)}, u32[]{:S(2)}, u32[]{:S(2)}) collective-permute-start(bf16[96,1536]{1,0:T(8,128)(2,1)} %get-tuple-element.125.refs_0_), channel_id=1, source_target_pairs={{0,16},{16,0},{1,17},{17,1},{2,18},{18,2},{3,19},{19,3},{4,20},{20... | collective-permute-start | bytes 884744 | tf_op jit(solution)/shard_map/ppermute | solution.py:1739
  678.7 0.7 copy-start.1

commit v11 on v10

--- a/solution.py
+++ b/solution.py
@@ -1043,8 +1043,12 @@
     )
 
 
+def crosses_early(layer, replicas):
+    return replicas == 2 and layer == 0
+
+
 def mix_back_kernel(count, layer, replicas, traffic, *refs):
-    crossing = replicas == 2
+    crossing = crosses_early(layer, replicas)
     inputs, outputs, scratch = split(refs, 10, 6 + crossing)
     d_ref, side_ref, m_ref, share_ref, params_ref, grad_ref, middle_ref = inputs[:7]
     mid_ref, branch_ref, gain_ref, part_ref, sum_ref, g_router_ref = outputs[:6]
@@ -1120,16 +1124,19 @@
             for index, (first, length) in enumerate(regions(half))
         ]
 
-    apart = width // 2
+    apart = width // 4
 
     def store(half):
+        parts = []
+        for first, length in regions(half):
+            if first == 0:
+                parts.append((pl.ds(0, apart), part_ref))
+                parts.append((pl.ds(apart, length - apart), sum_ref.at[pl.ds(0, length - apart)]))
+            else:
+                parts.append((pl.ds(first, length), sum_ref.at[pl.ds(first - apart, length)]))
         return [
-            pltpu.make_async_copy(
-                totals.at[0, pl.ds(first, length)],
-                sum_ref.at[pl.ds(first - apart, length)] if first else part_ref,
-                out_sem[0].at[half, index],
-            )
-            for index, (first, length) in enumerate(regions(half))
+            pltpu.make_async_copy(totals.at[0, rows], target, out_sem[0].at[half, index])
+            for index, (rows, target) in enumerate(parts)
         ]
 
     crossings = []
@@ -1163,6 +1170,13 @@
                 def _():
                     for copy in swap(h):
                         copy.wait_recv()
+
+        if place == 2:
+
+            @pl.when(s == 2)
+            def _():
+                for copy in crossings:
+                    copy.start()
 
         if place < strips:
             first = (half * strips + place) * strip
@@ -1184,7 +1198,7 @@
 
                 @pl.when(s == 2 + h)
                 def _():
-                    for copy in store(h) + (crossings if h == 0 else []):
+                    for copy in store(h):
                         copy.start()
 
     d_x, finish = ring.scatter(partial, land, scatter_sem, work)
@@ -1219,11 +1233,11 @@
             (own, OUT),
             (cells((rows, width), BF16), OUT),
             (cells((1, width), F32), OUT),
-            (cells((width // 2, ff), BF16), ANYWHERE),
-            (cells((3 * width - width // 2, ff), BF16), ANYWHERE),
+            (cells((width // 4, ff), BF16), ANYWHERE),
+            (cells((3 * width - width // 4, ff), BF16), ANYWHERE),
             (cells((2, width), F32), OUT),
         ]
-        + ([(cells((width // 2, ff), BF16), ANYWHERE)] if replicas == 2 else []),
+        + ([(cells((width // 4, ff), BF16), ANYWHERE)] if crosses_early(layer, replicas) else []),
         [everyone, everyone, land_scratch(count, rows, width), pltpu.VMEM((2 * rows, width), F32)]
         + expert_scratch(weights)
         + [
@@ -1236,7 +1250,7 @@
         ]
         + gather_sems(count, True)
         + scatter_sems(count)
-        + dmas((4,), (2, 2 + groups), (2, 2 + groups), (3,), (3,), (1,), (1,), (2, 2 + groups)),
+        + dmas((4,), (2, 2 + groups), (2, 2 + groups), (3,), (3,), (1,), (1,), (2, 3 + groups)),
         60,
         rides,
     )
@@ -1603,7 +1617,7 @@
         for layer in range(layers):
             pairs = experts_in[layer * 12 : (layer + 1) * 12]
             sums = [pairs[i][...].astype(F32) + pairs[i + 6][...].astype(F32) for i in range(6)]
-            early = pl.program_id(0) < pl.num_programs(0) // 2
+            early = pl.program_id(0) == 0
             expert_refs[0][layer, 0] = jnp.where(early, sums[0], sums[1])
             expert_refs[1][layer, 0] = sums[2]
             expert_refs[2][layer, 0] = jnp.concatenate(sums[3:], 1)
@@ -1640,15 +1654,15 @@
         (_, _), (rest, _) = experts[0]
         rows, ff = rest.shape
         tall, short = width // steps, ff // steps
-        apart = width // 2
+        apart = width // steps
         groups = (rows + apart - 2 * width) // ff
 
         def at(first, length):
             return pl.BlockSpec((length, ff), lambda i: ((first - apart) // length + i, 0))
 
         parts = [
-            pl.BlockSpec((tall, ff), lambda i: (jnp.minimum(i, steps // 2 - 1), 0)),
-            pl.BlockSpec((tall, ff), lambda i: (jnp.maximum(i - steps // 2, 0), 0)),
+            pl.BlockSpec((tall, ff), lambda i: (0, 0)),
+            pl.BlockSpec((tall, ff), lambda i: (jnp.maximum(i - 1, 0), 0)),
             at(width, tall),
         ] + [at(2 * width + g * ff, short) for g in range(groups)]
         for front, back in experts:
@@ -1741,10 +1755,11 @@
     grad = d_mix = cotangent
     (side,) = side
     expert_sums = [None] * LAYERS
+    fronts = [None] * LAYERS
     out_sums = [None] * LAYERS
     for layer in reversed(range(LAYERS)):
         hidden, x_all, query, kv, kv_other, att, lse, middle, mixed, m_all, share_all = saved[layer]
-        rides = [out_sums[layer + 1], early] if layer + 1 < LAYERS and replicas == 2 else []
+        rides = [out_sums[layer + 1], early, fronts[layer + 1][0]] if layer + 1 < LAYERS and replicas == 2 else []
         grad_mid, d_branch, gain_two, front, expert_sum, g_router, *rode = gather_mix_back_scatter(
             count, layer, replicas, d_mix, side, m_all, share_all, params, grad, middle, experts_w, rides
         )
@@ -1752,8 +1767,10 @@
             d_branch, expert_sums[layer + 1] = lax.optimization_barrier(
                 (d_branch, expert_sums[layer + 1])
             )
-        peer_front = rode.pop(0) if replicas == 2 else front
-        expert_sums[layer] = ((front, peer_front), (expert_sum, across(expert_sum)))
+        fronts[layer] = (front, rode.pop(0) if crosses_early(layer, replicas) else front)
+        if rides:
+            fronts[layer + 1] = (fronts[layer + 1][0], rode[2])
+        expert_sums[layer] = (expert_sum, across(expert_sum))
         out_sum, grad, d_mix, side, heads = gather_attend_back_scatter(
             count, layer, d_branch, outs_w, heads_w, x_all, att, query, kv, kv_other, begin, lse, tables,
             [params, grad_mid, hidden, saved[max(layer - 1, 0)][8], g_router, gain_two],
@@ -1765,12 +1782,12 @@
     if replicas == 2:
         outs = list(zip(out_sums, [across(out_sums[0]), rode[0]]))
         *results, g_gate, g_up, g_down = close(
-            count, outs, arrived, peer, [activations, grad], expert_sums
+            count, outs, arrived, peer, [activations, grad], list(zip(fronts, expert_sums))
         )
     else:
         outs = [(own, jnp.zeros_like(own)) for own in out_sums]
         results = close(count, outs, arrived, peer, [activations, grad], [])
-        sums = (*results[:7], jnp.stack([jnp.concatenate([a, b]) for (a, _), (b, _) in expert_sums]))
+        sums = (*results[:7], jnp.stack([jnp.concatenate([a, b]) for (a, _), (b, _) in zip(fronts, expert_sums)]))
         *summed, flat_sums = [lax.psum(array.astype(BF16), "rep").astype(F32) for array in sums]
         results = summed + list(results[7:])
         ff = w_gate.shape[3]

time: 705 us -> 689 us (0.977)
  Pallas kernels: 687 us -> 671 us
    pallas_call x6, Pallas kernels: 640 us -> 621 us  [ring_call(): pl.pallas_call(kernel, out_shape=tuple((shape for shape, _ in outputs)) +...]
where the time goes in v11:
time: 689 us; the launch traced here: 683 us
  Pallas kernels  671 us (97%)
    pallas_call x6, Pallas kernels, ring_call(): pl.pallas_call(kernel, out_shape=tuple((shape for shape, _ in outputs)) +...  621 us
    pallas_call x1, Pallas kernels, finish_heads(): pl.pallas_call(functools.partial(finish_kernel, count, replicas), out_sha...  33.9 us
    pallas_call x1, Pallas kernels, close(): pl.pallas_call(functools.partial(close_kernel, layers, count), grid=(step...  16.5 us
  transfers between devices with their start and end apart: 3, of which 0 were waited for; matrix products, arithmetic and copies ran while one was open for 0% of the time, Pallas kernels for 39%

profile of v11, /device:TPU:0, one launch (start us, length us, event | category | flops | bytes accessed | tf_op | source)
XLA Modules:
  0.0 683.4 jit_solution(10056697852432550169)
XLA Ops:
  0.7 0.7 convert_element_type.8
  1.3 0.8 convert_reduce_fusion
  2.2 0.8 select_reduce_fusion
  2.9 0.6 constant_dynamic-slice_fusion.refs_7_.refs_4_.refs_8_
  3.6 0.1 multiply_cosine_fusion
  3.7 0.6 pad_maximum_fusion.refs_6_
  4.3 1.3 fusion.8.refs_5_
  5.6 178.8 %forward.2 = (bf16[8,3,128,128]{3,2,1,0:T(8,128)(2,1)}, bf16[8,128,128]{2,1,0:T(8,128)(2,1)}, bf16[8,128,128]{2,1,0:T(8,128)(2,1)}, bf16[8,128,1536]{2,1,0:T(8,1...) custom-call(bf16[128,1536]{1,0:T(8,128)(2,1)} %refs_13_.1, ...), custom_call_target="tpu_custom_call" | custom-call | tf_op jit(solution)/shard_map/forward/pallas_call | solution.py:352
  184.5 137.7 %forward.3 = (bf16[8,3,128,128]{3,2,1,0:T(8,128)(2,1)}, bf16[8,128,128]{2,1,0:T(8,128)(2,1)}, bf16[8,128,128]{2,1,0:T(8,128)(2,1)}, bf16[8,128,1536]{2,1,0:T(8,1...) custom-call(bf16[128,1536]{1,0:T(8,128)(2,1)} %get-tuple-element.80., ...), custom_call_target="tpu_custom_call" | custom-call | tf_op jit(solution)/shard_map/forward/pallas_call | solution.py:352
  322.2 73.4 %mix_back.2 = (f32[128,1536]{1,0:T(8,128)}, bf16[128,1536]{1,0:T(8,128)(2,1)}, f32[1,1536]{1,0:T(1,128)}, bf16[384,512]{1,0:T(8,128)(2,1)}, bf16[4224,512]{1,0:T(8,128)(2,1)}, /*index=5*/f32[2,1536]{1,0:T(2,128)}) custom-call(bf16[128,1536]{1,0:T(8,128)(2,1)} %refs_5_.1, f32[8,128]{1,0:T(8,128)} %get-tuple-element.86.refs_1_, ...), custom_call_target="tpu_custom_call" | custom-call | tf_op jit(solution)/shard_map/mix_back/pallas_call | solution.py:352
  395.5 1.6 collective-permute-start
  397.1 78.7 %attend_back.2 = (bf16[96,1536]{1,0:T(8,128)(2,1)}, f32[128,1536]{1,0:T(8,128)}, bf16[128,1536]{1,0:T(8,128)(2,1)}, f32[8,128]{1,0:T(8,128)}, bf16[1536,384]{1,0:T(8,128)(2,1)}) custom-call(bf16[128,1536]{1,0:T(8,128)(2,1)} %get-tuple-element.90.refs_0_, bf16[2,2,96,1536]{3,2,1,0:T(8,128)(2,1)} %get-tuple-element.82.refs_2_.refs_1_, ...), custom_call_target="tpu_custom_call" | custom-call | tf_op jit(solution)/shard_map/attend_back/pallas_call | solution.py:352
  475.8 73.5 %mix_back.3 = (f32[128,1536]{1,0:T(8,128)}, bf16[128,1536]{1,0:T(8,128)(2,1)}, f32[1,1536]{1,0:T(1,128)}, bf16[384,512]{1,0:T(8,128)(2,1)}, bf16[4224,512]{1,0:T...) custom-call(bf16[128,1536]{1,0:T(8,128)(2,1)} %get-tuple-element.101, ...), custom_call_target="tpu_custom_call" | custom-call | tf_op jit(solution)/shard_map/mix_back/pallas_call | solution.py:352
  549.3 0.7 collective-permute-start.2
  550.1 0.0 collective-permute-done.refs_27_.refs_28_.refs_29_.refs_30_.refs_31_
  550.1 78.7 %attend_back.3 = (bf16[96,1536]{1,0:T(8,128)(2,1)}, f32[128,1536]{1,0:T(8,128)}, bf16[128,1536]{1,0:T(8,128)(2,1)}, f32[8,128]{1,0:T(8,128)}, bf16[1536,384]{1,0:T(8,128)(2,1)}) custom-call(bf16[128,1536]{1,0:T(8,128)(2,1)} %get-tuple-element.112.refs_0_, bf16[2,2,96,1536]{3,2,1,0:T(8,128)(2,1)} %get-tuple-element.82.refs_2_.refs_1_, ...), custom_call_target="tpu_custom_call" | custom-call | tf_op jit(solution)/shard_map/attend_back/pallas_call | solution.py:352
  628.8 1.4 collective-permute-start.1
  630.2 33.9 %finish_heads.1 = (bf16[2,8,96,384]{3,2,1,0:T(8,128)(2,1)}, bf16[8,96,384]{2,1,0:T(8,128)(2,1)}) custom-call(bf16[8,2,96,384]{3,2,1,0:T(8,128)(2,1)} %bitcast.10, bf16[8,2,96,384]{3,2,1,0:T(8,128)(2,1)} %bitcast.9, bf16[8,2,96,384]{3,2,1,0:T(8,128)(2,1)} %get-tuple-element.125.refs_2_), custom_call_target="tpu_custom_call" | custom-call | tf_op jit(solution)/shard_map/finish_heads/pallas_call | solution.py:1550
  664.1 0.0 collective-permute-done.2.refs_15_.refs_16_.refs_17_.refs_18_.refs_19_
  664.1 0.0 collective-permute-done.1.refs_1_
  664.1 0.0 copy-start
  664.1 0.7 copy-done
  664.8 16.5 %close.1 = (f32[2,96,1536]{2,1,0:T(8,128)}, f32[2,96,1536]{2,1,0:T(8,128)}, f32[2,96,512]{2,1,0:T(8,128)}, f32[2,96,512]{2,1,0:T(8,128)}, f32[2,96,16]{2,1,0:T(8...) custom-call(bf16[96,1536]{1,0:T(8,128)(2,1)} %get-tuple-element.122., ...), custom_call_target="tpu_custom_call" | custom-call | tf_op jit(solution)/shard_map/close/pallas_call | solution.py:1675
  681.3 1.6 copy.28
  (1 shorter events, 0.0 us)
Async XLA Ops:
  395.5 154.5 %collective-permute-start = (bf16[4224,512]{1,0:T(8,128)(2,1)}, bf16[4224,512]{1,0:T(8,128)(2,1)}, u32[]{:S(2)}, u32[]{:S(2)}) collective-permute-start(bf16[4224,512]{1,0:T(8,128)(2,1)} %get-tuple-element.133.refs_21_.refs_22_.refs_23_.refs_24_.refs_25_), channel_id=1, source_target_pairs={{0,16},{16,0},{1,17},{17,1},{2,18},{18,2},{3,19},{19,3},{4,20},{20... | collective-permute-start | bytes 12976136 | tf_op jit(solution)/shard_map/ppermute | solution.py:1753
  549.3 114.8 %collective-permute-start.2 = (bf16[4224,512]{1,0:T(8,128)(2,1)}, bf16[4224,512]{1,0:T(8,128)(2,1)}, u32[]{:S(2)}, u32[]{:S(2)}) collective-permute-start(bf16[4224,512]{1,0:T(8,128)(2,1)} %get-tuple-element.131.refs_9_.refs_10_.refs_11_.refs_12_.refs_13_), channel_id=1, source_target_pairs={{0,16},{16,0},{1,17},{17,1},{2,18},{18,2},{3,19},{19,3},{4,20},{20... | collective-permute-start | bytes 12976136 | tf_op jit(solution)/shard_map/ppermute | solution.py:1753
  628.8 35.3 %collective-permute-start.1 = (bf16[96,1536]{1,0:T(8,128)(2,1)}, bf16[96,1536]{1,0:T(8,128)(2,1)S(1)}, u32[]{:S(2)}, u32[]{:S(2)}) collective-permute-start(bf16[96,1536]{1,0:T(8,128)(2,1)} %get-tuple-element.122.refs_0_), channel_id=1, source_target_pairs={{0,16},{16,0},{1,17},{17,1},{2,18},{18,2},{3,19},{19,3},{4,20},{20... | collective-permute-start | bytes 884744 | tf_op jit(solution)/shard_map/ppermute | solution.py:1753
  664.1 0.7 copy-start

commit v12 on v11

--- a/solution.py
+++ b/solution.py
@@ -1617,7 +1617,7 @@
         for layer in range(layers):
             pairs = experts_in[layer * 12 : (layer + 1) * 12]
             sums = [pairs[i][...].astype(F32) + pairs[i + 6][...].astype(F32) for i in range(6)]
-            early = pl.program_id(0) == 0
+            early = pl.program_id(0) < pl.num_programs(0) // 4
             expert_refs[0][layer, 0] = jnp.where(early, sums[0], sums[1])
             expert_refs[1][layer, 0] = sums[2]
             expert_refs[2][layer, 0] = jnp.concatenate(sums[3:], 1)
@@ -1626,7 +1626,7 @@
 def close(count, outs, mine, peer, rows_out, experts):
     layers = len(outs)
     shard, width = outs[0][0].shape
-    steps = 4
+    steps = 8
 
     def whole(shape):
         return pl.BlockSpec(shape, lambda i: (0,) * len(shape))
@@ -1654,15 +1654,15 @@
         (_, _), (rest, _) = experts[0]
         rows, ff = rest.shape
         tall, short = width // steps, ff // steps
-        apart = width // steps
+        apart = width // 4
         groups = (rows + apart - 2 * width) // ff
 
         def at(first, length):
             return pl.BlockSpec((length, ff), lambda i: ((first - apart) // length + i, 0))
 
         parts = [
-            pl.BlockSpec((tall, ff), lambda i: (0, 0)),
-            pl.BlockSpec((tall, ff), lambda i: (jnp.maximum(i - 1, 0), 0)),
+            pl.BlockSpec((tall, ff), lambda i: (jnp.minimum(i, apart // tall - 1), 0)),
+            pl.BlockSpec((tall, ff), lambda i: (jnp.maximum(i - apart // tall, 0), 0)),
             at(width, tall),
         ] + [at(2 * width + g * ff, short) for g in range(groups)]
         for front, back in experts:

time: 689 us -> 691 us (level)
  no operation moved by 1% of the time
where the time goes in v12:
time: 691 us; the launch traced here: 685 us
  Pallas kernels  673 us (97%)
    pallas_call x6, Pallas kernels, ring_call(): pl.pallas_call(kernel, out_shape=tuple((shape for shape, _ in outputs)) +...  621 us
    pallas_call x1, Pallas kernels, finish_heads(): pl.pallas_call(functools.partial(finish_kernel, count, replicas), out_sha...  33.9 us
    pallas_call x1, Pallas kernels, close(): pl.pallas_call(functools.partial(close_kernel, layers, count), grid=(step...  18.2 us
  transfers between devices with their start and end apart: 3, of which 0 were waited for; matrix products, arithmetic and copies ran while one was open for 0% of the time, Pallas kernels for 39%

profile of v12, /device:TPU:0, one launch (start us, length us, event | category | flops | bytes accessed | tf_op | source)
XLA Modules:
  0.0 684.9 jit_solution(2814580905455152254)
XLA Ops:
  0.7 0.7 convert_element_type.8
  1.3 0.8 convert_reduce_fusion
  2.2 0.8 select_reduce_fusion
  2.9 0.6 constant_dynamic-slice_fusion.refs_7_.refs_4_.refs_8_
  3.6 0.1 multiply_cosine_fusion
  3.7 0.6 pad_maximum_fusion.refs_6_
  4.3 1.3 fusion.8.refs_5_
  5.6 178.8 %forward.2 = (bf16[8,3,128,128]{3,2,1,0:T(8,128)(2,1)}, bf16[8,128,128]{2,1,0:T(8,128)(2,1)}, bf16[8,128,128]{2,1,0:T(8,128)(2,1)}, bf16[8,128,1536]{2,1,0:T(8,1...) custom-call(bf16[128,1536]{1,0:T(8,128)(2,1)} %refs_13_.1, ...), custom_call_target="tpu_custom_call" | custom-call | tf_op jit(solution)/shard_map/forward/pallas_call | solution.py:352
  184.5 137.7 %forward.3 = (bf16[8,3,128,128]{3,2,1,0:T(8,128)(2,1)}, bf16[8,128,128]{2,1,0:T(8,128)(2,1)}, bf16[8,128,128]{2,1,0:T(8,128)(2,1)}, bf16[8,128,1536]{2,1,0:T(8,1...) custom-call(bf16[128,1536]{1,0:T(8,128)(2,1)} %get-tuple-element.80., ...), custom_call_target="tpu_custom_call" | custom-call | tf_op jit(solution)/shard_map/forward/pallas_call | solution.py:352
  322.2 73.4 %mix_back.2 = (f32[128,1536]{1,0:T(8,128)}, bf16[128,1536]{1,0:T(8,128)(2,1)}, f32[1,1536]{1,0:T(1,128)}, bf16[384,512]{1,0:T(8,128)(2,1)}, bf16[4224,512]{1,0:T(8,128)(2,1)}, /*index=5*/f32[2,1536]{1,0:T(2,128)}) custom-call(bf16[128,1536]{1,0:T(8,128)(2,1)} %refs_5_.1, f32[8,128]{1,0:T(8,128)} %get-tuple-element.86.refs_1_, ...), custom_call_target="tpu_custom_call" | custom-call | tf_op jit(solution)/shard_map/mix_back/pallas_call | solution.py:352
  395.5 1.4 collective-permute-start
  397.0 78.7 %attend_back.2 = (bf16[96,1536]{1,0:T(8,128)(2,1)}, f32[128,1536]{1,0:T(8,128)}, bf16[128,1536]{1,0:T(8,128)(2,1)}, f32[8,128]{1,0:T(8,128)}, bf16[1536,384]{1,0:T(8,128)(2,1)}) custom-call(bf16[128,1536]{1,0:T(8,128)(2,1)} %get-tuple-element.90.refs_0_, bf16[2,2,96,1536]{3,2,1,0:T(8,128)(2,1)} %get-tuple-element.82.refs_2_.refs_1_, ...), custom_call_target="tpu_custom_call" | custom-call | tf_op jit(solution)/shard_map/attend_back/pallas_call | solution.py:352
  475.7 73.5 %mix_back.3 = (f32[128,1536]{1,0:T(8,128)}, bf16[128,1536]{1,0:T(8,128)(2,1)}, f32[1,1536]{1,0:T(1,128)}, bf16[384,512]{1,0:T(8,128)(2,1)}, bf16[4224,512]{1,0:T...) custom-call(bf16[128,1536]{1,0:T(8,128)(2,1)} %get-tuple-element.101, ...), custom_call_target="tpu_custom_call" | custom-call | tf_op jit(solution)/shard_map/mix_back/pallas_call | solution.py:352
  549.2 0.8 collective-permute-start.2
  549.9 0.0 collective-permute-done.refs_27_.refs_28_.refs_29_.refs_30_.refs_31_
  550.0 78.7 %attend_back.3 = (bf16[96,1536]{1,0:T(8,128)(2,1)}, f32[128,1536]{1,0:T(8,128)}, bf16[128,1536]{1,0:T(8,128)(2,1)}, f32[8,128]{1,0:T(8,128)}, bf16[1536,384]{1,0:T(8,128)(2,1)}) custom-call(bf16[128,1536]{1,0:T(8,128)(2,1)} %get-tuple-element.112.refs_0_, bf16[2,2,96,1536]{3,2,1,0:T(8,128)(2,1)} %get-tuple-element.82.refs_2_.refs_1_, ...), custom_call_target="tpu_custom_call" | custom-call | tf_op jit(solution)/shard_map/attend_back/pallas_call | solution.py:352
  628.7 1.4 collective-permute-start.1
  630.1 33.9 %finish_heads.1 = (bf16[2,8,96,384]{3,2,1,0:T(8,128)(2,1)}, bf16[8,96,384]{2,1,0:T(8,128)(2,1)}) custom-call(bf16[8,2,96,384]{3,2,1,0:T(8,128)(2,1)} %bitcast.10, bf16[8,2,96,384]{3,2,1,0:T(8,128)(2,1)} %bitcast.9, bf16[8,2,96,384]{3,2,1,0:T(8,128)(2,1)} %get-tuple-element.125.refs_2_), custom_call_target="tpu_custom_call" | custom-call | tf_op jit(solution)/shard_map/finish_heads/pallas_call | solution.py:1550
  664.0 0.0 collective-permute-done.2.refs_15_.refs_16_.refs_17_.refs_18_.refs_19_
  664.0 0.0 collective-permute-done.1.refs_1_
  664.0 0.0 copy-start
  664.0 0.7 copy-done
  664.7 18.2 %close.1 = (f32[2,96,1536]{2,1,0:T(8,128)}, f32[2,96,1536]{2,1,0:T(8,128)}, f32[2,96,512]{2,1,0:T(8,128)}, f32[2,96,512]{2,1,0:T(8,128)}, f32[2,96,16]{2,1,0:T(8...) custom-call(bf16[96,1536]{1,0:T(8,128)(2,1)} %get-tuple-element.122., ...), custom_call_target="tpu_custom_call" | custom-call | tf_op jit(solution)/shard_map/close/pallas_call | solution.py:1675
  682.9 1.6 copy.28
  (1 shorter events, 0.0 us)
Async XLA Ops:
  395.5 154.4 %collective-permute-start = (bf16[4224,512]{1,0:T(8,128)(2,1)}, bf16[4224,512]{1,0:T(8,128)(2,1)}, u32[]{:S(2)}, u32[]{:S(2)}) collective-permute-start(bf16[4224,512]{1,0:T(8,128)(2,1)} %get-tuple-element.133.refs_21_.refs_22_.refs_23_.refs_24_.refs_25_), channel_id=1, source_target_pairs={{0,16},{16,0},{1,17},{17,1},{2,18},{18,2},{3,19},{19,3},{4,20},{20... | collective-permute-start | bytes 12976136 | tf_op jit(solution)/shard_map/ppermute | solution.py:1753
  549.2 114.8 %collective-permute-start.2 = (bf16[4224,512]{1,0:T(8,128)(2,1)}, bf16[4224,512]{1,0:T(8,128)(2,1)}, u32[]{:S(2)}, u32[]{:S(2)}) collective-permute-start(bf16[4224,512]{1,0:T(8,128)(2,1)} %get-tuple-element.131.refs_9_.refs_10_.refs_11_.refs_12_.refs_13_), channel_id=1, source_target_pairs={{0,16},{16,0},{1,17},{17,1},{2,18},{18,2},{3,19},{19,3},{4,20},{20... | collective-permute-start | bytes 12976136 | tf_op jit(solution)/shard_map/ppermute | solution.py:1753
  628.7 35.3 %collective-permute-start.1 = (bf16[96,1536]{1,0:T(8,128)(2,1)}, bf16[96,1536]{1,0:T(8,128)(2,1)S(1)}, u32[]{:S(2)}, u32[]{:S(2)}) collective-permute-start(bf16[96,1536]{1,0:T(8,128)(2,1)} %get-tuple-element.122.refs_0_), channel_id=1, source_target_pairs={{0,16},{16,0},{1,17},{17,1},{2,18},{18,2},{3,19},{19,3},{4,20},{20... | collective-permute-start | bytes 884744 | tf_op jit(solution)/shard_map/ppermute | solution.py:1753
  664.0 0.7 copy-start
